TPU v7x, 512 devices: a whole 4x8x8 slice. The times are simulated.
512 devices in a mesh: section: 8 (over z), dp: 32 (over y_lo, x, core), seq: 2 (over y_hi).
Axes of the slice: x: 4, y: 8 (y_hi: 2, y_lo: 4; y = y_hi * 4 + y_lo), z: 8, core: 2. Of those that a mesh axis runs over, the one named last changes fastest.
Arguments:
- section_input: bfloat16 [8, 2048, 5120], P('section', 'seq', 'dp'), as said below
- norm_gain: bfloat16 [8, 5120], P('section', 'dp'), may hold values from 0.5 to 2
- qkv_weight: bfloat16 [8, 5120, 12288], P('section', 'seq', 'dp'), as said below
- out_weight: bfloat16 [8, 4096, 5120], P('section', None, 'dp'), may hold values from -0.5 to 0.5
- random_blocks: int32 [8, 32, 3], P('section', 'seq'), may hold values from 0 to 31
- global_blocks: int32 [8, 2], P('section'), may hold values from 0 to 31, as said below
Outputs:
- handed_on: bfloat16 [8, 2048, 5120], P('section', 'seq', 'dp')
Inputs may be any that keep to these rules, and one draw needn't show every extreme that they name: `section_input`: real values, each token row and each feature column with its own scale. `qkv_weight`: real values of projections. `global_blocks`: 2 different block numbers for each section; the last section's document has the first and the last block as its global blocks.
All inputs are finite; a program needn't handle non-finite values.
Results may differ from a plain program's by a relative error of at most 0.0058.
Values may be sent and summed in bfloat16 or wider, within the bound.
No kernel may reach another device: no remote copies, remote signals or barrier semaphores. Data moves between devices by JAX's collectives and lax.ppermute only.
A program may use at most 64 MiB of HBM per device.

v0:
```python
import math

import jax
import jax.numpy as jnp
from jax import lax
from jax.sharding import PartitionSpec as P

BLOCK = 64


def shifted(block, axis, distance):
    devices = range(lax.axis_size(axis))
    route = [((i - distance) % len(devices), i) for i in devices]
    return lax.ppermute(block, axis, route)


def block_mask(query_ids, random_rows, global_ids, key_count):
    query_col = query_ids[:, None]
    key_ids = jnp.arange(key_count, dtype=jnp.int32)[None, :]
    adjacent = jnp.abs(query_col - key_ids) <= 1
    key_global = jnp.any(key_ids[:, :, None] == global_ids[None, None, :], axis=2)
    query_global = jnp.any(query_col[:, :, None] == global_ids[None, None, :], axis=2)
    chosen = jnp.any(random_rows[:, None, :] == key_ids[:, :, None], axis=2)
    return adjacent | key_global | query_global | chosen


def sparse_attention(query, keys, values, allowed, block_size):
    scores = lax.dot_general(
        query, keys, (((1,), (1,)), ((), ())), preferred_element_type=jnp.float32
    )
    scores = scores * (1.0 / math.sqrt(query.shape[1]))
    query_blocks, key_blocks = allowed.shape
    scores = scores.reshape(query_blocks, block_size, key_blocks, block_size)
    live = allowed[:, None, :, None]
    scores = jnp.where(live, scores, -1e30)
    highest = jnp.max(scores, axis=(2, 3), keepdims=True)
    weights = jnp.where(live, jnp.exp(scores - highest), 0.0)
    totals = jnp.sum(weights, axis=(2, 3), keepdims=True)
    probs = (
        (weights / totals)
        .reshape(query_blocks * block_size, key_blocks * block_size)
        .astype(jnp.bfloat16)
    )
    return jnp.dot(probs, values, preferred_element_type=jnp.float32).astype(jnp.bfloat16)


def shards(section_input, norm_gain, qkv_weight, out_weight, random_blocks, global_blocks):
    token_rows = section_input[0]
    token_count = token_rows.shape[0]
    width = norm_gain.shape[1] * lax.axis_size("dp")
    as_float = token_rows.astype(jnp.float32)
    local_squares = jnp.sum(as_float * as_float, axis=1)
    total_squares = lax.psum(local_squares, "dp")
    factor = lax.rsqrt(total_squares / width + 1e-05)[:, None]
    normed_part = (as_float * factor * norm_gain[0].astype(jnp.float32)).astype(jnp.bfloat16)
    normed = lax.all_gather(normed_part, "dp", axis=1, tiled=True)
    weight_half = qkv_weight[0]
    joined = jnp.dot(
        normed,
        lax.all_gather(weight_half, "seq", axis=0, tiled=True),
        preferred_element_type=jnp.float32,
    )
    head_size = joined.shape[1] // 3
    query = joined[:, :head_size].astype(jnp.bfloat16)
    keys_values = joined[:, head_size:].astype(jnp.bfloat16)
    document_kv = lax.all_gather(keys_values, "seq", axis=0, tiled=True)
    keys = document_kv[:, :head_size]
    values = document_kv[:, head_size:]
    own_blocks = token_count // BLOCK
    query_ids = lax.axis_index("seq") * own_blocks + jnp.arange(own_blocks, dtype=jnp.int32)
    allowed = block_mask(
        query_ids, random_blocks[0], global_blocks[0], document_kv.shape[0] // BLOCK
    )
    attended = sparse_attention(query, keys, values, allowed, BLOCK)
    out_columns = out_weight[0]
    added = jnp.dot(
        lax.all_gather(attended, "dp", axis=1, tiled=True),
        out_columns,
        preferred_element_type=jnp.float32,
    )
    result = (token_rows.astype(jnp.float32) + added).astype(jnp.bfloat16)
    return shifted(result[None], "section", 1)


def solution(mesh):
    placed = (
        P("section", "seq", "dp"),
        P("section", "dp"),
        P("section", "seq", "dp"),
        P("section", None, "dp"),
        P("section", "seq", None),
        P("section", None),
    )
    return jax.shard_map(
        shards, mesh=mesh, in_specs=placed, out_specs=P("section", "seq", "dp"), check_vma=False
    )
```

profile of v0, /device:TPU:1, one launch (start us, length us, event | category | flops | bytes accessed | tf_op | source)
XLA Modules:
  0.0 376.0 jit_solution(2593649868991785877)
XLA Ops:
  6.5 0.7 all-gather.12.cloned.1.call-update
  7.3 0.0 all-gather.6.cloned.1.call-start
  7.3 0.7 mul.43
  8.0 1.1 fusion.20
  9.0 84.4 %psum.7 = f32[1024]{0:T(1024)S(1)} all-reduce(f32[1024]{0:T(1024)S(1)} %fusion.20), channel_id=1, replica_groups=mesh['section'=8,'dp'=32,'seq'=2] {'dp'}, use_global_device_ids=true, to_apply=%region_4.0 | all-reduce | flops 1024 | bytes 8192 | tf_op jit(solution)/shard_map/psum | solution.py:53
  93.4 1.8 fusion.22
  95.2 0.0 all-gather.6.cloned.1.call-update
  95.2 0.0 copy-start.3
  95.3 0.0 all-gather.8.cloned.1.call-start
  95.3 25.4 %all-gather.12.cloned.1.call-done = bf16[1,5120,384]{2,1,0:T(8,128)(2,1)} async-done(((bf16[1,2560,384]{2,1,0:T(8,128)(2,1)}), bf16[1,5120,384]{2,1,0:T(8,128)(2,1)}) %all-gather.12.cloned.1.call-update) | async-done | bytes 3932176 | tf_op jit(solution)/shard_map/all_gather | solution.py:60
  120.8 76.5 %all-gather.6.cloned.1.call-done = bf16[1024,5120]{0,1:T(8,128)(2,1)} async-done(((bf16[1024,160]{0,1:T(8,128)(2,1)}), bf16[1024,5120]{0,1:T(8,128)(2,1)}) %all-gather.6.cloned.1.call-update) | async-done | bytes 10485776 | tf_op jit(solution)/shard_map/all_gather | solution.py:56
  197.3 9.5 %fusion.5 = bf16[1024,384]{1,0:T(8,128)(2,1)S(1)} fusion(bf16[1024,5120]{0,1:T(8,128)(2,1)} %all-gather.6.cloned.1.call-done, bf16[1,5120,384]{2,1,0:T(8,128)(2,1)} %all-gather.12.cloned.1.call-done), kind=kOutput, calls=%fused_computation.8 | convolution fusion | flops 4026925056 | bytes 15204352 | tf_op jit(solution)/shard_map/dot_general | solution.py:58
  206.8 0.9 copy-done.1
  207.7 0.8 slice.19
  208.5 0.0 all-gather.8.cloned.1.call-update
  208.6 0.2 all-gather.10.cloned.1.call-start
  208.9 0.1 compare_reduce_fusion.1
  208.9 0.1 compare_reduce_fusion
  209.0 0.1 fusion.27
  209.1 0.1 fusion.30
  209.2 3.1 broadcast_in_dim.30
  212.3 11.1 %broadcast_in_dim.31 = pred[1024,2048]{1,0:T(32,128)(4,1)S(1)} reshape(pred[16,64,32,64]{3,2,1,0:T(32,128)(4,1)} %broadcast_in_dim.30) | data formatting | bytes 4194304 | tf_op jit(solution)/shard_map/jit(_where)/broadcast_in_dim | solution.py:37
  223.4 28.7 %all-gather.8.cloned.1.call-done = bf16[2048,256]{1,0:T(8,128)(2,1)} async-done(((bf16[1024,256]{1,0:T(8,128)(2,1)}), bf16[2048,256]{1,0:T(8,128)(2,1)}) %all-gather.8.cloned.1.call-update) | async-done | bytes 1048592 | tf_op jit(solution)/shard_map/all_gather | solution.py:66
  252.1 3.1 fusion
  255.2 3.0 fusion.1
  258.2 3.9 %fusion.16 = bf16[1024,128]{1,0:T(8,128)(2,1)} fusion(pred[1024,2048]{1,0:T(32,128)(4,1)S(1)} %broadcast_in_dim.31, f32[1024,2048]{1,0:T(8,128)S(1)} %get-tuple-element.6, f32[1024]{0:T(1024)S(1)} %fusion.1, f32[1024]{0:T(1024)S(1)} %get-tuple-element.5, bf16[2048,256]{1,0:T(8,128)(2,1)S(1)} %copy-done.2), kind=kOutput, calls=%fused_computation.13 | convolution fusion | flops 549584896 | bytes 11280384 | tf_op jit(solution)/shard_map/dot_general | solution.py:44
  262.1 0.0 all-gather.10.cloned.1.call-update
  262.2 87.4 %all-gather.10.cloned.1.call-done = bf16[1024,4096]{1,0:T(8,128)(2,1)} async-done(((bf16[1024,128]{1,0:T(8,128)(2,1)}), bf16[1024,4096]{1,0:T(8,128)(2,1)}) %all-gather.10.cloned.1.call-update) | async-done | bytes 8388624 | tf_op jit(solution)/shard_map/all_gather | solution.py:77
  349.6 6.3 %fusion.17 = bf16[1,1024,160]{1,2,0:T(8,128)(2,1)S(1)} fusion(bf16[1024,4096]{1,0:T(8,128)(2,1)} %all-gather.10.cloned.1.call-done, bf16[1,4096,160]{1,2,0:T(8,128)(2,1)S(1)} %copy-done, bf16[1,1024,160]{1,2,0:T(8,128)(2,1)} %param.6), kind=kOutput, calls=%fused_computation.14 | convolution fusion | flops 1342668800 | bytes 10354688 | tf_op jit(solution)/shard_map/dot_general | solution.py:76
  355.9 2.7 collective-permute-start
  358.6 10.2 %collective-permute-done = bf16[1,1024,160]{1,2,0:T(8,128)(2,1)S(1)} collective-permute-done((bf16[1,1024,160]{1,2,0:T(8,128)(2,1)S(1)}, bf16[1,1024,160]{1,2,0:T(8,128)(2,1)S(1)}, u32[]{:S(2)}, u32[]{:S(2)}) %collective-permute-start) | collective-permute-done | bytes 327712 | tf_op jit(solution)/shard_map/ppermute | solution.py:14
  368.8 0.7 copy.15
  (12 shorter events, 0.0 us)
Async XLA Ops:
  6.5 343.1 %copy-start = (bf16[1,4096,160]{1,2,0:T(8,128)(2,1)S(1)}, bf16[1,4096,160]{1,2,0:T(8,128)(2,1)}, u32[]{:S(2)}) copy-start(bf16[1,4096,160]{1,2,0:T(8,128)(2,1)} %param.9) | copy-start | bytes 3932164
  6.5 114.2 %all-gather.12.cloned.1.call-start = ((), (), s32[]{:S(2)}) async-start(), calls=%async_computation.3 | async-start | bytes 5898240 | tf_op jit(solution)/shard_map/all_gather | solution.py:60
  7.3 190.0 %all-gather.6.cloned.1.call-start = ((), (), s32[]{:S(2)}) async-start(), calls=%async_computation | async-start | bytes 10813440 | tf_op jit(solution)/shard_map/all_gather | solution.py:56
  95.2 113.6 %copy-start.3 = (s32[1,16,3]{1,0,2:T(1,128)S(1)}, s32[1,16,3]{1,0,2:T(1,128)}, u32[]{:S(2)}) copy-start(s32[1,16,3]{1,0,2:T(1,128)} %param.10) | copy-start | bytes 580
  95.3 113.6 %copy-start.4 = (s32[1,2]{1,0:T(1,128)S(1)}, s32[1,2]{1,0:T(1,128)}, u32[]{:S(2)}) copy-start(s32[1,2]{1,0:T(1,128)} %param.11) | copy-start | bytes 28
  95.3 156.9 %all-gather.8.cloned.1.call-start = ((), (), s32[]{:S(2)}) async-start(), calls=%async_computation.1 | async-start | bytes 1572864 | tf_op jit(solution)/shard_map/all_gather | solution.py:66
  206.8 0.9 copy-start.1
  208.6 141.0 %all-gather.10.cloned.1.call-start = ((), (), s32[]{:S(2)}) async-start(), calls=%async_computation.2 | async-start | bytes 8650752 | tf_op jit(solution)/shard_map/all_gather | solution.py:77
  255.2 3.0 copy-start.2
  355.9 12.9 %collective-permute-start = (bf16[1,1024,160]{1,2,0:T(8,128)(2,1)S(1)}, bf16[1,1024,160]{1,2,0:T(8,128)(2,1)S(1)}, u32[]{:S(2)}, u32[]{:S(2)}) collective-permute-start(bf16[1,1024,160]{1,2,0:T(8,128)(2,1)S(1)} %fusion.17), channel_id=1, source_target_pairs={{448,0},{0,64},{64,128},{128,192},{192,256},{256,320},{320,384},{3... | collective-permute-start | bytes 983048 | tf_op jit(solution)/shard_map/ppermute | solution.py:14
Sparse Core Ops, SparseCore 0:
  9.5 111.2 all-gather.11
  122.9 74.3 all-gather.5
  208.7 43.3 all-gather.7
  262.3 87.2 all-gather.9
where the time goes:
time: 376 us
  waiting for transfers between devices  229 us (61%)
  blocking collectives  84.4 us (22%)
  matrix products  22.7 us (6%)
  local copies, waits for them, and re-layouts  16.7 us (4%)
  between operations  13.2 us (4%)
  other arithmetic  6.9 us (2%)
    all_gather x1, waiting for transfers between devices, shards(): lax.all_gather(attended, 'dp', axis=1, tiled=True)  87.4 us
    psum x1, blocking collectives, shards(): total_squares = lax.psum(local_squares, 'dp')  84.4 us
    all_gather x1, waiting for transfers between devices, shards(): normed = lax.all_gather(normed_part, 'dp', axis=1, tiled=True)  76.5 us
    all_gather x1, waiting for transfers between devices, shards(): document_kv = lax.all_gather(keys_values, 'seq', axis=0, tiled=True)  28.7 us
    all_gather x1, waiting for transfers between devices, shards(): lax.all_gather(weight_half, 'seq', axis=0, tiled=True)  25.4 us
    broadcast_in_dim x2, local copies, waits for them, and re-layouts, sparse_attention(): weights = jnp.where(live, jnp.exp(scores - highest), 0.0)  14.2 us
    ppermute x1, waiting for transfers between devices, shifted(): return lax.ppermute(block, axis, route)  10.2 us
    dot_general x1, matrix products, shards(): jnp.dot(normed, lax.all_gather(weight_half, 'seq', axis=0, tiled=True), p...  9.51 us
  transfers between devices with their start and end apart: 5, of which 5 were waited for; matrix products, arithmetic and copies ran while one was open for 5% of the time, Pallas kernels for 0%

commit v1 on v0

v1 whole, which is shorter than its diff:
```python
import math

import jax
import jax.numpy as jnp
from jax import lax
from jax.experimental import pallas as pl
from jax.experimental.pallas import tpu as pltpu
from jax.sharding import Mesh, PartitionSpec as P

BLOCK = 64
CHUNKS = 2
PLANE = ("yl", "x", "core", "seq")
DP = ("yl", "x", "core")
NEG = -1e30


def moved(value, where):
    pairs = []
    for yl in range(4):
        for x in range(4):
            for core in range(2):
                for seq in range(2):
                    target = where(seq * 4 + yl, x, core)
                    if target is None:
                        continue
                    ty, tx, tc = target
                    source_at = ((yl * 4 + x) * 2 + core) * 2 + seq
                    target_at = (((ty % 4) * 4 + tx) * 2 + tc) * 2 + ty // 4
                    pairs.append((source_at, target_at))
    return lax.ppermute(value, PLANE, pairs)


def swap_inner(y, x, core):
    if y in (2, 3):
        return y + 2, x, core
    if y in (4, 5):
        return y - 2, x, core
    return y, x, core


def sums_over_dp(value):
    for where in (
        lambda y, x, c: (y, x, 1 - c),
        lambda y, x, c: (y, x ^ 1, c),
        lambda y, x, c: (y, x ^ 2, c),
        lambda y, x, c: (y ^ 1, x, c),
        lambda y, x, c: (y ^ 2, x, c),
    ):
        value = value + moved(value, where)
    return value


def other_seq(y, x, core):
    return (y + 4) % 8, x, core


def block_mask(query_ids, random_rows, global_ids, key_count):
    query_col = query_ids[:, None]
    key_ids = jnp.arange(key_count, dtype=jnp.int32)[None, :]
    adjacent = jnp.abs(query_col - key_ids) <= 1
    key_global = jnp.any(key_ids[:, :, None] == global_ids[None, None, :], axis=2)
    query_global = jnp.any(query_col[:, :, None] == global_ids[None, None, :], axis=2)
    chosen = jnp.any(random_rows[:, None, :] == key_ids[:, :, None], axis=2)
    return adjacent | key_global | query_global | chosen


def attention_kernel(scale, query_ref, key_ref, value_ref, live_ref, out_ref, rows_ref):
    @pl.when(pl.program_id(0) == 0)
    def _():
        rows_ref[...] = key_ref[...].T

    scores = jnp.dot(rows_ref[...], query_ref[...], preferred_element_type=jnp.float32)
    keys, queries = scores.shape
    live = jnp.broadcast_to(live_ref[...][:, None, :] > 0, (keys // BLOCK, BLOCK, queries))
    scores = scores.reshape(keys // BLOCK, BLOCK, queries)
    scores = jnp.where(live, scores, NEG)
    highest = jnp.max(scores, axis=(0, 1), keepdims=True)
    weights = jnp.where(live, jnp.exp((scores - highest) * scale), 0.0)
    totals = jnp.sum(weights, axis=(0, 1), keepdims=True)[0]
    weights = weights.reshape(keys, queries).astype(jnp.bfloat16)
    mixed = jnp.dot(value_ref[...], weights, preferred_element_type=jnp.float32)
    out_ref[...] = (mixed / totals).astype(jnp.bfloat16)


def attention(query, key, value, live):
    size, count = query.shape
    tile = 128
    whole = pl.BlockSpec(key.shape, lambda i: (0, 0))
    return pl.pallas_call(
        lambda *refs: attention_kernel(1.0 / math.sqrt(size), *refs),
        grid=(count // tile,),
        in_specs=[
            pl.BlockSpec((size, tile), lambda i: (0, i)),
            whole,
            whole,
            pl.BlockSpec((live.shape[0], tile), lambda i: (0, i)),
        ],
        out_specs=pl.BlockSpec((size, tile), lambda i: (0, i)),
        out_shape=jax.ShapeDtypeStruct(query.shape, jnp.bfloat16),
        scratch_shapes=[pltpu.VMEM((key.shape[1], size), jnp.bfloat16)],
        name="attention",
    )(query, key, value, live)


def shards(section_input, norm_gain, qkv_weight, out_weight, random_blocks, global_blocks):
    seq, core = lax.axis_index("seq"), lax.axis_index("core")
    tokens_t = section_input[0].T
    part, length = tokens_t.shape
    devices = 32
    width = part * devices
    step = length // CHUNKS

    gathered = []
    for j in range(CHUNKS):
        piece = moved(tokens_t[:, j * step : (j + 1) * step], swap_inner)
        piece = lax.all_gather(piece, DP, axis=0, tiled=True)
        gathered.append(piece.reshape(2, width // 2, step))

    as_float = tokens_t.astype(jnp.float32)
    squares = jnp.sum(as_float * as_float, axis=0).reshape(length // 256, 256)
    slot = (lax.axis_index(DP) == jnp.arange(devices))[:, None]
    gains = jnp.where(slot, norm_gain.astype(jnp.float32), 0.0)
    gains = jnp.pad(gains, ((0, 0), (0, 256 - part)))
    both = sums_over_dp(jnp.concatenate([gains, squares], axis=0))
    mine = both[devices:]
    theirs = moved(mine, other_seq)
    squares = jnp.where(seq == 0, jnp.stack([mine, theirs]), jnp.stack([theirs, mine]))
    factor = lax.rsqrt(squares.reshape(2, length) / width + 1e-05)
    gain = lax.dynamic_slice_in_dim(both[:devices, :part], seq * (devices // 2), devices // 2, axis=0)
    gain = gain.reshape(width // 2, 1)

    other_rows = moved(random_blocks[0], other_seq)
    rows = jnp.where(core == seq, random_blocks[0], other_rows)
    own_blocks = length // BLOCK
    query_ids = core * own_blocks + jnp.arange(own_blocks, dtype=jnp.int32)
    allowed = block_mask(query_ids, rows, global_blocks[0], 2 * own_blocks)
    live = jnp.repeat(allowed.T.astype(jnp.float32), BLOCK, axis=1)

    weight_t = qkv_weight[0].T
    head = weight_t.shape[0] // 3
    totals = []
    for j in range(CHUNKS):
        partial = []
        for t in range(2):
            scale = factor[t, j * step : (j + 1) * step]
            normed = gathered[j][t].astype(jnp.float32) * scale[None, :] * gain
            normed = normed.astype(jnp.bfloat16)
            partial.append(jnp.dot(weight_t, normed, preferred_element_type=jnp.float32))
        partial = jnp.stack(partial, axis=1)
        came = moved(
            partial.astype(jnp.bfloat16),
            lambda y, x, c: ((y + 4) % 8, x, c) if c != y // 4 else None,
        )
        totals.append((partial + came.astype(jnp.float32)).astype(jnp.bfloat16))
    joined = jnp.stack(totals, axis=2).reshape(3 * head, 2 * length)
    beside = moved(joined, lambda y, x, c: (y, x, 1 - c) if c == y // 4 else None)
    joined = jnp.where(core == seq, joined, beside)

    query = lax.dynamic_slice_in_dim(joined[:head], core * length, length, axis=1)
    attended = attention(query, joined[head : 2 * head], joined[2 * head :], live)
    def cross(y, x, c):
        return (y, x, c) if c == y // 4 else ((y + 4) % 8, x, 1 - c)

    attended = moved(attended, cross)
    heads = lax.all_gather(attended, DP, axis=0, tiled=True)
    added = jnp.dot(out_weight[0].T, heads, preferred_element_type=jnp.float32)
    result = (as_float + added).astype(jnp.bfloat16)
    sections = lax.axis_size("section")
    route = [((i - 1) % sections, i) for i in range(sections)]
    return lax.ppermute(result.T[None], "section", route)


def solution(mesh):
    fine = Mesh(mesh.devices.reshape(8, 4, 4, 2, 2), ("section", "yl", "x", "core", "seq"))
    placed = (
        P("section", "seq", DP),
        P("section", DP),
        P("section", "seq", DP),
        P("section", None, DP),
        P("section", "seq", None),
        P("section", None),
    )
    return jax.shard_map(
        shards, mesh=fine, in_specs=placed, out_specs=P("section", "seq", DP), check_vma=False
    )
```

time: 376 us -> 353 us (0.939)
  blocking collectives: 84.4 us -> 0 us
  starting transfers between devices: 3.02 us -> 78.2 us
  waiting for transfers between devices: 229 us -> 209 us
  Pallas kernels: 0 us -> 9.89 us
  matrix products: 22.7 us -> 15.4 us
    psum x1 -> x0, blocking collectives: 84.4 us -> none  [shards(): total_squares = lax.psum(local_squares, 'dp')]
    ppermute x1 -> x14, starting transfers between devices: 2.72 us -> 78.1 us  [the longest x13 74.8 us: moved(): return lax.ppermute(value, PLANE, pairs)]
    all_gather x4 -> x3, waiting for transfers between devices: 218 us -> 166 us  [the longest x2 88 us: shards(): piece = lax.all_gather(piece, DP, axis=0, tiled=True)]
    ppermute x1 -> x14, waiting for transfers between devices: 10.2 us -> 42.3 us  [the longest x13 32.2 us: moved(): return lax.ppermute(value, PLANE, pairs)]
    broadcast_in_dim x2 -> x1, local copies, waits for them, and re-layouts: 14.2 us -> 0.84 us  [shards(): live = jnp.repeat(allowed.T.astype(jnp.float32), BLOCK, axis=1)]
    pallas_call x0 -> x1, Pallas kernels: none -> 9.89 us  [attention(): pl.pallas_call(lambda *refs: attention_kernel(1.0 / math.sqrt(size), *ref...]
    dot_general x4 -> x5, matrix products: 22.7 us -> 15.4 us  [the longest x4 10.5 us: shards(): jnp.dot(weight_t, normed, preferred_element_type=jnp.float32)]
    reshape x0 -> x3, local copies, waits for them, and re-layouts: none -> 4.58 us  [the longest x1 2.86 us: shards(): joined = jnp.stack(totals, axis=2).reshape(3 * head, 2 * length)]
  transfers between devices with their start and end apart: 5 -> 17, of which waited for: 5 -> 12; matrix products, arithmetic and copies ran while one was open for 5% -> 6% of each run, Pallas kernels for 0% -> 0%
where the time goes in v1:
time: 353 us; the launch traced here: 352 us
  waiting for transfers between devices  209 us (59%)
  starting transfers between devices  78.2 us (22%)
  local copies, waits for them, and re-layouts  15.8 us (4%)
  matrix products  15.4 us (4%)
  between operations  13.5 us (4%)
  other arithmetic  10.3 us (3%)
  Pallas kernels  9.89 us (3%)
    all_gather x2, waiting for transfers between devices, shards(): piece = lax.all_gather(piece, DP, axis=0, tiled=True)  88 us
    all_gather x1, waiting for transfers between devices, shards(): heads = lax.all_gather(attended, DP, axis=0, tiled=True)  78.4 us
    ppermute x13, starting transfers between devices, moved(): return lax.ppermute(value, PLANE, pairs)  74.8 us
    ppermute x13, waiting for transfers between devices, moved(): return lax.ppermute(value, PLANE, pairs)  32.2 us
    dot_general x4, matrix products, shards(): jnp.dot(weight_t, normed, preferred_element_type=jnp.float32)  10.5 us
    ppermute x1, waiting for transfers between devices, shards(): return lax.ppermute(result.T[None], 'section', route)  10.2 us
    pallas_call x1, Pallas kernels, attention(): pl.pallas_call(lambda *refs: attention_kernel(1.0 / math.sqrt(size), *ref...  9.89 us
  transfers between devices with their start and end apart: 17, of which 12 were waited for; matrix products, arithmetic and copies ran while one was open for 6% of the time, Pallas kernels for 0%

profile of v1, /device:TPU:1, one launch (start us, length us, event | category | flops | bytes accessed | tf_op | source)
XLA Modules:
  0.0 351.8 jit_solution(5671676324380882695)
XLA Ops:
  12.4 8.8 %collective-permute-start.1 = (f32[36,256]{1,0:T(8,128)S(1)}, f32[36,256]{1,0:T(8,128)S(1)}, u32[]{:S(2)}, u32[]{:S(2)}) collective-permute-start(f32[36,256]{1,0:T(8,128)S(1)} %select_maximum_fusion), channel_id=1, source_target_pairs={{0,2},{1,3},{2,0},{3,1},{4,6},{5,7},{6,4},{7,5},{8,10},{9,11},{10,... | collective-permute-start | bytes 110600 | tf_op jit(solution)/shard_map/ppermute | solution.py:30
  22.1 1.9 collective-permute-start.2
  24.0 2.8 collective-permute-done.2
  26.8 1.9 collective-permute-start.3
  28.8 4.3 %collective-permute-done.3 = f32[36,256]{1,0:T(8,128)S(1)} collective-permute-done((f32[36,256]{1,0:T(8,128)S(1)}, f32[36,256]{1,0:T(8,128)S(1)}, u32[]{:S(2)}, u32[]{:S(2)}) %collective-permute-start.3) | collective-permute-done | bytes 36896 | tf_op jit(solution)/shard_map/ppermute | solution.py:30
  33.1 1.9 collective-permute-start.4
  35.0 2.8 collective-permute-done.4
  37.8 25.1 %collective-permute-start.5 = (f32[36,256]{1,0:T(8,128)S(1)}, f32[36,256]{1,0:T(8,128)S(1)}, u32[]{:S(2)}, u32[]{:S(2)}) collective-permute-start(f32[36,256]{1,0:T(8,128)S(1)} %add.64), channel_id=1, source_target_pairs={{0,32},{1,33},{2,34},{3,35},{4,36},{5,37},{6,38},{7,39},{8,40},{9,... | collective-permute-start | bytes 110600 | tf_op jit(solution)/shard_map/ppermute | solution.py:30
  62.9 2.3 collective-permute-done.5
  65.3 4.9 %collective-permute-start.6 = (f32[4,256]{1,0:T(4,128)S(1)}, f32[4,256]{1,0:T(4,128)S(1)}, u32[]{:S(2)}, u32[]{:S(2)}) collective-permute-start(f32[4,256]{1,0:T(4,128)S(1)} %get-tuple-element.11), channel_id=1, source_target_pairs={{0,1},{1,0},{2,3},{3,2},{4,5},{5,4},{6,7},{7,6},{8,9},{9,8},{10,11... | collective-permute-start | bytes 12296 | tf_op jit(solution)/shard_map/ppermute | solution.py:30
  70.3 3.4 collective-permute-done.6
  74.3 20.8 %all-gather.4.cloned.1.call-done = bf16[5120,512]{1,0:T(8,128)(2,1)} async-done(((bf16[160,512]{1,0:T(8,128)(2,1)}), bf16[5120,512]{1,0:T(8,128)(2,1)}) %all-gather.4.cloned.1.call-update) | async-done | bytes 5242896 | tf_op jit(solution)/shard_map/all_gather | solution.py:116
  95.1 3.6 %fusion.28 = f32[384,1,512]{0,2,1:T(8,128)S(1)} fusion(bf16[1,2560,384]{2,1,0:T(8,128)(2,1)S(1)} %copy-done, bf16[5120,512]{1,0:T(8,128)(2,1)} %all-gather.4.cloned.1.call-done, f32[512]{0:T(512)S(1)} %bitcast.83, f32[2560]{0:T(1024)S(1)} %mul.101), kind=kOutput, calls=%fused_computation.34 | convolution fusion | flops 1011875840 | bytes 5386240 | tf_op jit(solution)/shard_map/dot_general | solution.py:148
  98.7 1.7 fusion.31
  101.4 6.9 %collective-permute-start.7 = (bf16[384,2,512]{0,2,1:T(8,128)(2,1)}, bf16[384,2,512]{0,2,1:T(8,128)(2,1)}, u32[]{:S(2)}, u32[]{:S(2)}) collective-permute-start(bf16[384,2,512]{0,2,1:T(8,128)(2,1)} %fusion.35), channel_id=1, source_target_pairs={{1,0},{2,3},{5,4},{6,7},{9,8},{10,11},{13,12},{14,15},{17,16},{18,... | collective-permute-start | bytes 2359304 | tf_op jit(solution)/shard_map/ppermute | solution.py:30
  108.3 67.2 %all-gather.6.cloned.1.call-done = bf16[5120,512]{1,0:T(8,128)(2,1)} async-done(((bf16[160,512]{1,0:T(8,128)(2,1)}), bf16[5120,512]{1,0:T(8,128)(2,1)}) %all-gather.6.cloned.1.call-update) | async-done | bytes 5242896 | tf_op jit(solution)/shard_map/all_gather | solution.py:116
  175.5 3.5 %fusion.25 = f32[384,1,512]{0,2,1:T(8,128)S(1)} fusion(bf16[1,2560,384]{2,1,0:T(8,128)(2,1)S(1)} %copy-done, bf16[5120,512]{1,0:T(8,128)(2,1)} %all-gather.6.cloned.1.call-done, f32[512]{0:T(512)} %bitcast.81, f32[2560]{0:T(1024)S(1)} %mul.101), kind=kOutput, calls=%fused_computation.33 | convolution fusion | flops 1011875840 | bytes 5386240 | tf_op jit(solution)/shard_map/dot_general | solution.py:148
  179.1 1.7 fusion.22
  180.9 3.9 %collective-permute-start.9 = (bf16[384,2,512]{0,2,1:T(8,128)(2,1)S(1)}, bf16[384,2,512]{0,2,1:T(8,128)(2,1)S(1)}, u32[]{:S(2)}, u32[]{:S(2)}) collective-permute-start(bf16[384,2,512]{0,2,1:T(8,128)(2,1)S(1)} %fusion.34), channel_id=1, source_target_pairs={{1,0},{2,3},{5,4},{6,7},{9,8},{10,11},{13,12},{14,15},{17,16},{18,... | collective-permute-start | bytes 2359304 | tf_op jit(solution)/shard_map/ppermute | solution.py:30
  186.1 11.4 %collective-permute-done.9 = bf16[384,2,512]{0,2,1:T(8,128)(2,1)S(1)} collective-permute-done((bf16[384,2,512]{0,2,1:T(8,128)(2,1)S(1)}, bf16[384,2,512]{0,2,1:T(8,128)(2,1)S(1)}, u32[]{:S(2)}, u32[]{:S(2)}) %collective-permute-start.9) | collective-permute-done | bytes 786464 | tf_op jit(solution)/shard_map/ppermute | solution.py:30
  198.0 3.1 copy.9
  201.1 2.9 reshape.180
  205.3 9.2 %collective-permute-start.11 = (s32[16,3]{0,1:T(4,128)S(1)}, s32[16,3]{0,1:T(4,128)S(1)}, u32[]{:S(2)}, u32[]{:S(2)}) collective-permute-start(s32[16,3]{0,1:T(4,128)S(1)} %bitcast.79), channel_id=1, source_target_pairs={{0,1},{1,0},{2,3},{3,2},{4,5},{5,4},{6,7},{7,6},{8,9},{9,8},{10,11... | collective-permute-start | bytes 584 | tf_op jit(solution)/shard_map/ppermute | solution.py:30
  220.2 1.7 reshape.181.refs_3_
  221.9 1.6 broadcast_select_fusion
  225.3 9.9 %attention.1 = bf16[128,1024]{1,0:T(8,128)(2,1)} custom-call(bf16[128,1024]{1,0:T(8,128)(2,1)} %constant_dynamic-slice_fusion.refs_0_, bf16[128,2048]{1,0:T(8,128)(2,1)} %get-tuple-element.6.refs_1_, bf16[128,2048]{1,0:T(8,128)(2,1)} %get-tuple-element.5.refs_2_, f32[32,1024]{1,0:T(8,128)} %reshape.181.refs_3_), custom_call_target="tpu_custom_call" | custom-call | tf_op jit(solution)/shard_map/attention/pallas_call | solution.py:89
  235.2 7.6 %collective-permute-start.12 = (bf16[128,1024]{1,0:T(8,128)(2,1)}, bf16[128,1024]{1,0:T(8,128)(2,1)S(1)}, u32[]{:S(2)}, u32[]{:S(2)}) collective-permute-start(bf16[128,1024]{1,0:T(8,128)(2,1)} %attention.1), channel_id=1, source_target_pairs={{0,0},{1,2},{2,1},{3,3},{4,4},{5,6},{6,5},{7,7},{8,8},{9,10},{10,9... | collective-permute-start | bytes 786440 | tf_op jit(solution)/shard_map/ppermute | solution.py:30
  242.8 4.3 %collective-permute-done.12 = bf16[128,1024]{1,0:T(8,128)(2,1)S(1)} collective-permute-done((bf16[128,1024]{1,0:T(8,128)(2,1)}, bf16[128,1024]{1,0:T(8,128)(2,1)S(1)}, u32[]{:S(2)}, u32[]{:S(2)}) %collective-permute-start.12) | collective-permute-done | bytes 262176 | tf_op jit(solution)/shard_map/ppermute | solution.py:30
  247.8 78.4 %all-gather.8.cloned.1.call-done = bf16[4096,1024]{1,0:T(8,128)(2,1)} async-done(((bf16[128,1024]{1,0:T(8,128)(2,1)}), bf16[4096,1024]{1,0:T(8,128)(2,1)}) %all-gather.8.cloned.1.call-update) | async-done | bytes 8388624 | tf_op jit(solution)/shard_map/all_gather | solution.py:165
  326.2 4.9 %fusion.42 = bf16[1,1024,160]{1,2,0:T(8,128)(2,1)S(1)} fusion(bf16[4096,1024]{1,0:T(8,128)(2,1)} %all-gather.8.cloned.1.call-done, bf16[1,4096,160]{1,2,0:T(8,128)(2,1)S(1)} %copy-done.1, bf16[1,1024,160]{1,2,0:T(8,128)(2,1)} %param.6), kind=kOutput, calls=%fused_computation.40 | convolution fusion | flops 1342668800 | bytes 10354688 | tf_op jit(solution)/shard_map/dot_general | solution.py:166
  331.1 3.3 collective-permute-start.13
  334.4 10.2 %collective-permute-done.13 = bf16[1,1024,160]{1,2,0:T(8,128)(2,1)S(1)} collective-permute-done((bf16[1,1024,160]{1,2,0:T(8,128)(2,1)S(1)}, bf16[1,1024,160]{1,2,0:T(8,128)(2,1)S(1)}, u32[]{:S(2)}, u32[]{:S(2)}) %collective-permute-start.13) | collective-permute-done | bytes 327712 | tf_op jit(solution)/shard_map/ppermute | solution.py:170
  (70 shorter events, 20.5 us)
Async XLA Ops:
  6.5 88.5 %copy-start = (bf16[1,2560,384]{2,1,0:T(8,128)(2,1)S(1)}, bf16[1,2560,384]{2,1,0:T(8,128)(2,1)}, u32[]{:S(2)}) copy-start(bf16[1,2560,384]{2,1,0:T(8,128)(2,1)} %param.8) | copy-start | bytes 5898244
  6.5 88.5 %all-gather.4.cloned.1.call-start = ((), (), s32[]{:S(2)}) async-start(), calls=%async_computation | async-start | bytes 5406720 | tf_op jit(solution)/shard_map/all_gather | solution.py:116
  7.7 0.7 collective-permute-start
  8.4 0.7 copy-start.3
  9.1 166.4 %all-gather.6.cloned.1.call-start = ((), (), s32[]{:S(2)}) async-start(), calls=%async_computation.1 | async-start | bytes 5406720 | tf_op jit(solution)/shard_map/all_gather | solution.py:116
  9.1 0.7 collective-permute-start.8
  9.8 0.7 copy-start.4
  10.5 315.7 %all-gather.8.cloned.1.call-start = ((), (), s32[]{:S(2)}) async-start(), calls=%async_computation.2 | async-start | bytes 8650752 | tf_op jit(solution)/shard_map/all_gather | solution.py:165
  12.4 9.6 %collective-permute-start.1 = (f32[36,256]{1,0:T(8,128)S(1)}, f32[36,256]{1,0:T(8,128)S(1)}, u32[]{:S(2)}, u32[]{:S(2)}) collective-permute-start(f32[36,256]{1,0:T(8,128)S(1)} %select_maximum_fusion), channel_id=1, source_target_pairs={{0,2},{1,3},{2,0},{3,1},{4,6},{5,7},{6,4},{7,5},{8,10},{9,11},{10,... | collective-permute-start | bytes 110600 | tf_op jit(solution)/shard_map/ppermute | solution.py:30
  22.1 4.7 %collective-permute-start.2 = (f32[36,256]{1,0:T(8,128)S(1)}, f32[36,256]{1,0:T(8,128)S(1)}, u32[]{:S(2)}, u32[]{:S(2)}) collective-permute-start(f32[36,256]{1,0:T(8,128)S(1)} %fusion.55), channel_id=1, source_target_pairs={{0,4},{1,5},{2,6},{3,7},{4,0},{5,1},{6,2},{7,3},{8,12},{9,13},{10,... | collective-permute-start | bytes 110600 | tf_op jit(solution)/shard_map/ppermute | solution.py:30
  26.8 6.2 %collective-permute-start.3 = (f32[36,256]{1,0:T(8,128)S(1)}, f32[36,256]{1,0:T(8,128)S(1)}, u32[]{:S(2)}, u32[]{:S(2)}) collective-permute-start(f32[36,256]{1,0:T(8,128)S(1)} %add.62), channel_id=1, source_target_pairs={{0,8},{1,9},{2,10},{3,11},{4,12},{5,13},{6,14},{7,15},{8,0},{9,1},... | collective-permute-start | bytes 110600 | tf_op jit(solution)/shard_map/ppermute | solution.py:30
  33.1 4.7 %collective-permute-start.4 = (f32[36,256]{1,0:T(8,128)S(1)}, f32[36,256]{1,0:T(8,128)S(1)}, u32[]{:S(2)}, u32[]{:S(2)}) collective-permute-start(f32[36,256]{1,0:T(8,128)S(1)} %add.63), channel_id=1, source_target_pairs={{0,16},{1,17},{2,18},{3,19},{4,20},{5,21},{6,22},{7,23},{8,24},{9,... | collective-permute-start | bytes 110600 | tf_op jit(solution)/shard_map/ppermute | solution.py:30
  37.8 27.4 %collective-permute-start.5 = (f32[36,256]{1,0:T(8,128)S(1)}, f32[36,256]{1,0:T(8,128)S(1)}, u32[]{:S(2)}, u32[]{:S(2)}) collective-permute-start(f32[36,256]{1,0:T(8,128)S(1)} %add.64), channel_id=1, source_target_pairs={{0,32},{1,33},{2,34},{3,35},{4,36},{5,37},{6,38},{7,39},{8,40},{9,... | collective-permute-start | bytes 110600 | tf_op jit(solution)/shard_map/ppermute | solution.py:30
  65.3 8.4 %collective-permute-start.6 = (f32[4,256]{1,0:T(4,128)S(1)}, f32[4,256]{1,0:T(4,128)S(1)}, u32[]{:S(2)}, u32[]{:S(2)}) collective-permute-start(f32[4,256]{1,0:T(4,128)S(1)} %get-tuple-element.11), channel_id=1, source_target_pairs={{0,1},{1,0},{2,3},{3,2},{4,5},{5,4},{6,7},{7,6},{8,9},{9,8},{10,11... | collective-permute-start | bytes 12296 | tf_op jit(solution)/shard_map/ppermute | solution.py:30
  95.1 3.6 %copy-start.6 = (f32[1,512]{1,0:T(1,128)S(1)}, f32[1,512]{1,0:T(1,128)}, u32[]{:S(2)}) copy-start(f32[1,512]{1,0:T(1,128)} %get-tuple-element.12) | copy-start | bytes 6148
  95.1 3.6 %copy-start.7 = (bf16[5120,512]{1,0:T(8,128)(2,1)S(1)}, bf16[5120,512]{1,0:T(8,128)(2,1)}, u32[]{:S(2)}) copy-start(bf16[5120,512]{1,0:T(8,128)(2,1)} %all-gather.4.cloned.1.call-done) | copy-start | bytes 15728644
  101.4 83.5 %collective-permute-start.7 = (bf16[384,2,512]{0,2,1:T(8,128)(2,1)}, bf16[384,2,512]{0,2,1:T(8,128)(2,1)}, u32[]{:S(2)}, u32[]{:S(2)}) collective-permute-start(bf16[384,2,512]{0,2,1:T(8,128)(2,1)} %fusion.35), channel_id=1, source_target_pairs={{1,0},{2,3},{5,4},{6,7},{9,8},{10,11},{13,12},{14,15},{17,16},{18,... | collective-permute-start | bytes 2359304 | tf_op jit(solution)/shard_map/ppermute | solution.py:30
  175.5 3.6 %copy-start.8 = (bf16[5120,512]{1,0:T(8,128)(2,1)S(1)}, bf16[5120,512]{1,0:T(8,128)(2,1)}, u32[]{:S(2)}) copy-start(bf16[5120,512]{1,0:T(8,128)(2,1)} %all-gather.6.cloned.1.call-done) | copy-start | bytes 15728644
  180.9 16.7 %collective-permute-start.9 = (bf16[384,2,512]{0,2,1:T(8,128)(2,1)S(1)}, bf16[384,2,512]{0,2,1:T(8,128)(2,1)S(1)}, u32[]{:S(2)}, u32[]{:S(2)}) collective-permute-start(bf16[384,2,512]{0,2,1:T(8,128)(2,1)S(1)} %fusion.34), channel_id=1, source_target_pairs={{1,0},{2,3},{5,4},{6,7},{9,8},{10,11},{13,12},{14,15},{17,16},{18,... | collective-permute-start | bytes 2359304 | tf_op jit(solution)/shard_map/ppermute | solution.py:30
  198.0 7.3 %copy-start.5 = (s32[1,16,3]{1,0,2:T(1,128)S(1)}, s32[1,16,3]{1,0,2:T(1,128)}, u32[]{:S(2)}) copy-start(s32[1,16,3]{1,0,2:T(1,128)} %param.10) | copy-start | bytes 580
  204.0 17.9 %collective-permute-start.10 = (bf16[384,2048]{1,0:T(8,128)(2,1)S(1)}, bf16[384,2048]{1,0:T(8,128)(2,1)}, u32[]{:S(2)}, u32[]{:S(2)}) collective-permute-start(bf16[384,2048]{1,0:T(8,128)(2,1)S(1)} %reshape.180), channel_id=1, source_target_pairs={{0,2},{3,1},{4,6},{7,5},{8,10},{11,9},{12,14},{15,13},{16,18},{19,... | collective-permute-start | bytes 4718600 | tf_op jit(solution)/shard_map/ppermute | solution.py:30
  205.3 11.9 %collective-permute-start.11 = (s32[16,3]{0,1:T(4,128)S(1)}, s32[16,3]{0,1:T(4,128)S(1)}, u32[]{:S(2)}, u32[]{:S(2)}) collective-permute-start(s32[16,3]{0,1:T(4,128)S(1)} %bitcast.79), channel_id=1, source_target_pairs={{0,1},{1,0},{2,3},{3,2},{4,5},{5,4},{6,7},{7,6},{8,9},{9,8},{10,11... | collective-permute-start | bytes 584 | tf_op jit(solution)/shard_map/ppermute | solution.py:30
  223.5 102.7 %copy-start.1 = (bf16[1,4096,160]{1,2,0:T(8,128)(2,1)S(1)}, bf16[1,4096,160]{1,2,0:T(8,128)(2,1)}, u32[]{:S(2)}) copy-start(bf16[1,4096,160]{1,2,0:T(8,128)(2,1)} %param.9) | copy-start | bytes 3932164
  235.2 11.9 %collective-permute-start.12 = (bf16[128,1024]{1,0:T(8,128)(2,1)}, bf16[128,1024]{1,0:T(8,128)(2,1)S(1)}, u32[]{:S(2)}, u32[]{:S(2)}) collective-permute-start(bf16[128,1024]{1,0:T(8,128)(2,1)} %attention.1), channel_id=1, source_target_pairs={{0,0},{1,2},{2,1},{3,3},{4,4},{5,6},{6,5},{7,7},{8,8},{9,10},{10,9... | collective-permute-start | bytes 786440 | tf_op jit(solution)/shard_map/ppermute | solution.py:30
  247.1 0.7 copy-start.2
  331.1 13.5 %collective-permute-start.13 = (bf16[1,1024,160]{1,2,0:T(8,128)(2,1)S(1)}, bf16[1,1024,160]{1,2,0:T(8,128)(2,1)S(1)}, u32[]{:S(2)}, u32[]{:S(2)}) collective-permute-start(bf16[1,1024,160]{1,2,0:T(8,128)(2,1)S(1)} %fusion.42), channel_id=1, source_target_pairs={{448,0},{0,64},{64,128},{128,192},{192,256},{256,320},{320,384},{3... | collective-permute-start | bytes 983048 | tf_op jit(solution)/shard_map/ppermute | solution.py:170
Sparse Core Ops, SparseCore 0:
  9.5 85.5 all-gather.3
  97.2 78.2 all-gather.5
  247.9 78.2 all-gather.7

commit v2 on v1

v2 whole, which is shorter than its diff:
```python
import math

import jax
import jax.numpy as jnp
from jax import lax
from jax.experimental import pallas as pl
from jax.experimental.pallas import tpu as pltpu
from jax.sharding import Mesh, PartitionSpec as P

BLOCK = 64
PLANE = ("yl", "x", "core", "seq")
DP = ("yl", "x", "core")
NEG = -1e30


def moved(value, where):
    pairs = []
    for yl in range(4):
        for x in range(4):
            for core in range(2):
                for seq in range(2):
                    target = where(seq * 4 + yl, x, core)
                    if target is None:
                        continue
                    ty, tx, tc = target
                    source_at = ((yl * 4 + x) * 2 + core) * 2 + seq
                    target_at = (((ty % 4) * 4 + tx) * 2 + tc) * 2 + ty // 4
                    pairs.append((source_at, target_at))
    return lax.ppermute(value, PLANE, pairs)


def swap_inner(y, x, core):
    if y in (2, 3):
        return y + 2, x, core
    if y in (4, 5):
        return y - 2, x, core
    return y, x, core


def other_seq(y, x, core):
    return (y + 4) % 8, x, core


def block_mask(query_ids, random_rows, global_ids, key_ids):
    query_col = query_ids[:, None]
    key_ids = key_ids[None, :]
    adjacent = jnp.abs(query_col - key_ids) <= 1
    key_global = jnp.any(key_ids[:, :, None] == global_ids[None, None, :], axis=2)
    query_global = jnp.any(query_col[:, :, None] == global_ids[None, None, :], axis=2)
    chosen = jnp.any(random_rows[:, None, :] == key_ids[:, :, None], axis=2)
    return adjacent | key_global | query_global | chosen


def attention_kernel(scale, own_ref, other_ref, live_ref, out_ref, rows_ref, value_ref):
    size = rows_ref.shape[1]

    @pl.when(pl.program_id(0) == 0)
    def _():
        step = own_ref.shape[2]
        for i in range(2):
            here, there = pl.ds(i * step, step), pl.ds((2 + i) * step, step)
            rows_ref[here, :] = own_ref[i, size : 2 * size, :].T
            rows_ref[there, :] = other_ref[i, :size, :].T
            value_ref[:, here] = own_ref[i, 2 * size :, :]
            value_ref[:, there] = other_ref[i, size:, :]

    tile = out_ref.shape[2]
    per = own_ref.shape[2] // tile
    at = pl.program_id(0)
    columns = pl.ds(pl.multiple_of(lax.rem(at, per) * tile, tile), tile)
    query = own_ref[at // per, :size, columns]
    scores = jnp.dot(rows_ref[...], query, preferred_element_type=jnp.float32)
    keys, queries = scores.shape
    live = jnp.broadcast_to(live_ref[...][:, None, :] > 0, (keys // BLOCK, BLOCK, queries))
    scores = scores.reshape(keys // BLOCK, BLOCK, queries)
    scores = jnp.where(live, scores, NEG)
    highest = jnp.max(scores, axis=(0, 1), keepdims=True)
    weights = jnp.where(live, jnp.exp((scores - highest) * scale), 0.0)
    totals = jnp.sum(weights, axis=(0, 1), keepdims=True)[0]
    weights = weights.reshape(keys, queries).astype(jnp.bfloat16)
    mixed = jnp.dot(value_ref[...], weights, preferred_element_type=jnp.float32)
    out_ref[0] = (mixed / totals).astype(jnp.bfloat16)


def attention(own, other, live):
    _, triple, step = own.shape
    size, tile = triple // 3, 128
    per = step // tile
    return pl.pallas_call(
        lambda *refs: attention_kernel(1.0 / math.sqrt(size), *refs),
        grid=(2 * per,),
        in_specs=[
            pl.BlockSpec(own.shape, lambda i: (0, 0, 0)),
            pl.BlockSpec(other.shape, lambda i: (0, 0, 0)),
            pl.BlockSpec((live.shape[0], tile), lambda i: (0, i)),
        ],
        out_specs=pl.BlockSpec((1, size, tile), lambda i: (i // per, 0, i % per)),
        out_shape=jax.ShapeDtypeStruct((2, size, step), jnp.bfloat16),
        scratch_shapes=[
            pltpu.VMEM((4 * step, size), jnp.bfloat16),
            pltpu.VMEM((size, 4 * step), jnp.bfloat16),
        ],
        name="attention",
    )(own, other, live)


def at_index(array, index, axis=0):
    return lax.dynamic_index_in_dim(array, index, axis=axis, keepdims=False)


def other_core(y, x, core):
    return y, x, 1 - core


def pair(y, x, core):
    return y ^ 1, x, core


def by_two(y, x, core):
    return y ^ 2, x, core


def around(y, x, core):
    return y, (x + 1 - 2 * core) % 4, core


def shards(section_input, norm_gain, qkv_weight, out_weight, random_blocks, global_blocks):
    yl, x, core, seq = (lax.axis_index(axis) for axis in PLANE)
    f32, bf16 = jnp.float32, jnp.bfloat16
    tokens_t = section_input[0].T
    part, length = tokens_t.shape
    step = length // 2
    width = part * 32
    first = yl // 2

    halves = tokens_t[:, :step], tokens_t[:, step:]
    own = jnp.where(core == 0, halves[0], halves[1])
    beside = moved(jnp.where(core == 0, halves[1], halves[0]), other_core)
    item = jnp.concatenate([own, beside], axis=0)

    e = moved(item, swap_inner)
    f = moved(e, by_two)
    e = jnp.concatenate([e, moved(e, pair)], axis=0)
    f = jnp.concatenate([f, moved(f, pair)], axis=0)

    as_float = item.astype(f32)
    squares = jnp.sum(as_float * as_float, axis=0).reshape(2, step // 2)
    gain = jnp.concatenate([norm_gain, moved(norm_gain, other_core)], axis=1).astype(f32)
    slot = (yl * 4 + x == jnp.arange(16))[:, None]
    lanes = 384
    table = jnp.concatenate(
        [
            jnp.pad(jnp.where(slot, gain, 0.0), ((0, 0), (0, lanes - 2 * part))),
            jnp.pad(squares, ((0, 0), (0, lanes - step // 2))),
        ],
        axis=0,
    )
    for where in (
        lambda y, x, c: (y, x ^ 1, c),
        lambda y, x, c: (y, x ^ 2, c),
        pair,
        by_two,
    ):
        table = table + moved(table, where)
    mine = table[16:, : step // 2]
    theirs = moved(mine, other_seq)
    factors = []
    for which in (mine, theirs):
        factors.append(lax.rsqrt(which.reshape(1, step) / width + 1e-05))
    factor_e = jnp.where(first == seq, factors[0], factors[1])
    factor_f = jnp.where(first == seq, factors[1], factors[0])
    gains = table[:16, : 2 * part].reshape(2, 2, 4, 2 * part)
    gains = at_index(gains, seq)

    weight = qkv_weight[0]
    beside = moved(weight, other_core)
    columns = weight.shape[1]
    weight = jnp.concatenate(
        [jnp.where(core == seq, weight, beside), jnp.where(core == seq, beside, weight)], axis=1
    )
    weight = weight.reshape(2, 4, 2, part, 2 * columns)
    weights, scales = [], []
    for k in range(4):
        source = (x - (1 - 2 * core) * k) % 4
        rows, scale = [], []
        for ab in range(2):
            which = ab ^ (yl % 2)
            block = at_index(at_index(weight, which), source)
            rows += [at_index(block, core), at_index(block, 1 - core)]
            scale.append(at_index(at_index(gains, which), source))
        weights.append(jnp.concatenate(rows, axis=0).T)
        scales.append(jnp.concatenate(scale).reshape(4 * part, 1))

    def project(block, k, factor):
        normed = (block.astype(f32) * factor * scales[k]).astype(bf16)
        return jnp.dot(weights[k], normed, preferred_element_type=f32)

    out_t = out_weight[0].T.reshape(part, 4, 4, -1)
    per = out_t.shape[3]
    out_cols = []
    for r in range(4):
        block = at_index(out_t, (x + r) % 4, axis=2).reshape(part, 4 * per)
        if r:
            block = moved(block, lambda y, x, c, r=r: (y, (x + r) % 4, c))
        out_cols.append(block)
    out_cols = jnp.stack(out_cols)
    out_cols = jnp.stack([out_cols, moved(out_cols, other_core)], axis=1)
    out_cols = out_cols.reshape(8 * part, 4, per)

    rows = jnp.stack([random_blocks[0], moved(random_blocks[0], other_seq)])
    rows = jnp.where(first == seq, rows, rows[::-1])
    count = step // BLOCK
    rows = lax.dynamic_slice_in_dim(rows, core * count, count, axis=1).reshape(2 * count, -1)
    halves = jnp.stack([first, 1 - first]) * 2 * count
    spot = jnp.arange(count, dtype=jnp.int32)
    query_ids = (halves[:, None] + core * count + spot[None, :]).reshape(-1)
    other_ids = (halves[:, None] + (1 - core) * count + spot[None, :]).reshape(-1)
    key_ids = jnp.concatenate([query_ids, other_ids])
    allowed = block_mask(query_ids, rows, global_blocks[0], key_ids)
    live = jnp.repeat(allowed.T.astype(f32), BLOCK, axis=1)

    partial_e, partial_f = project(e, 0, factor_e), project(f, 0, factor_f)
    for k in range(1, 4):
        e, f = moved(e, around), moved(f, around)
        partial_e = partial_e + project(e, k, factor_e)
        partial_f = partial_f + project(f, k, factor_f)
    joined = []
    for partial in (partial_e, partial_f):
        came = moved(partial[columns:].astype(bf16), other_seq)
        joined.append((partial[:columns] + came.astype(f32)).astype(bf16))
    joined = jnp.stack(joined)
    head = columns // 3
    attended = attention(joined, moved(joined[:, head:], other_core), live)

    kept = jnp.where(first == seq, attended[0], attended[1])
    came = moved(jnp.where(first == seq, attended[1], attended[0]), other_seq)
    heads = jnp.where(
        seq == 0,
        jnp.concatenate([kept, came], axis=0),
        jnp.concatenate([came, kept], axis=0),
    )
    far = moved(heads, by_two)
    blocks = [(heads, yl), (far, yl ^ 2), (moved(heads, pair), yl ^ 1), (moved(far, pair), yl ^ 3)]
    added = 0.0
    for block, row in blocks:
        added = added + jnp.dot(at_index(out_cols, row, axis=1), block, preferred_element_type=f32)
    added = added.reshape(4, 2 * part, step)
    total = added[0]
    for r in range(1, 4):
        total = total + moved(
            added[r].astype(bf16), lambda y, x, c, r=r: (y, (x - r) % 4, c)
        ).astype(f32)
    result = (as_float + total).astype(bf16)

    sections = lax.axis_size("section")
    straight = [(i * 2 + c, (i + 1) % sections * 2 + c) for i in range(sections) for c in range(2)]
    across = [(a, b ^ 1) for a, b in straight]
    straight = lax.ppermute(result[:part], ("section", "core"), straight)
    across = lax.ppermute(result[part:], ("section", "core"), across)
    handed_on = jnp.where(
        core == 0,
        jnp.concatenate([straight, across], axis=1),
        jnp.concatenate([across, straight], axis=1),
    )
    return handed_on.T[None]


def solution(mesh):
    fine = Mesh(mesh.devices.reshape(8, 4, 4, 2, 2), ("section", "yl", "x", "core", "seq"))
    placed = (
        P("section", "seq", DP),
        P("section", DP),
        P("section", "seq", DP),
        P("section", None, DP),
        P("section", "seq", None),
        P("section", None),
    )
    return jax.shard_map(
        shards, mesh=fine, in_specs=placed, out_specs=P("section", "seq", DP), check_vma=False
    )
```

time: 353 us -> 274 us (0.78)
  waiting for transfers between devices: 209 us -> 44.6 us
  starting transfers between devices: 78.2 us -> 155 us
  local copies, waits for them, and re-layouts: 15.8 us -> 34.3 us
  between operations: 13.5 us -> 0.97 us
    all_gather x3 -> x0, waiting for transfers between devices: 166 us -> none  [the longest x2 88 us: shards(): piece = lax.all_gather(piece, DP, axis=0, tiled=True)]
    ppermute x13 -> x33, starting transfers between devices: 74.8 us -> 146 us  [moved(): return lax.ppermute(value, PLANE, pairs)]
    dynamic_slice x2 -> x4, local copies, waits for them, and re-layouts: 0.74 us -> 13.9 us  [the longest x3 13.9 us: at_index(): return lax.dynamic_index_in_dim(array, index, axis=axis, keepdims=False)]
    ppermute x1 -> x2, starting transfers between devices: 3.27 us -> 9.23 us  [the longest x1 5.24 us: shards(): across = lax.ppermute(result[part:], ('section', 'core'), across)]
    ppermute x13 -> x33, waiting for transfers between devices: 32.2 us -> 36.5 us  [moved(): return lax.ppermute(value, PLANE, pairs)]
    another operation x3 -> x7, other arithmetic: 1.7 us -> 5.88 us  [the longest x2 3.82 us: shards(): out_cols = jnp.stack([out_cols, moved(out_cols, other_core)], axis=1)]
    reshape x3 -> x5, local copies, waits for them, and re-layouts: 4.58 us -> 8.36 us  [the longest x1 4.33 us: shards(): out_cols = out_cols.reshape(8 * part, 4, per)]
    ppermute x1 -> x2, waiting for transfers between devices: 10.2 us -> 8.09 us  [the longest x1 7.45 us: shards(): across = lax.ppermute(result[part:], ('section', 'core'), across)]
  transfers between devices with their start and end apart: 17 -> 35, of which waited for: 12 -> 15; matrix products, arithmetic and copies ran while one was open for 6% -> 21% of each run, Pallas kernels for 0% -> 4%
where the time goes in v2:
time: 274 us; the launch traced here: 271 us
  starting transfers between devices  155 us (57%)
  waiting for transfers between devices  44.6 us (16%)
  local copies, waits for them, and re-layouts  34.3 us (13%)
  matrix products  13.4 us (5%)
  other arithmetic  12.6 us (5%)
  Pallas kernels  10.1 us (4%)
    ppermute x33, starting transfers between devices, moved(): return lax.ppermute(value, PLANE, pairs)  146 us
    ppermute x33, waiting for transfers between devices, moved(): return lax.ppermute(value, PLANE, pairs)  36.5 us
    dynamic_slice x3, local copies, waits for them, and re-layouts, at_index(): return lax.dynamic_index_in_dim(array, index, axis=axis, keepdims=False)  13.9 us
    dot_general x8, matrix products, project(): return jnp.dot(weights[k], normed, preferred_element_type=f32)  11.3 us
    pallas_call x1, Pallas kernels, attention(): pl.pallas_call(lambda *refs: attention_kernel(1.0 / math.sqrt(size), *ref...  10.1 us
    ppermute x1, waiting for transfers between devices, shards(): across = lax.ppermute(result[part:], ('section', 'core'), across)  7.45 us
    unnamed x20, local copies, waits for them, and re-layouts  6.3 us
  transfers between devices with their start and end apart: 35, of which 15 were waited for; matrix products, arithmetic and copies ran while one was open for 21% of the time, Pallas kernels for 4%

profile of v2, /device:TPU:1, one launch (start us, length us, event | category | flops | bytes accessed | tf_op | source)
XLA Modules:
  0.0 271.0 jit_solution(2375565915068675649)
XLA Ops:
  1.0 8.8 %collective-permute-start = (bf16[160,512]{1,0:T(8,128)(2,1)S(1)}, bf16[160,512]{1,0:T(8,128)(2,1)S(1)}, u32[]{:S(2)}, u32[]{:S(2)}) collective-permute-start(bf16[160,512]{1,0:T(8,128)(2,1)S(1)} %get-tuple-element.47), channel_id=1, source_target_pairs={{0,2},{1,3},{2,0},{3,1},{4,6},{5,7},{6,4},{7,5},{8,10},{9,11},{10,... | collective-permute-start | bytes 491528 | tf_op jit(solution)/shard_map/ppermute | solution.py:29
  17.3 3.2 %reshape.365 = bf16[160,4,4,256]{3,2,1,0:T(4,128)(2,1)S(1)} reshape(bf16[160,4096]{1,0:T(8,128)(2,1)} %bitcast.107) | data formatting | bytes 2621440 | tf_op jit(solution)/shard_map/reshape | solution.py:198
  20.6 8.4 %dynamic-slice_reduce_fusion.3 = (bf16[160,4,256]{2,1,0:T(4,128)(2,1)S(1)}, bf16[160,4,256]{2,1,0:T(4,128)(2,1)S(1)}, bf16[160,4,256]{2,1,0:T(4,128)(2,1)S(1)}, bf16[160,4,256]{2,1,0:T(4,128)(2,1)S(1)}) fusion(bf16[160,4,4,256]{3,2,1,0:T(4,128)(2,1)S(1)} %reshape.365, s32[]{:T(128)S(6)} %select_n.276, s32[]{:T(128)S(6)} %select_n.280, s32[]{:T(128)S(6)} %select_n.278, ...), kind=kLoop, calls=%fused_computation.73 | loop fusion | bytes 2621456 | tf_op jit(solution)/shard_map/jit(dynamic_index_in_dim)/dynamic_slice | solution.py:108
  30.1 3.1 %collective-permute-start.9 = (f32[18,384]{1,0:T(8,128)S(1)}, f32[18,384]{1,0:T(8,128)S(1)}, u32[]{:S(2)}, u32[]{:S(2)}) collective-permute-start(f32[18,384]{1,0:T(8,128)S(1)} %select_maximum_fusion), channel_id=1, source_target_pairs={{0,4},{1,5},{2,6},{3,7},{4,0},{5,1},{6,2},{7,3},{8,12},{9,13},{10,... | collective-permute-start | bytes 82952 | tf_op jit(solution)/shard_map/ppermute | solution.py:29
  33.4 19.0 %collective-permute-start.18 = (bf16[320,512]{1,0:T(8,128)(2,1)S(1)}, bf16[320,512]{1,0:T(8,128)(2,1)}, u32[]{:S(2)}, u32[]{:S(2)}) collective-permute-start(bf16[320,512]{1,0:T(8,128)(2,1)S(1)} %collective-permute-done.6), channel_id=1, source_target_pairs={{0,32},{1,33},{2,34},{3,35},{4,36},{5,37},{6,38},{7,39},{8,40},{9,... | collective-permute-start | bytes 983048 | tf_op jit(solution)/shard_map/ppermute | solution.py:29
  52.5 4.4 %collective-permute-start.10 = (f32[18,384]{1,0:T(8,128)S(1)}, f32[18,384]{1,0:T(8,128)S(1)}, u32[]{:S(2)}, u32[]{:S(2)}) collective-permute-start(f32[18,384]{1,0:T(8,128)S(1)} %fusion.65), channel_id=1, source_target_pairs={{0,8},{1,9},{2,10},{3,11},{4,12},{5,13},{6,14},{7,15},{8,0},{9,1},... | collective-permute-start | bytes 82952 | tf_op jit(solution)/shard_map/ppermute | solution.py:29
  60.6 3.4 %collective-permute-start.7 = (bf16[320,512]{1,0:T(8,128)(2,1)S(1)}, bf16[320,512]{1,0:T(8,128)(2,1)}, u32[]{:S(2)}, u32[]{:S(2)}) collective-permute-start(bf16[320,512]{1,0:T(8,128)(2,1)S(1)} %collective-permute-done.6), channel_id=1, source_target_pairs={{0,16},{1,17},{2,18},{3,19},{4,20},{5,21},{6,22},{7,23},{8,24},{9,... | collective-permute-start | bytes 983048 | tf_op jit(solution)/shard_map/ppermute | solution.py:29
  66.8 4.4 %collective-permute-start.3 = (bf16[160,1024]{1,0:T(8,128)(2,1)}, bf16[160,1024]{1,0:T(8,128)(2,1)}, u32[]{:S(2)}, u32[]{:S(2)}) collective-permute-start(bf16[160,1024]{1,0:T(8,128)(2,1)} %bitcast.110), channel_id=1, source_target_pairs={{0,12},{1,13},{2,14},{3,15},{4,0},{5,1},{6,2},{7,3},{8,4},{9,5},{1... | collective-permute-start | bytes 983048 | tf_op jit(solution)/shard_map/ppermute | solution.py:29
  79.6 3.4 %collective-permute-start.14 = (bf16[640,512]{1,0:T(8,128)(2,1)}, bf16[640,512]{1,0:T(8,128)(2,1)}, u32[]{:S(2)}, u32[]{:S(2)}) collective-permute-start(bf16[640,512]{1,0:T(8,128)(2,1)} %constant_dynamic-update-slice_fusion), channel_id=1, source_target_pairs={{0,4},{1,5},{2,14},{3,15},{4,8},{5,9},{6,2},{7,3},{8,12},{9,13},{1... | collective-permute-start | bytes 1966088 | tf_op jit(solution)/shard_map/ppermute | solution.py:29
  85.9 5.2 %collective-permute-start.13 = (f32[2,256]{1,0:T(2,128)S(1)}, f32[2,256]{1,0:T(2,128)S(1)}, u32[]{:S(2)}, u32[]{:S(2)}) collective-permute-start(f32[2,256]{1,0:T(2,128)S(1)} %slice.81), channel_id=1, source_target_pairs={{0,1},{1,0},{2,3},{3,2},{4,5},{5,4},{6,7},{7,6},{8,9},{9,8},{10,11... | collective-permute-start | bytes 6152 | tf_op jit(solution)/shard_map/ppermute | solution.py:29
  94.2 3.4 %collective-permute-start.2 = (bf16[160,1024]{1,0:T(8,128)(2,1)S(1)}, bf16[160,1024]{1,0:T(8,128)(2,1)S(1)}, u32[]{:S(2)}, u32[]{:S(2)}) collective-permute-start(bf16[160,1024]{1,0:T(8,128)(2,1)S(1)} %bitcast.109), channel_id=1, source_target_pairs={{0,8},{1,9},{2,10},{3,11},{4,12},{5,13},{6,14},{7,15},{8,0},{9,1},... | collective-permute-start | bytes 983048 | tf_op jit(solution)/shard_map/ppermute | solution.py:29
  99.6 6.7 %collective-permute-start.15 = (bf16[640,512]{1,0:T(8,128)(2,1)}, bf16[640,512]{1,0:T(8,128)(2,1)S(1)}, u32[]{:S(2)}, u32[]{:S(2)}) collective-permute-start(bf16[640,512]{1,0:T(8,128)(2,1)} %collective-permute-done.14), channel_id=1, source_target_pairs={{0,4},{1,5},{2,14},{3,15},{4,8},{5,9},{6,2},{7,3},{8,12},{9,13},{1... | collective-permute-start | bytes 1966088 | tf_op jit(solution)/shard_map/ppermute | solution.py:29
  117.0 4.1 %collective-permute-start.16 = (bf16[640,512]{1,0:T(8,128)(2,1)S(1)}, bf16[640,512]{1,0:T(8,128)(2,1)S(1)}, u32[]{:S(2)}, u32[]{:S(2)}) collective-permute-start(bf16[640,512]{1,0:T(8,128)(2,1)S(1)} %collective-permute-done.15), channel_id=1, source_target_pairs={{0,4},{1,5},{2,14},{3,15},{4,8},{5,9},{6,2},{7,3},{8,12},{9,13},{1... | collective-permute-start | bytes 1966088 | tf_op jit(solution)/shard_map/ppermute | solution.py:29
  123.8 4.2 %collective-permute-start.22 = (bf16[640,512]{1,0:T(8,128)(2,1)S(1)}, bf16[640,512]{1,0:T(8,128)(2,1)S(1)}, u32[]{:S(2)}, u32[]{:S(2)}) collective-permute-start(bf16[640,512]{1,0:T(8,128)(2,1)S(1)} %collective-permute-done.21), channel_id=1, source_target_pairs={{0,4},{1,5},{2,14},{3,15},{4,8},{5,9},{6,2},{7,3},{8,12},{9,13},{1... | collective-permute-start | bytes 1966088 | tf_op jit(solution)/shard_map/ppermute | solution.py:29
  131.0 3.5 %collective-permute-start.17 = (bf16[384,512]{1,0:T(8,128)(2,1)S(1)}, bf16[384,512]{1,0:T(8,128)(2,1)S(1)}, u32[]{:S(2)}, u32[]{:S(2)}) collective-permute-start(bf16[384,512]{1,0:T(8,128)(2,1)S(1)} %slice.133), channel_id=1, source_target_pairs={{0,1},{1,0},{2,3},{3,2},{4,5},{5,4},{6,7},{7,6},{8,9},{9,8},{10,11... | collective-permute-start | bytes 1179656 | tf_op jit(solution)/shard_map/ppermute | solution.py:29
  138.0 3.5 %collective-permute-start.23 = (bf16[384,512]{1,0:T(8,128)(2,1)S(1)}, bf16[384,512]{1,0:T(8,128)(2,1)S(1)}, u32[]{:S(2)}, u32[]{:S(2)}) collective-permute-start(bf16[384,512]{1,0:T(8,128)(2,1)S(1)} %slice.132), channel_id=1, source_target_pairs={{0,1},{1,0},{2,3},{3,2},{4,5},{5,4},{6,7},{7,6},{8,9},{9,8},{10,11... | collective-permute-start | bytes 1179656 | tf_op jit(solution)/shard_map/ppermute | solution.py:29
  143.8 13.7 %collective-permute-start.4 = (bf16[4,160,1024]{2,1,0:T(8,128)(2,1)}, bf16[4,160,1024]{2,1,0:T(8,128)(2,1)}, u32[]{:S(2)}, u32[]{:S(2)}) collective-permute-start(bf16[4,160,1024]{2,1,0:T(8,128)(2,1)} %get-tuple-element.43), channel_id=1, source_target_pairs={{0,2},{1,3},{2,0},{3,1},{4,6},{5,7},{6,4},{7,5},{8,10},{9,11},{10,... | collective-permute-start | bytes 3932168 | tf_op jit(solution)/shard_map/ppermute | solution.py:29
  157.7 3.1 %collective-permute-done.23 = bf16[384,512]{1,0:T(8,128)(2,1)S(1)} collective-permute-done((bf16[384,512]{1,0:T(8,128)(2,1)S(1)}, bf16[384,512]{1,0:T(8,128)(2,1)S(1)}, u32[]{:S(2)}, u32[]{:S(2)}) %collective-permute-start.23) | collective-permute-done | bytes 393248 | tf_op jit(solution)/shard_map/ppermute | solution.py:29
  161.7 12.5 %collective-permute-start.24 = (bf16[2,256,512]{2,1,0:T(8,128)(2,1)}, bf16[2,256,512]{2,1,0:T(8,128)(2,1)S(1)}, u32[]{:S(2)}, u32[]{:S(2)}) collective-permute-start(bf16[2,256,512]{2,1,0:T(8,128)(2,1)} %fusion.39), channel_id=1, source_target_pairs={{0,2},{1,3},{2,0},{3,1},{4,6},{5,7},{6,4},{7,5},{8,10},{9,11},{10,... | collective-permute-start | bytes 1572872 | tf_op jit(solution)/shard_map/ppermute | solution.py:29
  177.3 10.1 %attention.1 = bf16[2,128,512]{2,1,0:T(8,128)(2,1)} custom-call(bf16[2,384,512]{2,1,0:T(8,128)(2,1)} %pad_maximum_fusion.7.refs_0_, bf16[2,256,512]{2,1,0:T(8,128)(2,1)} %copy-done.1, f32[32,1024]{1,0:T(8,128)} %reshape.373.refs_2_), custom_call_target="tpu_custom_call" | custom-call | tf_op jit(solution)/shard_map/attention/pallas_call | solution.py:89
  194.2 4.3 %reshape.369 = bf16[1280,4,256]{2,1,0:T(4,128)(2,1)S(1)} reshape(bf16[4,2,160,1024]{3,2,1,0:T(8,128)(2,1)} %copy.22) | data formatting | bytes 5242880 | tf_op jit(solution)/shard_map/reshape | solution.py:208
  199.4 7.4 %collective-permute-start.27 = (bf16[256,512]{1,0:T(8,128)(2,1)S(1)}, bf16[256,512]{1,0:T(8,128)(2,1)S(1)}, u32[]{:S(2)}, u32[]{:S(2)}) collective-permute-start(bf16[256,512]{1,0:T(8,128)(2,1)S(1)} %maximum_select_fusion.1), channel_id=1, source_target_pairs={{0,32},{1,33},{2,34},{3,35},{4,36},{5,37},{6,38},{7,39},{8,40},{9,... | collective-permute-start | bytes 786440 | tf_op jit(solution)/shard_map/ppermute | solution.py:29
  206.8 5.5 %constant_dynamic-slice_fusion.2 = (bf16[1280,1,256]{2,1,0:T(2,128)(2,1)S(1)}, bf16[1280,1,256]{2,1,0:T(2,128)(2,1)S(1)}, bf16[1280,1,256]{2,1,0:T(2,128)(2,1)S(1)}, bf16[1280,1,256]{2,1,0:T(2,128)(2,1)S(1)}) fusion(bf16[1280,4,256]{2,1,0:T(4,128)(2,1)S(1)} %reshape.369, s32[]{:T(128)S(6)} %select_n.327, s32[]{:T(128)S(6)} %select_n.326, s32[]{:T(128)S(6)} %select_n.325, ...), kind=kLoop, calls=%fused_computation.112 | loop fusion | bytes 5242896 | tf_op jit(solution)/shard_map/jit(dynamic_index_in_dim)/dynamic_slice | solution.py:108
  214.2 4.5 %collective-permute-done.27 = bf16[256,512]{1,0:T(8,128)(2,1)S(1)} collective-permute-done((bf16[256,512]{1,0:T(8,128)(2,1)S(1)}, bf16[256,512]{1,0:T(8,128)(2,1)S(1)}, u32[]{:S(2)}, u32[]{:S(2)}) %collective-permute-start.27) | collective-permute-done | bytes 262176 | tf_op jit(solution)/shard_map/ppermute | solution.py:29
  221.2 3.4 %collective-permute-done.28 = bf16[256,512]{1,0:T(8,128)(2,1)S(1)} collective-permute-done((bf16[256,512]{1,0:T(8,128)(2,1)S(1)}, bf16[256,512]{1,0:T(8,128)(2,1)S(1)}, u32[]{:S(2)}, u32[]{:S(2)}) %collective-permute-start.28) | collective-permute-done | bytes 262176 | tf_op jit(solution)/shard_map/ppermute | solution.py:29
  225.7 4.5 %collective-permute-done.29 = bf16[256,512]{1,0:T(8,128)(2,1)S(1)} collective-permute-done((bf16[256,512]{1,0:T(8,128)(2,1)S(1)}, bf16[256,512]{1,0:T(8,128)(2,1)S(1)}, u32[]{:S(2)}, u32[]{:S(2)}) %collective-permute-start.29) | collective-permute-done | bytes 262176 | tf_op jit(solution)/shard_map/ppermute | solution.py:29
  230.7 3.3 %collective-permute-start.32 = (bf16[320,512]{1,0:T(8,128)(2,1)S(1)}, bf16[320,512]{1,0:T(8,128)(2,1)S(1)}, u32[]{:S(2)}, u32[]{:S(2)}) collective-permute-start(bf16[320,512]{1,0:T(8,128)(2,1)S(1)} %get-tuple-element.40), channel_id=1, source_target_pairs={{0,4},{1,5},{2,6},{3,7},{4,8},{5,9},{6,10},{7,11},{8,12},{9,13},{1... | collective-permute-start | bytes 983048 | tf_op jit(solution)/shard_map/ppermute | solution.py:29
  234.1 4.7 %collective-permute-start.31 = (bf16[320,512]{1,0:T(8,128)(2,1)S(1)}, bf16[320,512]{1,0:T(8,128)(2,1)S(1)}, u32[]{:S(2)}, u32[]{:S(2)}) collective-permute-start(bf16[320,512]{1,0:T(8,128)(2,1)S(1)} %get-tuple-element.41), channel_id=1, source_target_pairs={{0,8},{1,9},{2,10},{3,11},{4,12},{5,13},{6,14},{7,15},{8,0},{9,1},... | collective-permute-start | bytes 983048 | tf_op jit(solution)/shard_map/ppermute | solution.py:29
  243.3 7.9 %collective-permute-done.31 = bf16[320,512]{1,0:T(8,128)(2,1)S(1)} collective-permute-done((bf16[320,512]{1,0:T(8,128)(2,1)S(1)}, bf16[320,512]{1,0:T(8,128)(2,1)S(1)}, u32[]{:S(2)}, u32[]{:S(2)}) %collective-permute-start.31) | collective-permute-done | bytes 327712 | tf_op jit(solution)/shard_map/ppermute | solution.py:29
  252.8 5.2 %collective-permute-start.34 = (bf16[160,512]{1,0:T(8,128)(2,1)S(1)}, bf16[160,512]{1,0:T(8,128)(2,1)S(1)}, u32[]{:S(2)}, u32[]{:S(2)}) collective-permute-start(bf16[160,512]{1,0:T(8,128)(2,1)S(1)} %get-tuple-element.45), channel_id=1, source_target_pairs={{0,66},{2,64},{64,130},{66,128},{128,194},{130,192},{192,258},{194... | collective-permute-start | bytes 491528 | tf_op jit(solution)/shard_map/ppermute | solution.py:259
  258.1 4.0 %collective-permute-start.33 = (bf16[160,512]{1,0:T(8,128)(2,1)S(1)}, bf16[160,512]{1,0:T(8,128)(2,1)S(1)}, u32[]{:S(2)}, u32[]{:S(2)}) collective-permute-start(bf16[160,512]{1,0:T(8,128)(2,1)S(1)} %get-tuple-element.44), channel_id=1, source_target_pairs={{0,64},{2,66},{64,128},{66,130},{128,192},{130,194},{192,256},{194... | collective-permute-start | bytes 491528 | tf_op jit(solution)/shard_map/ppermute | solution.py:258
  262.1 7.5 %collective-permute-done.34 = bf16[160,512]{1,0:T(8,128)(2,1)S(1)} collective-permute-done((bf16[160,512]{1,0:T(8,128)(2,1)S(1)}, bf16[160,512]{1,0:T(8,128)(2,1)S(1)}, u32[]{:S(2)}, u32[]{:S(2)}) %collective-permute-start.34) | collective-permute-done | bytes 163872 | tf_op jit(solution)/shard_map/ppermute | solution.py:259
  (137 shorter events, 79.9 us)
Async XLA Ops:
  1.0 28.2 %collective-permute-start = (bf16[160,512]{1,0:T(8,128)(2,1)S(1)}, bf16[160,512]{1,0:T(8,128)(2,1)S(1)}, u32[]{:S(2)}, u32[]{:S(2)}) collective-permute-start(bf16[160,512]{1,0:T(8,128)(2,1)S(1)} %get-tuple-element.47), channel_id=1, source_target_pairs={{0,2},{1,3},{2,0},{3,1},{4,6},{5,7},{6,4},{7,5},{8,10},{9,11},{10,... | collective-permute-start | bytes 491528 | tf_op jit(solution)/shard_map/ppermute | solution.py:29
  9.8 19.3 %collective-permute-start.8 = (bf16[1,160]{1,0:T(2,128)(2,1)}, bf16[1,160]{1,0:T(2,128)(2,1)S(1)}, u32[]{:S(2)}, u32[]{:S(2)}) collective-permute-start(bf16[1,160]{1,0:T(2,128)(2,1)} %param.7), channel_id=1, source_target_pairs={{0,2},{1,3},{2,0},{3,1},{4,6},{5,7},{6,4},{7,5},{8,10},{9,11},{10,... | collective-permute-start | bytes 968 | tf_op jit(solution)/shard_map/ppermute | solution.py:29
  11.7 94.6 %collective-permute-start.5 = (bf16[2560,384]{1,0:T(8,128)(2,1)}, bf16[2560,384]{1,0:T(8,128)(2,1)}, u32[]{:S(2)}, u32[]{:S(2)}) collective-permute-start(bf16[2560,384]{1,0:T(8,128)(2,1)} %bitcast.103), channel_id=1, source_target_pairs={{0,2},{1,3},{2,0},{3,1},{4,6},{5,7},{6,4},{7,5},{8,10},{9,11},{10,... | collective-permute-start | bytes 5898248 | tf_op jit(solution)/shard_map/ppermute | solution.py:29
  14.9 68.8 %collective-permute-start.25 = (s32[16,3]{0,1:T(4,128)S(1)}, s32[16,3]{0,1:T(4,128)S(1)}, u32[]{:S(2)}, u32[]{:S(2)}) collective-permute-start(s32[16,3]{0,1:T(4,128)S(1)} %bitcast.114), channel_id=1, source_target_pairs={{0,1},{1,0},{2,3},{3,2},{4,5},{5,4},{6,7},{7,6},{8,9},{9,8},{10,11... | collective-permute-start | bytes 584 | tf_op jit(solution)/shard_map/ppermute | solution.py:29
  30.1 22.4 %collective-permute-start.9 = (f32[18,384]{1,0:T(8,128)S(1)}, f32[18,384]{1,0:T(8,128)S(1)}, u32[]{:S(2)}, u32[]{:S(2)}) collective-permute-start(f32[18,384]{1,0:T(8,128)S(1)} %select_maximum_fusion), channel_id=1, source_target_pairs={{0,4},{1,5},{2,6},{3,7},{4,0},{5,1},{6,2},{7,3},{8,12},{9,13},{10,... | collective-permute-start | bytes 82952 | tf_op jit(solution)/shard_map/ppermute | solution.py:29
  33.4 37.8 %collective-permute-start.18 = (bf16[320,512]{1,0:T(8,128)(2,1)S(1)}, bf16[320,512]{1,0:T(8,128)(2,1)}, u32[]{:S(2)}, u32[]{:S(2)}) collective-permute-start(bf16[320,512]{1,0:T(8,128)(2,1)S(1)} %collective-permute-done.6), channel_id=1, source_target_pairs={{0,32},{1,33},{2,34},{3,35},{4,36},{5,37},{6,38},{7,39},{8,40},{9,... | collective-permute-start | bytes 983048 | tf_op jit(solution)/shard_map/ppermute | solution.py:29
  60.6 15.0 %collective-permute-start.7 = (bf16[320,512]{1,0:T(8,128)(2,1)S(1)}, bf16[320,512]{1,0:T(8,128)(2,1)}, u32[]{:S(2)}, u32[]{:S(2)}) collective-permute-start(bf16[320,512]{1,0:T(8,128)(2,1)S(1)} %collective-permute-done.6), channel_id=1, source_target_pairs={{0,16},{1,17},{2,18},{3,19},{4,20},{5,21},{6,22},{7,23},{8,24},{9,... | collective-permute-start | bytes 983048 | tf_op jit(solution)/shard_map/ppermute | solution.py:29
  66.8 74.7 %collective-permute-start.3 = (bf16[160,1024]{1,0:T(8,128)(2,1)}, bf16[160,1024]{1,0:T(8,128)(2,1)}, u32[]{:S(2)}, u32[]{:S(2)}) collective-permute-start(bf16[160,1024]{1,0:T(8,128)(2,1)} %bitcast.110), channel_id=1, source_target_pairs={{0,12},{1,13},{2,14},{3,15},{4,0},{5,1},{6,2},{7,3},{8,4},{9,5},{1... | collective-permute-start | bytes 983048 | tf_op jit(solution)/shard_map/ppermute | solution.py:29
  71.2 8.4 %collective-permute-start.19 = (bf16[320,512]{1,0:T(8,128)(2,1)}, bf16[320,512]{1,0:T(8,128)(2,1)S(1)}, u32[]{:S(2)}, u32[]{:S(2)}) collective-permute-start(bf16[320,512]{1,0:T(8,128)(2,1)} %collective-permute-done.18), channel_id=1, source_target_pairs={{0,16},{1,17},{2,18},{3,19},{4,20},{5,21},{6,22},{7,23},{8,24},{9,... | collective-permute-start | bytes 983048 | tf_op jit(solution)/shard_map/ppermute | solution.py:29
  75.6 10.3 %collective-permute-start.12 = (f32[18,384]{1,0:T(8,128)S(1)}, f32[18,384]{1,0:T(8,128)S(1)}, u32[]{:S(2)}, u32[]{:S(2)}) collective-permute-start(f32[18,384]{1,0:T(8,128)S(1)} %add.476), channel_id=1, source_target_pairs={{0,32},{1,33},{2,34},{3,35},{4,36},{5,37},{6,38},{7,39},{8,40},{9,... | collective-permute-start | bytes 82952 | tf_op jit(solution)/shard_map/ppermute | solution.py:29
  79.6 18.1 %collective-permute-start.14 = (bf16[640,512]{1,0:T(8,128)(2,1)}, bf16[640,512]{1,0:T(8,128)(2,1)}, u32[]{:S(2)}, u32[]{:S(2)}) collective-permute-start(bf16[640,512]{1,0:T(8,128)(2,1)} %constant_dynamic-update-slice_fusion), channel_id=1, source_target_pairs={{0,4},{1,5},{2,14},{3,15},{4,8},{5,9},{6,2},{7,3},{8,12},{9,13},{1... | collective-permute-start | bytes 1966088 | tf_op jit(solution)/shard_map/ppermute | solution.py:29
  83.7 15.9 %collective-permute-start.20 = (bf16[640,512]{1,0:T(8,128)(2,1)}, bf16[640,512]{1,0:T(8,128)(2,1)}, u32[]{:S(2)}, u32[]{:S(2)}) collective-permute-start(bf16[640,512]{1,0:T(8,128)(2,1)} %constant_dynamic-update-slice_fusion.2), channel_id=1, source_target_pairs={{0,4},{1,5},{2,14},{3,15},{4,8},{5,9},{6,2},{7,3},{8,12},{9,13},{1... | collective-permute-start | bytes 1966088 | tf_op jit(solution)/shard_map/ppermute | solution.py:29
  85.9 8.2 %collective-permute-start.13 = (f32[2,256]{1,0:T(2,128)S(1)}, f32[2,256]{1,0:T(2,128)S(1)}, u32[]{:S(2)}, u32[]{:S(2)}) collective-permute-start(f32[2,256]{1,0:T(2,128)S(1)} %slice.81), channel_id=1, source_target_pairs={{0,1},{1,0},{2,3},{3,2},{4,5},{5,4},{6,7},{7,6},{8,9},{9,8},{10,11... | collective-permute-start | bytes 6152 | tf_op jit(solution)/shard_map/ppermute | solution.py:29
  94.2 47.3 %collective-permute-start.2 = (bf16[160,1024]{1,0:T(8,128)(2,1)S(1)}, bf16[160,1024]{1,0:T(8,128)(2,1)S(1)}, u32[]{:S(2)}, u32[]{:S(2)}) collective-permute-start(bf16[160,1024]{1,0:T(8,128)(2,1)S(1)} %bitcast.109), channel_id=1, source_target_pairs={{0,8},{1,9},{2,10},{3,11},{4,12},{5,13},{6,14},{7,15},{8,0},{9,1},... | collective-permute-start | bytes 983048 | tf_op jit(solution)/shard_map/ppermute | solution.py:29
  97.7 43.8 %collective-permute-start.1 = (bf16[160,1024]{1,0:T(8,128)(2,1)S(1)}, bf16[160,1024]{1,0:T(8,128)(2,1)S(1)}, u32[]{:S(2)}, u32[]{:S(2)}) collective-permute-start(bf16[160,1024]{1,0:T(8,128)(2,1)S(1)} %bitcast.108), channel_id=1, source_target_pairs={{0,4},{1,5},{2,6},{3,7},{4,8},{5,9},{6,10},{7,11},{8,12},{9,13},{1... | collective-permute-start | bytes 983048 | tf_op jit(solution)/shard_map/ppermute | solution.py:29
  99.6 17.3 %collective-permute-start.15 = (bf16[640,512]{1,0:T(8,128)(2,1)}, bf16[640,512]{1,0:T(8,128)(2,1)S(1)}, u32[]{:S(2)}, u32[]{:S(2)}) collective-permute-start(bf16[640,512]{1,0:T(8,128)(2,1)} %collective-permute-done.14), channel_id=1, source_target_pairs={{0,4},{1,5},{2,14},{3,15},{4,8},{5,9},{6,2},{7,3},{8,12},{9,13},{1... | collective-permute-start | bytes 1966088 | tf_op jit(solution)/shard_map/ppermute | solution.py:29
  106.3 17.5 %collective-permute-start.21 = (bf16[640,512]{1,0:T(8,128)(2,1)}, bf16[640,512]{1,0:T(8,128)(2,1)S(1)}, u32[]{:S(2)}, u32[]{:S(2)}) collective-permute-start(bf16[640,512]{1,0:T(8,128)(2,1)} %collective-permute-done.20), channel_id=1, source_target_pairs={{0,4},{1,5},{2,14},{3,15},{4,8},{5,9},{6,2},{7,3},{8,12},{9,13},{1... | collective-permute-start | bytes 1966088 | tf_op jit(solution)/shard_map/ppermute | solution.py:29
  117.0 13.1 %collective-permute-start.16 = (bf16[640,512]{1,0:T(8,128)(2,1)S(1)}, bf16[640,512]{1,0:T(8,128)(2,1)S(1)}, u32[]{:S(2)}, u32[]{:S(2)}) collective-permute-start(bf16[640,512]{1,0:T(8,128)(2,1)S(1)} %collective-permute-done.15), channel_id=1, source_target_pairs={{0,4},{1,5},{2,14},{3,15},{4,8},{5,9},{6,2},{7,3},{8,12},{9,13},{1... | collective-permute-start | bytes 1966088 | tf_op jit(solution)/shard_map/ppermute | solution.py:29
  123.8 13.2 %collective-permute-start.22 = (bf16[640,512]{1,0:T(8,128)(2,1)S(1)}, bf16[640,512]{1,0:T(8,128)(2,1)S(1)}, u32[]{:S(2)}, u32[]{:S(2)}) collective-permute-start(bf16[640,512]{1,0:T(8,128)(2,1)S(1)} %collective-permute-done.21), channel_id=1, source_target_pairs={{0,4},{1,5},{2,14},{3,15},{4,8},{5,9},{6,2},{7,3},{8,12},{9,13},{1... | collective-permute-start | bytes 1966088 | tf_op jit(solution)/shard_map/ppermute | solution.py:29
  131.0 26.5 %collective-permute-start.17 = (bf16[384,512]{1,0:T(8,128)(2,1)S(1)}, bf16[384,512]{1,0:T(8,128)(2,1)S(1)}, u32[]{:S(2)}, u32[]{:S(2)}) collective-permute-start(bf16[384,512]{1,0:T(8,128)(2,1)S(1)} %slice.133), channel_id=1, source_target_pairs={{0,1},{1,0},{2,3},{3,2},{4,5},{5,4},{6,7},{7,6},{8,9},{9,8},{10,11... | collective-permute-start | bytes 1179656 | tf_op jit(solution)/shard_map/ppermute | solution.py:29
  138.0 22.7 %collective-permute-start.23 = (bf16[384,512]{1,0:T(8,128)(2,1)S(1)}, bf16[384,512]{1,0:T(8,128)(2,1)S(1)}, u32[]{:S(2)}, u32[]{:S(2)}) collective-permute-start(bf16[384,512]{1,0:T(8,128)(2,1)S(1)} %slice.132), channel_id=1, source_target_pairs={{0,1},{1,0},{2,3},{3,2},{4,5},{5,4},{6,7},{7,6},{8,9},{9,8},{10,11... | collective-permute-start | bytes 1179656 | tf_op jit(solution)/shard_map/ppermute | solution.py:29
  143.8 47.1 %collective-permute-start.4 = (bf16[4,160,1024]{2,1,0:T(8,128)(2,1)}, bf16[4,160,1024]{2,1,0:T(8,128)(2,1)}, u32[]{:S(2)}, u32[]{:S(2)}) collective-permute-start(bf16[4,160,1024]{2,1,0:T(8,128)(2,1)} %get-tuple-element.43), channel_id=1, source_target_pairs={{0,2},{1,3},{2,0},{3,1},{4,6},{5,7},{6,4},{7,5},{8,10},{9,11},{10,... | collective-permute-start | bytes 3932168 | tf_op jit(solution)/shard_map/ppermute | solution.py:29
  161.7 14.8 %collective-permute-start.24 = (bf16[2,256,512]{2,1,0:T(8,128)(2,1)}, bf16[2,256,512]{2,1,0:T(8,128)(2,1)S(1)}, u32[]{:S(2)}, u32[]{:S(2)}) collective-permute-start(bf16[2,256,512]{2,1,0:T(8,128)(2,1)} %fusion.39), channel_id=1, source_target_pairs={{0,2},{1,3},{2,0},{3,1},{4,6},{5,7},{6,4},{7,5},{8,10},{9,11},{10,... | collective-permute-start | bytes 1572872 | tf_op jit(solution)/shard_map/ppermute | solution.py:29
  188.4 10.9 %collective-permute-start.26 = (bf16[128,512]{1,0:T(8,128)(2,1)S(1)}, bf16[128,512]{1,0:T(8,128)(2,1)S(1)}, u32[]{:S(2)}, u32[]{:S(2)}) collective-permute-start(bf16[128,512]{1,0:T(8,128)(2,1)S(1)} %get-tuple-element.49), channel_id=1, source_target_pairs={{0,1},{1,0},{2,3},{3,2},{4,5},{5,4},{6,7},{7,6},{8,9},{9,8},{10,11... | collective-permute-start | bytes 393224 | tf_op jit(solution)/shard_map/ppermute | solution.py:29
  199.4 19.3 %collective-permute-start.27 = (bf16[256,512]{1,0:T(8,128)(2,1)S(1)}, bf16[256,512]{1,0:T(8,128)(2,1)S(1)}, u32[]{:S(2)}, u32[]{:S(2)}) collective-permute-start(bf16[256,512]{1,0:T(8,128)(2,1)S(1)} %maximum_select_fusion.1), channel_id=1, source_target_pairs={{0,32},{1,33},{2,34},{3,35},{4,36},{5,37},{6,38},{7,39},{8,40},{9,... | collective-permute-start | bytes 786440 | tf_op jit(solution)/shard_map/ppermute | solution.py:29
  212.3 12.3 %collective-permute-start.28 = (bf16[256,512]{1,0:T(8,128)(2,1)S(1)}, bf16[256,512]{1,0:T(8,128)(2,1)S(1)}, u32[]{:S(2)}, u32[]{:S(2)}) collective-permute-start(bf16[256,512]{1,0:T(8,128)(2,1)S(1)} %maximum_select_fusion.1), channel_id=1, source_target_pairs={{0,16},{1,17},{2,18},{3,19},{4,20},{5,21},{6,22},{7,23},{8,24},{9,... | collective-permute-start | bytes 786440 | tf_op jit(solution)/shard_map/ppermute | solution.py:29
  218.7 11.4 %collective-permute-start.29 = (bf16[256,512]{1,0:T(8,128)(2,1)S(1)}, bf16[256,512]{1,0:T(8,128)(2,1)S(1)}, u32[]{:S(2)}, u32[]{:S(2)}) collective-permute-start(bf16[256,512]{1,0:T(8,128)(2,1)S(1)} %collective-permute-done.27), channel_id=1, source_target_pairs={{0,16},{1,17},{2,18},{3,19},{4,20},{5,21},{6,22},{7,23},{8,24},{9,... | collective-permute-start | bytes 786440 | tf_op jit(solution)/shard_map/ppermute | solution.py:29
  230.7 12.6 %collective-permute-start.32 = (bf16[320,512]{1,0:T(8,128)(2,1)S(1)}, bf16[320,512]{1,0:T(8,128)(2,1)S(1)}, u32[]{:S(2)}, u32[]{:S(2)}) collective-permute-start(bf16[320,512]{1,0:T(8,128)(2,1)S(1)} %get-tuple-element.40), channel_id=1, source_target_pairs={{0,4},{1,5},{2,6},{3,7},{4,8},{5,9},{6,10},{7,11},{8,12},{9,13},{1... | collective-permute-start | bytes 983048 | tf_op jit(solution)/shard_map/ppermute | solution.py:29
  234.1 17.1 %collective-permute-start.31 = (bf16[320,512]{1,0:T(8,128)(2,1)S(1)}, bf16[320,512]{1,0:T(8,128)(2,1)S(1)}, u32[]{:S(2)}, u32[]{:S(2)}) collective-permute-start(bf16[320,512]{1,0:T(8,128)(2,1)S(1)} %get-tuple-element.41), channel_id=1, source_target_pairs={{0,8},{1,9},{2,10},{3,11},{4,12},{5,13},{6,14},{7,15},{8,0},{9,1},... | collective-permute-start | bytes 983048 | tf_op jit(solution)/shard_map/ppermute | solution.py:29
  238.8 13.8 %collective-permute-start.30 = (bf16[320,512]{1,0:T(8,128)(2,1)S(1)}, bf16[320,512]{1,0:T(8,128)(2,1)S(1)}, u32[]{:S(2)}, u32[]{:S(2)}) collective-permute-start(bf16[320,512]{1,0:T(8,128)(2,1)S(1)} %get-tuple-element.39), channel_id=1, source_target_pairs={{0,12},{1,13},{2,14},{3,15},{4,0},{5,1},{6,2},{7,3},{8,4},{9,5},{1... | collective-permute-start | bytes 983048 | tf_op jit(solution)/shard_map/ppermute | solution.py:29
  252.8 16.7 %collective-permute-start.34 = (bf16[160,512]{1,0:T(8,128)(2,1)S(1)}, bf16[160,512]{1,0:T(8,128)(2,1)S(1)}, u32[]{:S(2)}, u32[]{:S(2)}) collective-permute-start(bf16[160,512]{1,0:T(8,128)(2,1)S(1)} %get-tuple-element.45), channel_id=1, source_target_pairs={{0,66},{2,64},{64,130},{66,128},{128,194},{130,192},{192,258},{194... | collective-permute-start | bytes 491528 | tf_op jit(solution)/shard_map/ppermute | solution.py:259
  258.1 12.1 %collective-permute-start.33 = (bf16[160,512]{1,0:T(8,128)(2,1)S(1)}, bf16[160,512]{1,0:T(8,128)(2,1)S(1)}, u32[]{:S(2)}, u32[]{:S(2)}) collective-permute-start(bf16[160,512]{1,0:T(8,128)(2,1)S(1)} %get-tuple-element.44), channel_id=1, source_target_pairs={{0,64},{2,66},{64,128},{66,130},{128,192},{130,194},{192,256},{194... | collective-permute-start | bytes 491528 | tf_op jit(solution)/shard_map/ppermute | solution.py:258
  (9 other events, 131.4 us)

commit v3 on v2

v3 whole, which is shorter than its diff:
```python
import math

import jax
import jax.numpy as jnp
from jax import lax
from jax.experimental import pallas as pl
from jax.experimental.pallas import tpu as pltpu
from jax.sharding import Mesh, PartitionSpec as P

BLOCK = 64
PLANE = ("yl", "x", "core", "seq")
DP = ("yl", "x", "core")
NEG = -1e30


def pairs_of(where):
    pairs = []
    for yl in range(4):
        for x in range(4):
            for core in range(2):
                for seq in range(2):
                    target = where(seq * 4 + yl, x, core)
                    if target is None:
                        continue
                    ty, tx, tc = target
                    source_at = ((yl * 4 + x) * 2 + core) * 2 + seq
                    target_at = (((ty % 4) * 4 + tx) * 2 + tc) * 2 + ty // 4
                    pairs.append((source_at, target_at))
    return pairs


def moved(value, where):
    return lax.ppermute(value, PLANE, pairs_of(where))


def moved_on(value, where):
    sections, plane = lax.axis_size("section"), 64
    pairs = [
        (i * plane + a, (i + 1) % sections * plane + b)
        for i in range(sections)
        for a, b in pairs_of(where)
    ]
    return lax.ppermute(value, ("section", *PLANE), pairs)


def swap_inner(y, x, core):
    if y in (2, 3):
        return y + 2, x, core
    if y in (4, 5):
        return y - 2, x, core
    return y, x, core


def other_seq(y, x, core):
    return (y + 4) % 8, x, core


def block_mask(query_ids, random_rows, global_ids, key_ids):
    query_col = query_ids[:, None]
    key_ids = key_ids[None, :]
    adjacent = jnp.abs(query_col - key_ids) <= 1
    key_global = jnp.any(key_ids[:, :, None] == global_ids[None, None, :], axis=2)
    query_global = jnp.any(query_col[:, :, None] == global_ids[None, None, :], axis=2)
    chosen = jnp.any(random_rows[:, None, :] == key_ids[:, :, None], axis=2)
    return adjacent | key_global | query_global | chosen


def attention_kernel(scale, query_ref, own_ref, other_ref, live_ref, out_ref, rows_ref, value_ref):
    size = query_ref.shape[0]

    @pl.when(pl.program_id(0) == 0)
    def _():
        step = own_ref.shape[2]
        for i in range(2):
            here, there = pl.ds(i * step, step), pl.ds((2 + i) * step, step)
            rows_ref[here, :] = own_ref[i, size : 2 * size, :].T
            rows_ref[there, :] = other_ref[i, :size, :].T
            value_ref[:, here] = own_ref[i, 2 * size :, :]
            value_ref[:, there] = other_ref[i, size:, :]

    scores = jnp.dot(rows_ref[...], query_ref[...], preferred_element_type=jnp.float32)
    keys, queries = scores.shape
    live = jnp.broadcast_to(live_ref[...][:, None, :] > 0, (keys // BLOCK, BLOCK, queries))
    scores = scores.reshape(keys // BLOCK, BLOCK, queries)
    scores = jnp.where(live, scores, NEG)
    highest = jnp.max(scores, axis=(0, 1), keepdims=True)
    weights = jnp.where(live, jnp.exp((scores - highest) * scale), 0.0)
    totals = jnp.sum(weights, axis=(0, 1), keepdims=True)[0]
    weights = weights.reshape(keys, queries).astype(jnp.bfloat16)
    mixed = jnp.dot(value_ref[...], weights, preferred_element_type=jnp.float32)
    out_ref[...] = (mixed / totals).astype(jnp.bfloat16)


def attention(query, own, other, live, at):
    size, step = query.shape
    tile = 128
    per = step // tile
    return pl.pallas_call(
        lambda *refs: attention_kernel(1.0 / math.sqrt(size), *refs),
        grid=(per,),
        in_specs=[
            pl.BlockSpec((size, tile), lambda i: (0, i)),
            pl.BlockSpec(own.shape, lambda i: (0, 0, 0)),
            pl.BlockSpec(other.shape, lambda i: (0, 0, 0)),
            pl.BlockSpec((live.shape[0], tile), lambda i: (0, at * per + i)),
        ],
        out_specs=pl.BlockSpec((size, tile), lambda i: (0, i)),
        out_shape=jax.ShapeDtypeStruct(query.shape, jnp.bfloat16),
        scratch_shapes=[
            pltpu.VMEM((4 * step, size), jnp.bfloat16),
            pltpu.VMEM((size, 4 * step), jnp.bfloat16),
        ],
        cost_estimate=pl.CostEstimate(
            flops=16 * size * step * step, bytes_accessed=6 * size * step, transcendentals=4 * step * step
        ),
        name="attention",
    )(query, own, other, live)


def slices_kernel(at_ref, source_ref, out_ref, sems):
    rings, _, width = out_ref.shape
    per = width // 4
    copies = []
    for r in range(rings):
        for p in range(4):
            start = pl.multiple_of(at_ref[r * 4 + p] * per, per)
            copies.append(
                pltpu.make_async_copy(
                    source_ref.at[:, pl.ds(start, per)],
                    out_ref.at[r, :, pl.ds(p * per, per)],
                    sems.at[r * 4 + p],
                )
            )
    for copy in copies:
        copy.start()
    for copy in copies:
        copy.wait()


def column_slices(matrix, at):
    rows, width = matrix.shape
    return pl.pallas_call(
        slices_kernel,
        in_specs=[pl.BlockSpec(memory_space=pltpu.SMEM), pl.BlockSpec(memory_space=pl.ANY)],
        out_specs=pl.BlockSpec(memory_space=pl.ANY),
        out_shape=jax.ShapeDtypeStruct((4, rows, width // 4), matrix.dtype),
        scratch_shapes=[pltpu.SemaphoreType.DMA((16,))],
        cost_estimate=pl.CostEstimate(
            flops=0, bytes_accessed=4 * rows * width, transcendentals=0
        ),
        name="column_slices",
    )(at, matrix)


def at_index(array, index, axis=0):
    return lax.dynamic_index_in_dim(array, index, axis=axis, keepdims=False)


def other_core(y, x, core):
    return y, x, 1 - core


def pair(y, x, core):
    return y ^ 1, x, core


def by_two(y, x, core):
    return y ^ 2, x, core


def around(y, x, core):
    return y, (x + 1 - 2 * core) % 4, core


def same(y, x, core):
    return y, x, core


def shards(section_input, norm_gain, qkv_weight, out_weight, random_blocks, global_blocks):
    yl, x, core, seq = (lax.axis_index(axis) for axis in PLANE)
    f32, bf16 = jnp.float32, jnp.bfloat16
    tokens_t = section_input[0].T
    part, length = tokens_t.shape
    step = length // 2
    width = part * 32
    first = yl // 2

    def of_core(array):
        halves = array[:, :step], array[:, step:]
        return jnp.where(core == 0, *halves), jnp.where(core == 0, *halves[::-1])

    top = float(jnp.finfo(bf16).max)
    gained = tokens_t.astype(f32) * norm_gain.astype(f32).T
    gained = jnp.clip(gained, -top, top).astype(bf16)
    own, away = of_core(gained)
    crossed = moved(away, lambda *at: other_core(*swap_inner(*at)))
    e = jnp.concatenate([moved(own, swap_inner), crossed], axis=0)
    f = moved(e, by_two)
    e_pair = moved(e, pair)
    e = jnp.concatenate([e, e_pair], axis=0)
    f = jnp.concatenate([f, moved(f, pair)], axis=0)

    own, away = of_core(tokens_t)
    item = jnp.concatenate([own, moved(away, other_core)], axis=0)
    as_float = item.astype(f32)
    squares = jnp.sum(as_float * as_float, axis=0).reshape(step // 128, 128)
    squares = jnp.concatenate([squares, moved(squares, other_seq)], axis=0)
    for where in (
        lambda y, x, c: (y, x ^ 1, c),
        lambda y, x, c: (y, x ^ 2, c),
        pair,
        by_two,
    ):
        squares = squares + moved(squares, where)
    factors = lax.rsqrt(squares.reshape(2, 1, step) / width + 1e-05)
    factor_e = jnp.where(first == seq, factors[0], factors[1])
    factor_f = jnp.where(first == seq, factors[1], factors[0])

    out_t = out_weight[0].T
    order = jnp.stack([yl, yl ^ 2, yl ^ 1, yl ^ 3])
    ring = (x + jnp.arange(4, dtype=jnp.int32)) % 4
    slices = column_slices(out_t, (order[None, :] * 4 + ring[:, None]).reshape(-1))
    out_cols = jnp.stack(
        [moved_on(slices[r], lambda y, x, c, r=r: (y, (x + r) % 4, c)) for r in range(4)]
    )
    out_cols = jnp.stack([out_cols, moved(out_cols, other_core)])
    out_cols = out_cols.reshape(8 * part, -1)
    residual = moved_on(item, same)

    weight = qkv_weight[0]
    beside = moved(weight, other_core)
    columns = weight.shape[1]
    weight = jnp.concatenate(
        [jnp.where(core == seq, weight, beside), jnp.where(core == seq, beside, weight)], axis=1
    )
    weight = weight.reshape(2, 4, 2, part, 2 * columns)
    weights = []
    for k in range(4):
        source = (x - (1 - 2 * core) * k) % 4
        rows = []
        for ab in range(2):
            block = at_index(at_index(weight, ab ^ (yl % 2)), source)
            rows += [at_index(block, core), at_index(block, 1 - core)]
        weights.append(jnp.concatenate(rows, axis=0).T)

    def project(block, k, factor):
        normed = (block.astype(f32) * factor).astype(bf16)
        return jnp.dot(weights[k], normed, preferred_element_type=f32)

    count = step // BLOCK
    rows = jnp.stack([moved(random_blocks[0], other_seq), random_blocks[0]])
    rows = lax.dynamic_slice_in_dim(rows, core * count, count, axis=1).reshape(2 * count, -1)
    spot = jnp.arange(count, dtype=jnp.int32)

    def block_ids(halves, core):
        halves = jnp.stack(halves) * 2 * count
        return (halves[:, None] + core * count + spot[None, :]).reshape(-1)

    query_ids = block_ids([1 - seq, seq], core)
    key_ids = jnp.concatenate(
        [block_ids([first, 1 - first], core), block_ids([first, 1 - first], 1 - core)]
    )
    allowed = block_mask(query_ids, rows, global_blocks[0], key_ids)
    live = jnp.repeat(allowed.T.astype(f32), BLOCK, axis=1)

    partial_e, partial_f = project(e, 0, factor_e), project(f, 0, factor_f)
    for k in range(1, 4):
        e, f = moved(e, around), moved(f, around)
        partial_e = partial_e + project(e, k, factor_e)
        partial_f = partial_f + project(f, k, factor_f)
    joined = []
    for partial in (partial_e, partial_f):
        came = moved(partial[columns:].astype(bf16), other_seq)
        joined.append((partial[:columns] + came.astype(f32)).astype(bf16))
    head = columns // 3
    query_sent = jnp.where(first == seq, joined[1][:head], joined[0][:head])
    query_kept = jnp.where(first == seq, joined[0][:head], joined[1][:head])
    joined = jnp.stack(joined)
    other = moved(joined[:, head:], other_core)
    came = moved_on(attention(query_sent, joined, other, live, 0), other_seq)
    kept = moved_on(attention(query_kept, joined, other, live, 1), same)

    heads = jnp.concatenate(
        [jnp.where(seq == 0, kept, came), jnp.where(seq == 0, came, kept)], axis=0
    )
    far = moved(heads, by_two)
    blocks = [heads, far, moved(heads, pair), moved(far, pair)]
    per = heads.shape[0]
    added = 0.0
    for p, block in enumerate(blocks):
        added = added + jnp.dot(
            out_cols[:, p * per : (p + 1) * per], block, preferred_element_type=f32
        )
    added = added.reshape(2, 4, part, step)
    total = residual.astype(f32) + added[:, 0].reshape(2 * part, step)
    for r in range(1, 4):
        share = added[:, r].reshape(2 * part, step).astype(bf16)
        total = total + moved(share, lambda y, x, c, r=r: (y, (x - r) % 4, c)).astype(f32)
    result = total.astype(bf16)

    own, away = result[:part], moved(result[part:], other_core)
    handed_on = jnp.concatenate(
        [jnp.where(core == 0, own, away), jnp.where(core == 0, away, own)], axis=1
    )
    return handed_on.T[None]


def solution(mesh):
    fine = Mesh(mesh.devices.reshape(8, 4, 4, 2, 2), ("section", "yl", "x", "core", "seq"))
    placed = (
        P("section", "seq", DP),
        P("section", DP),
        P("section", "seq", DP),
        P("section", None, DP),
        P("section", "seq", None),
        P("section", None),
    )
    return jax.shard_map(
        shards, mesh=fine, in_specs=placed, out_specs=P("section", "seq", DP), check_vma=False
    )
```

time: 274 us -> 305 us (1.11)
  Pallas kernels: 10.1 us -> 53.7 us
  local copies, waits for them, and re-layouts: 34.3 us -> 13.5 us
  starting transfers between devices: 155 us -> 159 us
  waiting for transfers between devices: 44.6 us -> 47.9 us
    pallas_call x0 -> x1, Pallas kernels: none -> 41.6 us  [column_slices(): pl.pallas_call(slices_kernel, in_specs=[pl.BlockSpec(memory_space=pltpu.S...]
    dynamic_slice x3 -> x0, local copies, waits for them, and re-layouts: 13.9 us -> none  [at_index(): return lax.dynamic_index_in_dim(array, index, axis=axis, keepdims=False)]
    reshape x4 -> x0, local copies, waits for them, and re-layouts: 7.58 us -> none  [the longest x1 4.33 us: shards(): out_cols = out_cols.reshape(8 * part, 4, per)]
    ppermute x35 -> x37, starting transfers between devices: 155 us -> 159 us  [the longest x30 120 us: moved(): return lax.ppermute(value, PLANE, pairs_of(where))]
    ppermute x35 -> x37, waiting for transfers between devices: 44.6 us -> 47.9 us  [the longest x30 44 us: moved(): return lax.ppermute(value, PLANE, pairs_of(where))]
    pallas_call x1 -> x2, Pallas kernels: 10.1 us -> 12.1 us  [attention(): pl.pallas_call(lambda *refs: attention_kernel(1.0 / math.sqrt(size), *ref...]
    unnamed x20 -> x10, local copies, waits for them, and re-layouts: 6.3 us -> 5.18 us
  transfers between devices with their start and end apart: 35 -> 37, of which waited for: 15 -> 16; matrix products, arithmetic and copies ran while one was open for 21% -> 13% of each run, Pallas kernels for 4% -> 18%
where the time goes in v3:
time: 305 us; the launch traced here: 303 us
  starting transfers between devices  159 us (52%)
  Pallas kernels  53.7 us (18%)
  waiting for transfers between devices  47.9 us (16%)
  matrix products  14.1 us (5%)
  other arithmetic  14 us (5%)
  local copies, waits for them, and re-layouts  13.5 us (4%)
    ppermute x30, starting transfers between devices, moved(): return lax.ppermute(value, PLANE, pairs_of(where))  120 us
    ppermute x30, waiting for transfers between devices, moved(): return lax.ppermute(value, PLANE, pairs_of(where))  44 us
    pallas_call x1, Pallas kernels, column_slices(): pl.pallas_call(slices_kernel, in_specs=[pl.BlockSpec(memory_space=pltpu.S...  41.6 us
    ppermute x7, starting transfers between devices, moved_on(): return lax.ppermute(value, ('section', *PLANE), pairs)  38.4 us
    pallas_call x2, Pallas kernels, attention(): pl.pallas_call(lambda *refs: attention_kernel(1.0 / math.sqrt(size), *ref...  12.1 us
    dot_general x8, matrix products, project(): return jnp.dot(weights[k], normed, preferred_element_type=f32)  12 us
  transfers between devices with their start and end apart: 37, of which 16 were waited for; matrix products, arithmetic and copies ran while one was open for 13% of the time, Pallas kernels for 18%

profile of v3, /device:TPU:1, one launch (start us, length us, event | category | flops | bytes accessed | tf_op | source)
XLA Modules:
  0.0 303.0 jit_solution(14445036425064192862)
XLA Ops:
  0.0 8.9 %collective-permute-start.7 = (bf16[2560,384]{1,0:T(8,128)(2,1)}, bf16[2560,384]{1,0:T(8,128)(2,1)}, u32[]{:S(2)}, u32[]{:S(2)}) collective-permute-start(bf16[2560,384]{1,0:T(8,128)(2,1)} %bitcast.116), channel_id=1, source_target_pairs={{0,2},{1,3},{2,0},{3,1},{4,6},{5,7},{6,4},{7,5},{8,10},{9,11},{10,... | collective-permute-start | bytes 5898248 | tf_op jit(solution)/shard_map/ppermute | solution.py:33
  19.7 4.9 %collective-permute-start.27 = (s32[16,3]{0,1:T(4,128)S(1)}, s32[16,3]{0,1:T(4,128)S(1)}, u32[]{:S(2)}, u32[]{:S(2)}) collective-permute-start(s32[16,3]{0,1:T(4,128)S(1)} %bitcast.128), channel_id=1, source_target_pairs={{0,1},{1,0},{2,3},{3,2},{4,5},{5,4},{6,7},{7,6},{8,9},{9,8},{10,11... | collective-permute-start | bytes 584 | tf_op jit(solution)/shard_map/ppermute | solution.py:33
  25.6 41.6 %column_slices.1 = bf16[4,160,1024]{2,1,0:T(8,128)(2,1)} custom-call(s32[16]{0:T(128)} %add.403.at_ref, bf16[160,4096]{1,0:T(8,128)(2,1)} %bitcast.118), custom_call_target="tpu_custom_call" | custom-call | bytes 2621440 | tf_op jit(solution)/shard_map/column_slices/pallas_call | solution.py:142
  77.7 4.9 %collective-permute-start.11 = (f32[4,128]{1,0:T(4,128)S(1)}, f32[4,128]{1,0:T(4,128)S(1)}, u32[]{:S(2)}, u32[]{:S(2)}) collective-permute-start(f32[4,128]{1,0:T(4,128)S(1)} %bitcast.125), channel_id=1, source_target_pairs={{0,1},{1,0},{2,3},{3,2},{4,5},{5,4},{6,7},{7,6},{8,9},{9,8},{10,11... | collective-permute-start | bytes 6152 | tf_op jit(solution)/shard_map/ppermute | solution.py:33
  87.0 4.4 %collective-permute-start.16 = (bf16[640,512]{1,0:T(8,128)(2,1)}, bf16[640,512]{1,0:T(8,128)(2,1)}, u32[]{:S(2)}, u32[]{:S(2)}) collective-permute-start(bf16[640,512]{1,0:T(8,128)(2,1)} %constant_dynamic-update-slice_fusion.2), channel_id=1, source_target_pairs={{0,4},{1,5},{2,14},{3,15},{4,8},{5,9},{6,2},{7,3},{8,12},{9,13},{1... | collective-permute-start | bytes 1966088 | tf_op jit(solution)/shard_map/ppermute | solution.py:33
  99.1 4.7 %collective-permute-start.13 = (f32[8,128]{1,0:T(8,128)S(1)}, f32[8,128]{1,0:T(8,128)S(1)}, u32[]{:S(2)}, u32[]{:S(2)}) collective-permute-start(f32[8,128]{1,0:T(8,128)S(1)} %fusion.43), channel_id=1, source_target_pairs={{0,8},{1,9},{2,10},{3,11},{4,12},{5,13},{6,14},{7,15},{8,0},{9,1},... | collective-permute-start | bytes 12296 | tf_op jit(solution)/shard_map/ppermute | solution.py:33
  104.9 4.0 %collective-permute-start.2 = (bf16[160,1024]{1,0:T(8,128)(2,1)}, bf16[160,1024]{1,0:T(8,128)(2,1)}, u32[]{:S(2)}, u32[]{:S(2)}) collective-permute-start(bf16[160,1024]{1,0:T(8,128)(2,1)} %get-tuple-element.28), channel_id=1, source_target_pairs={{0,64},{1,65},{2,66},{3,67},{4,68},{5,69},{6,70},{7,71},{8,72},{9,... | collective-permute-start | bytes 983048 | tf_op jit(solution)/shard_map/ppermute | solution.py:43
  114.3 3.6 %collective-permute-start.22 = (bf16[640,512]{1,0:T(8,128)(2,1)}, bf16[640,512]{1,0:T(8,128)(2,1)}, u32[]{:S(2)}, u32[]{:S(2)}) collective-permute-start(bf16[640,512]{1,0:T(8,128)(2,1)} %constant_dynamic-update-slice_fusion.5), channel_id=1, source_target_pairs={{0,4},{1,5},{2,14},{3,15},{4,8},{5,9},{6,2},{7,3},{8,12},{9,13},{1... | collective-permute-start | bytes 1966088 | tf_op jit(solution)/shard_map/ppermute | solution.py:33
  117.9 3.2 %collective-permute-start.17 = (bf16[640,512]{1,0:T(8,128)(2,1)}, bf16[640,512]{1,0:T(8,128)(2,1)}, u32[]{:S(2)}, u32[]{:S(2)}) collective-permute-start(bf16[640,512]{1,0:T(8,128)(2,1)} %collective-permute-done.16), channel_id=1, source_target_pairs={{0,4},{1,5},{2,14},{3,15},{4,8},{5,9},{6,2},{7,3},{8,12},{9,13},{1... | collective-permute-start | bytes 1966088 | tf_op jit(solution)/shard_map/ppermute | solution.py:33
  123.3 3.6 %collective-permute-done.15 = f32[8,128]{1,0:T(8,128)S(1)} collective-permute-done((f32[8,128]{1,0:T(8,128)S(1)}, f32[8,128]{1,0:T(8,128)S(1)}, u32[]{:S(2)}, u32[]{:S(2)}) %collective-permute-start.15) | collective-permute-done | bytes 4128 | tf_op jit(solution)/shard_map/ppermute | solution.py:33
  127.0 3.4 %collective-permute-start.3 = (bf16[160,1024]{1,0:T(8,128)(2,1)S(1)}, bf16[160,1024]{1,0:T(8,128)(2,1)S(1)}, u32[]{:S(2)}, u32[]{:S(2)}) collective-permute-start(bf16[160,1024]{1,0:T(8,128)(2,1)S(1)} %get-tuple-element.31), channel_id=1, source_target_pairs={{0,68},{1,69},{2,70},{3,71},{4,72},{5,73},{6,74},{7,75},{8,76},{9,... | collective-permute-start | bytes 983048 | tf_op jit(solution)/shard_map/ppermute | solution.py:43
  130.5 4.8 %collective-permute-start.4 = (bf16[160,1024]{1,0:T(8,128)(2,1)S(1)}, bf16[160,1024]{1,0:T(8,128)(2,1)S(1)}, u32[]{:S(2)}, u32[]{:S(2)}) collective-permute-start(bf16[160,1024]{1,0:T(8,128)(2,1)S(1)} %get-tuple-element.30), channel_id=1, source_target_pairs={{0,72},{1,73},{2,74},{3,75},{4,76},{5,77},{6,78},{7,79},{8,64},{9,... | collective-permute-start | bytes 983048 | tf_op jit(solution)/shard_map/ppermute | solution.py:43
  135.3 3.0 collective-permute-start.23
  138.3 3.0 collective-permute-start.18
  153.7 4.3 %collective-permute-start.24 = (bf16[640,512]{1,0:T(8,128)(2,1)S(1)}, bf16[640,512]{1,0:T(8,128)(2,1)S(1)}, u32[]{:S(2)}, u32[]{:S(2)}) collective-permute-start(bf16[640,512]{1,0:T(8,128)(2,1)S(1)} %collective-permute-done.23), channel_id=1, source_target_pairs={{0,4},{1,5},{2,14},{3,15},{4,8},{5,9},{6,2},{7,3},{8,12},{9,13},{1... | collective-permute-start | bytes 1966088 | tf_op jit(solution)/shard_map/ppermute | solution.py:33
  160.9 5.7 %collective-permute-start.5 = (bf16[160,1024]{1,0:T(8,128)(2,1)S(1)}, bf16[160,1024]{1,0:T(8,128)(2,1)S(1)}, u32[]{:S(2)}, u32[]{:S(2)}) collective-permute-start(bf16[160,1024]{1,0:T(8,128)(2,1)S(1)} %get-tuple-element.29), channel_id=1, source_target_pairs={{0,76},{1,77},{2,78},{3,79},{4,64},{5,65},{6,66},{7,67},{8,68},{9,... | collective-permute-start | bytes 983048 | tf_op jit(solution)/shard_map/ppermute | solution.py:43
  167.9 5.3 %collective-permute-start.19 = (bf16[384,512]{1,0:T(8,128)(2,1)S(1)}, bf16[384,512]{1,0:T(8,128)(2,1)S(1)}, u32[]{:S(2)}, u32[]{:S(2)}) collective-permute-start(bf16[384,512]{1,0:T(8,128)(2,1)S(1)} %slice.190), channel_id=1, source_target_pairs={{0,1},{1,0},{2,3},{3,2},{4,5},{5,4},{6,7},{7,6},{8,9},{9,8},{10,11... | collective-permute-start | bytes 1179656 | tf_op jit(solution)/shard_map/ppermute | solution.py:33
  174.1 3.9 %collective-permute-start.25 = (bf16[384,512]{1,0:T(8,128)(2,1)S(1)}, bf16[384,512]{1,0:T(8,128)(2,1)S(1)}, u32[]{:S(2)}, u32[]{:S(2)}) collective-permute-start(bf16[384,512]{1,0:T(8,128)(2,1)S(1)} %slice.189), channel_id=1, source_target_pairs={{0,1},{1,0},{2,3},{3,2},{4,5},{5,4},{6,7},{7,6},{8,9},{9,8},{10,11... | collective-permute-start | bytes 1179656 | tf_op jit(solution)/shard_map/ppermute | solution.py:33
  180.3 17.5 %collective-permute-start.6 = (bf16[4,160,1024]{2,1,0:T(8,128)(2,1)}, bf16[4,160,1024]{2,1,0:T(8,128)(2,1)}, u32[]{:S(2)}, u32[]{:S(2)}) collective-permute-start(bf16[4,160,1024]{2,1,0:T(8,128)(2,1)} %get-tuple-element.27), channel_id=1, source_target_pairs={{0,2},{1,3},{2,0},{3,1},{4,6},{5,7},{6,4},{7,5},{8,10},{9,11},{10,... | collective-permute-start | bytes 3932168 | tf_op jit(solution)/shard_map/ppermute | solution.py:33
  198.2 11.8 %collective-permute-start.26 = (bf16[2,256,512]{2,1,0:T(8,128)(2,1)S(1)}, bf16[2,256,512]{2,1,0:T(8,128)(2,1)}, u32[]{:S(2)}, u32[]{:S(2)}) collective-permute-start(bf16[2,256,512]{2,1,0:T(8,128)(2,1)S(1)} %fusion.27), channel_id=1, source_target_pairs={{0,2},{1,3},{2,0},{3,1},{4,6},{5,7},{6,4},{7,5},{8,10},{9,11},{10,... | collective-permute-start | bytes 1572872 | tf_op jit(solution)/shard_map/ppermute | solution.py:33
  212.7 6.0 %attention.3 = bf16[128,512]{1,0:T(8,128)(2,1)} custom-call(bf16[128,512]{1,0:T(8,128)(2,1)} %get-tuple-element.33.refs_0_, bf16[2,384,512]{2,1,0:T(8,128)(2,1)} %pad_maximum_fusion.7.refs_1_, bf16[2,256,512]{2,1,0:T(8,128)(2,1)} %collective-permute-done.26.refs_2_, f32[32,1024]{1,0:T(8,128)} %reshape.380.refs_3_), custom_call_target="tpu_custom_call" | custom-call | flops 536870912 | bytes 393216 | tf_op jit(solution)/shard_map/attention/pallas_call | solution.py:98
  218.7 13.5 %collective-permute-start.29 = (bf16[128,512]{1,0:T(8,128)(2,1)}, bf16[128,512]{1,0:T(8,128)(2,1)S(1)}, u32[]{:S(2)}, u32[]{:S(2)}) collective-permute-start(bf16[128,512]{1,0:T(8,128)(2,1)} %attention.3), channel_id=1, source_target_pairs={{0,65},{1,64},{2,67},{3,66},{4,69},{5,68},{6,71},{7,70},{8,73},{9,... | collective-permute-start | bytes 393224 | tf_op jit(solution)/shard_map/ppermute | solution.py:43
  232.3 6.1 %attention.2 = bf16[128,512]{1,0:T(8,128)(2,1)} custom-call(bf16[128,512]{1,0:T(8,128)(2,1)} %get-tuple-element.32.refs_0_, bf16[2,384,512]{2,1,0:T(8,128)(2,1)} %pad_maximum_fusion.7.refs_1_, bf16[2,256,512]{2,1,0:T(8,128)(2,1)} %collective-permute-done.26.refs_2_, f32[32,1024]{1,0:T(8,128)} %reshape.380.refs_3_), custom_call_target="tpu_custom_call" | custom-call | flops 536870912 | bytes 393216 | tf_op jit(solution)/shard_map/attention/pallas_call | solution.py:98
  238.3 4.2 %collective-permute-start.28 = (bf16[128,512]{1,0:T(8,128)(2,1)}, bf16[128,512]{1,0:T(8,128)(2,1)S(1)}, u32[]{:S(2)}, u32[]{:S(2)}) collective-permute-start(bf16[128,512]{1,0:T(8,128)(2,1)} %attention.2), channel_id=1, source_target_pairs={{0,64},{1,65},{2,66},{3,67},{4,68},{5,69},{6,70},{7,71},{8,72},{9,... | collective-permute-start | bytes 393224 | tf_op jit(solution)/shard_map/ppermute | solution.py:43
  242.6 3.9 %collective-permute-done.28 = bf16[128,512]{1,0:T(8,128)(2,1)S(1)} collective-permute-done((bf16[128,512]{1,0:T(8,128)(2,1)}, bf16[128,512]{1,0:T(8,128)(2,1)S(1)}, u32[]{:S(2)}, u32[]{:S(2)}) %collective-permute-start.28) | collective-permute-done | bytes 131104 | tf_op jit(solution)/shard_map/ppermute | solution.py:43
  246.5 3.7 %collective-permute-start.30 = (bf16[256,512]{1,0:T(8,128)(2,1)S(1)}, bf16[256,512]{1,0:T(8,128)(2,1)S(1)}, u32[]{:S(2)}, u32[]{:S(2)}) collective-permute-start(bf16[256,512]{1,0:T(8,128)(2,1)S(1)} %pad_maximum_fusion.9), channel_id=1, source_target_pairs={{0,32},{1,33},{2,34},{3,35},{4,36},{5,37},{6,38},{7,39},{8,40},{9,... | collective-permute-start | bytes 786440 | tf_op jit(solution)/shard_map/ppermute | solution.py:33
  256.6 5.5 %collective-permute-done.30 = bf16[256,512]{1,0:T(8,128)(2,1)S(1)} collective-permute-done((bf16[256,512]{1,0:T(8,128)(2,1)S(1)}, bf16[256,512]{1,0:T(8,128)(2,1)S(1)}, u32[]{:S(2)}, u32[]{:S(2)}) %collective-permute-start.30) | collective-permute-done | bytes 262176 | tf_op jit(solution)/shard_map/ppermute | solution.py:33
  264.5 4.3 %collective-permute-done.31 = bf16[256,512]{1,0:T(8,128)(2,1)S(1)} collective-permute-done((bf16[256,512]{1,0:T(8,128)(2,1)S(1)}, bf16[256,512]{1,0:T(8,128)(2,1)S(1)}, u32[]{:S(2)}, u32[]{:S(2)}) %collective-permute-start.31) | collective-permute-done | bytes 262176 | tf_op jit(solution)/shard_map/ppermute | solution.py:33
  269.9 4.5 %collective-permute-done.32 = bf16[256,512]{1,0:T(8,128)(2,1)S(1)} collective-permute-done((bf16[256,512]{1,0:T(8,128)(2,1)S(1)}, bf16[256,512]{1,0:T(8,128)(2,1)S(1)}, u32[]{:S(2)}, u32[]{:S(2)}) %collective-permute-start.32) | collective-permute-done | bytes 262176 | tf_op jit(solution)/shard_map/ppermute | solution.py:33
  275.2 3.3 %collective-permute-start.33 = (bf16[320,512]{1,0:T(8,128)(2,1)S(1)}, bf16[320,512]{1,0:T(8,128)(2,1)S(1)}, u32[]{:S(2)}, u32[]{:S(2)}) collective-permute-start(bf16[320,512]{1,0:T(8,128)(2,1)S(1)} %bitcast.124), channel_id=1, source_target_pairs={{0,12},{1,13},{2,14},{3,15},{4,0},{5,1},{6,2},{7,3},{8,4},{9,5},{1... | collective-permute-start | bytes 983048 | tf_op jit(solution)/shard_map/ppermute | solution.py:33
  285.9 4.5 %collective-permute-done.34 = bf16[320,512]{1,0:T(8,128)(2,1)S(1)} collective-permute-done((bf16[320,512]{1,0:T(8,128)(2,1)S(1)}, bf16[320,512]{1,0:T(8,128)(2,1)S(1)}, u32[]{:S(2)}, u32[]{:S(2)}) %collective-permute-start.34) | collective-permute-done | bytes 327712 | tf_op jit(solution)/shard_map/ppermute | solution.py:33
  290.4 8.2 %collective-permute-done.35 = bf16[320,512]{1,0:T(8,128)(2,1)S(1)} collective-permute-done((bf16[320,512]{1,0:T(8,128)(2,1)S(1)}, bf16[320,512]{1,0:T(8,128)(2,1)S(1)}, u32[]{:S(2)}, u32[]{:S(2)}) %collective-permute-start.35) | collective-permute-done | bytes 327712 | tf_op jit(solution)/shard_map/ppermute | solution.py:33
  (125 shorter events, 88.0 us)
Async XLA Ops:
  0.0 138.3 %collective-permute-start.7 = (bf16[2560,384]{1,0:T(8,128)(2,1)}, bf16[2560,384]{1,0:T(8,128)(2,1)}, u32[]{:S(2)}, u32[]{:S(2)}) collective-permute-start(bf16[2560,384]{1,0:T(8,128)(2,1)} %bitcast.116), channel_id=1, source_target_pairs={{0,2},{1,3},{2,0},{3,1},{4,6},{5,7},{6,4},{7,5},{8,10},{9,11},{10,... | collective-permute-start | bytes 5898248 | tf_op jit(solution)/shard_map/ppermute | solution.py:33
  10.0 67.6 %collective-permute-start = (bf16[160,512]{1,0:T(8,128)(2,1)S(1)}, bf16[160,512]{1,0:T(8,128)(2,1)S(1)}, u32[]{:S(2)}, u32[]{:S(2)}) collective-permute-start(bf16[160,512]{1,0:T(8,128)(2,1)S(1)} %get-tuple-element.37), channel_id=1, source_target_pairs={{0,2},{1,3},{2,0},{3,1},{4,6},{5,7},{6,4},{7,5},{8,10},{9,11},{10,... | collective-permute-start | bytes 491528 | tf_op jit(solution)/shard_map/ppermute | solution.py:33
  14.4 55.0 %collective-permute-start.8 = (bf16[160,512]{1,0:T(8,128)(2,1)}, bf16[160,512]{1,0:T(8,128)(2,1)}, u32[]{:S(2)}, u32[]{:S(2)}) collective-permute-start(bf16[160,512]{1,0:T(8,128)(2,1)} %get-tuple-element.39), channel_id=1, source_target_pairs={{0,0},{1,32},{2,2},{3,34},{4,4},{5,36},{6,6},{7,38},{8,8},{9,40},{... | collective-permute-start | bytes 491528 | tf_op jit(solution)/shard_map/ppermute | solution.py:33
  17.3 53.9 %collective-permute-start.9 = (bf16[160,512]{1,0:T(8,128)(2,1)}, bf16[160,512]{1,0:T(8,128)(2,1)}, u32[]{:S(2)}, u32[]{:S(2)}) collective-permute-start(bf16[160,512]{1,0:T(8,128)(2,1)} %get-tuple-element.38), channel_id=1, source_target_pairs={{0,2},{1,34},{2,0},{3,32},{4,6},{5,38},{6,4},{7,36},{8,10},{9,42},... | collective-permute-start | bytes 491528 | tf_op jit(solution)/shard_map/ppermute | solution.py:33
  19.7 94.6 %collective-permute-start.27 = (s32[16,3]{0,1:T(4,128)S(1)}, s32[16,3]{0,1:T(4,128)S(1)}, u32[]{:S(2)}, u32[]{:S(2)}) collective-permute-start(s32[16,3]{0,1:T(4,128)S(1)} %bitcast.128), channel_id=1, source_target_pairs={{0,1},{1,0},{2,3},{3,2},{4,5},{5,4},{6,7},{7,6},{8,9},{9,8},{10,11... | collective-permute-start | bytes 584 | tf_op jit(solution)/shard_map/ppermute | solution.py:33
  72.9 12.4 %collective-permute-start.10 = (bf16[320,512]{1,0:T(8,128)(2,1)}, bf16[320,512]{1,0:T(8,128)(2,1)}, u32[]{:S(2)}, u32[]{:S(2)}) collective-permute-start(bf16[320,512]{1,0:T(8,128)(2,1)} %get-tuple-element.43), channel_id=1, source_target_pairs={{0,16},{1,17},{2,18},{3,19},{4,20},{5,21},{6,22},{7,23},{8,24},{9,... | collective-permute-start | bytes 983048 | tf_op jit(solution)/shard_map/ppermute | solution.py:33
  75.7 19.2 %collective-permute-start.20 = (bf16[320,512]{1,0:T(8,128)(2,1)}, bf16[320,512]{1,0:T(8,128)(2,1)}, u32[]{:S(2)}, u32[]{:S(2)}) collective-permute-start(bf16[320,512]{1,0:T(8,128)(2,1)} %get-tuple-element.43), channel_id=1, source_target_pairs={{0,32},{1,33},{2,34},{3,35},{4,36},{5,37},{6,38},{7,39},{8,40},{9,... | collective-permute-start | bytes 983048 | tf_op jit(solution)/shard_map/ppermute | solution.py:33
  77.7 14.5 %collective-permute-start.11 = (f32[4,128]{1,0:T(4,128)S(1)}, f32[4,128]{1,0:T(4,128)S(1)}, u32[]{:S(2)}, u32[]{:S(2)}) collective-permute-start(f32[4,128]{1,0:T(4,128)S(1)} %bitcast.125), channel_id=1, source_target_pairs={{0,1},{1,0},{2,3},{3,2},{4,5},{5,4},{6,7},{7,6},{8,9},{9,8},{10,11... | collective-permute-start | bytes 6152 | tf_op jit(solution)/shard_map/ppermute | solution.py:33
  87.0 30.9 %collective-permute-start.16 = (bf16[640,512]{1,0:T(8,128)(2,1)}, bf16[640,512]{1,0:T(8,128)(2,1)}, u32[]{:S(2)}, u32[]{:S(2)}) collective-permute-start(bf16[640,512]{1,0:T(8,128)(2,1)} %constant_dynamic-update-slice_fusion.2), channel_id=1, source_target_pairs={{0,4},{1,5},{2,14},{3,15},{4,8},{5,9},{6,2},{7,3},{8,12},{9,13},{1... | collective-permute-start | bytes 1966088 | tf_op jit(solution)/shard_map/ppermute | solution.py:33
  94.9 15.7 %collective-permute-start.21 = (bf16[320,512]{1,0:T(8,128)(2,1)}, bf16[320,512]{1,0:T(8,128)(2,1)}, u32[]{:S(2)}, u32[]{:S(2)}) collective-permute-start(bf16[320,512]{1,0:T(8,128)(2,1)} %collective-permute-done.20), channel_id=1, source_target_pairs={{0,16},{1,17},{2,18},{3,19},{4,20},{5,21},{6,22},{7,23},{8,24},{9,... | collective-permute-start | bytes 983048 | tf_op jit(solution)/shard_map/ppermute | solution.py:33
  104.9 69.2 %collective-permute-start.2 = (bf16[160,1024]{1,0:T(8,128)(2,1)}, bf16[160,1024]{1,0:T(8,128)(2,1)}, u32[]{:S(2)}, u32[]{:S(2)}) collective-permute-start(bf16[160,1024]{1,0:T(8,128)(2,1)} %get-tuple-element.28), channel_id=1, source_target_pairs={{0,64},{1,65},{2,66},{3,67},{4,68},{5,69},{6,70},{7,71},{8,72},{9,... | collective-permute-start | bytes 983048 | tf_op jit(solution)/shard_map/ppermute | solution.py:43
  110.6 10.7 %collective-permute-start.14 = (f32[8,128]{1,0:T(8,128)S(1)}, f32[8,128]{1,0:T(8,128)S(1)}, u32[]{:S(2)}, u32[]{:S(2)}) collective-permute-start(f32[8,128]{1,0:T(8,128)S(1)} %add.412), channel_id=1, source_target_pairs={{0,16},{1,17},{2,18},{3,19},{4,20},{5,21},{6,22},{7,23},{8,24},{9,... | collective-permute-start | bytes 12296 | tf_op jit(solution)/shard_map/ppermute | solution.py:33
  114.3 16.2 %collective-permute-start.22 = (bf16[640,512]{1,0:T(8,128)(2,1)}, bf16[640,512]{1,0:T(8,128)(2,1)}, u32[]{:S(2)}, u32[]{:S(2)}) collective-permute-start(bf16[640,512]{1,0:T(8,128)(2,1)} %constant_dynamic-update-slice_fusion.5), channel_id=1, source_target_pairs={{0,4},{1,5},{2,14},{3,15},{4,8},{5,9},{6,2},{7,3},{8,12},{9,13},{1... | collective-permute-start | bytes 1966088 | tf_op jit(solution)/shard_map/ppermute | solution.py:33
  117.9 17.3 %collective-permute-start.17 = (bf16[640,512]{1,0:T(8,128)(2,1)}, bf16[640,512]{1,0:T(8,128)(2,1)}, u32[]{:S(2)}, u32[]{:S(2)}) collective-permute-start(bf16[640,512]{1,0:T(8,128)(2,1)} %collective-permute-done.16), channel_id=1, source_target_pairs={{0,4},{1,5},{2,14},{3,15},{4,8},{5,9},{6,2},{7,3},{8,12},{9,13},{1... | collective-permute-start | bytes 1966088 | tf_op jit(solution)/shard_map/ppermute | solution.py:33
  127.0 51.0 %collective-permute-start.3 = (bf16[160,1024]{1,0:T(8,128)(2,1)S(1)}, bf16[160,1024]{1,0:T(8,128)(2,1)S(1)}, u32[]{:S(2)}, u32[]{:S(2)}) collective-permute-start(bf16[160,1024]{1,0:T(8,128)(2,1)S(1)} %get-tuple-element.31), channel_id=1, source_target_pairs={{0,68},{1,69},{2,70},{3,71},{4,72},{5,73},{6,74},{7,75},{8,76},{9,... | collective-permute-start | bytes 983048 | tf_op jit(solution)/shard_map/ppermute | solution.py:43
  130.5 47.5 %collective-permute-start.4 = (bf16[160,1024]{1,0:T(8,128)(2,1)S(1)}, bf16[160,1024]{1,0:T(8,128)(2,1)S(1)}, u32[]{:S(2)}, u32[]{:S(2)}) collective-permute-start(bf16[160,1024]{1,0:T(8,128)(2,1)S(1)} %get-tuple-element.30), channel_id=1, source_target_pairs={{0,72},{1,73},{2,74},{3,75},{4,76},{5,77},{6,78},{7,79},{8,64},{9,... | collective-permute-start | bytes 983048 | tf_op jit(solution)/shard_map/ppermute | solution.py:43
  135.3 18.4 %collective-permute-start.23 = (bf16[640,512]{1,0:T(8,128)(2,1)}, bf16[640,512]{1,0:T(8,128)(2,1)S(1)}, u32[]{:S(2)}, u32[]{:S(2)}) collective-permute-start(bf16[640,512]{1,0:T(8,128)(2,1)} %collective-permute-done.22), channel_id=1, source_target_pairs={{0,4},{1,5},{2,14},{3,15},{4,8},{5,9},{6,2},{7,3},{8,12},{9,13},{1... | collective-permute-start | bytes 1966088 | tf_op jit(solution)/shard_map/ppermute | solution.py:33
  138.3 22.6 %collective-permute-start.18 = (bf16[640,512]{1,0:T(8,128)(2,1)}, bf16[640,512]{1,0:T(8,128)(2,1)S(1)}, u32[]{:S(2)}, u32[]{:S(2)}) collective-permute-start(bf16[640,512]{1,0:T(8,128)(2,1)} %collective-permute-done.17), channel_id=1, source_target_pairs={{0,4},{1,5},{2,14},{3,15},{4,8},{5,9},{6,2},{7,3},{8,12},{9,13},{1... | collective-permute-start | bytes 1966088 | tf_op jit(solution)/shard_map/ppermute | solution.py:33
  153.7 14.2 %collective-permute-start.24 = (bf16[640,512]{1,0:T(8,128)(2,1)S(1)}, bf16[640,512]{1,0:T(8,128)(2,1)S(1)}, u32[]{:S(2)}, u32[]{:S(2)}) collective-permute-start(bf16[640,512]{1,0:T(8,128)(2,1)S(1)} %collective-permute-done.23), channel_id=1, source_target_pairs={{0,4},{1,5},{2,14},{3,15},{4,8},{5,9},{6,2},{7,3},{8,12},{9,13},{1... | collective-permute-start | bytes 1966088 | tf_op jit(solution)/shard_map/ppermute | solution.py:33
  160.9 17.1 %collective-permute-start.5 = (bf16[160,1024]{1,0:T(8,128)(2,1)S(1)}, bf16[160,1024]{1,0:T(8,128)(2,1)S(1)}, u32[]{:S(2)}, u32[]{:S(2)}) collective-permute-start(bf16[160,1024]{1,0:T(8,128)(2,1)S(1)} %get-tuple-element.29), channel_id=1, source_target_pairs={{0,76},{1,77},{2,78},{3,79},{4,64},{5,65},{6,66},{7,67},{8,68},{9,... | collective-permute-start | bytes 983048 | tf_op jit(solution)/shard_map/ppermute | solution.py:43
  167.9 29.9 %collective-permute-start.19 = (bf16[384,512]{1,0:T(8,128)(2,1)S(1)}, bf16[384,512]{1,0:T(8,128)(2,1)S(1)}, u32[]{:S(2)}, u32[]{:S(2)}) collective-permute-start(bf16[384,512]{1,0:T(8,128)(2,1)S(1)} %slice.190), channel_id=1, source_target_pairs={{0,1},{1,0},{2,3},{3,2},{4,5},{5,4},{6,7},{7,6},{8,9},{9,8},{10,11... | collective-permute-start | bytes 1179656 | tf_op jit(solution)/shard_map/ppermute | solution.py:33
  174.1 23.9 %collective-permute-start.25 = (bf16[384,512]{1,0:T(8,128)(2,1)S(1)}, bf16[384,512]{1,0:T(8,128)(2,1)S(1)}, u32[]{:S(2)}, u32[]{:S(2)}) collective-permute-start(bf16[384,512]{1,0:T(8,128)(2,1)S(1)} %slice.189), channel_id=1, source_target_pairs={{0,1},{1,0},{2,3},{3,2},{4,5},{5,4},{6,7},{7,6},{8,9},{9,8},{10,11... | collective-permute-start | bytes 1179656 | tf_op jit(solution)/shard_map/ppermute | solution.py:33
  180.3 72.8 %collective-permute-start.6 = (bf16[4,160,1024]{2,1,0:T(8,128)(2,1)}, bf16[4,160,1024]{2,1,0:T(8,128)(2,1)}, u32[]{:S(2)}, u32[]{:S(2)}) collective-permute-start(bf16[4,160,1024]{2,1,0:T(8,128)(2,1)} %get-tuple-element.27), channel_id=1, source_target_pairs={{0,2},{1,3},{2,0},{3,1},{4,6},{5,7},{6,4},{7,5},{8,10},{9,11},{10,... | collective-permute-start | bytes 3932168 | tf_op jit(solution)/shard_map/ppermute | solution.py:33
  198.2 14.5 %collective-permute-start.26 = (bf16[2,256,512]{2,1,0:T(8,128)(2,1)S(1)}, bf16[2,256,512]{2,1,0:T(8,128)(2,1)}, u32[]{:S(2)}, u32[]{:S(2)}) collective-permute-start(bf16[2,256,512]{2,1,0:T(8,128)(2,1)S(1)} %fusion.27), channel_id=1, source_target_pairs={{0,2},{1,3},{2,0},{3,1},{4,6},{5,7},{6,4},{7,5},{8,10},{9,11},{10,... | collective-permute-start | bytes 1572872 | tf_op jit(solution)/shard_map/ppermute | solution.py:33
  218.7 23.8 %collective-permute-start.29 = (bf16[128,512]{1,0:T(8,128)(2,1)}, bf16[128,512]{1,0:T(8,128)(2,1)S(1)}, u32[]{:S(2)}, u32[]{:S(2)}) collective-permute-start(bf16[128,512]{1,0:T(8,128)(2,1)} %attention.3), channel_id=1, source_target_pairs={{0,65},{1,64},{2,67},{3,66},{4,69},{5,68},{6,71},{7,70},{8,73},{9,... | collective-permute-start | bytes 393224 | tf_op jit(solution)/shard_map/ppermute | solution.py:43
  246.5 15.6 %collective-permute-start.30 = (bf16[256,512]{1,0:T(8,128)(2,1)S(1)}, bf16[256,512]{1,0:T(8,128)(2,1)S(1)}, u32[]{:S(2)}, u32[]{:S(2)}) collective-permute-start(bf16[256,512]{1,0:T(8,128)(2,1)S(1)} %pad_maximum_fusion.9), channel_id=1, source_target_pairs={{0,32},{1,33},{2,34},{3,35},{4,36},{5,37},{6,38},{7,39},{8,40},{9,... | collective-permute-start | bytes 786440 | tf_op jit(solution)/shard_map/ppermute | solution.py:33
  250.3 33.1 %collective-permute-start.1 = (bf16[320,512]{1,0:T(8,128)(2,1)S(1)}, bf16[320,512]{1,0:T(8,128)(2,1)S(1)}, u32[]{:S(2)}, u32[]{:S(2)}) collective-permute-start(bf16[320,512]{1,0:T(8,128)(2,1)S(1)} %pad_maximum_fusion.8), channel_id=1, source_target_pairs={{0,64},{1,65},{2,66},{3,67},{4,68},{5,69},{6,70},{7,71},{8,72},{9,... | collective-permute-start | bytes 983048 | tf_op jit(solution)/shard_map/ppermute | solution.py:43
  254.7 14.1 %collective-permute-start.31 = (bf16[256,512]{1,0:T(8,128)(2,1)S(1)}, bf16[256,512]{1,0:T(8,128)(2,1)S(1)}, u32[]{:S(2)}, u32[]{:S(2)}) collective-permute-start(bf16[256,512]{1,0:T(8,128)(2,1)S(1)} %pad_maximum_fusion.9), channel_id=1, source_target_pairs={{0,16},{1,17},{2,18},{3,19},{4,20},{5,21},{6,22},{7,23},{8,24},{9,... | collective-permute-start | bytes 786440 | tf_op jit(solution)/shard_map/ppermute | solution.py:33
  262.1 12.3 %collective-permute-start.32 = (bf16[256,512]{1,0:T(8,128)(2,1)S(1)}, bf16[256,512]{1,0:T(8,128)(2,1)S(1)}, u32[]{:S(2)}, u32[]{:S(2)}) collective-permute-start(bf16[256,512]{1,0:T(8,128)(2,1)S(1)} %collective-permute-done.30), channel_id=1, source_target_pairs={{0,16},{1,17},{2,18},{3,19},{4,20},{5,21},{6,22},{7,23},{8,24},{9,... | collective-permute-start | bytes 786440 | tf_op jit(solution)/shard_map/ppermute | solution.py:33
  275.2 10.7 %collective-permute-start.33 = (bf16[320,512]{1,0:T(8,128)(2,1)S(1)}, bf16[320,512]{1,0:T(8,128)(2,1)S(1)}, u32[]{:S(2)}, u32[]{:S(2)}) collective-permute-start(bf16[320,512]{1,0:T(8,128)(2,1)S(1)} %bitcast.124), channel_id=1, source_target_pairs={{0,12},{1,13},{2,14},{3,15},{4,0},{5,1},{6,2},{7,3},{8,4},{9,5},{1... | collective-permute-start | bytes 983048 | tf_op jit(solution)/shard_map/ppermute | solution.py:33
  278.5 11.9 %collective-permute-start.34 = (bf16[320,512]{1,0:T(8,128)(2,1)S(1)}, bf16[320,512]{1,0:T(8,128)(2,1)S(1)}, u32[]{:S(2)}, u32[]{:S(2)}) collective-permute-start(bf16[320,512]{1,0:T(8,128)(2,1)S(1)} %bitcast.123), channel_id=1, source_target_pairs={{0,8},{1,9},{2,10},{3,11},{4,12},{5,13},{6,14},{7,15},{8,0},{9,1},... | collective-permute-start | bytes 983048 | tf_op jit(solution)/shard_map/ppermute | solution.py:33
  281.4 17.1 %collective-permute-start.35 = (bf16[320,512]{1,0:T(8,128)(2,1)S(1)}, bf16[320,512]{1,0:T(8,128)(2,1)S(1)}, u32[]{:S(2)}, u32[]{:S(2)}) collective-permute-start(bf16[320,512]{1,0:T(8,128)(2,1)S(1)} %bitcast.122), channel_id=1, source_target_pairs={{0,4},{1,5},{2,6},{3,7},{4,8},{5,9},{6,10},{7,11},{8,12},{9,13},{1... | collective-permute-start | bytes 983048 | tf_op jit(solution)/shard_map/ppermute | solution.py:33
  (8 other events, 129.9 us)

commit v4 on v3

v4 whole, which is shorter than its diff:
```python
import math

import jax
import jax.numpy as jnp
from jax import lax
from jax.experimental import pallas as pl
from jax.experimental.pallas import tpu as pltpu
from jax.sharding import Mesh, PartitionSpec as P

BLOCK = 64
PLANE = ("yl", "x", "core", "seq")
DP = ("yl", "x", "core")
NEG = -1e30


def pairs_of(where):
    pairs = []
    for yl in range(4):
        for x in range(4):
            for core in range(2):
                for seq in range(2):
                    target = where(seq * 4 + yl, x, core)
                    if target is None:
                        continue
                    ty, tx, tc = target
                    source_at = ((yl * 4 + x) * 2 + core) * 2 + seq
                    target_at = (((ty % 4) * 4 + tx) * 2 + tc) * 2 + ty // 4
                    pairs.append((source_at, target_at))
    return pairs


def moved(value, where):
    return lax.ppermute(value, PLANE, pairs_of(where))


def moved_on(value, where):
    sections, plane = lax.axis_size("section"), 64
    pairs = [
        (i * plane + a, (i + 1) % sections * plane + b)
        for i in range(sections)
        for a, b in pairs_of(where)
    ]
    return lax.ppermute(value, ("section", *PLANE), pairs)


def swap_inner(y, x, core):
    if y in (2, 3):
        return y + 2, x, core
    if y in (4, 5):
        return y - 2, x, core
    return y, x, core


def other_seq(y, x, core):
    return (y + 4) % 8, x, core


def block_mask(query_ids, random_rows, global_ids, key_ids):
    query_col = query_ids[:, None]
    key_ids = key_ids[None, :]
    adjacent = jnp.abs(query_col - key_ids) <= 1
    key_global = jnp.any(key_ids[:, :, None] == global_ids[None, None, :], axis=2)
    query_global = jnp.any(query_col[:, :, None] == global_ids[None, None, :], axis=2)
    chosen = jnp.any(random_rows[:, None, :] == key_ids[:, :, None], axis=2)
    return adjacent | key_global | query_global | chosen


def attention_kernel(scale, query_ref, own_ref, other_ref, bias_ref, out_ref, rows_ref, value_ref, wide_ref):
    size = query_ref.shape[0]

    @pl.when(pl.program_id(0) == 0)
    def _():
        step = own_ref.shape[2]
        for i in range(2):
            here, there = pl.ds(i * step, step), pl.ds((2 + i) * step, step)
            rows_ref[here, :size] = own_ref[i, size : 2 * size, :].T
            rows_ref[there, :size] = other_ref[i, :size, :].T
            value_ref[:, here] = own_ref[i, 2 * size :, :]
            value_ref[:, there] = other_ref[i, size:, :]
        shape = (rows_ref.shape[0], size)
        block = lax.broadcasted_iota(jnp.int32, shape, 0) // BLOCK
        column = lax.broadcasted_iota(jnp.int32, shape, 1)
        rows_ref[:, size:] = jnp.where(block == column, 1.0, 0.0).astype(jnp.bfloat16)
        wide_ref[...] = jnp.zeros_like(wide_ref)

    wide_ref[:size, :] = query_ref[...]
    wide_ref[size : size + bias_ref.shape[0], :] = bias_ref[...]
    scores = jnp.dot(rows_ref[...], wide_ref[...], preferred_element_type=jnp.float32)
    highest = jnp.max(scores, axis=0, keepdims=True)
    weights = jnp.exp((scores - highest) * scale)
    totals = jnp.sum(weights, axis=0, keepdims=True)
    mixed = jnp.dot(
        value_ref[...], weights.astype(jnp.bfloat16), preferred_element_type=jnp.float32
    )
    out_ref[...] = (mixed / totals).astype(jnp.bfloat16)


def attention(query, own, other, bias, at):
    size, step = query.shape
    tile = 128
    per = step // tile
    return pl.pallas_call(
        lambda *refs: attention_kernel(1.0 / math.sqrt(size), *refs),
        grid=(per,),
        in_specs=[
            pl.BlockSpec((size, tile), lambda i: (0, i)),
            pl.BlockSpec(own.shape, lambda i: (0, 0, 0)),
            pl.BlockSpec(other.shape, lambda i: (0, 0, 0)),
            pl.BlockSpec((bias.shape[0], tile), lambda i: (0, at * per + i)),
        ],
        out_specs=pl.BlockSpec((size, tile), lambda i: (0, i)),
        out_shape=jax.ShapeDtypeStruct(query.shape, jnp.bfloat16),
        scratch_shapes=[
            pltpu.VMEM((4 * step, 2 * size), jnp.bfloat16),
            pltpu.VMEM((size, 4 * step), jnp.bfloat16),
            pltpu.VMEM((2 * size, tile), jnp.bfloat16),
        ],
        cost_estimate=pl.CostEstimate(
            flops=16 * size * step * step, bytes_accessed=6 * size * step, transcendentals=4 * step * step
        ),
        name="attention",
    )(query, own, other, bias)


def slices_kernel(order_ref, ring_ref, source_ref, *out_refs):
    for r, out_ref in enumerate(out_refs):
        per = out_ref.shape[1]
        start = pl.multiple_of(ring_ref[r] * per, per)
        out_ref[...] = source_ref[:, pl.ds(start, per)]


def column_slices(matrix, order, ring):
    rows, width = matrix.shape
    block = pl.BlockSpec((rows, width // 16), lambda p, order, ring: (0, p))
    return pl.pallas_call(
        slices_kernel,
        grid_spec=pltpu.PrefetchScalarGridSpec(
            num_scalar_prefetch=2,
            grid=(4,),
            in_specs=[pl.BlockSpec((rows, width // 4), lambda p, order, ring: (0, order[p]))],
            out_specs=[block] * 4,
        ),
        out_shape=[jax.ShapeDtypeStruct((rows, width // 4), matrix.dtype)] * 4,
        cost_estimate=pl.CostEstimate(
            flops=0, bytes_accessed=4 * rows * width, transcendentals=0
        ),
        name="column_slices",
    )(order, ring, matrix)


def rows_kernel(*refs):
    *parts, out_ref = refs
    start = 0
    for part in parts:
        out_ref[start : start + part.shape[0], :] = part[...]
        start += part.shape[0]


def stacked_rows(*parts):
    rows = sum(part.shape[0] for part in parts)
    vmem = pl.BlockSpec(memory_space=pltpu.VMEM)
    return pl.pallas_call(
        rows_kernel,
        in_specs=[vmem] * len(parts),
        out_specs=vmem,
        out_shape=jax.ShapeDtypeStruct((rows, parts[0].shape[1]), parts[0].dtype),
        cost_estimate=pl.CostEstimate(
            flops=0, bytes_accessed=4 * rows * parts[0].shape[1], transcendentals=0
        ),
        name="stacked_rows",
    )(*parts)


def after(value, earlier):
    return lax.optimization_barrier((value, earlier))[0]


def at_index(array, index, axis=0):
    return lax.dynamic_index_in_dim(array, index, axis=axis, keepdims=False)


def other_core(y, x, core):
    return y, x, 1 - core


def pair(y, x, core):
    return y ^ 1, x, core


def by_two(y, x, core):
    return y ^ 2, x, core


def around(y, x, core):
    return y, (x + 1 - 2 * core) % 4, core


def same(y, x, core):
    return y, x, core


def shards(section_input, norm_gain, qkv_weight, out_weight, random_blocks, global_blocks):
    yl, x, core, seq = (lax.axis_index(axis) for axis in PLANE)
    f32, bf16 = jnp.float32, jnp.bfloat16
    tokens_t = section_input[0].T
    part, length = tokens_t.shape
    step = length // 2
    width = part * 32
    first = yl // 2

    def of_core(array):
        halves = array[:, :step], array[:, step:]
        return jnp.where(core == 0, *halves), jnp.where(core == 0, *halves[::-1])

    own, away = of_core(tokens_t)
    crossed = moved(away, lambda *at: other_core(*swap_inner(*at)))
    e = stacked_rows(moved(own, swap_inner), crossed)
    f = moved(e, by_two)
    e_two = stacked_rows(e, moved(e, pair))
    f_two = stacked_rows(f, moved(f, pair))

    gain = norm_gain
    gain_row = jnp.pad(gain, ((0, 15), (0, step - part)))
    beside = moved(jnp.concatenate([away, gain_row], axis=0), other_core)
    gain = jnp.concatenate([gain, beside[part : part + 1, :part]], axis=1).astype(f32)
    item = jnp.concatenate([own, beside[:part]], axis=0)
    as_float = item.astype(f32)
    squares = jnp.sum(as_float * as_float, axis=0)
    random = random_blocks[0]
    numbers = jnp.pad(random.astype(f32).reshape(-1), (0, step - random.size))
    mine = jnp.stack([squares, numbers])
    theirs = moved(mine, other_seq)
    random = jnp.stack([theirs[1, : random.size].astype(jnp.int32).reshape(random.shape), random])
    slot = (yl * 4 + x == jnp.arange(16))[:, None]
    table = jnp.where(slot, jnp.pad(gain, ((0, 0), (0, step - 2 * part))), 0.0)
    table = jnp.concatenate([table, mine[:1], theirs[:1]], axis=0)
    for where in (
        lambda y, x, c: (y, x ^ 1, c),
        lambda y, x, c: (y, x ^ 2, c),
        pair,
        by_two,
    ):
        table = table + moved(table, where)
    factors = lax.rsqrt(table[16:] / width + 1e-05)
    factor_e = jnp.where(first == seq, factors[:1], factors[1:])
    factor_f = jnp.where(first == seq, factors[1:], factors[:1])
    gains = table[:16, : 2 * part].reshape(2, 2, 4, 2 * part)
    gains = at_index(gains, seq)

    weight = after(qkv_weight[0], beside)
    beside = moved(weight, other_core)
    columns = weight.shape[1]
    weight = jnp.concatenate(
        [jnp.where(core == seq, weight, beside), jnp.where(core == seq, beside, weight)], axis=1
    )
    weight = weight.reshape(2, 4, 2, part, 2 * columns)
    weights, scales = [], []
    for k in range(4):
        source = (x - (1 - 2 * core) * k) % 4
        rows, scale = [], []
        for ab in range(2):
            which = ab ^ (yl % 2)
            block = at_index(at_index(weight, which), source)
            rows += [at_index(block, core), at_index(block, 1 - core)]
            scale.append(at_index(at_index(gains, which), source))
        weights.append(jnp.concatenate(rows, axis=0).T)
        scales.append(jnp.concatenate(scale).reshape(4 * part, 1))

    order = after(jnp.stack([yl, yl ^ 2, yl ^ 1, yl ^ 3]), e)
    ring = (x + jnp.arange(4, dtype=jnp.int32)) % 4
    slices = column_slices(out_weight[0].T, order, ring)
    laid = jnp.concatenate([item[:part], item[part:]], axis=1)
    ahead = moved_on(stacked_rows(slices[0], laid), same)
    residual = ahead[part:]
    out_own = [ahead[:part]]
    for r in range(1, 4):
        out_own.append(moved_on(slices[r], lambda y, x, c, r=r: (y, (x + r) % 4, c)))
    out_own = stacked_rows(*out_own)
    out_cols = out_own, moved(out_own, other_core)

    def project(block, k, factor):
        normed = (block.astype(f32) * factor * scales[k]).astype(bf16)
        return jnp.dot(weights[k], normed, preferred_element_type=f32)

    count = step // BLOCK
    rows = lax.dynamic_slice_in_dim(random, core * count, count, axis=1).reshape(2 * count, -1)
    spot = jnp.arange(count, dtype=jnp.int32)

    def block_ids(halves, core):
        halves = jnp.stack(halves) * 2 * count
        return (halves[:, None] + core * count + spot[None, :]).reshape(-1)

    query_ids = block_ids([1 - seq, seq], core)
    key_ids = jnp.concatenate(
        [block_ids([first, 1 - first], core), block_ids([first, 1 - first], 1 - core)]
    )
    allowed = block_mask(query_ids, rows, global_blocks[0], key_ids)
    bias = jnp.repeat(jnp.where(allowed.T, 0.0, NEG), BLOCK, axis=1).astype(bf16)

    e, f = e_two, f_two
    partial_e, partial_f = project(e, 0, factor_e), project(f, 0, factor_f)
    for k in range(1, 4):
        e, f = moved(e, around), moved(f, around)
        partial_e = partial_e + project(e, k, factor_e)
        partial_f = partial_f + project(f, k, factor_f)
    joined = []
    for partial in (partial_e, partial_f):
        came = moved(partial[columns:].astype(bf16), other_seq)
        joined.append((partial[:columns] + came.astype(f32)).astype(bf16))
    head = columns // 3
    query_sent = jnp.where(first == seq, joined[1][:head], joined[0][:head])
    query_kept = jnp.where(first == seq, joined[0][:head], joined[1][:head])
    joined = jnp.stack(joined)
    other = moved(joined[:, head:], other_core)
    came = moved_on(attention(query_sent, joined, other, bias, 0), other_seq)
    kept = moved_on(attention(query_kept, joined, other, bias, 1), same)

    heads = jnp.concatenate(
        [jnp.where(seq == 0, kept, came), jnp.where(seq == 0, came, kept)], axis=0
    )
    far = moved(heads, by_two)
    blocks = [heads, far, moved(heads, pair), moved(far, pair)]
    per = heads.shape[0]
    added = []
    for cols in out_cols:
        total = 0.0
        for p, block in enumerate(blocks):
            total = total + jnp.dot(
                cols[:, p * per : (p + 1) * per], block, preferred_element_type=f32
            )
        added.append(total)
    total = jnp.concatenate([residual[:, :step], residual[:, step:]], axis=0).astype(f32)
    total = total + jnp.concatenate([half[:part] for half in added], axis=0)
    for r in range(1, 4):
        share = jnp.concatenate(
            [half[r * part : (r + 1) * part].astype(bf16) for half in added], axis=0
        )
        total = total + moved(share, lambda y, x, c, r=r: (y, (x - r) % 4, c)).astype(f32)
    result = total.astype(bf16)

    own, away = result[:part], moved(result[part:], other_core)
    handed_on = jnp.concatenate(
        [jnp.where(core == 0, own, away), jnp.where(core == 0, away, own)], axis=1
    )
    return handed_on.T[None]


def solution(mesh):
    fine = Mesh(mesh.devices.reshape(8, 4, 4, 2, 2), ("section", "yl", "x", "core", "seq"))
    placed = (
        P("section", "seq", DP),
        P("section", DP),
        P("section", "seq", DP),
        P("section", None, DP),
        P("section", "seq", None),
        P("section", None),
    )
    return jax.shard_map(
        shards, mesh=fine, in_specs=placed, out_specs=P("section", "seq", DP), check_vma=False
    )
```

time: 305 us -> 275 us (0.902)
  Pallas kernels: 53.7 us -> 27.2 us
  waiting for transfers between devices: 47.9 us -> 65 us
  starting transfers between devices: 159 us -> 143 us
  local copies, waits for them, and re-layouts: 13.5 us -> 10.4 us
    pallas_call x1 -> x6, Pallas kernels: 41.6 us -> 14.2 us  [the longest x5 10 us: stacked_rows(): pl.pallas_call(rows_kernel, in_specs=[vmem] * len(parts), out_specs=vmem,...]
    ppermute x30 -> x29, waiting for transfers between devices: 44 us -> 65 us  [moved(): return lax.ppermute(value, PLANE, pairs_of(where))]
    ppermute x30 -> x29, starting transfers between devices: 120 us -> 105 us  [moved(): return lax.ppermute(value, PLANE, pairs_of(where))]
    dot_general x8, matrix products: 12 us -> 7.91 us  [project(): return jnp.dot(weights[k], normed, preferred_element_type=f32)]
    ppermute x7 -> x6, waiting for transfers between devices: 3.88 us -> 0.02 us  [moved_on(): return lax.ppermute(value, ('section', *PLANE), pairs)]
    concatenate x2 -> x0, local copies, waits for them, and re-layouts: 3.45 us -> none  [the longest x1 1.73 us: shards(): f = jnp.concatenate([f, moved(f, pair)], axis=0)]
    another operation x4 -> x3, other arithmetic: 4.09 us -> 0.76 us  [the longest x1 0.66 us: shards(): order = after(jnp.stack([yl, yl ^ 2, yl ^ 1, yl ^ 3]), e)]
    ppermute x7 -> x6, starting transfers between devices: 38.4 us -> 37.4 us  [moved_on(): return lax.ppermute(value, ('section', *PLANE), pairs)]
  transfers between devices with their start and end apart: 37 -> 35, of which waited for: 16 -> 13; matrix products, arithmetic and copies ran while one was open for 13% -> 11% of each run, Pallas kernels for 18% -> 10%
where the time goes in v4:
time: 275 us; the launch traced here: 273 us
  starting transfers between devices  143 us (52%)
  waiting for transfers between devices  65 us (24%)
  Pallas kernels  27.2 us (10%)
  other arithmetic  15 us (5%)
  matrix products  11.5 us (4%)
  local copies, waits for them, and re-layouts  10.4 us (4%)
    ppermute x29, starting transfers between devices, moved(): return lax.ppermute(value, PLANE, pairs_of(where))  105 us
    ppermute x29, waiting for transfers between devices, moved(): return lax.ppermute(value, PLANE, pairs_of(where))  65 us
    ppermute x6, starting transfers between devices, moved_on(): return lax.ppermute(value, ('section', *PLANE), pairs)  37.4 us
    pallas_call x2, Pallas kernels, attention(): pl.pallas_call(lambda *refs: attention_kernel(1.0 / math.sqrt(size), *ref...  13 us
    pallas_call x5, Pallas kernels, stacked_rows(): pl.pallas_call(rows_kernel, in_specs=[vmem] * len(parts), out_specs=vmem,...  10 us
    dot_general x8, matrix products, project(): return jnp.dot(weights[k], normed, preferred_element_type=f32)  7.91 us
  transfers between devices with their start and end apart: 35, of which 13 were waited for; matrix products, arithmetic and copies ran while one was open for 11% of the time, Pallas kernels for 10%

profile of v4, /device:TPU:1, one launch (start us, length us, event | category | flops | bytes accessed | tf_op | source)
XLA Modules:
  0.0 273.0 jit_solution(3850975134697814568)
XLA Ops:
  1.0 8.8 %collective-permute-start.1 = (bf16[160,512]{1,0:T(8,128)(2,1)S(1)}, bf16[160,512]{1,0:T(8,128)(2,1)S(1)}, u32[]{:S(2)}, u32[]{:S(2)}) collective-permute-start(bf16[160,512]{1,0:T(8,128)(2,1)S(1)} %get-tuple-element.55), channel_id=1, source_target_pairs={{0,2},{1,34},{2,0},{3,32},{4,6},{5,38},{6,4},{7,36},{8,10},{9,42},... | collective-permute-start | bytes 491528 | tf_op jit(solution)/shard_map/ppermute | solution.py:33
  19.8 11.4 %collective-permute-start.18 = (bf16[320,512]{1,0:T(8,128)(2,1)}, bf16[320,512]{1,0:T(8,128)(2,1)S(1)}, u32[]{:S(2)}, u32[]{:S(2)}) collective-permute-start(bf16[320,512]{1,0:T(8,128)(2,1)} %stacked_rows.5.refs_0_), channel_id=1, source_target_pairs={{0,32},{1,33},{2,34},{3,35},{4,36},{5,37},{6,38},{7,39},{8,40},{9,... | collective-permute-start | bytes 983048 | tf_op jit(solution)/shard_map/ppermute | solution.py:33
  33.2 2.8 %collective-permute-start.7 = (bf16[2560,384]{1,0:T(8,128)(2,1)}, bf16[2560,384]{1,0:T(8,128)(2,1)}, u32[]{:S(2)}, u32[]{:S(2)}) collective-permute-start(bf16[2560,384]{1,0:T(8,128)(2,1)} %bitcast.75), channel_id=1, source_target_pairs={{0,2},{1,3},{2,0},{3,1},{4,6},{5,7},{6,4},{7,5},{8,10},{9,11},{10,... | collective-permute-start | bytes 5898248 | tf_op jit(solution)/shard_map/ppermute | solution.py:33
  36.2 4.5 %collective-permute-start.9 = (f32[2,512]{1,0:T(2,128)S(1)}, f32[2,512]{1,0:T(2,128)S(1)}, u32[]{:S(2)}, u32[]{:S(2)}) collective-permute-start(f32[2,512]{1,0:T(2,128)S(1)} %pad_maximum_fusion.20), channel_id=1, source_target_pairs={{0,1},{1,0},{2,3},{3,2},{4,5},{5,4},{6,7},{7,6},{8,9},{9,8},{10,11... | collective-permute-start | bytes 12296 | tf_op jit(solution)/shard_map/ppermute | solution.py:33
  40.8 4.5 %collective-permute-done.18.refs_0_ = bf16[320,512]{1,0:T(8,128)(2,1)S(1)} collective-permute-done((bf16[320,512]{1,0:T(8,128)(2,1)}, bf16[320,512]{1,0:T(8,128)(2,1)S(1)}, u32[]{:S(2)}, u32[]{:S(2)}) %collective-permute-start.18) | collective-permute-done | bytes 327712 | tf_op jit(solution)/shard_map/ppermute | solution.py:33
  47.3 3.1 %collective-permute-start.10 = (f32[18,512]{1,0:T(8,128)S(1)}, f32[18,512]{1,0:T(8,128)S(1)}, u32[]{:S(2)}, u32[]{:S(2)}) collective-permute-start(f32[18,512]{1,0:T(8,128)S(1)} %pad_maximum_fusion.19), channel_id=1, source_target_pairs={{0,4},{1,5},{2,6},{3,7},{4,0},{5,1},{6,2},{7,3},{8,12},{9,13},{10,... | collective-permute-start | bytes 110600 | tf_op jit(solution)/shard_map/ppermute | solution.py:33
  53.6 3.7 %collective-permute-start.14 = (bf16[640,512]{1,0:T(8,128)(2,1)}, bf16[640,512]{1,0:T(8,128)(2,1)S(1)}, u32[]{:S(2)}, u32[]{:S(2)}) collective-permute-start(bf16[640,512]{1,0:T(8,128)(2,1)} %stacked_rows.8), channel_id=1, source_target_pairs={{0,4},{1,5},{2,14},{3,15},{4,8},{5,9},{6,2},{7,3},{8,12},{9,13},{1... | collective-permute-start | bytes 1966088 | tf_op jit(solution)/shard_map/ppermute | solution.py:33
  60.1 3.6 %collective-permute-start.20 = (bf16[640,512]{1,0:T(8,128)(2,1)}, bf16[640,512]{1,0:T(8,128)(2,1)}, u32[]{:S(2)}, u32[]{:S(2)}) collective-permute-start(bf16[640,512]{1,0:T(8,128)(2,1)} %stacked_rows.9), channel_id=1, source_target_pairs={{0,4},{1,5},{2,14},{3,15},{4,8},{5,9},{6,2},{7,3},{8,12},{9,13},{1... | collective-permute-start | bytes 1966088 | tf_op jit(solution)/shard_map/ppermute | solution.py:33
  66.9 4.2 %column_slices.1 = (bf16[160,1024]{1,0:T(8,128)(2,1)}, bf16[160,1024]{1,0:T(8,128)(2,1)}, bf16[160,1024]{1,0:T(8,128)(2,1)}, bf16[160,1024]{1,0:T(8,128)(2,1)}) custom-call(s32[4]{0:T(128)} %pad_add_fusion.order_ref, s32[4]{0:T(128)} %and_select_fusion.ring_ref, bf16[160,4096]{1,0:T(8,128)(2,1)} %bitcast.77), custom_call_target="tpu_custom_call" | custom-call | bytes 2621440 | tf_op jit(solution)/shard_map/column_slices/pallas_call | solution.py:135
  71.1 4.4 %collective-permute-start.4 = (bf16[160,1024]{1,0:T(8,128)(2,1)}, bf16[160,1024]{1,0:T(8,128)(2,1)}, u32[]{:S(2)}, u32[]{:S(2)}) collective-permute-start(bf16[160,1024]{1,0:T(8,128)(2,1)} %get-tuple-element.13), channel_id=1, source_target_pairs={{0,68},{1,69},{2,70},{3,71},{4,72},{5,73},{6,74},{7,75},{8,76},{9,... | collective-permute-start | bytes 983048 | tf_op jit(solution)/shard_map/ppermute | solution.py:43
  80.4 6.1 %collective-permute-start.13 = (f32[18,512]{1,0:T(8,128)S(1)}, f32[18,512]{1,0:T(8,128)S(1)}, u32[]{:S(2)}, u32[]{:S(2)}) collective-permute-start(f32[18,512]{1,0:T(8,128)S(1)} %add.456), channel_id=1, source_target_pairs={{0,32},{1,33},{2,34},{3,35},{4,36},{5,37},{6,38},{7,39},{8,40},{9,... | collective-permute-start | bytes 110600 | tf_op jit(solution)/shard_map/ppermute | solution.py:33
  88.4 7.2 %collective-permute-start.5 = (bf16[160,1024]{1,0:T(8,128)(2,1)}, bf16[160,1024]{1,0:T(8,128)(2,1)}, u32[]{:S(2)}, u32[]{:S(2)}) collective-permute-start(bf16[160,1024]{1,0:T(8,128)(2,1)} %get-tuple-element.14), channel_id=1, source_target_pairs={{0,72},{1,73},{2,74},{3,75},{4,76},{5,77},{6,78},{7,79},{8,64},{9,... | collective-permute-start | bytes 983048 | tf_op jit(solution)/shard_map/ppermute | solution.py:43
  95.8 2.8 %collective-permute-start.15 = (bf16[640,512]{1,0:T(8,128)(2,1)S(1)}, bf16[640,512]{1,0:T(8,128)(2,1)S(1)}, u32[]{:S(2)}, u32[]{:S(2)}) collective-permute-start(bf16[640,512]{1,0:T(8,128)(2,1)S(1)} %collective-permute-done.14), channel_id=1, source_target_pairs={{0,4},{1,5},{2,14},{3,15},{4,8},{5,9},{6,2},{7,3},{8,12},{9,13},{1... | collective-permute-start | bytes 1966088 | tf_op jit(solution)/shard_map/ppermute | solution.py:33
  100.8 13.8 %collective-permute-done.15 = bf16[640,512]{1,0:T(8,128)(2,1)S(1)} collective-permute-done((bf16[640,512]{1,0:T(8,128)(2,1)S(1)}, bf16[640,512]{1,0:T(8,128)(2,1)S(1)}, u32[]{:S(2)}, u32[]{:S(2)}) %collective-permute-start.15) | collective-permute-done | bytes 655392 | tf_op jit(solution)/shard_map/ppermute | solution.py:33
  116.5 5.0 %collective-permute-done.21 = bf16[640,512]{1,0:T(8,128)(2,1)S(1)} collective-permute-done((bf16[640,512]{1,0:T(8,128)(2,1)}, bf16[640,512]{1,0:T(8,128)(2,1)S(1)}, u32[]{:S(2)}, u32[]{:S(2)}) %collective-permute-start.21) | collective-permute-done | bytes 655392 | tf_op jit(solution)/shard_map/ppermute | solution.py:33
  121.5 3.7 %collective-permute-start.16 = (bf16[640,512]{1,0:T(8,128)(2,1)S(1)}, bf16[640,512]{1,0:T(8,128)(2,1)S(1)}, u32[]{:S(2)}, u32[]{:S(2)}) collective-permute-start(bf16[640,512]{1,0:T(8,128)(2,1)S(1)} %collective-permute-done.15), channel_id=1, source_target_pairs={{0,4},{1,5},{2,14},{3,15},{4,8},{5,9},{6,2},{7,3},{8,12},{9,13},{1... | collective-permute-start | bytes 1966088 | tf_op jit(solution)/shard_map/ppermute | solution.py:33
  137.9 5.3 %collective-permute-start.17 = (bf16[384,512]{1,0:T(8,128)(2,1)S(1)}, bf16[384,512]{1,0:T(8,128)(2,1)}, u32[]{:S(2)}, u32[]{:S(2)}) collective-permute-start(bf16[384,512]{1,0:T(8,128)(2,1)S(1)} %slice.259), channel_id=1, source_target_pairs={{0,1},{1,0},{2,3},{3,2},{4,5},{5,4},{6,7},{7,6},{8,9},{9,8},{10,11... | collective-permute-start | bytes 1179656 | tf_op jit(solution)/shard_map/ppermute | solution.py:33
  145.3 5.3 %collective-permute-start.23 = (bf16[384,512]{1,0:T(8,128)(2,1)}, bf16[384,512]{1,0:T(8,128)(2,1)}, u32[]{:S(2)}, u32[]{:S(2)}) collective-permute-start(bf16[384,512]{1,0:T(8,128)(2,1)} %slice.258), channel_id=1, source_target_pairs={{0,1},{1,0},{2,3},{3,2},{4,5},{5,4},{6,7},{7,6},{8,9},{9,8},{10,11... | collective-permute-start | bytes 1179656 | tf_op jit(solution)/shard_map/ppermute | solution.py:33
  150.8 5.9 %collective-permute-done.17 = bf16[384,512]{1,0:T(8,128)(2,1)} collective-permute-done((bf16[384,512]{1,0:T(8,128)(2,1)S(1)}, bf16[384,512]{1,0:T(8,128)(2,1)}, u32[]{:S(2)}, u32[]{:S(2)}) %collective-permute-start.17) | collective-permute-done | bytes 393248 | tf_op jit(solution)/shard_map/ppermute | solution.py:33
  156.7 8.6 %collective-permute-start.3 = (bf16[320,1024]{1,0:T(8,128)(2,1)}, bf16[320,1024]{1,0:T(8,128)(2,1)}, u32[]{:S(2)}, u32[]{:S(2)}) collective-permute-start(bf16[320,1024]{1,0:T(8,128)(2,1)} %stacked_rows.6), channel_id=1, source_target_pairs={{0,64},{1,65},{2,66},{3,67},{4,68},{5,69},{6,70},{7,71},{8,72},{9,... | collective-permute-start | bytes 1966088 | tf_op jit(solution)/shard_map/ppermute | solution.py:43
  166.4 5.2 %collective-permute-done.23 = bf16[384,512]{1,0:T(8,128)(2,1)} collective-permute-done((bf16[384,512]{1,0:T(8,128)(2,1)}, bf16[384,512]{1,0:T(8,128)(2,1)}, u32[]{:S(2)}, u32[]{:S(2)}) %collective-permute-start.23) | collective-permute-done | bytes 393248 | tf_op jit(solution)/shard_map/ppermute | solution.py:33
  172.8 8.5 %collective-permute-start.24 = (bf16[2,256,512]{2,1,0:T(8,128)(2,1)S(1)}, bf16[2,256,512]{2,1,0:T(8,128)(2,1)S(1)}, u32[]{:S(2)}, u32[]{:S(2)}) collective-permute-start(bf16[2,256,512]{2,1,0:T(8,128)(2,1)S(1)} %fusion.30), channel_id=1, source_target_pairs={{0,2},{1,3},{2,0},{3,1},{4,6},{5,7},{6,4},{7,5},{8,10},{9,11},{10,... | collective-permute-start | bytes 1572872 | tf_op jit(solution)/shard_map/ppermute | solution.py:33
  184.9 6.5 %attention.3 = bf16[128,512]{1,0:T(8,128)(2,1)} custom-call(bf16[128,512]{1,0:T(8,128)(2,1)} %get-tuple-element.44.refs_0_, bf16[2,384,512]{2,1,0:T(8,128)(2,1)} %pad_maximum_fusion.5.refs_1_, bf16[2,256,512]{2,1,0:T(8,128)(2,1)} %copy-done.14, bf16[32,1024]{1,0:T(8,128)(2,1)} %convert_element_type.153.refs_3_), custom_call_target="tpu_custom_call" | custom-call | flops 536870912 | bytes 393216 | tf_op jit(solution)/shard_map/attention/pallas_call | solution.py:102
  191.4 10.1 %collective-permute-start.26 = (bf16[128,512]{1,0:T(8,128)(2,1)}, bf16[128,512]{1,0:T(8,128)(2,1)S(1)}, u32[]{:S(2)}, u32[]{:S(2)}) collective-permute-start(bf16[128,512]{1,0:T(8,128)(2,1)} %attention.3), channel_id=1, source_target_pairs={{0,65},{1,64},{2,67},{3,66},{4,69},{5,68},{6,71},{7,70},{8,73},{9,... | collective-permute-start | bytes 393224 | tf_op jit(solution)/shard_map/ppermute | solution.py:43
  201.4 6.5 %attention.2 = bf16[128,512]{1,0:T(8,128)(2,1)} custom-call(bf16[128,512]{1,0:T(8,128)(2,1)} %get-tuple-element.43.refs_0_, bf16[2,384,512]{2,1,0:T(8,128)(2,1)} %pad_maximum_fusion.5.refs_1_, bf16[2,256,512]{2,1,0:T(8,128)(2,1)} %copy-done.14, bf16[32,1024]{1,0:T(8,128)(2,1)} %convert_element_type.153.refs_3_), custom_call_target="tpu_custom_call" | custom-call | flops 536870912 | bytes 393216 | tf_op jit(solution)/shard_map/attention/pallas_call | solution.py:102
  208.0 5.2 %collective-permute-start.25 = (bf16[128,512]{1,0:T(8,128)(2,1)}, bf16[128,512]{1,0:T(8,128)(2,1)S(1)}, u32[]{:S(2)}, u32[]{:S(2)}) collective-permute-start(bf16[128,512]{1,0:T(8,128)(2,1)} %attention.2), channel_id=1, source_target_pairs={{0,64},{1,65},{2,66},{3,67},{4,68},{5,69},{6,70},{7,71},{8,72},{9,... | collective-permute-start | bytes 393224 | tf_op jit(solution)/shard_map/ppermute | solution.py:43
  224.1 10.3 %collective-permute-done.27 = bf16[256,512]{1,0:T(8,128)(2,1)S(1)} collective-permute-done((bf16[256,512]{1,0:T(8,128)(2,1)S(1)}, bf16[256,512]{1,0:T(8,128)(2,1)S(1)}, u32[]{:S(2)}, u32[]{:S(2)}) %collective-permute-start.27) | collective-permute-done | bytes 262176 | tf_op jit(solution)/shard_map/ppermute | solution.py:33
  239.3 4.3 %collective-permute-done.29 = bf16[256,512]{1,0:T(8,128)(2,1)S(1)} collective-permute-done((bf16[256,512]{1,0:T(8,128)(2,1)S(1)}, bf16[256,512]{1,0:T(8,128)(2,1)S(1)}, u32[]{:S(2)}, u32[]{:S(2)}) %collective-permute-start.29) | collective-permute-done | bytes 262176 | tf_op jit(solution)/shard_map/ppermute | solution.py:33
  244.4 4.0 %collective-permute-start.31 = (bf16[320,512]{1,0:T(8,128)(2,1)S(1)}, bf16[320,512]{1,0:T(8,128)(2,1)S(1)}, u32[]{:S(2)}, u32[]{:S(2)}) collective-permute-start(bf16[320,512]{1,0:T(8,128)(2,1)S(1)} %pad_maximum_fusion.7), channel_id=1, source_target_pairs={{0,12},{1,13},{2,14},{3,15},{4,0},{5,1},{6,2},{7,3},{8,4},{9,5},{1... | collective-permute-start | bytes 983048 | tf_op jit(solution)/shard_map/ppermute | solution.py:33
  248.5 3.2 %collective-permute-start.32 = (bf16[320,512]{1,0:T(8,128)(2,1)S(1)}, bf16[320,512]{1,0:T(8,128)(2,1)S(1)}, u32[]{:S(2)}, u32[]{:S(2)}) collective-permute-start(bf16[320,512]{1,0:T(8,128)(2,1)S(1)} %pad_maximum_fusion.8), channel_id=1, source_target_pairs={{0,8},{1,9},{2,10},{3,11},{4,12},{5,13},{6,14},{7,15},{8,0},{9,1},... | collective-permute-start | bytes 983048 | tf_op jit(solution)/shard_map/ppermute | solution.py:33
  255.6 3.9 %collective-permute-done.32 = bf16[320,512]{1,0:T(8,128)(2,1)S(1)} collective-permute-done((bf16[320,512]{1,0:T(8,128)(2,1)S(1)}, bf16[320,512]{1,0:T(8,128)(2,1)S(1)}, u32[]{:S(2)}, u32[]{:S(2)}) %collective-permute-start.32) | collective-permute-done | bytes 327712 | tf_op jit(solution)/shard_map/ppermute | solution.py:33
  259.5 9.0 %collective-permute-done.33 = bf16[320,512]{1,0:T(8,128)(2,1)S(1)} collective-permute-done((bf16[320,512]{1,0:T(8,128)(2,1)S(1)}, bf16[320,512]{1,0:T(8,128)(2,1)S(1)}, u32[]{:S(2)}, u32[]{:S(2)}) %collective-permute-start.33) | collective-permute-done | bytes 327712 | tf_op jit(solution)/shard_map/ppermute | solution.py:33
  (168 shorter events, 80.7 us)
Async XLA Ops:
  1.0 15.8 %collective-permute-start.1 = (bf16[160,512]{1,0:T(8,128)(2,1)S(1)}, bf16[160,512]{1,0:T(8,128)(2,1)S(1)}, u32[]{:S(2)}, u32[]{:S(2)}) collective-permute-start(bf16[160,512]{1,0:T(8,128)(2,1)S(1)} %get-tuple-element.55), channel_id=1, source_target_pairs={{0,2},{1,34},{2,0},{3,32},{4,6},{5,38},{6,4},{7,36},{8,10},{9,42},... | collective-permute-start | bytes 491528 | tf_op jit(solution)/shard_map/ppermute | solution.py:33
  10.5 22.7 %collective-permute-start.2 = (bf16[176,512]{1,0:T(8,128)(2,1)S(1)}, bf16[176,512]{1,0:T(8,128)(2,1)S(1)}, u32[]{:S(2)}, u32[]{:S(2)}) collective-permute-start(bf16[176,512]{1,0:T(8,128)(2,1)S(1)} %fusion.44), channel_id=1, source_target_pairs={{0,2},{1,3},{2,0},{3,1},{4,6},{5,7},{6,4},{7,5},{8,10},{9,11},{10,... | collective-permute-start | bytes 540680 | tf_op jit(solution)/shard_map/ppermute | solution.py:33
  19.8 25.4 %collective-permute-start.18 = (bf16[320,512]{1,0:T(8,128)(2,1)}, bf16[320,512]{1,0:T(8,128)(2,1)S(1)}, u32[]{:S(2)}, u32[]{:S(2)}) collective-permute-start(bf16[320,512]{1,0:T(8,128)(2,1)} %stacked_rows.5.refs_0_), channel_id=1, source_target_pairs={{0,32},{1,33},{2,34},{3,35},{4,36},{5,37},{6,38},{7,39},{8,40},{9,... | collective-permute-start | bytes 983048 | tf_op jit(solution)/shard_map/ppermute | solution.py:33
  31.3 19.6 %collective-permute-start.8 = (bf16[320,512]{1,0:T(8,128)(2,1)}, bf16[320,512]{1,0:T(8,128)(2,1)S(1)}, u32[]{:S(2)}, u32[]{:S(2)}) collective-permute-start(bf16[320,512]{1,0:T(8,128)(2,1)} %stacked_rows.5.refs_0_), channel_id=1, source_target_pairs={{0,16},{1,17},{2,18},{3,19},{4,20},{5,21},{6,22},{7,23},{8,24},{9,... | collective-permute-start | bytes 983048 | tf_op jit(solution)/shard_map/ppermute | solution.py:33
  33.2 92.0 %collective-permute-start.7 = (bf16[2560,384]{1,0:T(8,128)(2,1)}, bf16[2560,384]{1,0:T(8,128)(2,1)}, u32[]{:S(2)}, u32[]{:S(2)}) collective-permute-start(bf16[2560,384]{1,0:T(8,128)(2,1)} %bitcast.75), channel_id=1, source_target_pairs={{0,2},{1,3},{2,0},{3,1},{4,6},{5,7},{6,4},{7,5},{8,10},{9,11},{10,... | collective-permute-start | bytes 5898248 | tf_op jit(solution)/shard_map/ppermute | solution.py:33
  36.2 11.1 %collective-permute-start.9 = (f32[2,512]{1,0:T(2,128)S(1)}, f32[2,512]{1,0:T(2,128)S(1)}, u32[]{:S(2)}, u32[]{:S(2)}) collective-permute-start(f32[2,512]{1,0:T(2,128)S(1)} %pad_maximum_fusion.20), channel_id=1, source_target_pairs={{0,1},{1,0},{2,3},{3,2},{4,5},{5,4},{6,7},{7,6},{8,9},{9,8},{10,11... | collective-permute-start | bytes 12296 | tf_op jit(solution)/shard_map/ppermute | solution.py:33
  45.3 12.1 %collective-permute-start.19 = (bf16[320,512]{1,0:T(8,128)(2,1)S(1)}, bf16[320,512]{1,0:T(8,128)(2,1)S(1)}, u32[]{:S(2)}, u32[]{:S(2)}) collective-permute-start(bf16[320,512]{1,0:T(8,128)(2,1)S(1)} %collective-permute-done.18.refs_0_), channel_id=1, source_target_pairs={{0,16},{1,17},{2,18},{3,19},{4,20},{5,21},{6,22},{7,23},{8,24},{9,... | collective-permute-start | bytes 983048 | tf_op jit(solution)/shard_map/ppermute | solution.py:33
  47.3 16.4 %collective-permute-start.10 = (f32[18,512]{1,0:T(8,128)S(1)}, f32[18,512]{1,0:T(8,128)S(1)}, u32[]{:S(2)}, u32[]{:S(2)}) collective-permute-start(f32[18,512]{1,0:T(8,128)S(1)} %pad_maximum_fusion.19), channel_id=1, source_target_pairs={{0,4},{1,5},{2,6},{3,7},{4,0},{5,1},{6,2},{7,3},{8,12},{9,13},{10,... | collective-permute-start | bytes 110600 | tf_op jit(solution)/shard_map/ppermute | solution.py:33
  53.6 42.2 %collective-permute-start.14 = (bf16[640,512]{1,0:T(8,128)(2,1)}, bf16[640,512]{1,0:T(8,128)(2,1)S(1)}, u32[]{:S(2)}, u32[]{:S(2)}) collective-permute-start(bf16[640,512]{1,0:T(8,128)(2,1)} %stacked_rows.8), channel_id=1, source_target_pairs={{0,4},{1,5},{2,14},{3,15},{4,8},{5,9},{6,2},{7,3},{8,12},{9,13},{1... | collective-permute-start | bytes 1966088 | tf_op jit(solution)/shard_map/ppermute | solution.py:33
  60.1 38.6 %collective-permute-start.20 = (bf16[640,512]{1,0:T(8,128)(2,1)}, bf16[640,512]{1,0:T(8,128)(2,1)}, u32[]{:S(2)}, u32[]{:S(2)}) collective-permute-start(bf16[640,512]{1,0:T(8,128)(2,1)} %stacked_rows.9), channel_id=1, source_target_pairs={{0,4},{1,5},{2,14},{3,15},{4,8},{5,9},{6,2},{7,3},{8,12},{9,13},{1... | collective-permute-start | bytes 1966088 | tf_op jit(solution)/shard_map/ppermute | solution.py:33
  63.8 11.8 %collective-permute-start.11 = (f32[18,512]{1,0:T(8,128)S(1)}, f32[18,512]{1,0:T(8,128)S(1)}, u32[]{:S(2)}, u32[]{:S(2)}) collective-permute-start(f32[18,512]{1,0:T(8,128)S(1)} %fusion.72), channel_id=1, source_target_pairs={{0,8},{1,9},{2,10},{3,11},{4,12},{5,13},{6,14},{7,15},{8,0},{9,1},... | collective-permute-start | bytes 110600 | tf_op jit(solution)/shard_map/ppermute | solution.py:33
  71.1 143.9 %collective-permute-start.4 = (bf16[160,1024]{1,0:T(8,128)(2,1)}, bf16[160,1024]{1,0:T(8,128)(2,1)}, u32[]{:S(2)}, u32[]{:S(2)}) collective-permute-start(bf16[160,1024]{1,0:T(8,128)(2,1)} %get-tuple-element.13), channel_id=1, source_target_pairs={{0,68},{1,69},{2,70},{3,71},{4,72},{5,73},{6,74},{7,75},{8,76},{9,... | collective-permute-start | bytes 983048 | tf_op jit(solution)/shard_map/ppermute | solution.py:43
  80.4 8.0 %collective-permute-start.13 = (f32[18,512]{1,0:T(8,128)S(1)}, f32[18,512]{1,0:T(8,128)S(1)}, u32[]{:S(2)}, u32[]{:S(2)}) collective-permute-start(f32[18,512]{1,0:T(8,128)S(1)} %add.456), channel_id=1, source_target_pairs={{0,32},{1,33},{2,34},{3,35},{4,36},{5,37},{6,38},{7,39},{8,40},{9,... | collective-permute-start | bytes 110600 | tf_op jit(solution)/shard_map/ppermute | solution.py:33
  88.4 126.5 %collective-permute-start.5 = (bf16[160,1024]{1,0:T(8,128)(2,1)}, bf16[160,1024]{1,0:T(8,128)(2,1)}, u32[]{:S(2)}, u32[]{:S(2)}) collective-permute-start(bf16[160,1024]{1,0:T(8,128)(2,1)} %get-tuple-element.14), channel_id=1, source_target_pairs={{0,72},{1,73},{2,74},{3,75},{4,76},{5,77},{6,78},{7,79},{8,64},{9,... | collective-permute-start | bytes 983048 | tf_op jit(solution)/shard_map/ppermute | solution.py:43
  95.8 18.7 %collective-permute-start.15 = (bf16[640,512]{1,0:T(8,128)(2,1)S(1)}, bf16[640,512]{1,0:T(8,128)(2,1)S(1)}, u32[]{:S(2)}, u32[]{:S(2)}) collective-permute-start(bf16[640,512]{1,0:T(8,128)(2,1)S(1)} %collective-permute-done.14), channel_id=1, source_target_pairs={{0,4},{1,5},{2,14},{3,15},{4,8},{5,9},{6,2},{7,3},{8,12},{9,13},{1... | collective-permute-start | bytes 1966088 | tf_op jit(solution)/shard_map/ppermute | solution.py:33
  98.6 22.8 %collective-permute-start.21 = (bf16[640,512]{1,0:T(8,128)(2,1)}, bf16[640,512]{1,0:T(8,128)(2,1)S(1)}, u32[]{:S(2)}, u32[]{:S(2)}) collective-permute-start(bf16[640,512]{1,0:T(8,128)(2,1)} %collective-permute-done.20), channel_id=1, source_target_pairs={{0,4},{1,5},{2,14},{3,15},{4,8},{5,9},{6,2},{7,3},{8,12},{9,13},{1... | collective-permute-start | bytes 1966088 | tf_op jit(solution)/shard_map/ppermute | solution.py:33
  114.6 100.4 %collective-permute-start.6 = (bf16[160,1024]{1,0:T(8,128)(2,1)}, bf16[160,1024]{1,0:T(8,128)(2,1)}, u32[]{:S(2)}, u32[]{:S(2)}) collective-permute-start(bf16[160,1024]{1,0:T(8,128)(2,1)} %get-tuple-element.15), channel_id=1, source_target_pairs={{0,76},{1,77},{2,78},{3,79},{4,64},{5,65},{6,66},{7,67},{8,68},{9,... | collective-permute-start | bytes 983048 | tf_op jit(solution)/shard_map/ppermute | solution.py:43
  121.5 15.5 %collective-permute-start.16 = (bf16[640,512]{1,0:T(8,128)(2,1)S(1)}, bf16[640,512]{1,0:T(8,128)(2,1)S(1)}, u32[]{:S(2)}, u32[]{:S(2)}) collective-permute-start(bf16[640,512]{1,0:T(8,128)(2,1)S(1)} %collective-permute-done.15), channel_id=1, source_target_pairs={{0,4},{1,5},{2,14},{3,15},{4,8},{5,9},{6,2},{7,3},{8,12},{9,13},{1... | collective-permute-start | bytes 1966088 | tf_op jit(solution)/shard_map/ppermute | solution.py:33
  125.2 18.4 %collective-permute-start.22 = (bf16[640,512]{1,0:T(8,128)(2,1)S(1)}, bf16[640,512]{1,0:T(8,128)(2,1)S(1)}, u32[]{:S(2)}, u32[]{:S(2)}) collective-permute-start(bf16[640,512]{1,0:T(8,128)(2,1)S(1)} %collective-permute-done.21), channel_id=1, source_target_pairs={{0,4},{1,5},{2,14},{3,15},{4,8},{5,9},{6,2},{7,3},{8,12},{9,13},{1... | collective-permute-start | bytes 1966088 | tf_op jit(solution)/shard_map/ppermute | solution.py:33
  137.9 18.8 %collective-permute-start.17 = (bf16[384,512]{1,0:T(8,128)(2,1)S(1)}, bf16[384,512]{1,0:T(8,128)(2,1)}, u32[]{:S(2)}, u32[]{:S(2)}) collective-permute-start(bf16[384,512]{1,0:T(8,128)(2,1)S(1)} %slice.259), channel_id=1, source_target_pairs={{0,1},{1,0},{2,3},{3,2},{4,5},{5,4},{6,7},{7,6},{8,9},{9,8},{10,11... | collective-permute-start | bytes 1179656 | tf_op jit(solution)/shard_map/ppermute | solution.py:33
  145.3 26.3 %collective-permute-start.23 = (bf16[384,512]{1,0:T(8,128)(2,1)}, bf16[384,512]{1,0:T(8,128)(2,1)}, u32[]{:S(2)}, u32[]{:S(2)}) collective-permute-start(bf16[384,512]{1,0:T(8,128)(2,1)} %slice.258), channel_id=1, source_target_pairs={{0,1},{1,0},{2,3},{3,2},{4,5},{5,4},{6,7},{7,6},{8,9},{9,8},{10,11... | collective-permute-start | bytes 1179656 | tf_op jit(solution)/shard_map/ppermute | solution.py:33
  156.7 51.3 %collective-permute-start.3 = (bf16[320,1024]{1,0:T(8,128)(2,1)}, bf16[320,1024]{1,0:T(8,128)(2,1)}, u32[]{:S(2)}, u32[]{:S(2)}) collective-permute-start(bf16[320,1024]{1,0:T(8,128)(2,1)} %stacked_rows.6), channel_id=1, source_target_pairs={{0,64},{1,65},{2,66},{3,67},{4,68},{5,69},{6,70},{7,71},{8,72},{9,... | collective-permute-start | bytes 1966088 | tf_op jit(solution)/shard_map/ppermute | solution.py:43
  172.8 11.3 %collective-permute-start.24 = (bf16[2,256,512]{2,1,0:T(8,128)(2,1)S(1)}, bf16[2,256,512]{2,1,0:T(8,128)(2,1)S(1)}, u32[]{:S(2)}, u32[]{:S(2)}) collective-permute-start(bf16[2,256,512]{2,1,0:T(8,128)(2,1)S(1)} %fusion.30), channel_id=1, source_target_pairs={{0,2},{1,3},{2,0},{3,1},{4,6},{5,7},{6,4},{7,5},{8,10},{9,11},{10,... | collective-permute-start | bytes 1572872 | tf_op jit(solution)/shard_map/ppermute | solution.py:33
  191.4 28.6 %collective-permute-start.26 = (bf16[128,512]{1,0:T(8,128)(2,1)}, bf16[128,512]{1,0:T(8,128)(2,1)S(1)}, u32[]{:S(2)}, u32[]{:S(2)}) collective-permute-start(bf16[128,512]{1,0:T(8,128)(2,1)} %attention.3), channel_id=1, source_target_pairs={{0,65},{1,64},{2,67},{3,66},{4,69},{5,68},{6,71},{7,70},{8,73},{9,... | collective-permute-start | bytes 393224 | tf_op jit(solution)/shard_map/ppermute | solution.py:43
  208.0 12.0 %collective-permute-start.25 = (bf16[128,512]{1,0:T(8,128)(2,1)}, bf16[128,512]{1,0:T(8,128)(2,1)S(1)}, u32[]{:S(2)}, u32[]{:S(2)}) collective-permute-start(bf16[128,512]{1,0:T(8,128)(2,1)} %attention.2), channel_id=1, source_target_pairs={{0,64},{1,65},{2,66},{3,67},{4,68},{5,69},{6,70},{7,71},{8,72},{9,... | collective-permute-start | bytes 393224 | tf_op jit(solution)/shard_map/ppermute | solution.py:43
  217.3 20.9 %collective-permute-start.30 = (bf16[640,1024]{1,0:T(8,128)(2,1)}, bf16[640,1024]{1,0:T(8,128)(2,1)S(1)}, u32[]{:S(2)}, u32[]{:S(2)}) collective-permute-start(bf16[640,1024]{1,0:T(8,128)(2,1)} %stacked_rows.7), channel_id=1, source_target_pairs={{0,2},{1,3},{2,0},{3,1},{4,6},{5,7},{6,4},{7,5},{8,10},{9,11},{10,... | collective-permute-start | bytes 3932168 | tf_op jit(solution)/shard_map/ppermute | solution.py:33
  220.0 14.3 %collective-permute-start.27 = (bf16[256,512]{1,0:T(8,128)(2,1)S(1)}, bf16[256,512]{1,0:T(8,128)(2,1)S(1)}, u32[]{:S(2)}, u32[]{:S(2)}) collective-permute-start(bf16[256,512]{1,0:T(8,128)(2,1)S(1)} %pad_maximum_fusion.10), channel_id=1, source_target_pairs={{0,32},{1,33},{2,34},{3,35},{4,36},{5,37},{6,38},{7,39},{8,40},{9,... | collective-permute-start | bytes 786440 | tf_op jit(solution)/shard_map/ppermute | solution.py:33
  222.0 15.6 %collective-permute-start.28 = (bf16[256,512]{1,0:T(8,128)(2,1)S(1)}, bf16[256,512]{1,0:T(8,128)(2,1)S(1)}, u32[]{:S(2)}, u32[]{:S(2)}) collective-permute-start(bf16[256,512]{1,0:T(8,128)(2,1)S(1)} %pad_maximum_fusion.10), channel_id=1, source_target_pairs={{0,16},{1,17},{2,18},{3,19},{4,20},{5,21},{6,22},{7,23},{8,24},{9,... | collective-permute-start | bytes 786440 | tf_op jit(solution)/shard_map/ppermute | solution.py:33
  234.4 9.3 %collective-permute-start.29 = (bf16[256,512]{1,0:T(8,128)(2,1)S(1)}, bf16[256,512]{1,0:T(8,128)(2,1)S(1)}, u32[]{:S(2)}, u32[]{:S(2)}) collective-permute-start(bf16[256,512]{1,0:T(8,128)(2,1)S(1)} %collective-permute-done.27), channel_id=1, source_target_pairs={{0,16},{1,17},{2,18},{3,19},{4,20},{5,21},{6,22},{7,23},{8,24},{9,... | collective-permute-start | bytes 786440 | tf_op jit(solution)/shard_map/ppermute | solution.py:33
  244.4 11.2 %collective-permute-start.31 = (bf16[320,512]{1,0:T(8,128)(2,1)S(1)}, bf16[320,512]{1,0:T(8,128)(2,1)S(1)}, u32[]{:S(2)}, u32[]{:S(2)}) collective-permute-start(bf16[320,512]{1,0:T(8,128)(2,1)S(1)} %pad_maximum_fusion.7), channel_id=1, source_target_pairs={{0,12},{1,13},{2,14},{3,15},{4,0},{5,1},{6,2},{7,3},{8,4},{9,5},{1... | collective-permute-start | bytes 983048 | tf_op jit(solution)/shard_map/ppermute | solution.py:33
  248.5 11.0 %collective-permute-start.32 = (bf16[320,512]{1,0:T(8,128)(2,1)S(1)}, bf16[320,512]{1,0:T(8,128)(2,1)S(1)}, u32[]{:S(2)}, u32[]{:S(2)}) collective-permute-start(bf16[320,512]{1,0:T(8,128)(2,1)S(1)} %pad_maximum_fusion.8), channel_id=1, source_target_pairs={{0,8},{1,9},{2,10},{3,11},{4,12},{5,13},{6,14},{7,15},{8,0},{9,1},... | collective-permute-start | bytes 983048 | tf_op jit(solution)/shard_map/ppermute | solution.py:33
  251.7 16.7 %collective-permute-start.33 = (bf16[320,512]{1,0:T(8,128)(2,1)S(1)}, bf16[320,512]{1,0:T(8,128)(2,1)S(1)}, u32[]{:S(2)}, u32[]{:S(2)}) collective-permute-start(bf16[320,512]{1,0:T(8,128)(2,1)S(1)} %pad_maximum_fusion.9), channel_id=1, source_target_pairs={{0,4},{1,5},{2,6},{3,7},{4,8},{5,9},{6,10},{7,11},{8,12},{9,13},{1... | collective-permute-start | bytes 983048 | tf_op jit(solution)/shard_map/ppermute | solution.py:33
  (18 other events, 205.9 us)

commit v5 on v4

--- a/solution.py
+++ b/solution.py
@@ -65,25 +65,38 @@
     return adjacent | key_global | query_global | chosen
 
 
-def attention_kernel(scale, query_ref, own_ref, other_ref, bias_ref, out_ref, rows_ref, value_ref, wide_ref):
-    size = query_ref.shape[0]
-
-    @pl.when(pl.program_id(0) == 0)
-    def _():
-        step = own_ref.shape[2]
+def attention_kernel(scale, per, flag_ref, *refs):
+    own_refs, other_refs = refs[:2], refs[2:4]
+    bias_ref, sent_ref, kept_ref, rows_ref, value_ref, wide_ref = refs[4:]
+    size, tile = sent_ref.shape
+    at = pl.program_id(0)
+
+    @pl.when(at == 0)
+    def _():
+        step = per * tile
         for i in range(2):
             here, there = pl.ds(i * step, step), pl.ds((2 + i) * step, step)
-            rows_ref[here, :size] = own_ref[i, size : 2 * size, :].T
-            rows_ref[there, :size] = other_ref[i, :size, :].T
-            value_ref[:, here] = own_ref[i, 2 * size :, :]
-            value_ref[:, there] = other_ref[i, size:, :]
+            rows_ref[here, :size] = own_refs[i][size : 2 * size, :].T
+            rows_ref[there, :size] = other_refs[i][:size, :].T
+            value_ref[:, here] = own_refs[i][2 * size :, :]
+            value_ref[:, there] = other_refs[i][size:, :]
         shape = (rows_ref.shape[0], size)
         block = lax.broadcasted_iota(jnp.int32, shape, 0) // BLOCK
         column = lax.broadcasted_iota(jnp.int32, shape, 1)
         rows_ref[:, size:] = jnp.where(block == column, 1.0, 0.0).astype(jnp.bfloat16)
         wide_ref[...] = jnp.zeros_like(wide_ref)
 
-    wide_ref[:size, :] = query_ref[...]
+    columns = pl.ds(pl.multiple_of(lax.rem(at, per) * tile, tile), tile)
+    use_f = (at < per) == (flag_ref[0] > 0)
+
+    @pl.when(use_f)
+    def _():
+        wide_ref[:size, :] = own_refs[1][:size, columns]
+
+    @pl.when(jnp.logical_not(use_f))
+    def _():
+        wide_ref[:size, :] = own_refs[0][:size, columns]
+
     wide_ref[size : size + bias_ref.shape[0], :] = bias_ref[...]
     scores = jnp.dot(rows_ref[...], wide_ref[...], preferred_element_type=jnp.float32)
     highest = jnp.max(scores, axis=0, keepdims=True)
@@ -92,34 +105,48 @@
     mixed = jnp.dot(
         value_ref[...], weights.astype(jnp.bfloat16), preferred_element_type=jnp.float32
     )
-    out_ref[...] = (mixed / totals).astype(jnp.bfloat16)
-
-
-def attention(query, own, other, bias, at):
-    size, step = query.shape
-    tile = 128
+    mixed = (mixed / totals).astype(jnp.bfloat16)
+
+    @pl.when(at < per)
+    def _():
+        sent_ref[...] = mixed
+
+    @pl.when(at >= per)
+    def _():
+        kept_ref[...] = mixed
+
+
+def attention(flag, own, other, bias):
+    triple, step = own[0].shape
+    size, tile = triple // 3, 256
     per = step // tile
+
+    def whole(array):
+        return pl.BlockSpec(array.shape, lambda i, flag: (0, 0))
+
     return pl.pallas_call(
-        lambda *refs: attention_kernel(1.0 / math.sqrt(size), *refs),
-        grid=(per,),
-        in_specs=[
-            pl.BlockSpec((size, tile), lambda i: (0, i)),
-            pl.BlockSpec(own.shape, lambda i: (0, 0, 0)),
-            pl.BlockSpec(other.shape, lambda i: (0, 0, 0)),
-            pl.BlockSpec((bias.shape[0], tile), lambda i: (0, at * per + i)),
-        ],
-        out_specs=pl.BlockSpec((size, tile), lambda i: (0, i)),
-        out_shape=jax.ShapeDtypeStruct(query.shape, jnp.bfloat16),
-        scratch_shapes=[
-            pltpu.VMEM((4 * step, 2 * size), jnp.bfloat16),
-            pltpu.VMEM((size, 4 * step), jnp.bfloat16),
-            pltpu.VMEM((2 * size, tile), jnp.bfloat16),
-        ],
+        lambda *refs: attention_kernel(1.0 / math.sqrt(size), per, *refs),
+        grid_spec=pltpu.PrefetchScalarGridSpec(
+            num_scalar_prefetch=1,
+            grid=(2 * per,),
+            in_specs=[whole(array) for array in (*own, *other)]
+            + [pl.BlockSpec((bias.shape[0], tile), lambda i, flag: (0, i))],
+            out_specs=[
+                pl.BlockSpec((size, tile), lambda i, flag: (0, jnp.minimum(i, per - 1))),
+                pl.BlockSpec((size, tile), lambda i, flag: (0, jnp.maximum(i - per, 0))),
+            ],
+            scratch_shapes=[
+                pltpu.VMEM((4 * step, 2 * size), jnp.bfloat16),
+                pltpu.VMEM((size, 4 * step), jnp.bfloat16),
+                pltpu.VMEM((2 * size, tile), jnp.bfloat16),
+            ],
+        ),
+        out_shape=[jax.ShapeDtypeStruct((size, step), jnp.bfloat16)] * 2,
         cost_estimate=pl.CostEstimate(
-            flops=16 * size * step * step, bytes_accessed=6 * size * step, transcendentals=4 * step * step
+            flops=32 * size * step * step, bytes_accessed=12 * size * step, transcendentals=8 * step * step
         ),
         name="attention",
-    )(query, own, other, bias)
+    )(flag, *own, *other, bias)
 
 
 def slices_kernel(order_ref, ring_ref, source_ref, *out_refs):
@@ -215,9 +242,7 @@
     own, away = of_core(tokens_t)
     crossed = moved(away, lambda *at: other_core(*swap_inner(*at)))
     e = stacked_rows(moved(own, swap_inner), crossed)
-    f = moved(e, by_two)
-    e_two = stacked_rows(e, moved(e, pair))
-    f_two = stacked_rows(f, moved(f, pair))
+    out_next = moved_on(out_weight[0].T, same)
 
     gain = norm_gain
     gain_row = jnp.pad(gain, ((0, 15), (0, step - part)))
@@ -226,6 +251,7 @@
     item = jnp.concatenate([own, beside[:part]], axis=0)
     as_float = item.astype(f32)
     squares = jnp.sum(as_float * as_float, axis=0)
+    residual = moved_on(item, same)
     random = random_blocks[0]
     numbers = jnp.pad(random.astype(f32).reshape(-1), (0, step - random.size))
     mine = jnp.stack([squares, numbers])
@@ -234,12 +260,12 @@
     slot = (yl * 4 + x == jnp.arange(16))[:, None]
     table = jnp.where(slot, jnp.pad(gain, ((0, 0), (0, step - 2 * part))), 0.0)
     table = jnp.concatenate([table, mine[:1], theirs[:1]], axis=0)
-    for where in (
-        lambda y, x, c: (y, x ^ 1, c),
-        lambda y, x, c: (y, x ^ 2, c),
-        pair,
-        by_two,
-    ):
+    table = table + moved(table, lambda y, x, c: (y, x ^ 1, c))
+    e = after(e, table)
+    f = moved(e, by_two)
+    e_two = stacked_rows(e, moved(e, pair))
+    f_two = stacked_rows(f, moved(f, pair))
+    for where in (lambda y, x, c: (y, x ^ 2, c), pair, by_two):
         table = table + moved(table, where)
     factors = lax.rsqrt(table[16:] / width + 1e-05)
     factor_e = jnp.where(first == seq, factors[:1], factors[1:])
@@ -266,18 +292,6 @@
         weights.append(jnp.concatenate(rows, axis=0).T)
         scales.append(jnp.concatenate(scale).reshape(4 * part, 1))
 
-    order = after(jnp.stack([yl, yl ^ 2, yl ^ 1, yl ^ 3]), e)
-    ring = (x + jnp.arange(4, dtype=jnp.int32)) % 4
-    slices = column_slices(out_weight[0].T, order, ring)
-    laid = jnp.concatenate([item[:part], item[part:]], axis=1)
-    ahead = moved_on(stacked_rows(slices[0], laid), same)
-    residual = ahead[part:]
-    out_own = [ahead[:part]]
-    for r in range(1, 4):
-        out_own.append(moved_on(slices[r], lambda y, x, c, r=r: (y, (x + r) % 4, c)))
-    out_own = stacked_rows(*out_own)
-    out_cols = out_own, moved(out_own, other_core)
-
     def project(block, k, factor):
         normed = (block.astype(f32) * factor * scales[k]).astype(bf16)
         return jnp.dot(weights[k], normed, preferred_element_type=f32)
@@ -303,17 +317,26 @@
         e, f = moved(e, around), moved(f, around)
         partial_e = partial_e + project(e, k, factor_e)
         partial_f = partial_f + project(f, k, factor_f)
-    joined = []
-    for partial in (partial_e, partial_f):
-        came = moved(partial[columns:].astype(bf16), other_seq)
+    order = after(jnp.stack([yl, yl ^ 2, yl ^ 1, yl ^ 3]), f_two)
+    ring = (x + jnp.arange(4, dtype=jnp.int32)) % 4
+    slices = column_slices(out_next, order, ring)
+    sends = [partial[columns:].astype(bf16) for partial in (partial_e, partial_f)]
+    sends[0], slices = lax.optimization_barrier((sends[0], slices))
+    out_own = [slices[0]]
+    for r in range(1, 4):
+        out_own.append(moved(slices[r], lambda y, x, c, r=r: (y, (x + r) % 4, c)))
+    joined, other = [], []
+    head = columns // 3
+    for partial, send in zip((partial_e, partial_f), sends):
+        came = moved(send, other_seq)
         joined.append((partial[:columns] + came.astype(f32)).astype(bf16))
-    head = columns // 3
-    query_sent = jnp.where(first == seq, joined[1][:head], joined[0][:head])
-    query_kept = jnp.where(first == seq, joined[0][:head], joined[1][:head])
-    joined = jnp.stack(joined)
-    other = moved(joined[:, head:], other_core)
-    came = moved_on(attention(query_sent, joined, other, bias, 0), other_seq)
-    kept = moved_on(attention(query_kept, joined, other, bias, 1), same)
+        other.append(moved(joined[-1][head:], other_core))
+
+    flag = after((first == seq).astype(jnp.int32).reshape(1), (out_own, residual))
+    out_own = stacked_rows(*out_own)
+    out_cols = out_own, moved(out_own, other_core)
+    sent, kept = attention(flag, joined, other, bias)
+    came, kept = moved_on(sent, other_seq), moved_on(kept, same)
 
     heads = jnp.concatenate(
         [jnp.where(seq == 0, kept, came), jnp.where(seq == 0, came, kept)], axis=0
@@ -329,8 +352,7 @@
                 cols[:, p * per : (p + 1) * per], block, preferred_element_type=f32
             )
         added.append(total)
-    total = jnp.concatenate([residual[:, :step], residual[:, step:]], axis=0).astype(f32)
-    total = total + jnp.concatenate([half[:part] for half in added], axis=0)
+    total = residual.astype(f32) + jnp.concatenate([half[:part] for half in added], axis=0)
     for r in range(1, 4):
         share = jnp.concatenate(
             [half[r * part : (r + 1) * part].astype(bf16) for half in added], axis=0

time: 275 us -> 254 us (0.924)
  starting transfers between devices: 143 us -> 135 us
  Pallas kernels: 27.2 us -> 19.9 us
  waiting for transfers between devices: 65 us -> 61.5 us
    ppermute x6 -> x4, starting transfers between devices: 37.4 us -> 17.8 us  [moved_on(): return lax.ppermute(value, ('section', *PLANE), pairs)]
    ppermute x29 -> x33, starting transfers between devices: 105 us -> 117 us  [moved(): return lax.ppermute(value, PLANE, pairs_of(where))]
    pallas_call x2 -> x1, Pallas kernels: 13 us -> 7.58 us  [attention(): pl.pallas_call(lambda *refs: attention_kernel(1.0 / math.sqrt(size), per,...]
    ppermute x29 -> x33, waiting for transfers between devices: 65 us -> 61.5 us  [moved(): return lax.ppermute(value, PLANE, pairs_of(where))]
    pallas_call x5 -> x4, Pallas kernels: 10 us -> 8.09 us  [stacked_rows(): pl.pallas_call(rows_kernel, in_specs=[vmem] * len(parts), out_specs=vmem,...]
  transfers between devices with their start and end apart: 35 -> 37, of which waited for: 13 -> 15; matrix products, arithmetic and copies ran while one was open for 11% -> 10% of each run, Pallas kernels for 10% -> 5%
where the time goes in v5:
time: 254 us; the launch traced here: 252 us
  starting transfers between devices  135 us (53%)
  waiting for transfers between devices  61.5 us (24%)
  Pallas kernels  19.9 us (8%)
  other arithmetic  14 us (6%)
  matrix products  11.7 us (5%)
  local copies, waits for them, and re-layouts  8.9 us (4%)
    ppermute x33, starting transfers between devices, moved(): return lax.ppermute(value, PLANE, pairs_of(where))  117 us
    ppermute x33, waiting for transfers between devices, moved(): return lax.ppermute(value, PLANE, pairs_of(where))  61.5 us
    ppermute x4, starting transfers between devices, moved_on(): return lax.ppermute(value, ('section', *PLANE), pairs)  17.8 us
    pallas_call x4, Pallas kernels, stacked_rows(): pl.pallas_call(rows_kernel, in_specs=[vmem] * len(parts), out_specs=vmem,...  8.09 us
    dot_general x8, matrix products, project(): return jnp.dot(weights[k], normed, preferred_element_type=f32)  8.03 us
    pallas_call x1, Pallas kernels, attention(): pl.pallas_call(lambda *refs: attention_kernel(1.0 / math.sqrt(size), per,...  7.58 us
  transfers between devices with their start and end apart: 37, of which 15 were waited for; matrix products, arithmetic and copies ran while one was open for 10% of the time, Pallas kernels for 5%

profile of v5, /device:TPU:1, one launch (start us, length us, event | category | flops | bytes accessed | tf_op | source)
XLA Modules:
  0.0 251.6 jit_solution(5911479953424323976)
XLA Ops:
  1.8 8.8 %collective-permute-start.4 = (bf16[160,512]{1,0:T(8,128)(2,1)S(1)}, bf16[160,512]{1,0:T(8,128)(2,1)S(1)}, u32[]{:S(2)}, u32[]{:S(2)}) collective-permute-start(bf16[160,512]{1,0:T(8,128)(2,1)S(1)} %get-tuple-element.69), channel_id=1, source_target_pairs={{0,2},{1,34},{2,0},{3,32},{4,6},{5,38},{6,4},{7,36},{8,10},{9,42},... | collective-permute-start | bytes 491528 | tf_op jit(solution)/shard_map/ppermute | solution.py:33
  16.4 9.1 %collective-permute-start.5 = (f32[2,512]{1,0:T(2,128)S(1)}, f32[2,512]{1,0:T(2,128)S(1)}, u32[]{:S(2)}, u32[]{:S(2)}) collective-permute-start(f32[2,512]{1,0:T(2,128)S(1)} %pad_maximum_fusion.19), channel_id=1, source_target_pairs={{0,1},{1,0},{2,3},{3,2},{4,5},{5,4},{6,7},{7,6},{8,9},{9,8},{10,11... | collective-permute-start | bytes 12296 | tf_op jit(solution)/shard_map/ppermute | solution.py:33
  27.0 3.1 %collective-permute-start.6 = (f32[18,512]{1,0:T(8,128)S(1)}, f32[18,512]{1,0:T(8,128)S(1)}, u32[]{:S(2)}, u32[]{:S(2)}) collective-permute-start(f32[18,512]{1,0:T(8,128)S(1)} %pad_maximum_fusion.18), channel_id=1, source_target_pairs={{0,4},{1,5},{2,6},{3,7},{4,0},{5,1},{6,2},{7,3},{8,12},{9,13},{10,... | collective-permute-start | bytes 110600 | tf_op jit(solution)/shard_map/ppermute | solution.py:33
  33.3 3.4 %collective-permute-start.2 = (bf16[2560,384]{1,0:T(8,128)(2,1)S(1)}, bf16[2560,384]{1,0:T(8,128)(2,1)}, u32[]{:S(2)}, u32[]{:S(2)}) collective-permute-start(bf16[2560,384]{1,0:T(8,128)(2,1)S(1)} %bitcast.70), channel_id=1, source_target_pairs={{0,2},{1,3},{2,0},{3,1},{4,6},{5,7},{6,4},{7,5},{8,10},{9,11},{10,... | collective-permute-start | bytes 5898248 | tf_op jit(solution)/shard_map/ppermute | solution.py:33
  39.4 5.2 %collective-permute-start.14 = (bf16[320,512]{1,0:T(8,128)(2,1)}, bf16[320,512]{1,0:T(8,128)(2,1)S(1)}, u32[]{:S(2)}, u32[]{:S(2)}) collective-permute-start(bf16[320,512]{1,0:T(8,128)(2,1)} %stacked_rows.4.refs_0_), channel_id=1, source_target_pairs={{0,32},{1,33},{2,34},{3,35},{4,36},{5,37},{6,38},{7,39},{8,40},{9,... | collective-permute-start | bytes 983048 | tf_op jit(solution)/shard_map/ppermute | solution.py:33
  44.6 8.2 %collective-permute-done.7.refs_1_ = bf16[320,512]{1,0:T(8,128)(2,1)S(1)} collective-permute-done((bf16[320,512]{1,0:T(8,128)(2,1)}, bf16[320,512]{1,0:T(8,128)(2,1)S(1)}, u32[]{:S(2)}, u32[]{:S(2)}) %collective-permute-start.7) | collective-permute-done | bytes 327712 | tf_op jit(solution)/shard_map/ppermute | solution.py:33
  55.5 3.7 %collective-permute-start.11 = (bf16[640,512]{1,0:T(8,128)(2,1)}, bf16[640,512]{1,0:T(8,128)(2,1)}, u32[]{:S(2)}, u32[]{:S(2)}) collective-permute-start(bf16[640,512]{1,0:T(8,128)(2,1)} %stacked_rows.5), channel_id=1, source_target_pairs={{0,4},{1,5},{2,14},{3,15},{4,8},{5,9},{6,2},{7,3},{8,12},{9,13},{1... | collective-permute-start | bytes 1966088 | tf_op jit(solution)/shard_map/ppermute | solution.py:33
  70.0 3.3 %collective-permute-done.9 = f32[18,512]{1,0:T(8,128)S(1)} collective-permute-done((f32[18,512]{1,0:T(8,128)S(1)}, f32[18,512]{1,0:T(8,128)S(1)}, u32[]{:S(2)}, u32[]{:S(2)}) %collective-permute-start.9) | collective-permute-done | bytes 36896 | tf_op jit(solution)/shard_map/ppermute | solution.py:33
  79.6 4.0 %collective-permute-start.1 = (bf16[320,512]{1,0:T(8,128)(2,1)}, bf16[320,512]{1,0:T(8,128)(2,1)}, u32[]{:S(2)}, u32[]{:S(2)}) collective-permute-start(bf16[320,512]{1,0:T(8,128)(2,1)} %pad_maximum_fusion.5), channel_id=1, source_target_pairs={{0,64},{1,65},{2,66},{3,67},{4,68},{5,69},{6,70},{7,71},{8,72},{9,... | collective-permute-start | bytes 983048 | tf_op jit(solution)/shard_map/ppermute | solution.py:43
  86.4 4.6 %collective-permute-start.21 = (bf16[640,512]{1,0:T(8,128)(2,1)}, bf16[640,512]{1,0:T(8,128)(2,1)S(1)}, u32[]{:S(2)}, u32[]{:S(2)}) collective-permute-start(bf16[640,512]{1,0:T(8,128)(2,1)} %stacked_rows.6), channel_id=1, source_target_pairs={{0,4},{1,5},{2,14},{3,15},{4,8},{5,9},{6,2},{7,3},{8,12},{9,13},{1... | collective-permute-start | bytes 1966088 | tf_op jit(solution)/shard_map/ppermute | solution.py:33
  91.1 4.9 %collective-permute-start.12 = (bf16[640,512]{1,0:T(8,128)(2,1)}, bf16[640,512]{1,0:T(8,128)(2,1)S(1)}, u32[]{:S(2)}, u32[]{:S(2)}) collective-permute-start(bf16[640,512]{1,0:T(8,128)(2,1)} %collective-permute-done.11), channel_id=1, source_target_pairs={{0,4},{1,5},{2,14},{3,15},{4,8},{5,9},{6,2},{7,3},{8,12},{9,13},{1... | collective-permute-start | bytes 1966088 | tf_op jit(solution)/shard_map/ppermute | solution.py:33
  96.2 4.2 %column_slices.1 = (bf16[160,1024]{1,0:T(8,128)(2,1)}, bf16[160,1024]{1,0:T(8,128)(2,1)}, bf16[160,1024]{1,0:T(8,128)(2,1)}, bf16[160,1024]{1,0:T(8,128)(2,1)}) custom-call(s32[4]{0:T(128)} %pad_add_fusion.order_ref, s32[4]{0:T(128)} %and_select_fusion.ring_ref, bf16[160,4096]{1,0:T(8,128)(2,1)} %collective-permute-done.16.source_ref), custom_call_target="tpu_custom_call" | custom-call | bytes 2621440 | tf_op jit(solution)/shard_map/column_slices/pallas_call | solution.py:162
  100.4 3.4 %collective-permute-start.22 = (bf16[640,512]{1,0:T(8,128)(2,1)S(1)}, bf16[640,512]{1,0:T(8,128)(2,1)S(1)}, u32[]{:S(2)}, u32[]{:S(2)}) collective-permute-start(bf16[640,512]{1,0:T(8,128)(2,1)S(1)} %collective-permute-done.21), channel_id=1, source_target_pairs={{0,4},{1,5},{2,14},{3,15},{4,8},{5,9},{6,2},{7,3},{8,12},{9,13},{1... | collective-permute-start | bytes 1966088 | tf_op jit(solution)/shard_map/ppermute | solution.py:33
  105.9 4.9 %collective-permute-start.13 = (bf16[640,512]{1,0:T(8,128)(2,1)S(1)}, bf16[640,512]{1,0:T(8,128)(2,1)S(1)}, u32[]{:S(2)}, u32[]{:S(2)}) collective-permute-start(bf16[640,512]{1,0:T(8,128)(2,1)S(1)} %collective-permute-done.12), channel_id=1, source_target_pairs={{0,4},{1,5},{2,14},{3,15},{4,8},{5,9},{6,2},{7,3},{8,12},{9,13},{1... | collective-permute-start | bytes 1966088 | tf_op jit(solution)/shard_map/ppermute | solution.py:33
  119.8 4.0 %collective-permute-start.23 = (bf16[640,512]{1,0:T(8,128)(2,1)S(1)}, bf16[640,512]{1,0:T(8,128)(2,1)S(1)}, u32[]{:S(2)}, u32[]{:S(2)}) collective-permute-start(bf16[640,512]{1,0:T(8,128)(2,1)S(1)} %collective-permute-done.22), channel_id=1, source_target_pairs={{0,4},{1,5},{2,14},{3,15},{4,8},{5,9},{6,2},{7,3},{8,12},{9,13},{1... | collective-permute-start | bytes 1966088 | tf_op jit(solution)/shard_map/ppermute | solution.py:33
  128.0 3.4 %collective-permute-done.23 = bf16[640,512]{1,0:T(8,128)(2,1)S(1)} collective-permute-done((bf16[640,512]{1,0:T(8,128)(2,1)S(1)}, bf16[640,512]{1,0:T(8,128)(2,1)S(1)}, u32[]{:S(2)}, u32[]{:S(2)}) %collective-permute-start.23) | collective-permute-done | bytes 655392 | tf_op jit(solution)/shard_map/ppermute | solution.py:33
  133.1 3.8 %collective-permute-start.24 = (bf16[384,512]{1,0:T(8,128)(2,1)}, bf16[384,512]{1,0:T(8,128)(2,1)}, u32[]{:S(2)}, u32[]{:S(2)}) collective-permute-start(bf16[384,512]{1,0:T(8,128)(2,1)} %slice.222), channel_id=1, source_target_pairs={{0,1},{1,0},{2,3},{3,2},{4,5},{5,4},{6,7},{7,6},{8,9},{9,8},{10,11... | collective-permute-start | bytes 1179656 | tf_op jit(solution)/shard_map/ppermute | solution.py:33
  140.3 4.6 %collective-permute-start.18 = (bf16[160,1024]{1,0:T(8,128)(2,1)}, bf16[160,1024]{1,0:T(8,128)(2,1)}, u32[]{:S(2)}, u32[]{:S(2)}) collective-permute-start(bf16[160,1024]{1,0:T(8,128)(2,1)} %get-tuple-element.29), channel_id=1, source_target_pairs={{0,8},{1,9},{2,10},{3,11},{4,12},{5,13},{6,14},{7,15},{8,0},{9,1},... | collective-permute-start | bytes 983048 | tf_op jit(solution)/shard_map/ppermute | solution.py:33
  144.9 6.8 %collective-permute-done.20 = bf16[384,512]{1,0:T(8,128)(2,1)} collective-permute-done((bf16[384,512]{1,0:T(8,128)(2,1)S(1)}, bf16[384,512]{1,0:T(8,128)(2,1)}, u32[]{:S(2)}, u32[]{:S(2)}) %collective-permute-start.20) | collective-permute-done | bytes 393248 | tf_op jit(solution)/shard_map/ppermute | solution.py:33
  154.9 9.0 %collective-permute-done.24 = bf16[384,512]{1,0:T(8,128)(2,1)} collective-permute-done((bf16[384,512]{1,0:T(8,128)(2,1)}, bf16[384,512]{1,0:T(8,128)(2,1)}, u32[]{:S(2)}, u32[]{:S(2)}) %collective-permute-start.24) | collective-permute-done | bytes 393248 | tf_op jit(solution)/shard_map/ppermute | solution.py:33
  163.9 4.1 %collective-permute-start.25 = (bf16[256,512]{1,0:T(8,128)(2,1)S(1)}, bf16[256,512]{1,0:T(8,128)(2,1)S(1)}, u32[]{:S(2)}, u32[]{:S(2)}) collective-permute-start(bf16[256,512]{1,0:T(8,128)(2,1)S(1)} %slice.160), channel_id=1, source_target_pairs={{0,2},{1,3},{2,0},{3,1},{4,6},{5,7},{6,4},{7,5},{8,10},{9,11},{10,... | collective-permute-start | bytes 786440 | tf_op jit(solution)/shard_map/ppermute | solution.py:33
  173.9 7.6 %attention.1 = (bf16[128,512]{1,0:T(8,128)(2,1)}, bf16[128,512]{1,0:T(8,128)(2,1)}) custom-call(s32[1]{0:T(128)} %bitcast.31.refs_0_, bf16[384,512]{1,0:T(8,128)(2,1)} %copy-done.2, bf16[384,512]{1,0:T(8,128)(2,1)} %copy-done.3, bf16[256,512]{1,0:T(8,128)(2,1)} %copy-done.19, bf16[256,512]{1,0:T(8,128)(2,1)} %copy-done.20, ...), custom_call_target="tpu_custom_call" | custom-call | flops 1073741824 | bytes 786432 | tf_op jit(solution)/shard_map/attention/pallas_call | solution.py:127
  181.5 4.0 %collective-permute-start.27 = (bf16[128,512]{1,0:T(8,128)(2,1)}, bf16[128,512]{1,0:T(8,128)(2,1)S(1)}, u32[]{:S(2)}, u32[]{:S(2)}) collective-permute-start(bf16[128,512]{1,0:T(8,128)(2,1)} %get-tuple-element.33), channel_id=1, source_target_pairs={{0,64},{1,65},{2,66},{3,67},{4,68},{5,69},{6,70},{7,71},{8,72},{9,... | collective-permute-start | bytes 393224 | tf_op jit(solution)/shard_map/ppermute | solution.py:43
  185.5 7.9 %collective-permute-start.28 = (bf16[128,512]{1,0:T(8,128)(2,1)}, bf16[128,512]{1,0:T(8,128)(2,1)S(1)}, u32[]{:S(2)}, u32[]{:S(2)}) collective-permute-start(bf16[128,512]{1,0:T(8,128)(2,1)} %get-tuple-element.34), channel_id=1, source_target_pairs={{0,65},{1,64},{2,67},{3,66},{4,69},{5,68},{6,71},{7,70},{8,73},{9,... | collective-permute-start | bytes 393224 | tf_op jit(solution)/shard_map/ppermute | solution.py:43
  195.9 3.1 %collective-permute-start.32 = (bf16[640,1024]{1,0:T(8,128)(2,1)}, bf16[640,1024]{1,0:T(8,128)(2,1)S(1)}, u32[]{:S(2)}, u32[]{:S(2)}) collective-permute-start(bf16[640,1024]{1,0:T(8,128)(2,1)} %stacked_rows.7), channel_id=1, source_target_pairs={{0,2},{1,3},{2,0},{3,1},{4,6},{5,7},{6,4},{7,5},{8,10},{9,11},{10,... | collective-permute-start | bytes 3932168 | tf_op jit(solution)/shard_map/ppermute | solution.py:33
  201.0 5.6 %collective-permute-start.30 = (bf16[256,512]{1,0:T(8,128)(2,1)S(1)}, bf16[256,512]{1,0:T(8,128)(2,1)S(1)}, u32[]{:S(2)}, u32[]{:S(2)}) collective-permute-start(bf16[256,512]{1,0:T(8,128)(2,1)S(1)} %pad_maximum_fusion.9), channel_id=1, source_target_pairs={{0,16},{1,17},{2,18},{3,19},{4,20},{5,21},{6,22},{7,23},{8,24},{9,... | collective-permute-start | bytes 786440 | tf_op jit(solution)/shard_map/ppermute | solution.py:33
  206.6 8.2 %collective-permute-done.29 = bf16[256,512]{1,0:T(8,128)(2,1)S(1)} collective-permute-done((bf16[256,512]{1,0:T(8,128)(2,1)S(1)}, bf16[256,512]{1,0:T(8,128)(2,1)S(1)}, u32[]{:S(2)}, u32[]{:S(2)}) %collective-permute-start.29) | collective-permute-done | bytes 262176 | tf_op jit(solution)/shard_map/ppermute | solution.py:33
  219.8 3.3 %collective-permute-done.31 = bf16[256,512]{1,0:T(8,128)(2,1)S(1)} collective-permute-done((bf16[256,512]{1,0:T(8,128)(2,1)S(1)}, bf16[256,512]{1,0:T(8,128)(2,1)S(1)}, u32[]{:S(2)}, u32[]{:S(2)}) %collective-permute-start.31) | collective-permute-done | bytes 262176 | tf_op jit(solution)/shard_map/ppermute | solution.py:33
  223.8 3.7 %collective-permute-start.35 = (bf16[320,512]{1,0:T(8,128)(2,1)S(1)}, bf16[320,512]{1,0:T(8,128)(2,1)S(1)}, u32[]{:S(2)}, u32[]{:S(2)}) collective-permute-start(bf16[320,512]{1,0:T(8,128)(2,1)S(1)} %pad_maximum_fusion.8), channel_id=1, source_target_pairs={{0,4},{1,5},{2,6},{3,7},{4,8},{5,9},{6,10},{7,11},{8,12},{9,13},{1... | collective-permute-start | bytes 983048 | tf_op jit(solution)/shard_map/ppermute | solution.py:33
  230.3 4.0 %collective-permute-start.33 = (bf16[320,512]{1,0:T(8,128)(2,1)S(1)}, bf16[320,512]{1,0:T(8,128)(2,1)S(1)}, u32[]{:S(2)}, u32[]{:S(2)}) collective-permute-start(bf16[320,512]{1,0:T(8,128)(2,1)S(1)} %pad_maximum_fusion.6), channel_id=1, source_target_pairs={{0,12},{1,13},{2,14},{3,15},{4,0},{5,1},{6,2},{7,3},{8,4},{9,5},{1... | collective-permute-start | bytes 983048 | tf_op jit(solution)/shard_map/ppermute | solution.py:33
  234.4 7.7 %collective-permute-done.34 = bf16[320,512]{1,0:T(8,128)(2,1)S(1)} collective-permute-done((bf16[320,512]{1,0:T(8,128)(2,1)S(1)}, bf16[320,512]{1,0:T(8,128)(2,1)S(1)}, u32[]{:S(2)}, u32[]{:S(2)}) %collective-permute-start.34) | collective-permute-done | bytes 327712 | tf_op jit(solution)/shard_map/ppermute | solution.py:33
  245.4 4.3 %collective-permute-start.36 = (bf16[160,512]{1,0:T(8,128)(2,1)S(1)}, bf16[160,512]{1,0:T(8,128)(2,1)S(1)}, u32[]{:S(2)}, u32[]{:S(2)}) collective-permute-start(bf16[160,512]{1,0:T(8,128)(2,1)S(1)} %slice.179), channel_id=1, source_target_pairs={{0,2},{1,3},{2,0},{3,1},{4,6},{5,7},{6,4},{7,5},{8,10},{9,11},{10,... | collective-permute-start | bytes 491528 | tf_op jit(solution)/shard_map/ppermute | solution.py:33
  (180 shorter events, 84.6 us)
Async XLA Ops:
  1.2 29.0 %collective-permute-start.3 = (bf16[160,512]{1,0:T(8,128)(2,1)S(1)}, bf16[160,512]{1,0:T(8,128)(2,1)S(1)}, u32[]{:S(2)}, u32[]{:S(2)}) collective-permute-start(bf16[160,512]{1,0:T(8,128)(2,1)S(1)} %get-tuple-element.70), channel_id=1, source_target_pairs={{0,0},{1,32},{2,2},{3,34},{4,4},{5,36},{6,6},{7,38},{8,8},{9,40},{... | collective-permute-start | bytes 491528 | tf_op jit(solution)/shard_map/ppermute | solution.py:33
  1.8 28.3 %collective-permute-start.4 = (bf16[160,512]{1,0:T(8,128)(2,1)S(1)}, bf16[160,512]{1,0:T(8,128)(2,1)S(1)}, u32[]{:S(2)}, u32[]{:S(2)}) collective-permute-start(bf16[160,512]{1,0:T(8,128)(2,1)S(1)} %get-tuple-element.69), channel_id=1, source_target_pairs={{0,2},{1,34},{2,0},{3,32},{4,6},{5,38},{6,4},{7,36},{8,10},{9,42},... | collective-permute-start | bytes 491528 | tf_op jit(solution)/shard_map/ppermute | solution.py:33
  13.3 82.9 %collective-permute-start.16 = (bf16[160,4096]{1,0:T(8,128)(2,1)}, bf16[160,4096]{1,0:T(8,128)(2,1)}, u32[]{:S(2)}, u32[]{:S(2)}) collective-permute-start(bf16[160,4096]{1,0:T(8,128)(2,1)} %bitcast.86), channel_id=1, source_target_pairs={{0,64},{1,65},{2,66},{3,67},{4,68},{5,69},{6,70},{7,71},{8,72},{9,... | collective-permute-start | bytes 3932168 | tf_op jit(solution)/shard_map/ppermute | solution.py:43
  16.4 10.5 %collective-permute-start.5 = (f32[2,512]{1,0:T(2,128)S(1)}, f32[2,512]{1,0:T(2,128)S(1)}, u32[]{:S(2)}, u32[]{:S(2)}) collective-permute-start(f32[2,512]{1,0:T(2,128)S(1)} %pad_maximum_fusion.19), channel_id=1, source_target_pairs={{0,1},{1,0},{2,3},{3,2},{4,5},{5,4},{6,7},{7,6},{8,9},{9,8},{10,11... | collective-permute-start | bytes 12296 | tf_op jit(solution)/shard_map/ppermute | solution.py:33
  27.0 9.7 %collective-permute-start.6 = (f32[18,512]{1,0:T(8,128)S(1)}, f32[18,512]{1,0:T(8,128)S(1)}, u32[]{:S(2)}, u32[]{:S(2)}) collective-permute-start(f32[18,512]{1,0:T(8,128)S(1)} %pad_maximum_fusion.18), channel_id=1, source_target_pairs={{0,4},{1,5},{2,6},{3,7},{4,0},{5,1},{6,2},{7,3},{8,12},{9,13},{10,... | collective-permute-start | bytes 110600 | tf_op jit(solution)/shard_map/ppermute | solution.py:33
  33.3 77.5 %collective-permute-start.2 = (bf16[2560,384]{1,0:T(8,128)(2,1)S(1)}, bf16[2560,384]{1,0:T(8,128)(2,1)}, u32[]{:S(2)}, u32[]{:S(2)}) collective-permute-start(bf16[2560,384]{1,0:T(8,128)(2,1)S(1)} %bitcast.70), channel_id=1, source_target_pairs={{0,2},{1,3},{2,0},{3,1},{4,6},{5,7},{6,4},{7,5},{8,10},{9,11},{10,... | collective-permute-start | bytes 5898248 | tf_op jit(solution)/shard_map/ppermute | solution.py:33
  36.7 16.1 %collective-permute-start.7 = (bf16[320,512]{1,0:T(8,128)(2,1)}, bf16[320,512]{1,0:T(8,128)(2,1)S(1)}, u32[]{:S(2)}, u32[]{:S(2)}) collective-permute-start(bf16[320,512]{1,0:T(8,128)(2,1)} %stacked_rows.4.refs_0_), channel_id=1, source_target_pairs={{0,16},{1,17},{2,18},{3,19},{4,20},{5,21},{6,22},{7,23},{8,24},{9,... | collective-permute-start | bytes 983048 | tf_op jit(solution)/shard_map/ppermute | solution.py:33
  39.4 23.6 %collective-permute-start.14 = (bf16[320,512]{1,0:T(8,128)(2,1)}, bf16[320,512]{1,0:T(8,128)(2,1)S(1)}, u32[]{:S(2)}, u32[]{:S(2)}) collective-permute-start(bf16[320,512]{1,0:T(8,128)(2,1)} %stacked_rows.4.refs_0_), channel_id=1, source_target_pairs={{0,32},{1,33},{2,34},{3,35},{4,36},{5,37},{6,38},{7,39},{8,40},{9,... | collective-permute-start | bytes 983048 | tf_op jit(solution)/shard_map/ppermute | solution.py:33
  55.5 35.5 %collective-permute-start.11 = (bf16[640,512]{1,0:T(8,128)(2,1)}, bf16[640,512]{1,0:T(8,128)(2,1)}, u32[]{:S(2)}, u32[]{:S(2)}) collective-permute-start(bf16[640,512]{1,0:T(8,128)(2,1)} %stacked_rows.5), channel_id=1, source_target_pairs={{0,4},{1,5},{2,14},{3,15},{4,8},{5,9},{6,2},{7,3},{8,12},{9,13},{1... | collective-permute-start | bytes 1966088 | tf_op jit(solution)/shard_map/ppermute | solution.py:33
  60.5 6.9 %collective-permute-start.8 = (f32[18,512]{1,0:T(8,128)S(1)}, f32[18,512]{1,0:T(8,128)S(1)}, u32[]{:S(2)}, u32[]{:S(2)}) collective-permute-start(f32[18,512]{1,0:T(8,128)S(1)} %fusion.71), channel_id=1, source_target_pairs={{0,8},{1,9},{2,10},{3,11},{4,12},{5,13},{6,14},{7,15},{8,0},{9,1},... | collective-permute-start | bytes 110600 | tf_op jit(solution)/shard_map/ppermute | solution.py:33
  63.1 20.6 %collective-permute-start.15 = (bf16[320,512]{1,0:T(8,128)(2,1)S(1)}, bf16[320,512]{1,0:T(8,128)(2,1)S(1)}, u32[]{:S(2)}, u32[]{:S(2)}) collective-permute-start(bf16[320,512]{1,0:T(8,128)(2,1)S(1)} %collective-permute-done.14.refs_0_), channel_id=1, source_target_pairs={{0,16},{1,17},{2,18},{3,19},{4,20},{5,21},{6,22},{7,23},{8,24},{9,... | collective-permute-start | bytes 983048 | tf_op jit(solution)/shard_map/ppermute | solution.py:33
  79.6 89.5 %collective-permute-start.1 = (bf16[320,512]{1,0:T(8,128)(2,1)}, bf16[320,512]{1,0:T(8,128)(2,1)}, u32[]{:S(2)}, u32[]{:S(2)}) collective-permute-start(bf16[320,512]{1,0:T(8,128)(2,1)} %pad_maximum_fusion.5), channel_id=1, source_target_pairs={{0,64},{1,65},{2,66},{3,67},{4,68},{5,69},{6,70},{7,71},{8,72},{9,... | collective-permute-start | bytes 983048 | tf_op jit(solution)/shard_map/ppermute | solution.py:43
  86.4 13.9 %collective-permute-start.21 = (bf16[640,512]{1,0:T(8,128)(2,1)}, bf16[640,512]{1,0:T(8,128)(2,1)S(1)}, u32[]{:S(2)}, u32[]{:S(2)}) collective-permute-start(bf16[640,512]{1,0:T(8,128)(2,1)} %stacked_rows.6), channel_id=1, source_target_pairs={{0,4},{1,5},{2,14},{3,15},{4,8},{5,9},{6,2},{7,3},{8,12},{9,13},{1... | collective-permute-start | bytes 1966088 | tf_op jit(solution)/shard_map/ppermute | solution.py:33
  91.1 14.8 %collective-permute-start.12 = (bf16[640,512]{1,0:T(8,128)(2,1)}, bf16[640,512]{1,0:T(8,128)(2,1)S(1)}, u32[]{:S(2)}, u32[]{:S(2)}) collective-permute-start(bf16[640,512]{1,0:T(8,128)(2,1)} %collective-permute-done.11), channel_id=1, source_target_pairs={{0,4},{1,5},{2,14},{3,15},{4,8},{5,9},{6,2},{7,3},{8,12},{9,13},{1... | collective-permute-start | bytes 1966088 | tf_op jit(solution)/shard_map/ppermute | solution.py:33
  100.4 19.4 %collective-permute-start.22 = (bf16[640,512]{1,0:T(8,128)(2,1)S(1)}, bf16[640,512]{1,0:T(8,128)(2,1)S(1)}, u32[]{:S(2)}, u32[]{:S(2)}) collective-permute-start(bf16[640,512]{1,0:T(8,128)(2,1)S(1)} %collective-permute-done.21), channel_id=1, source_target_pairs={{0,4},{1,5},{2,14},{3,15},{4,8},{5,9},{6,2},{7,3},{8,12},{9,13},{1... | collective-permute-start | bytes 1966088 | tf_op jit(solution)/shard_map/ppermute | solution.py:33
  105.9 18.8 %collective-permute-start.13 = (bf16[640,512]{1,0:T(8,128)(2,1)S(1)}, bf16[640,512]{1,0:T(8,128)(2,1)S(1)}, u32[]{:S(2)}, u32[]{:S(2)}) collective-permute-start(bf16[640,512]{1,0:T(8,128)(2,1)S(1)} %collective-permute-done.12), channel_id=1, source_target_pairs={{0,4},{1,5},{2,14},{3,15},{4,8},{5,9},{6,2},{7,3},{8,12},{9,13},{1... | collective-permute-start | bytes 1966088 | tf_op jit(solution)/shard_map/ppermute | solution.py:33
  119.8 11.6 %collective-permute-start.23 = (bf16[640,512]{1,0:T(8,128)(2,1)S(1)}, bf16[640,512]{1,0:T(8,128)(2,1)S(1)}, u32[]{:S(2)}, u32[]{:S(2)}) collective-permute-start(bf16[640,512]{1,0:T(8,128)(2,1)S(1)} %collective-permute-done.22), channel_id=1, source_target_pairs={{0,4},{1,5},{2,14},{3,15},{4,8},{5,9},{6,2},{7,3},{8,12},{9,13},{1... | collective-permute-start | bytes 1966088 | tf_op jit(solution)/shard_map/ppermute | solution.py:33
  125.7 26.1 %collective-permute-start.20 = (bf16[384,512]{1,0:T(8,128)(2,1)S(1)}, bf16[384,512]{1,0:T(8,128)(2,1)}, u32[]{:S(2)}, u32[]{:S(2)}) collective-permute-start(bf16[384,512]{1,0:T(8,128)(2,1)S(1)} %slice.223), channel_id=1, source_target_pairs={{0,1},{1,0},{2,3},{3,2},{4,5},{5,4},{6,7},{7,6},{8,9},{9,8},{10,11... | collective-permute-start | bytes 1179656 | tf_op jit(solution)/shard_map/ppermute | solution.py:33
  133.1 30.8 %collective-permute-start.24 = (bf16[384,512]{1,0:T(8,128)(2,1)}, bf16[384,512]{1,0:T(8,128)(2,1)}, u32[]{:S(2)}, u32[]{:S(2)}) collective-permute-start(bf16[384,512]{1,0:T(8,128)(2,1)} %slice.222), channel_id=1, source_target_pairs={{0,1},{1,0},{2,3},{3,2},{4,5},{5,4},{6,7},{7,6},{8,9},{9,8},{10,11... | collective-permute-start | bytes 1179656 | tf_op jit(solution)/shard_map/ppermute | solution.py:33
  138.4 34.1 %collective-permute-start.17 = (bf16[160,1024]{1,0:T(8,128)(2,1)}, bf16[160,1024]{1,0:T(8,128)(2,1)}, u32[]{:S(2)}, u32[]{:S(2)}) collective-permute-start(bf16[160,1024]{1,0:T(8,128)(2,1)} %get-tuple-element.28), channel_id=1, source_target_pairs={{0,4},{1,5},{2,6},{3,7},{4,8},{5,9},{6,10},{7,11},{8,12},{9,13},{1... | collective-permute-start | bytes 983048 | tf_op jit(solution)/shard_map/ppermute | solution.py:33
  140.3 32.2 %collective-permute-start.18 = (bf16[160,1024]{1,0:T(8,128)(2,1)}, bf16[160,1024]{1,0:T(8,128)(2,1)}, u32[]{:S(2)}, u32[]{:S(2)}) collective-permute-start(bf16[160,1024]{1,0:T(8,128)(2,1)} %get-tuple-element.29), channel_id=1, source_target_pairs={{0,8},{1,9},{2,10},{3,11},{4,12},{5,13},{6,14},{7,15},{8,0},{9,1},... | collective-permute-start | bytes 983048 | tf_op jit(solution)/shard_map/ppermute | solution.py:33
  151.8 20.7 %collective-permute-start.19 = (bf16[160,1024]{1,0:T(8,128)(2,1)}, bf16[160,1024]{1,0:T(8,128)(2,1)}, u32[]{:S(2)}, u32[]{:S(2)}) collective-permute-start(bf16[160,1024]{1,0:T(8,128)(2,1)} %get-tuple-element.30), channel_id=1, source_target_pairs={{0,12},{1,13},{2,14},{3,15},{4,0},{5,1},{6,2},{7,3},{8,4},{9,5},{1... | collective-permute-start | bytes 983048 | tf_op jit(solution)/shard_map/ppermute | solution.py:33
  163.9 8.6 %collective-permute-start.25 = (bf16[256,512]{1,0:T(8,128)(2,1)S(1)}, bf16[256,512]{1,0:T(8,128)(2,1)S(1)}, u32[]{:S(2)}, u32[]{:S(2)}) collective-permute-start(bf16[256,512]{1,0:T(8,128)(2,1)S(1)} %slice.160), channel_id=1, source_target_pairs={{0,2},{1,3},{2,0},{3,1},{4,6},{5,7},{6,4},{7,5},{8,10},{9,11},{10,... | collective-permute-start | bytes 786440 | tf_op jit(solution)/shard_map/ppermute | solution.py:33
  181.5 17.5 %collective-permute-start.27 = (bf16[128,512]{1,0:T(8,128)(2,1)}, bf16[128,512]{1,0:T(8,128)(2,1)S(1)}, u32[]{:S(2)}, u32[]{:S(2)}) collective-permute-start(bf16[128,512]{1,0:T(8,128)(2,1)} %get-tuple-element.33), channel_id=1, source_target_pairs={{0,64},{1,65},{2,66},{3,67},{4,68},{5,69},{6,70},{7,71},{8,72},{9,... | collective-permute-start | bytes 393224 | tf_op jit(solution)/shard_map/ppermute | solution.py:43
  185.5 13.5 %collective-permute-start.28 = (bf16[128,512]{1,0:T(8,128)(2,1)}, bf16[128,512]{1,0:T(8,128)(2,1)S(1)}, u32[]{:S(2)}, u32[]{:S(2)}) collective-permute-start(bf16[128,512]{1,0:T(8,128)(2,1)} %get-tuple-element.34), channel_id=1, source_target_pairs={{0,65},{1,64},{2,67},{3,66},{4,69},{5,68},{6,71},{7,70},{8,73},{9,... | collective-permute-start | bytes 393224 | tf_op jit(solution)/shard_map/ppermute | solution.py:43
  195.9 22.9 %collective-permute-start.32 = (bf16[640,1024]{1,0:T(8,128)(2,1)}, bf16[640,1024]{1,0:T(8,128)(2,1)S(1)}, u32[]{:S(2)}, u32[]{:S(2)}) collective-permute-start(bf16[640,1024]{1,0:T(8,128)(2,1)} %stacked_rows.7), channel_id=1, source_target_pairs={{0,2},{1,3},{2,0},{3,1},{4,6},{5,7},{6,4},{7,5},{8,10},{9,11},{10,... | collective-permute-start | bytes 3932168 | tf_op jit(solution)/shard_map/ppermute | solution.py:33
  199.0 15.8 %collective-permute-start.29 = (bf16[256,512]{1,0:T(8,128)(2,1)S(1)}, bf16[256,512]{1,0:T(8,128)(2,1)S(1)}, u32[]{:S(2)}, u32[]{:S(2)}) collective-permute-start(bf16[256,512]{1,0:T(8,128)(2,1)S(1)} %pad_maximum_fusion.9), channel_id=1, source_target_pairs={{0,32},{1,33},{2,34},{3,35},{4,36},{5,37},{6,38},{7,39},{8,40},{9,... | collective-permute-start | bytes 786440 | tf_op jit(solution)/shard_map/ppermute | solution.py:33
  201.0 17.1 %collective-permute-start.30 = (bf16[256,512]{1,0:T(8,128)(2,1)S(1)}, bf16[256,512]{1,0:T(8,128)(2,1)S(1)}, u32[]{:S(2)}, u32[]{:S(2)}) collective-permute-start(bf16[256,512]{1,0:T(8,128)(2,1)S(1)} %pad_maximum_fusion.9), channel_id=1, source_target_pairs={{0,16},{1,17},{2,18},{3,19},{4,20},{5,21},{6,22},{7,23},{8,24},{9,... | collective-permute-start | bytes 786440 | tf_op jit(solution)/shard_map/ppermute | solution.py:33
  214.8 8.2 %collective-permute-start.31 = (bf16[256,512]{1,0:T(8,128)(2,1)S(1)}, bf16[256,512]{1,0:T(8,128)(2,1)S(1)}, u32[]{:S(2)}, u32[]{:S(2)}) collective-permute-start(bf16[256,512]{1,0:T(8,128)(2,1)S(1)} %collective-permute-done.29), channel_id=1, source_target_pairs={{0,16},{1,17},{2,18},{3,19},{4,20},{5,21},{6,22},{7,23},{8,24},{9,... | collective-permute-start | bytes 786440 | tf_op jit(solution)/shard_map/ppermute | solution.py:33
  223.8 10.5 %collective-permute-start.35 = (bf16[320,512]{1,0:T(8,128)(2,1)S(1)}, bf16[320,512]{1,0:T(8,128)(2,1)S(1)}, u32[]{:S(2)}, u32[]{:S(2)}) collective-permute-start(bf16[320,512]{1,0:T(8,128)(2,1)S(1)} %pad_maximum_fusion.8), channel_id=1, source_target_pairs={{0,4},{1,5},{2,6},{3,7},{4,8},{5,9},{6,10},{7,11},{8,12},{9,13},{1... | collective-permute-start | bytes 983048 | tf_op jit(solution)/shard_map/ppermute | solution.py:33
  227.6 14.4 %collective-permute-start.34 = (bf16[320,512]{1,0:T(8,128)(2,1)S(1)}, bf16[320,512]{1,0:T(8,128)(2,1)S(1)}, u32[]{:S(2)}, u32[]{:S(2)}) collective-permute-start(bf16[320,512]{1,0:T(8,128)(2,1)S(1)} %pad_maximum_fusion.7), channel_id=1, source_target_pairs={{0,8},{1,9},{2,10},{3,11},{4,12},{5,13},{6,14},{7,15},{8,0},{9,1},... | collective-permute-start | bytes 983048 | tf_op jit(solution)/shard_map/ppermute | solution.py:33
  230.3 13.9 %collective-permute-start.33 = (bf16[320,512]{1,0:T(8,128)(2,1)S(1)}, bf16[320,512]{1,0:T(8,128)(2,1)S(1)}, u32[]{:S(2)}, u32[]{:S(2)}) collective-permute-start(bf16[320,512]{1,0:T(8,128)(2,1)S(1)} %pad_maximum_fusion.6), channel_id=1, source_target_pairs={{0,12},{1,13},{2,14},{3,15},{4,0},{5,1},{6,2},{7,3},{8,4},{9,5},{1... | collective-permute-start | bytes 983048 | tf_op jit(solution)/shard_map/ppermute | solution.py:33
  (27 other events, 311.8 us)

commit v6 on v5

--- a/solution.py
+++ b/solution.py
@@ -251,7 +251,6 @@
     item = jnp.concatenate([own, beside[:part]], axis=0)
     as_float = item.astype(f32)
     squares = jnp.sum(as_float * as_float, axis=0)
-    residual = moved_on(item, same)
     random = random_blocks[0]
     numbers = jnp.pad(random.astype(f32).reshape(-1), (0, step - random.size))
     mine = jnp.stack([squares, numbers])
@@ -263,8 +262,17 @@
     table = table + moved(table, lambda y, x, c: (y, x ^ 1, c))
     e = after(e, table)
     f = moved(e, by_two)
-    e_two = stacked_rows(e, moved(e, pair))
-    f_two = stacked_rows(f, moved(f, pair))
+    e_pair = moved(e, pair)
+    e_ring = [e]
+    for _ in range(3):
+        e_ring.append(moved(e_ring[-1], around))
+    f = after(f, e_ring[1])
+    e_pair = after(e_pair, e_ring[2])
+    f_two = after(stacked_rows(f, moved(f, pair)), e_ring[3])
+    pair_ring = [e_pair]
+    for _ in range(3):
+        pair_ring.append(moved(pair_ring[-1], around))
+    table = after(table, pair_ring[1])
     for where in (lambda y, x, c: (y, x ^ 2, c), pair, by_two):
         table = table + moved(table, where)
     factors = lax.rsqrt(table[16:] / width + 1e-05)
@@ -273,7 +281,7 @@
     gains = table[:16, : 2 * part].reshape(2, 2, 4, 2 * part)
     gains = at_index(gains, seq)
 
-    weight = after(qkv_weight[0], beside)
+    weight = after(qkv_weight[0], e_pair)
     beside = moved(weight, other_core)
     columns = weight.shape[1]
     weight = jnp.concatenate(
@@ -283,18 +291,23 @@
     weights, scales = [], []
     for k in range(4):
         source = (x - (1 - 2 * core) * k) % 4
-        rows, scale = [], []
+        weights.append([])
+        scales.append([])
         for ab in range(2):
             which = ab ^ (yl % 2)
             block = at_index(at_index(weight, which), source)
-            rows += [at_index(block, core), at_index(block, 1 - core)]
-            scale.append(at_index(at_index(gains, which), source))
-        weights.append(jnp.concatenate(rows, axis=0).T)
-        scales.append(jnp.concatenate(scale).reshape(4 * part, 1))
-
-    def project(block, k, factor):
-        normed = (block.astype(f32) * factor * scales[k]).astype(bf16)
-        return jnp.dot(weights[k], normed, preferred_element_type=f32)
+            weights[k].append(
+                jnp.concatenate([at_index(block, core), at_index(block, 1 - core)], axis=0)
+            )
+            scales[k].append(at_index(at_index(gains, which), source))
+
+    def project(block, k, which, factor):
+        rows = jnp.concatenate([weights[k][ab] for ab in which], axis=0)
+        scale = jnp.concatenate([scales[k][ab] for ab in which]).reshape(-1, 1)
+        normed = (block.astype(f32) * factor * scale).astype(bf16)
+        return lax.dot_general(
+            rows, normed, (((0,), (0,)), ((), ())), preferred_element_type=f32
+        )
 
     count = step // BLOCK
     rows = lax.dynamic_slice_in_dim(random, core * count, count, axis=1).reshape(2 * count, -1)
@@ -311,24 +324,27 @@
     allowed = block_mask(query_ids, rows, global_blocks[0], key_ids)
     bias = jnp.repeat(jnp.where(allowed.T, 0.0, NEG), BLOCK, axis=1).astype(bf16)
 
-    e, f = e_two, f_two
-    partial_e, partial_f = project(e, 0, factor_e), project(f, 0, factor_f)
+    f = f_two
+    partial_e = project(e, 0, (0,), factor_e) + project(e_pair, 0, (1,), factor_e)
+    partial_f = project(f, 0, (0, 1), factor_f)
     for k in range(1, 4):
-        e, f = moved(e, around), moved(f, around)
-        partial_e = partial_e + project(e, k, factor_e)
-        partial_f = partial_f + project(f, k, factor_f)
+        f = moved(f, around)
+        partial_e = partial_e + project(e_ring[k], k, (0,), factor_e)
+        partial_e = partial_e + project(pair_ring[k], k, (1,), factor_e)
+        partial_f = partial_f + project(f, k, (0, 1), factor_f)
     order = after(jnp.stack([yl, yl ^ 2, yl ^ 1, yl ^ 3]), f_two)
     ring = (x + jnp.arange(4, dtype=jnp.int32)) % 4
     slices = column_slices(out_next, order, ring)
     sends = [partial[columns:].astype(bf16) for partial in (partial_e, partial_f)]
     sends[0], slices = lax.optimization_barrier((sends[0], slices))
+    residual = moved_on(after(item, sends[1]), same)
     out_own = [slices[0]]
     for r in range(1, 4):
         out_own.append(moved(slices[r], lambda y, x, c, r=r: (y, (x + r) % 4, c)))
     joined, other = [], []
     head = columns // 3
     for partial, send in zip((partial_e, partial_f), sends):
-        came = moved(send, other_seq)
+        came = after(moved(send, other_seq), other)
         joined.append((partial[:columns] + came.astype(f32)).astype(bf16))
         other.append(moved(joined[-1][head:], other_core))
 

time: 254 us -> 276 us (1.087)
  starting transfers between devices: 135 us -> 147 us
  waiting for transfers between devices: 61.5 us -> 73.3 us
  matrix products: 11.7 us -> 16.8 us
  local copies, waits for them, and re-layouts: 8.9 us -> 4.95 us
  other arithmetic: 14 us -> 10.7 us
    ppermute x33 -> x36, starting transfers between devices: 117 us -> 131 us  [moved(): return lax.ppermute(value, PLANE, pairs_of(where))]
    ppermute x33 -> x36, waiting for transfers between devices: 61.5 us -> 70.2 us  [moved(): return lax.ppermute(value, PLANE, pairs_of(where))]
    dot_general x8 -> x12, matrix products: 8.03 us -> 13.1 us  [project(): lax.dot_general(rows, normed, (((0,), (0,)), ((), ())), preferred_element...]
    ppermute x4, waiting for transfers between devices: 0.01 us -> 3.09 us  [moved_on(): return lax.ppermute(value, ('section', *PLANE), pairs)]
    pallas_call x4 -> x3, Pallas kernels: 8.09 us -> 6.13 us  [stacked_rows(): pl.pallas_call(rows_kernel, in_specs=[vmem] * len(parts), out_specs=vmem,...]
  transfers between devices with their start and end apart: 37 -> 40, of which waited for: 15 -> 17; matrix products, arithmetic and copies ran while one was open for 10% -> 10% of each run, Pallas kernels for 5% -> 4%
where the time goes in v6:
time: 276 us; the launch traced here: 272 us
  starting transfers between devices  147 us (53%)
  waiting for transfers between devices  73.3 us (27%)
  Pallas kernels  18 us (7%)
  matrix products  16.8 us (6%)
  other arithmetic  10.7 us (4%)
  local copies, waits for them, and re-layouts  4.95 us (2%)
    ppermute x36, starting transfers between devices, moved(): return lax.ppermute(value, PLANE, pairs_of(where))  131 us
    ppermute x36, waiting for transfers between devices, moved(): return lax.ppermute(value, PLANE, pairs_of(where))  70.2 us
    ppermute x4, starting transfers between devices, moved_on(): return lax.ppermute(value, ('section', *PLANE), pairs)  16.6 us
    dot_general x12, matrix products, project(): lax.dot_general(rows, normed, (((0,), (0,)), ((), ())), preferred_element...  13.1 us
    pallas_call x1, Pallas kernels, attention(): pl.pallas_call(lambda *refs: attention_kernel(1.0 / math.sqrt(size), per,...  7.55 us
    pallas_call x3, Pallas kernels, stacked_rows(): pl.pallas_call(rows_kernel, in_specs=[vmem] * len(parts), out_specs=vmem,...  6.13 us
  transfers between devices with their start and end apart: 40, of which 17 were waited for; matrix products, arithmetic and copies ran while one was open for 10% of the time, Pallas kernels for 4%

profile of v6, /device:TPU:1, one launch (start us, length us, event | category | flops | bytes accessed | tf_op | source)
XLA Modules:
  0.0 272.1 jit_solution(5193150490737534254)
XLA Ops:
  1.9 8.8 %collective-permute-start = (bf16[176,512]{1,0:T(8,128)(2,1)S(1)}, bf16[176,512]{1,0:T(8,128)(2,1)S(1)}, u32[]{:S(2)}, u32[]{:S(2)}) collective-permute-start(bf16[176,512]{1,0:T(8,128)(2,1)S(1)} %fusion.107), channel_id=1, source_target_pairs={{0,2},{1,3},{2,0},{3,1},{4,6},{5,7},{6,4},{7,5},{8,10},{9,11},{10,... | collective-permute-start | bytes 540680 | tf_op jit(solution)/shard_map/ppermute | solution.py:33
  15.1 6.8 %collective-permute-start.3 = (f32[2,512]{1,0:T(2,128)S(1)}, f32[2,512]{1,0:T(2,128)S(1)}, u32[]{:S(2)}, u32[]{:S(2)}) collective-permute-start(f32[2,512]{1,0:T(2,128)S(1)} %pad_maximum_fusion.7), channel_id=1, source_target_pairs={{0,1},{1,0},{2,3},{3,2},{4,5},{5,4},{6,7},{7,6},{8,9},{9,8},{10,11... | collective-permute-start | bytes 12296 | tf_op jit(solution)/shard_map/ppermute | solution.py:33
  29.1 3.7 %collective-permute-start.6 = (bf16[320,512]{1,0:T(8,128)(2,1)}, bf16[320,512]{1,0:T(8,128)(2,1)S(1)}, u32[]{:S(2)}, u32[]{:S(2)}) collective-permute-start(bf16[320,512]{1,0:T(8,128)(2,1)} %stacked_rows.3), channel_id=1, source_target_pairs={{0,4},{1,5},{2,14},{3,15},{4,8},{5,9},{6,2},{7,3},{8,12},{9,13},{1... | collective-permute-start | bytes 983048 | tf_op jit(solution)/shard_map/ppermute | solution.py:33
  37.1 4.9 %collective-permute-start.7 = (bf16[320,512]{1,0:T(8,128)(2,1)S(1)}, bf16[320,512]{1,0:T(8,128)(2,1)S(1)}, u32[]{:S(2)}, u32[]{:S(2)}) collective-permute-start(bf16[320,512]{1,0:T(8,128)(2,1)S(1)} %collective-permute-done.6), channel_id=1, source_target_pairs={{0,4},{1,5},{2,14},{3,15},{4,8},{5,9},{6,2},{7,3},{8,12},{9,13},{1... | collective-permute-start | bytes 983048 | tf_op jit(solution)/shard_map/ppermute | solution.py:33
  42.0 4.0 %collective-permute-start.22 = (bf16[160,4096]{1,0:T(8,128)(2,1)}, bf16[160,4096]{1,0:T(8,128)(2,1)}, u32[]{:S(2)}, u32[]{:S(2)}) collective-permute-start(bf16[160,4096]{1,0:T(8,128)(2,1)} %bitcast.90), channel_id=1, source_target_pairs={{0,64},{1,65},{2,66},{3,67},{4,68},{5,69},{6,70},{7,71},{8,72},{9,... | collective-permute-start | bytes 3932168 | tf_op jit(solution)/shard_map/ppermute | solution.py:43
  46.2 4.5 %collective-permute-start.9 = (bf16[320,512]{1,0:T(8,128)(2,1)}, bf16[320,512]{1,0:T(8,128)(2,1)}, u32[]{:S(2)}, u32[]{:S(2)}) collective-permute-start(bf16[320,512]{1,0:T(8,128)(2,1)} %stacked_rows.3), channel_id=1, source_target_pairs={{0,32},{1,33},{2,34},{3,35},{4,36},{5,37},{6,38},{7,39},{8,40},{9,... | collective-permute-start | bytes 983048 | tf_op jit(solution)/shard_map/ppermute | solution.py:33
  50.7 3.6 %collective-permute-start.8 = (bf16[2560,384]{1,0:T(8,128)(2,1)S(1)}, bf16[2560,384]{1,0:T(8,128)(2,1)}, u32[]{:S(2)}, u32[]{:S(2)}) collective-permute-start(bf16[2560,384]{1,0:T(8,128)(2,1)S(1)} %bitcast.70), channel_id=1, source_target_pairs={{0,2},{1,3},{2,0},{3,1},{4,6},{5,7},{6,4},{7,5},{8,10},{9,11},{10,... | collective-permute-start | bytes 5898248 | tf_op jit(solution)/shard_map/ppermute | solution.py:33
  54.4 11.0 %collective-permute-done.9.refs_0_ = bf16[320,512]{1,0:T(8,128)(2,1)} collective-permute-done((bf16[320,512]{1,0:T(8,128)(2,1)}, bf16[320,512]{1,0:T(8,128)(2,1)}, u32[]{:S(2)}, u32[]{:S(2)}) %collective-permute-start.9) | collective-permute-done | bytes 327712 | tf_op jit(solution)/shard_map/ppermute | solution.py:33
  72.2 3.5 %collective-permute-done.10.refs_1_ = bf16[320,512]{1,0:T(8,128)(2,1)} collective-permute-done((bf16[320,512]{1,0:T(8,128)(2,1)}, bf16[320,512]{1,0:T(8,128)(2,1)}, u32[]{:S(2)}, u32[]{:S(2)}) %collective-permute-start.10) | collective-permute-done | bytes 327712 | tf_op jit(solution)/shard_map/ppermute | solution.py:33
  82.2 4.4 %collective-permute-done.13 = f32[18,512]{1,0:T(8,128)S(1)} collective-permute-done((f32[18,512]{1,0:T(8,128)S(1)}, f32[18,512]{1,0:T(8,128)S(1)}, u32[]{:S(2)}, u32[]{:S(2)}) %collective-permute-start.13) | collective-permute-done | bytes 36896 | tf_op jit(solution)/shard_map/ppermute | solution.py:33
  86.6 2.9 %collective-permute-start.14 = (f32[18,512]{1,0:T(8,128)S(1)}, f32[18,512]{1,0:T(8,128)S(1)}, u32[]{:S(2)}, u32[]{:S(2)}) collective-permute-start(f32[18,512]{1,0:T(8,128)S(1)} %add.464), channel_id=1, source_target_pairs={{0,16},{1,17},{2,18},{3,19},{4,20},{5,21},{6,22},{7,23},{8,24},{9,... | collective-permute-start | bytes 110600 | tf_op jit(solution)/shard_map/ppermute | solution.py:33
  91.9 5.0 %collective-permute-start.15 = (f32[18,512]{1,0:T(8,128)S(1)}, f32[18,512]{1,0:T(8,128)S(1)}, u32[]{:S(2)}, u32[]{:S(2)}) collective-permute-start(f32[18,512]{1,0:T(8,128)S(1)} %add.465), channel_id=1, source_target_pairs={{0,32},{1,33},{2,34},{3,35},{4,36},{5,37},{6,38},{7,39},{8,40},{9,... | collective-permute-start | bytes 110600 | tf_op jit(solution)/shard_map/ppermute | solution.py:33
  97.5 7.8 %collective-permute-start.20 = (bf16[320,512]{1,0:T(8,128)(2,1)}, bf16[320,512]{1,0:T(8,128)(2,1)}, u32[]{:S(2)}, u32[]{:S(2)}) collective-permute-start(bf16[320,512]{1,0:T(8,128)(2,1)} %collective-permute-done.12), channel_id=1, source_target_pairs={{0,4},{1,5},{2,14},{3,15},{4,8},{5,9},{6,2},{7,3},{8,12},{9,13},{1... | collective-permute-start | bytes 983048 | tf_op jit(solution)/shard_map/ppermute | solution.py:33
  105.3 4.3 %column_slices.1 = (bf16[160,1024]{1,0:T(8,128)(2,1)}, bf16[160,1024]{1,0:T(8,128)(2,1)}, bf16[160,1024]{1,0:T(8,128)(2,1)}, bf16[160,1024]{1,0:T(8,128)(2,1)}) custom-call(s32[4]{0:T(128)} %pad_add_fusion.order_ref, s32[4]{0:T(128)} %and_select_fusion.ring_ref, bf16[160,4096]{1,0:T(8,128)(2,1)} %collective-permute-done.22.source_ref), custom_call_target="tpu_custom_call" | custom-call | bytes 2621440 | tf_op jit(solution)/shard_map/column_slices/pallas_call | solution.py:162
  114.6 7.0 %collective-permute-done.17 = bf16[640,512]{1,0:T(8,128)(2,1)S(1)} collective-permute-done((bf16[640,512]{1,0:T(8,128)(2,1)}, bf16[640,512]{1,0:T(8,128)(2,1)S(1)}, u32[]{:S(2)}, u32[]{:S(2)}) %collective-permute-start.17) | collective-permute-done | bytes 655392 | tf_op jit(solution)/shard_map/ppermute | solution.py:33
  136.3 4.8 %collective-permute-start.26 = (bf16[384,512]{1,0:T(8,128)(2,1)S(1)}, bf16[384,512]{1,0:T(8,128)(2,1)S(1)}, u32[]{:S(2)}, u32[]{:S(2)}) collective-permute-start(bf16[384,512]{1,0:T(8,128)(2,1)S(1)} %slice.222), channel_id=1, source_target_pairs={{0,1},{1,0},{2,3},{3,2},{4,5},{5,4},{6,7},{7,6},{8,9},{9,8},{10,11... | collective-permute-start | bytes 1179656 | tf_op jit(solution)/shard_map/ppermute | solution.py:33
  145.7 4.4 %collective-permute-start.27 = (bf16[384,512]{1,0:T(8,128)(2,1)S(1)}, bf16[384,512]{1,0:T(8,128)(2,1)S(1)}, u32[]{:S(2)}, u32[]{:S(2)}) collective-permute-start(bf16[384,512]{1,0:T(8,128)(2,1)S(1)} %slice.223), channel_id=1, source_target_pairs={{0,1},{1,0},{2,3},{3,2},{4,5},{5,4},{6,7},{7,6},{8,9},{9,8},{10,11... | collective-permute-start | bytes 1179656 | tf_op jit(solution)/shard_map/ppermute | solution.py:33
  150.1 5.9 %collective-permute-done.26 = bf16[384,512]{1,0:T(8,128)(2,1)S(1)} collective-permute-done((bf16[384,512]{1,0:T(8,128)(2,1)S(1)}, bf16[384,512]{1,0:T(8,128)(2,1)S(1)}, u32[]{:S(2)}, u32[]{:S(2)}) %collective-permute-start.26) | collective-permute-done | bytes 393248 | tf_op jit(solution)/shard_map/ppermute | solution.py:33
  156.2 9.1 %collective-permute-start.28 = (bf16[256,512]{1,0:T(8,128)(2,1)S(1)}, bf16[256,512]{1,0:T(8,128)(2,1)}, u32[]{:S(2)}, u32[]{:S(2)}) collective-permute-start(bf16[256,512]{1,0:T(8,128)(2,1)S(1)} %slice.160), channel_id=1, source_target_pairs={{0,2},{1,3},{2,0},{3,1},{4,6},{5,7},{6,4},{7,5},{8,10},{9,11},{10,... | collective-permute-start | bytes 786440 | tf_op jit(solution)/shard_map/ppermute | solution.py:33
  171.4 3.6 %collective-permute-start.25 = (bf16[160,1024]{1,0:T(8,128)(2,1)}, bf16[160,1024]{1,0:T(8,128)(2,1)}, u32[]{:S(2)}, u32[]{:S(2)}) collective-permute-start(bf16[160,1024]{1,0:T(8,128)(2,1)} %get-tuple-element.41), channel_id=1, source_target_pairs={{0,12},{1,13},{2,14},{3,15},{4,0},{5,1},{6,2},{7,3},{8,4},{9,5},{1... | collective-permute-start | bytes 983048 | tf_op jit(solution)/shard_map/ppermute | solution.py:33
  175.1 4.2 %collective-permute-start.19 = (bf16[320,512]{1,0:T(8,128)(2,1)}, bf16[320,512]{1,0:T(8,128)(2,1)S(1)}, u32[]{:S(2)}, u32[]{:S(2)}) collective-permute-start(bf16[320,512]{1,0:T(8,128)(2,1)} %pad_maximum_fusion.1), channel_id=1, source_target_pairs={{0,64},{1,65},{2,66},{3,67},{4,68},{5,69},{6,70},{7,71},{8,72},{9,... | collective-permute-start | bytes 983048 | tf_op jit(solution)/shard_map/ppermute | solution.py:43
  188.4 3.1 %collective-permute-done.19 = bf16[320,512]{1,0:T(8,128)(2,1)S(1)} collective-permute-done((bf16[320,512]{1,0:T(8,128)(2,1)}, bf16[320,512]{1,0:T(8,128)(2,1)S(1)}, u32[]{:S(2)}, u32[]{:S(2)}) %collective-permute-start.19) | collective-permute-done | bytes 327712 | tf_op jit(solution)/shard_map/ppermute | solution.py:43
  192.2 7.6 %attention.1 = (bf16[128,512]{1,0:T(8,128)(2,1)}, bf16[128,512]{1,0:T(8,128)(2,1)}) custom-call(s32[1]{0:T(128)} %bitcast.32.refs_0_, bf16[384,512]{1,0:T(8,128)(2,1)} %copy-done.3, bf16[384,512]{1,0:T(8,128)(2,1)} %copy-done.4, bf16[256,512]{1,0:T(8,128)(2,1)} %collective-permute-done.28.refs_3_, bf16[256,512]{1,0:T(8,128)(2,1)} %copy-done.10, ...), custom_call_target="tpu_custom_call" | custom-call | flops 1073741824 | bytes 786432 | tf_op jit(solution)/shard_map/attention/pallas_call | solution.py:127
  201.6 6.5 %collective-permute-start.31 = (bf16[128,512]{1,0:T(8,128)(2,1)}, bf16[128,512]{1,0:T(8,128)(2,1)S(1)}, u32[]{:S(2)}, u32[]{:S(2)}) collective-permute-start(bf16[128,512]{1,0:T(8,128)(2,1)} %get-tuple-element.46), channel_id=1, source_target_pairs={{0,65},{1,64},{2,67},{3,66},{4,69},{5,68},{6,71},{7,70},{8,73},{9,... | collective-permute-start | bytes 393224 | tf_op jit(solution)/shard_map/ppermute | solution.py:43
  210.6 3.9 %collective-permute-start.35 = (bf16[640,1024]{1,0:T(8,128)(2,1)}, bf16[640,1024]{1,0:T(8,128)(2,1)S(1)}, u32[]{:S(2)}, u32[]{:S(2)}) collective-permute-start(bf16[640,1024]{1,0:T(8,128)(2,1)} %stacked_rows.5), channel_id=1, source_target_pairs={{0,2},{1,3},{2,0},{3,1},{4,6},{5,7},{6,4},{7,5},{8,10},{9,11},{10,... | collective-permute-start | bytes 3932168 | tf_op jit(solution)/shard_map/ppermute | solution.py:33
  214.6 8.0 %collective-permute-start.32 = (bf16[256,512]{1,0:T(8,128)(2,1)S(1)}, bf16[256,512]{1,0:T(8,128)(2,1)S(1)}, u32[]{:S(2)}, u32[]{:S(2)}) collective-permute-start(bf16[256,512]{1,0:T(8,128)(2,1)S(1)} %pad_maximum_fusion.5), channel_id=1, source_target_pairs={{0,32},{1,33},{2,34},{3,35},{4,36},{5,37},{6,38},{7,39},{8,40},{9,... | collective-permute-start | bytes 786440 | tf_op jit(solution)/shard_map/ppermute | solution.py:33
  224.5 9.4 %collective-permute-done.32 = bf16[256,512]{1,0:T(8,128)(2,1)S(1)} collective-permute-done((bf16[256,512]{1,0:T(8,128)(2,1)S(1)}, bf16[256,512]{1,0:T(8,128)(2,1)S(1)}, u32[]{:S(2)}, u32[]{:S(2)}) %collective-permute-start.32) | collective-permute-done | bytes 262176 | tf_op jit(solution)/shard_map/ppermute | solution.py:33
  238.8 3.1 %collective-permute-done.34 = bf16[256,512]{1,0:T(8,128)(2,1)S(1)} collective-permute-done((bf16[256,512]{1,0:T(8,128)(2,1)S(1)}, bf16[256,512]{1,0:T(8,128)(2,1)S(1)}, u32[]{:S(2)}, u32[]{:S(2)}) %collective-permute-start.34) | collective-permute-done | bytes 262176 | tf_op jit(solution)/shard_map/ppermute | solution.py:33
  242.7 4.9 %collective-permute-start.36 = (bf16[320,512]{1,0:T(8,128)(2,1)S(1)}, bf16[320,512]{1,0:T(8,128)(2,1)S(1)}, u32[]{:S(2)}, u32[]{:S(2)}) collective-permute-start(bf16[320,512]{1,0:T(8,128)(2,1)S(1)} %pad_maximum_fusion.2), channel_id=1, source_target_pairs={{0,12},{1,13},{2,14},{3,15},{4,0},{5,1},{6,2},{7,3},{8,4},{9,5},{1... | collective-permute-start | bytes 983048 | tf_op jit(solution)/shard_map/ppermute | solution.py:33
  253.8 3.5 %collective-permute-done.37 = bf16[320,512]{1,0:T(8,128)(2,1)S(1)} collective-permute-done((bf16[320,512]{1,0:T(8,128)(2,1)S(1)}, bf16[320,512]{1,0:T(8,128)(2,1)S(1)}, u32[]{:S(2)}, u32[]{:S(2)}) %collective-permute-start.37) | collective-permute-done | bytes 327712 | tf_op jit(solution)/shard_map/ppermute | solution.py:33
  257.3 9.6 %collective-permute-done.38 = bf16[320,512]{1,0:T(8,128)(2,1)S(1)} collective-permute-done((bf16[320,512]{1,0:T(8,128)(2,1)S(1)}, bf16[320,512]{1,0:T(8,128)(2,1)S(1)}, u32[]{:S(2)}, u32[]{:S(2)}) %collective-permute-start.38) | collective-permute-done | bytes 327712 | tf_op jit(solution)/shard_map/ppermute | solution.py:33
  267.1 3.1 %collective-permute-start.39 = (bf16[160,512]{1,0:T(8,128)(2,1)S(1)}, bf16[160,512]{1,0:T(8,128)(2,1)S(1)}, u32[]{:S(2)}, u32[]{:S(2)}) collective-permute-start(bf16[160,512]{1,0:T(8,128)(2,1)S(1)} %slice.179), channel_id=1, source_target_pairs={{0,2},{1,3},{2,0},{3,1},{4,6},{5,7},{6,4},{7,5},{8,10},{9,11},{10,... | collective-permute-start | bytes 491528 | tf_op jit(solution)/shard_map/ppermute | solution.py:33
  (170 shorter events, 94.6 us)
Async XLA Ops:
  1.9 12.3 %collective-permute-start = (bf16[176,512]{1,0:T(8,128)(2,1)S(1)}, bf16[176,512]{1,0:T(8,128)(2,1)S(1)}, u32[]{:S(2)}, u32[]{:S(2)}) collective-permute-start(bf16[176,512]{1,0:T(8,128)(2,1)S(1)} %fusion.107), channel_id=1, source_target_pairs={{0,2},{1,3},{2,0},{3,1},{4,6},{5,7},{6,4},{7,5},{8,10},{9,11},{10,... | collective-permute-start | bytes 540680 | tf_op jit(solution)/shard_map/ppermute | solution.py:33
  10.7 15.3 %collective-permute-start.2 = (bf16[160,512]{1,0:T(8,128)(2,1)S(1)}, bf16[160,512]{1,0:T(8,128)(2,1)S(1)}, u32[]{:S(2)}, u32[]{:S(2)}) collective-permute-start(bf16[160,512]{1,0:T(8,128)(2,1)S(1)} %get-tuple-element.81), channel_id=1, source_target_pairs={{0,2},{1,34},{2,0},{3,32},{4,6},{5,38},{6,4},{7,36},{8,10},{9,42},... | collective-permute-start | bytes 491528 | tf_op jit(solution)/shard_map/ppermute | solution.py:33
  12.6 13.4 %collective-permute-start.1 = (bf16[160,512]{1,0:T(8,128)(2,1)S(1)}, bf16[160,512]{1,0:T(8,128)(2,1)S(1)}, u32[]{:S(2)}, u32[]{:S(2)}) collective-permute-start(bf16[160,512]{1,0:T(8,128)(2,1)S(1)} %get-tuple-element.82), channel_id=1, source_target_pairs={{0,0},{1,32},{2,2},{3,34},{4,4},{5,36},{6,6},{7,38},{8,8},{9,40},{... | collective-permute-start | bytes 491528 | tf_op jit(solution)/shard_map/ppermute | solution.py:33
  32.8 17.8 %collective-permute-start.5 = (bf16[320,512]{1,0:T(8,128)(2,1)}, bf16[320,512]{1,0:T(8,128)(2,1)S(1)}, u32[]{:S(2)}, u32[]{:S(2)}) collective-permute-start(bf16[320,512]{1,0:T(8,128)(2,1)} %stacked_rows.3), channel_id=1, source_target_pairs={{0,16},{1,17},{2,18},{3,19},{4,20},{5,21},{6,22},{7,23},{8,24},{9,... | collective-permute-start | bytes 983048 | tf_op jit(solution)/shard_map/ppermute | solution.py:33
  37.1 13.5 %collective-permute-start.7 = (bf16[320,512]{1,0:T(8,128)(2,1)S(1)}, bf16[320,512]{1,0:T(8,128)(2,1)S(1)}, u32[]{:S(2)}, u32[]{:S(2)}) collective-permute-start(bf16[320,512]{1,0:T(8,128)(2,1)S(1)} %collective-permute-done.6), channel_id=1, source_target_pairs={{0,4},{1,5},{2,14},{3,15},{4,8},{5,9},{6,2},{7,3},{8,12},{9,13},{1... | collective-permute-start | bytes 983048 | tf_op jit(solution)/shard_map/ppermute | solution.py:33
  42.0 63.2 %collective-permute-start.22 = (bf16[160,4096]{1,0:T(8,128)(2,1)}, bf16[160,4096]{1,0:T(8,128)(2,1)}, u32[]{:S(2)}, u32[]{:S(2)}) collective-permute-start(bf16[160,4096]{1,0:T(8,128)(2,1)} %bitcast.90), channel_id=1, source_target_pairs={{0,64},{1,65},{2,66},{3,67},{4,68},{5,69},{6,70},{7,71},{8,72},{9,... | collective-permute-start | bytes 3932168 | tf_op jit(solution)/shard_map/ppermute | solution.py:43
  46.2 19.3 %collective-permute-start.9 = (bf16[320,512]{1,0:T(8,128)(2,1)}, bf16[320,512]{1,0:T(8,128)(2,1)}, u32[]{:S(2)}, u32[]{:S(2)}) collective-permute-start(bf16[320,512]{1,0:T(8,128)(2,1)} %stacked_rows.3), channel_id=1, source_target_pairs={{0,32},{1,33},{2,34},{3,35},{4,36},{5,37},{6,38},{7,39},{8,40},{9,... | collective-permute-start | bytes 983048 | tf_op jit(solution)/shard_map/ppermute | solution.py:33
  50.7 73.7 %collective-permute-start.8 = (bf16[2560,384]{1,0:T(8,128)(2,1)S(1)}, bf16[2560,384]{1,0:T(8,128)(2,1)}, u32[]{:S(2)}, u32[]{:S(2)}) collective-permute-start(bf16[2560,384]{1,0:T(8,128)(2,1)S(1)} %bitcast.70), channel_id=1, source_target_pairs={{0,2},{1,3},{2,0},{3,1},{4,6},{5,7},{6,4},{7,5},{8,10},{9,11},{10,... | collective-permute-start | bytes 5898248 | tf_op jit(solution)/shard_map/ppermute | solution.py:33
  65.4 10.2 %collective-permute-start.10 = (bf16[320,512]{1,0:T(8,128)(2,1)}, bf16[320,512]{1,0:T(8,128)(2,1)}, u32[]{:S(2)}, u32[]{:S(2)}) collective-permute-start(bf16[320,512]{1,0:T(8,128)(2,1)} %collective-permute-done.9.refs_0_), channel_id=1, source_target_pairs={{0,16},{1,17},{2,18},{3,19},{4,20},{5,21},{6,22},{7,23},{8,24},{9,... | collective-permute-start | bytes 983048 | tf_op jit(solution)/shard_map/ppermute | solution.py:33
  69.9 9.8 %collective-permute-start.12 = (bf16[320,512]{1,0:T(8,128)(2,1)S(1)}, bf16[320,512]{1,0:T(8,128)(2,1)}, u32[]{:S(2)}, u32[]{:S(2)}) collective-permute-start(bf16[320,512]{1,0:T(8,128)(2,1)S(1)} %collective-permute-done.5), channel_id=1, source_target_pairs={{0,4},{1,5},{2,14},{3,15},{4,8},{5,9},{6,2},{7,3},{8,12},{9,13},{1... | collective-permute-start | bytes 983048 | tf_op jit(solution)/shard_map/ppermute | solution.py:33
  77.6 32.2 %collective-permute-start.16 = (bf16[640,512]{1,0:T(8,128)(2,1)}, bf16[640,512]{1,0:T(8,128)(2,1)}, u32[]{:S(2)}, u32[]{:S(2)}) collective-permute-start(bf16[640,512]{1,0:T(8,128)(2,1)} %stacked_rows.4), channel_id=1, source_target_pairs={{0,4},{1,5},{2,14},{3,15},{4,8},{5,9},{6,2},{7,3},{8,12},{9,13},{1... | collective-permute-start | bytes 1966088 | tf_op jit(solution)/shard_map/ppermute | solution.py:33
  91.9 17.7 %collective-permute-start.15 = (f32[18,512]{1,0:T(8,128)S(1)}, f32[18,512]{1,0:T(8,128)S(1)}, u32[]{:S(2)}, u32[]{:S(2)}) collective-permute-start(f32[18,512]{1,0:T(8,128)S(1)} %add.465), channel_id=1, source_target_pairs={{0,32},{1,33},{2,34},{3,35},{4,36},{5,37},{6,38},{7,39},{8,40},{9,... | collective-permute-start | bytes 110600 | tf_op jit(solution)/shard_map/ppermute | solution.py:33
  97.5 14.4 %collective-permute-start.20 = (bf16[320,512]{1,0:T(8,128)(2,1)}, bf16[320,512]{1,0:T(8,128)(2,1)}, u32[]{:S(2)}, u32[]{:S(2)}) collective-permute-start(bf16[320,512]{1,0:T(8,128)(2,1)} %collective-permute-done.12), channel_id=1, source_target_pairs={{0,4},{1,5},{2,14},{3,15},{4,8},{5,9},{6,2},{7,3},{8,12},{9,13},{1... | collective-permute-start | bytes 983048 | tf_op jit(solution)/shard_map/ppermute | solution.py:33
  109.8 11.8 %collective-permute-start.17 = (bf16[640,512]{1,0:T(8,128)(2,1)}, bf16[640,512]{1,0:T(8,128)(2,1)S(1)}, u32[]{:S(2)}, u32[]{:S(2)}) collective-permute-start(bf16[640,512]{1,0:T(8,128)(2,1)} %collective-permute-done.16), channel_id=1, source_target_pairs={{0,4},{1,5},{2,14},{3,15},{4,8},{5,9},{6,2},{7,3},{8,12},{9,13},{1... | collective-permute-start | bytes 1966088 | tf_op jit(solution)/shard_map/ppermute | solution.py:33
  111.9 23.2 %collective-permute-start.21 = (bf16[320,512]{1,0:T(8,128)(2,1)}, bf16[320,512]{1,0:T(8,128)(2,1)S(1)}, u32[]{:S(2)}, u32[]{:S(2)}) collective-permute-start(bf16[320,512]{1,0:T(8,128)(2,1)} %collective-permute-done.20), channel_id=1, source_target_pairs={{0,4},{1,5},{2,14},{3,15},{4,8},{5,9},{6,2},{7,3},{8,12},{9,13},{1... | collective-permute-start | bytes 983048 | tf_op jit(solution)/shard_map/ppermute | solution.py:33
  121.6 23.2 %collective-permute-start.18 = (bf16[640,512]{1,0:T(8,128)(2,1)S(1)}, bf16[640,512]{1,0:T(8,128)(2,1)S(1)}, u32[]{:S(2)}, u32[]{:S(2)}) collective-permute-start(bf16[640,512]{1,0:T(8,128)(2,1)S(1)} %collective-permute-done.17), channel_id=1, source_target_pairs={{0,4},{1,5},{2,14},{3,15},{4,8},{5,9},{6,2},{7,3},{8,12},{9,13},{1... | collective-permute-start | bytes 1966088 | tf_op jit(solution)/shard_map/ppermute | solution.py:33
  136.3 19.7 %collective-permute-start.26 = (bf16[384,512]{1,0:T(8,128)(2,1)S(1)}, bf16[384,512]{1,0:T(8,128)(2,1)S(1)}, u32[]{:S(2)}, u32[]{:S(2)}) collective-permute-start(bf16[384,512]{1,0:T(8,128)(2,1)S(1)} %slice.222), channel_id=1, source_target_pairs={{0,1},{1,0},{2,3},{3,2},{4,5},{5,4},{6,7},{7,6},{8,9},{9,8},{10,11... | collective-permute-start | bytes 1179656 | tf_op jit(solution)/shard_map/ppermute | solution.py:33
  145.7 33.5 %collective-permute-start.27 = (bf16[384,512]{1,0:T(8,128)(2,1)S(1)}, bf16[384,512]{1,0:T(8,128)(2,1)S(1)}, u32[]{:S(2)}, u32[]{:S(2)}) collective-permute-start(bf16[384,512]{1,0:T(8,128)(2,1)S(1)} %slice.223), channel_id=1, source_target_pairs={{0,1},{1,0},{2,3},{3,2},{4,5},{5,4},{6,7},{7,6},{8,9},{9,8},{10,11... | collective-permute-start | bytes 1179656 | tf_op jit(solution)/shard_map/ppermute | solution.py:33
  156.2 18.9 %collective-permute-start.28 = (bf16[256,512]{1,0:T(8,128)(2,1)S(1)}, bf16[256,512]{1,0:T(8,128)(2,1)}, u32[]{:S(2)}, u32[]{:S(2)}) collective-permute-start(bf16[256,512]{1,0:T(8,128)(2,1)S(1)} %slice.160), channel_id=1, source_target_pairs={{0,2},{1,3},{2,0},{3,1},{4,6},{5,7},{6,4},{7,5},{8,10},{9,11},{10,... | collective-permute-start | bytes 786440 | tf_op jit(solution)/shard_map/ppermute | solution.py:33
  166.4 19.8 %collective-permute-start.23 = (bf16[160,1024]{1,0:T(8,128)(2,1)}, bf16[160,1024]{1,0:T(8,128)(2,1)}, u32[]{:S(2)}, u32[]{:S(2)}) collective-permute-start(bf16[160,1024]{1,0:T(8,128)(2,1)} %get-tuple-element.39), channel_id=1, source_target_pairs={{0,4},{1,5},{2,6},{3,7},{4,8},{5,9},{6,10},{7,11},{8,12},{9,13},{1... | collective-permute-start | bytes 983048 | tf_op jit(solution)/shard_map/ppermute | solution.py:33
  168.8 17.3 %collective-permute-start.24 = (bf16[160,1024]{1,0:T(8,128)(2,1)}, bf16[160,1024]{1,0:T(8,128)(2,1)}, u32[]{:S(2)}, u32[]{:S(2)}) collective-permute-start(bf16[160,1024]{1,0:T(8,128)(2,1)} %get-tuple-element.40), channel_id=1, source_target_pairs={{0,8},{1,9},{2,10},{3,11},{4,12},{5,13},{6,14},{7,15},{8,0},{9,1},... | collective-permute-start | bytes 983048 | tf_op jit(solution)/shard_map/ppermute | solution.py:33
  171.4 17.0 %collective-permute-start.25 = (bf16[160,1024]{1,0:T(8,128)(2,1)}, bf16[160,1024]{1,0:T(8,128)(2,1)}, u32[]{:S(2)}, u32[]{:S(2)}) collective-permute-start(bf16[160,1024]{1,0:T(8,128)(2,1)} %get-tuple-element.41), channel_id=1, source_target_pairs={{0,12},{1,13},{2,14},{3,15},{4,0},{5,1},{6,2},{7,3},{8,4},{9,5},{1... | collective-permute-start | bytes 983048 | tf_op jit(solution)/shard_map/ppermute | solution.py:33
  175.1 16.4 %collective-permute-start.19 = (bf16[320,512]{1,0:T(8,128)(2,1)}, bf16[320,512]{1,0:T(8,128)(2,1)S(1)}, u32[]{:S(2)}, u32[]{:S(2)}) collective-permute-start(bf16[320,512]{1,0:T(8,128)(2,1)} %pad_maximum_fusion.1), channel_id=1, source_target_pairs={{0,64},{1,65},{2,66},{3,67},{4,68},{5,69},{6,70},{7,71},{8,72},{9,... | collective-permute-start | bytes 983048 | tf_op jit(solution)/shard_map/ppermute | solution.py:43
  179.5 12.0 %collective-permute-start.29 = (bf16[256,512]{1,0:T(8,128)(2,1)S(1)}, bf16[256,512]{1,0:T(8,128)(2,1)S(1)}, u32[]{:S(2)}, u32[]{:S(2)}) collective-permute-start(bf16[256,512]{1,0:T(8,128)(2,1)S(1)} %slice.161), channel_id=1, source_target_pairs={{0,2},{1,3},{2,0},{3,1},{4,6},{5,7},{6,4},{7,5},{8,10},{9,11},{10,... | collective-permute-start | bytes 786440 | tf_op jit(solution)/shard_map/ppermute | solution.py:33
  199.7 14.8 %collective-permute-start.30 = (bf16[128,512]{1,0:T(8,128)(2,1)}, bf16[128,512]{1,0:T(8,128)(2,1)S(1)}, u32[]{:S(2)}, u32[]{:S(2)}) collective-permute-start(bf16[128,512]{1,0:T(8,128)(2,1)} %get-tuple-element.45), channel_id=1, source_target_pairs={{0,64},{1,65},{2,66},{3,67},{4,68},{5,69},{6,70},{7,71},{8,72},{9,... | collective-permute-start | bytes 393224 | tf_op jit(solution)/shard_map/ppermute | solution.py:43
  201.6 12.9 %collective-permute-start.31 = (bf16[128,512]{1,0:T(8,128)(2,1)}, bf16[128,512]{1,0:T(8,128)(2,1)S(1)}, u32[]{:S(2)}, u32[]{:S(2)}) collective-permute-start(bf16[128,512]{1,0:T(8,128)(2,1)} %get-tuple-element.46), channel_id=1, source_target_pairs={{0,65},{1,64},{2,67},{3,66},{4,69},{5,68},{6,71},{7,70},{8,73},{9,... | collective-permute-start | bytes 393224 | tf_op jit(solution)/shard_map/ppermute | solution.py:43
  210.6 27.2 %collective-permute-start.35 = (bf16[640,1024]{1,0:T(8,128)(2,1)}, bf16[640,1024]{1,0:T(8,128)(2,1)S(1)}, u32[]{:S(2)}, u32[]{:S(2)}) collective-permute-start(bf16[640,1024]{1,0:T(8,128)(2,1)} %stacked_rows.5), channel_id=1, source_target_pairs={{0,2},{1,3},{2,0},{3,1},{4,6},{5,7},{6,4},{7,5},{8,10},{9,11},{10,... | collective-permute-start | bytes 3932168 | tf_op jit(solution)/shard_map/ppermute | solution.py:33
  214.6 19.3 %collective-permute-start.32 = (bf16[256,512]{1,0:T(8,128)(2,1)S(1)}, bf16[256,512]{1,0:T(8,128)(2,1)S(1)}, u32[]{:S(2)}, u32[]{:S(2)}) collective-permute-start(bf16[256,512]{1,0:T(8,128)(2,1)S(1)} %pad_maximum_fusion.5), channel_id=1, source_target_pairs={{0,32},{1,33},{2,34},{3,35},{4,36},{5,37},{6,38},{7,39},{8,40},{9,... | collective-permute-start | bytes 786440 | tf_op jit(solution)/shard_map/ppermute | solution.py:33
  222.6 14.5 %collective-permute-start.33 = (bf16[256,512]{1,0:T(8,128)(2,1)S(1)}, bf16[256,512]{1,0:T(8,128)(2,1)S(1)}, u32[]{:S(2)}, u32[]{:S(2)}) collective-permute-start(bf16[256,512]{1,0:T(8,128)(2,1)S(1)} %pad_maximum_fusion.5), channel_id=1, source_target_pairs={{0,16},{1,17},{2,18},{3,19},{4,20},{5,21},{6,22},{7,23},{8,24},{9,... | collective-permute-start | bytes 786440 | tf_op jit(solution)/shard_map/ppermute | solution.py:33
  242.7 11.2 %collective-permute-start.36 = (bf16[320,512]{1,0:T(8,128)(2,1)S(1)}, bf16[320,512]{1,0:T(8,128)(2,1)S(1)}, u32[]{:S(2)}, u32[]{:S(2)}) collective-permute-start(bf16[320,512]{1,0:T(8,128)(2,1)S(1)} %pad_maximum_fusion.2), channel_id=1, source_target_pairs={{0,12},{1,13},{2,14},{3,15},{4,0},{5,1},{6,2},{7,3},{8,4},{9,5},{1... | collective-permute-start | bytes 983048 | tf_op jit(solution)/shard_map/ppermute | solution.py:33
  247.6 9.8 %collective-permute-start.37 = (bf16[320,512]{1,0:T(8,128)(2,1)S(1)}, bf16[320,512]{1,0:T(8,128)(2,1)S(1)}, u32[]{:S(2)}, u32[]{:S(2)}) collective-permute-start(bf16[320,512]{1,0:T(8,128)(2,1)S(1)} %pad_maximum_fusion.3), channel_id=1, source_target_pairs={{0,8},{1,9},{2,10},{3,11},{4,12},{5,13},{6,14},{7,15},{8,0},{9,1},... | collective-permute-start | bytes 983048 | tf_op jit(solution)/shard_map/ppermute | solution.py:33
  249.5 17.4 %collective-permute-start.38 = (bf16[320,512]{1,0:T(8,128)(2,1)S(1)}, bf16[320,512]{1,0:T(8,128)(2,1)S(1)}, u32[]{:S(2)}, u32[]{:S(2)}) collective-permute-start(bf16[320,512]{1,0:T(8,128)(2,1)S(1)} %pad_maximum_fusion.4), channel_id=1, source_target_pairs={{0,4},{1,5},{2,6},{3,7},{4,8},{5,9},{6,10},{7,11},{8,12},{9,13},{1... | collective-permute-start | bytes 983048 | tf_op jit(solution)/shard_map/ppermute | solution.py:33
  (20 other events, 302.0 us)

commit v7 on v5

--- a/solution.py
+++ b/solution.py
@@ -156,8 +156,8 @@
         out_ref[...] = source_ref[:, pl.ds(start, per)]
 
 
-def column_slices(matrix, order, ring):
-    rows, width = matrix.shape
+def column_slices(matrix, order, ring, width):
+    rows = matrix.shape[0]
     block = pl.BlockSpec((rows, width // 16), lambda p, order, ring: (0, p))
     return pl.pallas_call(
         slices_kernel,
@@ -242,8 +242,6 @@
     own, away = of_core(tokens_t)
     crossed = moved(away, lambda *at: other_core(*swap_inner(*at)))
     e = stacked_rows(moved(own, swap_inner), crossed)
-    out_next = moved_on(out_weight[0].T, same)
-
     gain = norm_gain
     gain_row = jnp.pad(gain, ((0, 15), (0, step - part)))
     beside = moved(jnp.concatenate([away, gain_row], axis=0), other_core)
@@ -251,7 +249,7 @@
     item = jnp.concatenate([own, beside[:part]], axis=0)
     as_float = item.astype(f32)
     squares = jnp.sum(as_float * as_float, axis=0)
-    residual = moved_on(item, same)
+    ahead = moved_on(out_weight[0].T, same)
     random = random_blocks[0]
     numbers = jnp.pad(random.astype(f32).reshape(-1), (0, step - random.size))
     mine = jnp.stack([squares, numbers])
@@ -263,17 +261,25 @@
     table = table + moved(table, lambda y, x, c: (y, x ^ 1, c))
     e = after(e, table)
     f = moved(e, by_two)
-    e_two = stacked_rows(e, moved(e, pair))
-    f_two = stacked_rows(f, moved(f, pair))
-    for where in (lambda y, x, c: (y, x ^ 2, c), pair, by_two):
-        table = table + moved(table, where)
+    table = table + moved(table, lambda y, x, c: (y, x ^ 2, c))
+    e_two = stacked_rows(e, after(moved(e, pair), (table, f)))
+    f_pair = moved(f, pair)
+    table = table + moved(table, pair)
+    e_next = moved(e_two, around)
+    f_two = after(stacked_rows(f, after(f_pair, table)), e_next)
+    table = table + moved(table, by_two)
+    e_ring, f_ring = [e_two, e_next], [f_two, moved(f_two, around)]
+    f_ring[1] = after(f_ring[1], table)
+    for _ in range(2):
+        e_ring.append(moved(e_ring[-1], around))
+        f_ring.append(moved(f_ring[-1], around))
     factors = lax.rsqrt(table[16:] / width + 1e-05)
     factor_e = jnp.where(first == seq, factors[:1], factors[1:])
     factor_f = jnp.where(first == seq, factors[1:], factors[:1])
     gains = table[:16, : 2 * part].reshape(2, 2, 4, 2 * part)
     gains = at_index(gains, seq)
 
-    weight = after(qkv_weight[0], beside)
+    weight = after(qkv_weight[0], theirs)
     beside = moved(weight, other_core)
     columns = weight.shape[1]
     weight = jnp.concatenate(
@@ -311,15 +317,13 @@
     allowed = block_mask(query_ids, rows, global_blocks[0], key_ids)
     bias = jnp.repeat(jnp.where(allowed.T, 0.0, NEG), BLOCK, axis=1).astype(bf16)
 
-    e, f = e_two, f_two
-    partial_e, partial_f = project(e, 0, factor_e), project(f, 0, factor_f)
-    for k in range(1, 4):
-        e, f = moved(e, around), moved(f, around)
-        partial_e = partial_e + project(e, k, factor_e)
-        partial_f = partial_f + project(f, k, factor_f)
+    partial_e = partial_f = 0.0
+    for k in range(4):
+        partial_e = partial_e + project(e_ring[k], k, factor_e)
+        partial_f = partial_f + project(f_ring[k], k, factor_f)
     order = after(jnp.stack([yl, yl ^ 2, yl ^ 1, yl ^ 3]), f_two)
     ring = (x + jnp.arange(4, dtype=jnp.int32)) % 4
-    slices = column_slices(out_next, order, ring)
+    slices = column_slices(ahead, order, ring, out_weight.shape[1])
     sends = [partial[columns:].astype(bf16) for partial in (partial_e, partial_f)]
     sends[0], slices = lax.optimization_barrier((sends[0], slices))
     out_own = [slices[0]]
@@ -328,15 +332,16 @@
     joined, other = [], []
     head = columns // 3
     for partial, send in zip((partial_e, partial_f), sends):
-        came = moved(send, other_seq)
+        came = after(moved(send, other_seq), (other, sends[1]))
         joined.append((partial[:columns] + came.astype(f32)).astype(bf16))
         other.append(moved(joined[-1][head:], other_core))
 
-    flag = after((first == seq).astype(jnp.int32).reshape(1), (out_own, residual))
+    flag = after((first == seq).astype(jnp.int32).reshape(1), out_own)
     out_own = stacked_rows(*out_own)
     out_cols = out_own, moved(out_own, other_core)
     sent, kept = attention(flag, joined, other, bias)
     came, kept = moved_on(sent, other_seq), moved_on(kept, same)
+    residual = moved_on(after(item, sent), same)
 
     heads = jnp.concatenate(
         [jnp.where(seq == 0, kept, came), jnp.where(seq == 0, came, kept)], axis=0

time: 254 us -> 271 us (1.067)
  waiting for transfers between devices: 61.5 us -> 85.1 us
  other arithmetic: 14 us -> 8.69 us
    ppermute x33, waiting for transfers between devices: 61.5 us -> 85.1 us  [moved(): return lax.ppermute(value, PLANE, pairs_of(where))]
  transfers between devices with their start and end apart: 37 -> 37, of which waited for: 15 -> 17; matrix products, arithmetic and copies ran while one was open for 10% -> 8% of each run, Pallas kernels for 5% -> 5%
where the time goes in v7:
time: 271 us; the launch traced here: 270 us
  starting transfers between devices  135 us (50%)
  waiting for transfers between devices  85.1 us (31%)
  Pallas kernels  20 us (7%)
  matrix products  12.8 us (5%)
  other arithmetic  8.69 us (3%)
  local copies, waits for them, and re-layouts  6.88 us (3%)
    ppermute x33, starting transfers between devices, moved(): return lax.ppermute(value, PLANE, pairs_of(where))  117 us
    ppermute x33, waiting for transfers between devices, moved(): return lax.ppermute(value, PLANE, pairs_of(where))  85.1 us
    ppermute x4, starting transfers between devices, moved_on(): return lax.ppermute(value, ('section', *PLANE), pairs)  17.8 us
    dot_general x8, matrix products, project(): return jnp.dot(weights[k], normed, preferred_element_type=f32)  10.2 us
    pallas_call x4, Pallas kernels, stacked_rows(): pl.pallas_call(rows_kernel, in_specs=[vmem] * len(parts), out_specs=vmem,...  8.21 us
    pallas_call x1, Pallas kernels, attention(): pl.pallas_call(lambda *refs: attention_kernel(1.0 / math.sqrt(size), per,...  7.56 us
  transfers between devices with their start and end apart: 37, of which 17 were waited for; matrix products, arithmetic and copies ran while one was open for 8% of the time, Pallas kernels for 5%

profile of v7, /device:TPU:1, one launch (start us, length us, event | category | flops | bytes accessed | tf_op | source)
XLA Modules:
  0.0 269.6 jit_solution(3406944708445698850)
XLA Ops:
  1.7 8.8 %collective-permute-start.4 = (bf16[160,512]{1,0:T(8,128)(2,1)S(1)}, bf16[160,512]{1,0:T(8,128)(2,1)S(1)}, u32[]{:S(2)}, u32[]{:S(2)}) collective-permute-start(bf16[160,512]{1,0:T(8,128)(2,1)S(1)} %get-tuple-element.83), channel_id=1, source_target_pairs={{0,2},{1,34},{2,0},{3,32},{4,6},{5,38},{6,4},{7,36},{8,10},{9,42},... | collective-permute-start | bytes 491528 | tf_op jit(solution)/shard_map/ppermute | solution.py:33
  16.2 9.1 %collective-permute-start.1 = (f32[2,512]{1,0:T(2,128)S(1)}, f32[2,512]{1,0:T(2,128)S(1)}, u32[]{:S(2)}, u32[]{:S(2)}) collective-permute-start(f32[2,512]{1,0:T(2,128)S(1)} %pad_maximum_fusion.19), channel_id=1, source_target_pairs={{0,1},{1,0},{2,3},{3,2},{4,5},{5,4},{6,7},{7,6},{8,9},{9,8},{10,11... | collective-permute-start | bytes 12296 | tf_op jit(solution)/shard_map/ppermute | solution.py:33
  26.8 3.1 %collective-permute-start.5 = (f32[18,512]{1,0:T(8,128)S(1)}, f32[18,512]{1,0:T(8,128)S(1)}, u32[]{:S(2)}, u32[]{:S(2)}) collective-permute-start(f32[18,512]{1,0:T(8,128)S(1)} %pad_maximum_fusion.18), channel_id=1, source_target_pairs={{0,4},{1,5},{2,6},{3,7},{4,0},{5,1},{6,2},{7,3},{8,12},{9,13},{10,... | collective-permute-start | bytes 110600 | tf_op jit(solution)/shard_map/ppermute | solution.py:33
  29.9 3.4 %collective-permute-start.2 = (bf16[2560,384]{1,0:T(8,128)(2,1)}, bf16[2560,384]{1,0:T(8,128)(2,1)}, u32[]{:S(2)}, u32[]{:S(2)}) collective-permute-start(bf16[2560,384]{1,0:T(8,128)(2,1)} %bitcast.70), channel_id=1, source_target_pairs={{0,2},{1,3},{2,0},{3,1},{4,6},{5,7},{6,4},{7,5},{8,10},{9,11},{10,... | collective-permute-start | bytes 5898248 | tf_op jit(solution)/shard_map/ppermute | solution.py:33
  38.8 5.2 %collective-permute-start.8 = (bf16[320,512]{1,0:T(8,128)(2,1)}, bf16[320,512]{1,0:T(8,128)(2,1)S(1)}, u32[]{:S(2)}, u32[]{:S(2)}) collective-permute-start(bf16[320,512]{1,0:T(8,128)(2,1)} %stacked_rows.4.refs_0_), channel_id=1, source_target_pairs={{0,32},{1,33},{2,34},{3,35},{4,36},{5,37},{6,38},{7,39},{8,40},{9,... | collective-permute-start | bytes 983048 | tf_op jit(solution)/shard_map/ppermute | solution.py:33
  44.1 4.3 %collective-permute-start.7 = (f32[18,512]{1,0:T(8,128)S(1)}, f32[18,512]{1,0:T(8,128)S(1)}, u32[]{:S(2)}, u32[]{:S(2)}) collective-permute-start(f32[18,512]{1,0:T(8,128)S(1)} %fusion.71), channel_id=1, source_target_pairs={{0,8},{1,9},{2,10},{3,11},{4,12},{5,13},{6,14},{7,15},{8,0},{9,1},... | collective-permute-start | bytes 110600 | tf_op jit(solution)/shard_map/ppermute | solution.py:33
  53.0 6.2 %collective-permute-done.8.refs_0_ = bf16[320,512]{1,0:T(8,128)(2,1)S(1)} collective-permute-done((bf16[320,512]{1,0:T(8,128)(2,1)}, bf16[320,512]{1,0:T(8,128)(2,1)S(1)}, u32[]{:S(2)}, u32[]{:S(2)}) %collective-permute-start.8) | collective-permute-done | bytes 327712 | tf_op jit(solution)/shard_map/ppermute | solution.py:33
  61.2 3.7 %collective-permute-start.11 = (bf16[640,512]{1,0:T(8,128)(2,1)}, bf16[640,512]{1,0:T(8,128)(2,1)}, u32[]{:S(2)}, u32[]{:S(2)}) collective-permute-start(bf16[640,512]{1,0:T(8,128)(2,1)} %stacked_rows.5), channel_id=1, source_target_pairs={{0,4},{1,5},{2,14},{3,15},{4,8},{5,9},{6,2},{7,3},{8,12},{9,13},{1... | collective-permute-start | bytes 1966088 | tf_op jit(solution)/shard_map/ppermute | solution.py:33
  67.7 3.4 %collective-permute-start.9 = (f32[18,512]{1,0:T(8,128)S(1)}, f32[18,512]{1,0:T(8,128)S(1)}, u32[]{:S(2)}, u32[]{:S(2)}) collective-permute-start(f32[18,512]{1,0:T(8,128)S(1)} %add.452), channel_id=1, source_target_pairs={{0,16},{1,17},{2,18},{3,19},{4,20},{5,21},{6,22},{7,23},{8,24},{9,... | collective-permute-start | bytes 110600 | tf_op jit(solution)/shard_map/ppermute | solution.py:33
  71.1 6.7 %collective-permute-done.9 = f32[18,512]{1,0:T(8,128)S(1)} collective-permute-done((f32[18,512]{1,0:T(8,128)S(1)}, f32[18,512]{1,0:T(8,128)S(1)}, u32[]{:S(2)}, u32[]{:S(2)}) %collective-permute-start.9) | collective-permute-done | bytes 36896 | tf_op jit(solution)/shard_map/ppermute | solution.py:33
  81.2 3.4 %collective-permute-done.10 = f32[18,512]{1,0:T(8,128)S(1)} collective-permute-done((f32[18,512]{1,0:T(8,128)S(1)}, f32[18,512]{1,0:T(8,128)S(1)}, u32[]{:S(2)}, u32[]{:S(2)}) %collective-permute-start.10) | collective-permute-done | bytes 36896 | tf_op jit(solution)/shard_map/ppermute | solution.py:33
  91.4 4.2 %column_slices.1 = (bf16[160,1024]{1,0:T(8,128)(2,1)}, bf16[160,1024]{1,0:T(8,128)(2,1)}, bf16[160,1024]{1,0:T(8,128)(2,1)}, bf16[160,1024]{1,0:T(8,128)(2,1)}) custom-call(s32[4]{0:T(128)} %pad_add_fusion.order_ref, s32[4]{0:T(128)} %and_select_fusion.ring_ref, bf16[160,4096]{1,0:T(8,128)(2,1)} %collective-permute-done.15.source_ref), custom_call_target="tpu_custom_call" | custom-call | bytes 2621440 | tf_op jit(solution)/shard_map/column_slices/pallas_call | solution.py:162
  95.6 3.7 %collective-permute-done.20 = bf16[640,512]{1,0:T(8,128)(2,1)} collective-permute-done((bf16[640,512]{1,0:T(8,128)(2,1)}, bf16[640,512]{1,0:T(8,128)(2,1)}, u32[]{:S(2)}, u32[]{:S(2)}) %collective-permute-start.20) | collective-permute-done | bytes 655392 | tf_op jit(solution)/shard_map/ppermute | solution.py:33
  102.2 4.2 %collective-permute-done.12 = bf16[640,512]{1,0:T(8,128)(2,1)} collective-permute-done((bf16[640,512]{1,0:T(8,128)(2,1)}, bf16[640,512]{1,0:T(8,128)(2,1)}, u32[]{:S(2)}, u32[]{:S(2)}) %collective-permute-start.12) | collective-permute-done | bytes 655392 | tf_op jit(solution)/shard_map/ppermute | solution.py:33
  123.3 6.5 %collective-permute-start.19 = (bf16[384,512]{1,0:T(8,128)(2,1)S(1)}, bf16[384,512]{1,0:T(8,128)(2,1)S(1)}, u32[]{:S(2)}, u32[]{:S(2)}) collective-permute-start(bf16[384,512]{1,0:T(8,128)(2,1)S(1)} %slice.223), channel_id=1, source_target_pairs={{0,1},{1,0},{2,3},{3,2},{4,5},{5,4},{6,7},{7,6},{8,9},{9,8},{10,11... | collective-permute-start | bytes 1179656 | tf_op jit(solution)/shard_map/ppermute | solution.py:33
  132.9 6.5 %collective-permute-start.23 = (bf16[384,512]{1,0:T(8,128)(2,1)S(1)}, bf16[384,512]{1,0:T(8,128)(2,1)S(1)}, u32[]{:S(2)}, u32[]{:S(2)}) collective-permute-start(bf16[384,512]{1,0:T(8,128)(2,1)S(1)} %slice.222), channel_id=1, source_target_pairs={{0,1},{1,0},{2,3},{3,2},{4,5},{5,4},{6,7},{7,6},{8,9},{9,8},{10,11... | collective-permute-start | bytes 1179656 | tf_op jit(solution)/shard_map/ppermute | solution.py:33
  139.4 16.7 %collective-permute-done.19 = bf16[384,512]{1,0:T(8,128)(2,1)S(1)} collective-permute-done((bf16[384,512]{1,0:T(8,128)(2,1)S(1)}, bf16[384,512]{1,0:T(8,128)(2,1)S(1)}, u32[]{:S(2)}, u32[]{:S(2)}) %collective-permute-start.19) | collective-permute-done | bytes 393248 | tf_op jit(solution)/shard_map/ppermute | solution.py:33
  157.0 4.2 %collective-permute-start.24 = (bf16[256,512]{1,0:T(8,128)(2,1)}, bf16[256,512]{1,0:T(8,128)(2,1)}, u32[]{:S(2)}, u32[]{:S(2)}) collective-permute-start(bf16[256,512]{1,0:T(8,128)(2,1)} %slice.159), channel_id=1, source_target_pairs={{0,2},{1,3},{2,0},{3,1},{4,6},{5,7},{6,4},{7,5},{8,10},{9,11},{10,... | collective-permute-start | bytes 786440 | tf_op jit(solution)/shard_map/ppermute | solution.py:33
  161.7 3.4 %collective-permute-start.16 = (bf16[160,1024]{1,0:T(8,128)(2,1)}, bf16[160,1024]{1,0:T(8,128)(2,1)S(1)}, u32[]{:S(2)}, u32[]{:S(2)}) collective-permute-start(bf16[160,1024]{1,0:T(8,128)(2,1)} %get-tuple-element.38), channel_id=1, source_target_pairs={{0,4},{1,5},{2,6},{3,7},{4,8},{5,9},{6,10},{7,11},{8,12},{9,13},{1... | collective-permute-start | bytes 983048 | tf_op jit(solution)/shard_map/ppermute | solution.py:33
  167.9 4.0 %collective-permute-start.18 = (bf16[160,1024]{1,0:T(8,128)(2,1)}, bf16[160,1024]{1,0:T(8,128)(2,1)}, u32[]{:S(2)}, u32[]{:S(2)}) collective-permute-start(bf16[160,1024]{1,0:T(8,128)(2,1)} %get-tuple-element.40), channel_id=1, source_target_pairs={{0,12},{1,13},{2,14},{3,15},{4,0},{5,1},{6,2},{7,3},{8,4},{9,5},{1... | collective-permute-start | bytes 983048 | tf_op jit(solution)/shard_map/ppermute | solution.py:33
  176.2 5.2 %collective-permute-done.17.refs_2_ = bf16[160,1024]{1,0:T(8,128)(2,1)} collective-permute-done((bf16[160,1024]{1,0:T(8,128)(2,1)}, bf16[160,1024]{1,0:T(8,128)(2,1)}, u32[]{:S(2)}, u32[]{:S(2)}) %collective-permute-start.17) | collective-permute-done | bytes 327712 | tf_op jit(solution)/shard_map/ppermute | solution.py:33
  184.4 7.6 %attention.1 = (bf16[128,512]{1,0:T(8,128)(2,1)}, bf16[128,512]{1,0:T(8,128)(2,1)}) custom-call(s32[1]{0:T(128)} %bitcast.3.refs_0_, bf16[384,512]{1,0:T(8,128)(2,1)} %copy-done.2, bf16[384,512]{1,0:T(8,128)(2,1)} %copy-done.3, bf16[256,512]{1,0:T(8,128)(2,1)} %collective-permute-done.24.refs_3_, bf16[256,512]{1,0:T(8,128)(2,1)} %copy-done.14, ...), custom_call_target="tpu_custom_call" | custom-call | flops 1073741824 | bytes 786432 | tf_op jit(solution)/shard_map/attention/pallas_call | solution.py:127
  192.0 4.0 %collective-permute-start.27 = (bf16[128,512]{1,0:T(8,128)(2,1)}, bf16[128,512]{1,0:T(8,128)(2,1)S(1)}, u32[]{:S(2)}, u32[]{:S(2)}) collective-permute-start(bf16[128,512]{1,0:T(8,128)(2,1)} %get-tuple-element.48), channel_id=1, source_target_pairs={{0,64},{1,65},{2,66},{3,67},{4,68},{5,69},{6,70},{7,71},{8,72},{9,... | collective-permute-start | bytes 393224 | tf_op jit(solution)/shard_map/ppermute | solution.py:43
  196.0 6.7 %collective-permute-start.28 = (bf16[128,512]{1,0:T(8,128)(2,1)}, bf16[128,512]{1,0:T(8,128)(2,1)S(1)}, u32[]{:S(2)}, u32[]{:S(2)}) collective-permute-start(bf16[128,512]{1,0:T(8,128)(2,1)} %get-tuple-element.46), channel_id=1, source_target_pairs={{0,65},{1,64},{2,67},{3,66},{4,69},{5,68},{6,71},{7,70},{8,73},{9,... | collective-permute-start | bytes 393224 | tf_op jit(solution)/shard_map/ppermute | solution.py:43
  205.2 3.7 %collective-permute-start.32 = (bf16[640,1024]{1,0:T(8,128)(2,1)}, bf16[640,1024]{1,0:T(8,128)(2,1)S(1)}, u32[]{:S(2)}, u32[]{:S(2)}) collective-permute-start(bf16[640,1024]{1,0:T(8,128)(2,1)} %stacked_rows.7), channel_id=1, source_target_pairs={{0,2},{1,3},{2,0},{3,1},{4,6},{5,7},{6,4},{7,5},{8,10},{9,11},{10,... | collective-permute-start | bytes 3932168 | tf_op jit(solution)/shard_map/ppermute | solution.py:33
  210.9 5.2 %collective-permute-start.26 = (bf16[320,512]{1,0:T(8,128)(2,1)S(1)}, bf16[320,512]{1,0:T(8,128)(2,1)S(1)}, u32[]{:S(2)}, u32[]{:S(2)}) collective-permute-start(bf16[320,512]{1,0:T(8,128)(2,1)S(1)} %pad_maximum_fusion.5), channel_id=1, source_target_pairs={{0,64},{1,65},{2,66},{3,67},{4,68},{5,69},{6,70},{7,71},{8,72},{9,... | collective-permute-start | bytes 983048 | tf_op jit(solution)/shard_map/ppermute | solution.py:43
  219.3 12.8 %collective-permute-done.29 = bf16[256,512]{1,0:T(8,128)(2,1)S(1)} collective-permute-done((bf16[256,512]{1,0:T(8,128)(2,1)S(1)}, bf16[256,512]{1,0:T(8,128)(2,1)S(1)}, u32[]{:S(2)}, u32[]{:S(2)}) %collective-permute-start.29) | collective-permute-done | bytes 262176 | tf_op jit(solution)/shard_map/ppermute | solution.py:33
  235.8 6.3 %collective-permute-done.31 = bf16[256,512]{1,0:T(8,128)(2,1)S(1)} collective-permute-done((bf16[256,512]{1,0:T(8,128)(2,1)S(1)}, bf16[256,512]{1,0:T(8,128)(2,1)S(1)}, u32[]{:S(2)}, u32[]{:S(2)}) %collective-permute-start.31) | collective-permute-done | bytes 262176 | tf_op jit(solution)/shard_map/ppermute | solution.py:33
  242.8 3.7 %collective-permute-start.35 = (bf16[320,512]{1,0:T(8,128)(2,1)S(1)}, bf16[320,512]{1,0:T(8,128)(2,1)S(1)}, u32[]{:S(2)}, u32[]{:S(2)}) collective-permute-start(bf16[320,512]{1,0:T(8,128)(2,1)S(1)} %pad_maximum_fusion.8), channel_id=1, source_target_pairs={{0,4},{1,5},{2,6},{3,7},{4,8},{5,9},{6,10},{7,11},{8,12},{9,13},{1... | collective-permute-start | bytes 983048 | tf_op jit(solution)/shard_map/ppermute | solution.py:33
  246.6 3.7 %collective-permute-start.34 = (bf16[320,512]{1,0:T(8,128)(2,1)S(1)}, bf16[320,512]{1,0:T(8,128)(2,1)S(1)}, u32[]{:S(2)}, u32[]{:S(2)}) collective-permute-start(bf16[320,512]{1,0:T(8,128)(2,1)S(1)} %pad_maximum_fusion.7), channel_id=1, source_target_pairs={{0,8},{1,9},{2,10},{3,11},{4,12},{5,13},{6,14},{7,15},{8,0},{9,1},... | collective-permute-start | bytes 983048 | tf_op jit(solution)/shard_map/ppermute | solution.py:33
  253.2 7.8 %collective-permute-done.34 = bf16[320,512]{1,0:T(8,128)(2,1)S(1)} collective-permute-done((bf16[320,512]{1,0:T(8,128)(2,1)S(1)}, bf16[320,512]{1,0:T(8,128)(2,1)S(1)}, u32[]{:S(2)}, u32[]{:S(2)}) %collective-permute-start.34) | collective-permute-done | bytes 327712 | tf_op jit(solution)/shard_map/ppermute | solution.py:33
  263.2 4.6 %collective-permute-start.36 = (bf16[160,512]{1,0:T(8,128)(2,1)S(1)}, bf16[160,512]{1,0:T(8,128)(2,1)S(1)}, u32[]{:S(2)}, u32[]{:S(2)}) collective-permute-start(bf16[160,512]{1,0:T(8,128)(2,1)S(1)} %slice.179), channel_id=1, source_target_pairs={{0,2},{1,3},{2,0},{3,1},{4,6},{5,7},{6,4},{7,5},{8,10},{9,11},{10,... | collective-permute-start | bytes 491528 | tf_op jit(solution)/shard_map/ppermute | solution.py:33
  (168 shorter events, 86.8 us)
Async XLA Ops:
  1.0 32.4 %collective-permute-start.3 = (bf16[160,512]{1,0:T(8,128)(2,1)S(1)}, bf16[160,512]{1,0:T(8,128)(2,1)S(1)}, u32[]{:S(2)}, u32[]{:S(2)}) collective-permute-start(bf16[160,512]{1,0:T(8,128)(2,1)S(1)} %get-tuple-element.84), channel_id=1, source_target_pairs={{0,0},{1,32},{2,2},{3,34},{4,4},{5,36},{6,6},{7,38},{8,8},{9,40},{... | collective-permute-start | bytes 491528 | tf_op jit(solution)/shard_map/ppermute | solution.py:33
  1.7 31.7 %collective-permute-start.4 = (bf16[160,512]{1,0:T(8,128)(2,1)S(1)}, bf16[160,512]{1,0:T(8,128)(2,1)S(1)}, u32[]{:S(2)}, u32[]{:S(2)}) collective-permute-start(bf16[160,512]{1,0:T(8,128)(2,1)S(1)} %get-tuple-element.83), channel_id=1, source_target_pairs={{0,2},{1,34},{2,0},{3,32},{4,6},{5,38},{6,4},{7,36},{8,10},{9,42},... | collective-permute-start | bytes 491528 | tf_op jit(solution)/shard_map/ppermute | solution.py:33
  13.1 78.3 %collective-permute-start.15 = (bf16[160,4096]{1,0:T(8,128)(2,1)}, bf16[160,4096]{1,0:T(8,128)(2,1)}, u32[]{:S(2)}, u32[]{:S(2)}) collective-permute-start(bf16[160,4096]{1,0:T(8,128)(2,1)} %bitcast.86), channel_id=1, source_target_pairs={{0,64},{1,65},{2,66},{3,67},{4,68},{5,69},{6,70},{7,71},{8,72},{9,... | collective-permute-start | bytes 3932168 | tf_op jit(solution)/shard_map/ppermute | solution.py:43
  16.2 10.5 %collective-permute-start.1 = (f32[2,512]{1,0:T(2,128)S(1)}, f32[2,512]{1,0:T(2,128)S(1)}, u32[]{:S(2)}, u32[]{:S(2)}) collective-permute-start(f32[2,512]{1,0:T(2,128)S(1)} %pad_maximum_fusion.19), channel_id=1, source_target_pairs={{0,1},{1,0},{2,3},{3,2},{4,5},{5,4},{6,7},{7,6},{8,9},{9,8},{10,11... | collective-permute-start | bytes 12296 | tf_op jit(solution)/shard_map/ppermute | solution.py:33
  26.8 9.7 %collective-permute-start.5 = (f32[18,512]{1,0:T(8,128)S(1)}, f32[18,512]{1,0:T(8,128)S(1)}, u32[]{:S(2)}, u32[]{:S(2)}) collective-permute-start(f32[18,512]{1,0:T(8,128)S(1)} %pad_maximum_fusion.18), channel_id=1, source_target_pairs={{0,4},{1,5},{2,6},{3,7},{4,0},{5,1},{6,2},{7,3},{8,12},{9,13},{10,... | collective-permute-start | bytes 110600 | tf_op jit(solution)/shard_map/ppermute | solution.py:33
  29.9 79.3 %collective-permute-start.2 = (bf16[2560,384]{1,0:T(8,128)(2,1)}, bf16[2560,384]{1,0:T(8,128)(2,1)}, u32[]{:S(2)}, u32[]{:S(2)}) collective-permute-start(bf16[2560,384]{1,0:T(8,128)(2,1)} %bitcast.70), channel_id=1, source_target_pairs={{0,2},{1,3},{2,0},{3,1},{4,6},{5,7},{6,4},{7,5},{8,10},{9,11},{10,... | collective-permute-start | bytes 5898248 | tf_op jit(solution)/shard_map/ppermute | solution.py:33
  36.5 16.5 %collective-permute-start.6 = (bf16[320,512]{1,0:T(8,128)(2,1)}, bf16[320,512]{1,0:T(8,128)(2,1)S(1)}, u32[]{:S(2)}, u32[]{:S(2)}) collective-permute-start(bf16[320,512]{1,0:T(8,128)(2,1)} %stacked_rows.4.refs_0_), channel_id=1, source_target_pairs={{0,16},{1,17},{2,18},{3,19},{4,20},{5,21},{6,22},{7,23},{8,24},{9,... | collective-permute-start | bytes 983048 | tf_op jit(solution)/shard_map/ppermute | solution.py:33
  38.8 20.4 %collective-permute-start.8 = (bf16[320,512]{1,0:T(8,128)(2,1)}, bf16[320,512]{1,0:T(8,128)(2,1)S(1)}, u32[]{:S(2)}, u32[]{:S(2)}) collective-permute-start(bf16[320,512]{1,0:T(8,128)(2,1)} %stacked_rows.4.refs_0_), channel_id=1, source_target_pairs={{0,32},{1,33},{2,34},{3,35},{4,36},{5,37},{6,38},{7,39},{8,40},{9,... | collective-permute-start | bytes 983048 | tf_op jit(solution)/shard_map/ppermute | solution.py:33
  61.2 26.2 %collective-permute-start.11 = (bf16[640,512]{1,0:T(8,128)(2,1)}, bf16[640,512]{1,0:T(8,128)(2,1)}, u32[]{:S(2)}, u32[]{:S(2)}) collective-permute-start(bf16[640,512]{1,0:T(8,128)(2,1)} %stacked_rows.5), channel_id=1, source_target_pairs={{0,4},{1,5},{2,14},{3,15},{4,8},{5,9},{6,2},{7,3},{8,12},{9,13},{1... | collective-permute-start | bytes 1966088 | tf_op jit(solution)/shard_map/ppermute | solution.py:33
  65.2 19.5 %collective-permute-start.14 = (bf16[320,512]{1,0:T(8,128)(2,1)S(1)}, bf16[320,512]{1,0:T(8,128)(2,1)S(1)}, u32[]{:S(2)}, u32[]{:S(2)}) collective-permute-start(bf16[320,512]{1,0:T(8,128)(2,1)S(1)} %collective-permute-done.8.refs_0_), channel_id=1, source_target_pairs={{0,16},{1,17},{2,18},{3,19},{4,20},{5,21},{6,22},{7,23},{8,24},{9,... | collective-permute-start | bytes 983048 | tf_op jit(solution)/shard_map/ppermute | solution.py:33
  67.7 10.1 %collective-permute-start.9 = (f32[18,512]{1,0:T(8,128)S(1)}, f32[18,512]{1,0:T(8,128)S(1)}, u32[]{:S(2)}, u32[]{:S(2)}) collective-permute-start(f32[18,512]{1,0:T(8,128)S(1)} %add.452), channel_id=1, source_target_pairs={{0,16},{1,17},{2,18},{3,19},{4,20},{5,21},{6,22},{7,23},{8,24},{9,... | collective-permute-start | bytes 110600 | tf_op jit(solution)/shard_map/ppermute | solution.py:33
  87.4 11.9 %collective-permute-start.20 = (bf16[640,512]{1,0:T(8,128)(2,1)}, bf16[640,512]{1,0:T(8,128)(2,1)}, u32[]{:S(2)}, u32[]{:S(2)}) collective-permute-start(bf16[640,512]{1,0:T(8,128)(2,1)} %stacked_rows.6), channel_id=1, source_target_pairs={{0,4},{1,5},{2,14},{3,15},{4,8},{5,9},{6,2},{7,3},{8,12},{9,13},{1... | collective-permute-start | bytes 1966088 | tf_op jit(solution)/shard_map/ppermute | solution.py:33
  89.3 17.0 %collective-permute-start.12 = (bf16[640,512]{1,0:T(8,128)(2,1)}, bf16[640,512]{1,0:T(8,128)(2,1)}, u32[]{:S(2)}, u32[]{:S(2)}) collective-permute-start(bf16[640,512]{1,0:T(8,128)(2,1)} %collective-permute-done.11), channel_id=1, source_target_pairs={{0,4},{1,5},{2,14},{3,15},{4,8},{5,9},{6,2},{7,3},{8,12},{9,13},{1... | collective-permute-start | bytes 1966088 | tf_op jit(solution)/shard_map/ppermute | solution.py:33
  99.3 21.0 %collective-permute-start.21 = (bf16[640,512]{1,0:T(8,128)(2,1)}, bf16[640,512]{1,0:T(8,128)(2,1)S(1)}, u32[]{:S(2)}, u32[]{:S(2)}) collective-permute-start(bf16[640,512]{1,0:T(8,128)(2,1)} %collective-permute-done.20), channel_id=1, source_target_pairs={{0,4},{1,5},{2,14},{3,15},{4,8},{5,9},{6,2},{7,3},{8,12},{9,13},{1... | collective-permute-start | bytes 1966088 | tf_op jit(solution)/shard_map/ppermute | solution.py:33
  106.3 15.9 %collective-permute-start.13 = (bf16[640,512]{1,0:T(8,128)(2,1)}, bf16[640,512]{1,0:T(8,128)(2,1)S(1)}, u32[]{:S(2)}, u32[]{:S(2)}) collective-permute-start(bf16[640,512]{1,0:T(8,128)(2,1)} %collective-permute-done.12), channel_id=1, source_target_pairs={{0,4},{1,5},{2,14},{3,15},{4,8},{5,9},{6,2},{7,3},{8,12},{9,13},{1... | collective-permute-start | bytes 1966088 | tf_op jit(solution)/shard_map/ppermute | solution.py:33
  120.3 11.6 %collective-permute-start.22 = (bf16[640,512]{1,0:T(8,128)(2,1)S(1)}, bf16[640,512]{1,0:T(8,128)(2,1)S(1)}, u32[]{:S(2)}, u32[]{:S(2)}) collective-permute-start(bf16[640,512]{1,0:T(8,128)(2,1)S(1)} %collective-permute-done.21), channel_id=1, source_target_pairs={{0,4},{1,5},{2,14},{3,15},{4,8},{5,9},{6,2},{7,3},{8,12},{9,13},{1... | collective-permute-start | bytes 1966088 | tf_op jit(solution)/shard_map/ppermute | solution.py:33
  123.3 32.8 %collective-permute-start.19 = (bf16[384,512]{1,0:T(8,128)(2,1)S(1)}, bf16[384,512]{1,0:T(8,128)(2,1)S(1)}, u32[]{:S(2)}, u32[]{:S(2)}) collective-permute-start(bf16[384,512]{1,0:T(8,128)(2,1)S(1)} %slice.223), channel_id=1, source_target_pairs={{0,1},{1,0},{2,3},{3,2},{4,5},{5,4},{6,7},{7,6},{8,9},{9,8},{10,11... | collective-permute-start | bytes 1179656 | tf_op jit(solution)/shard_map/ppermute | solution.py:33
  132.9 39.0 %collective-permute-start.23 = (bf16[384,512]{1,0:T(8,128)(2,1)S(1)}, bf16[384,512]{1,0:T(8,128)(2,1)S(1)}, u32[]{:S(2)}, u32[]{:S(2)}) collective-permute-start(bf16[384,512]{1,0:T(8,128)(2,1)S(1)} %slice.222), channel_id=1, source_target_pairs={{0,1},{1,0},{2,3},{3,2},{4,5},{5,4},{6,7},{7,6},{8,9},{9,8},{10,11... | collective-permute-start | bytes 1179656 | tf_op jit(solution)/shard_map/ppermute | solution.py:33
  157.0 14.9 %collective-permute-start.24 = (bf16[256,512]{1,0:T(8,128)(2,1)}, bf16[256,512]{1,0:T(8,128)(2,1)}, u32[]{:S(2)}, u32[]{:S(2)}) collective-permute-start(bf16[256,512]{1,0:T(8,128)(2,1)} %slice.159), channel_id=1, source_target_pairs={{0,2},{1,3},{2,0},{3,1},{4,6},{5,7},{6,4},{7,5},{8,10},{9,11},{10,... | collective-permute-start | bytes 786440 | tf_op jit(solution)/shard_map/ppermute | solution.py:33
  161.7 14.5 %collective-permute-start.16 = (bf16[160,1024]{1,0:T(8,128)(2,1)}, bf16[160,1024]{1,0:T(8,128)(2,1)S(1)}, u32[]{:S(2)}, u32[]{:S(2)}) collective-permute-start(bf16[160,1024]{1,0:T(8,128)(2,1)} %get-tuple-element.38), channel_id=1, source_target_pairs={{0,4},{1,5},{2,6},{3,7},{4,8},{5,9},{6,10},{7,11},{8,12},{9,13},{1... | collective-permute-start | bytes 983048 | tf_op jit(solution)/shard_map/ppermute | solution.py:33
  165.1 16.3 %collective-permute-start.17 = (bf16[160,1024]{1,0:T(8,128)(2,1)}, bf16[160,1024]{1,0:T(8,128)(2,1)}, u32[]{:S(2)}, u32[]{:S(2)}) collective-permute-start(bf16[160,1024]{1,0:T(8,128)(2,1)} %get-tuple-element.39), channel_id=1, source_target_pairs={{0,8},{1,9},{2,10},{3,11},{4,12},{5,13},{6,14},{7,15},{8,0},{9,1},... | collective-permute-start | bytes 983048 | tf_op jit(solution)/shard_map/ppermute | solution.py:33
  167.9 15.8 %collective-permute-start.18 = (bf16[160,1024]{1,0:T(8,128)(2,1)}, bf16[160,1024]{1,0:T(8,128)(2,1)}, u32[]{:S(2)}, u32[]{:S(2)}) collective-permute-start(bf16[160,1024]{1,0:T(8,128)(2,1)} %get-tuple-element.40), channel_id=1, source_target_pairs={{0,12},{1,13},{2,14},{3,15},{4,0},{5,1},{6,2},{7,3},{8,4},{9,5},{1... | collective-permute-start | bytes 983048 | tf_op jit(solution)/shard_map/ppermute | solution.py:33
  172.1 11.6 %collective-permute-start.25 = (bf16[256,512]{1,0:T(8,128)(2,1)S(1)}, bf16[256,512]{1,0:T(8,128)(2,1)S(1)}, u32[]{:S(2)}, u32[]{:S(2)}) collective-permute-start(bf16[256,512]{1,0:T(8,128)(2,1)S(1)} %slice.160), channel_id=1, source_target_pairs={{0,2},{1,3},{2,0},{3,1},{4,6},{5,7},{6,4},{7,5},{8,10},{9,11},{10,... | collective-permute-start | bytes 786440 | tf_op jit(solution)/shard_map/ppermute | solution.py:33
  192.0 16.9 %collective-permute-start.27 = (bf16[128,512]{1,0:T(8,128)(2,1)}, bf16[128,512]{1,0:T(8,128)(2,1)S(1)}, u32[]{:S(2)}, u32[]{:S(2)}) collective-permute-start(bf16[128,512]{1,0:T(8,128)(2,1)} %get-tuple-element.48), channel_id=1, source_target_pairs={{0,64},{1,65},{2,66},{3,67},{4,68},{5,69},{6,70},{7,71},{8,72},{9,... | collective-permute-start | bytes 393224 | tf_op jit(solution)/shard_map/ppermute | solution.py:43
  196.0 12.9 %collective-permute-start.28 = (bf16[128,512]{1,0:T(8,128)(2,1)}, bf16[128,512]{1,0:T(8,128)(2,1)S(1)}, u32[]{:S(2)}, u32[]{:S(2)}) collective-permute-start(bf16[128,512]{1,0:T(8,128)(2,1)} %get-tuple-element.46), channel_id=1, source_target_pairs={{0,65},{1,64},{2,67},{3,66},{4,69},{5,68},{6,71},{7,70},{8,73},{9,... | collective-permute-start | bytes 393224 | tf_op jit(solution)/shard_map/ppermute | solution.py:43
  205.2 27.7 %collective-permute-start.32 = (bf16[640,1024]{1,0:T(8,128)(2,1)}, bf16[640,1024]{1,0:T(8,128)(2,1)S(1)}, u32[]{:S(2)}, u32[]{:S(2)}) collective-permute-start(bf16[640,1024]{1,0:T(8,128)(2,1)} %stacked_rows.7), channel_id=1, source_target_pairs={{0,2},{1,3},{2,0},{3,1},{4,6},{5,7},{6,4},{7,5},{8,10},{9,11},{10,... | collective-permute-start | bytes 3932168 | tf_op jit(solution)/shard_map/ppermute | solution.py:33
  208.9 10.0 %collective-permute-start.30 = (bf16[256,512]{1,0:T(8,128)(2,1)S(1)}, bf16[256,512]{1,0:T(8,128)(2,1)S(1)}, u32[]{:S(2)}, u32[]{:S(2)}) collective-permute-start(bf16[256,512]{1,0:T(8,128)(2,1)S(1)} %pad_maximum_fusion.9), channel_id=1, source_target_pairs={{0,16},{1,17},{2,18},{3,19},{4,20},{5,21},{6,22},{7,23},{8,24},{9,... | collective-permute-start | bytes 786440 | tf_op jit(solution)/shard_map/ppermute | solution.py:33
  210.9 42.3 %collective-permute-start.26 = (bf16[320,512]{1,0:T(8,128)(2,1)S(1)}, bf16[320,512]{1,0:T(8,128)(2,1)S(1)}, u32[]{:S(2)}, u32[]{:S(2)}) collective-permute-start(bf16[320,512]{1,0:T(8,128)(2,1)S(1)} %pad_maximum_fusion.5), channel_id=1, source_target_pairs={{0,64},{1,65},{2,66},{3,67},{4,68},{5,69},{6,70},{7,71},{8,72},{9,... | collective-permute-start | bytes 983048 | tf_op jit(solution)/shard_map/ppermute | solution.py:43
  216.1 16.0 %collective-permute-start.29 = (bf16[256,512]{1,0:T(8,128)(2,1)S(1)}, bf16[256,512]{1,0:T(8,128)(2,1)S(1)}, u32[]{:S(2)}, u32[]{:S(2)}) collective-permute-start(bf16[256,512]{1,0:T(8,128)(2,1)S(1)} %pad_maximum_fusion.9), channel_id=1, source_target_pairs={{0,32},{1,33},{2,34},{3,35},{4,36},{5,37},{6,38},{7,39},{8,40},{9,... | collective-permute-start | bytes 786440 | tf_op jit(solution)/shard_map/ppermute | solution.py:33
  242.8 10.4 %collective-permute-start.35 = (bf16[320,512]{1,0:T(8,128)(2,1)S(1)}, bf16[320,512]{1,0:T(8,128)(2,1)S(1)}, u32[]{:S(2)}, u32[]{:S(2)}) collective-permute-start(bf16[320,512]{1,0:T(8,128)(2,1)S(1)} %pad_maximum_fusion.8), channel_id=1, source_target_pairs={{0,4},{1,5},{2,6},{3,7},{4,8},{5,9},{6,10},{7,11},{8,12},{9,13},{1... | collective-permute-start | bytes 983048 | tf_op jit(solution)/shard_map/ppermute | solution.py:33
  246.6 14.4 %collective-permute-start.34 = (bf16[320,512]{1,0:T(8,128)(2,1)S(1)}, bf16[320,512]{1,0:T(8,128)(2,1)S(1)}, u32[]{:S(2)}, u32[]{:S(2)}) collective-permute-start(bf16[320,512]{1,0:T(8,128)(2,1)S(1)} %pad_maximum_fusion.7), channel_id=1, source_target_pairs={{0,8},{1,9},{2,10},{3,11},{4,12},{5,13},{6,14},{7,15},{8,0},{9,1},... | collective-permute-start | bytes 983048 | tf_op jit(solution)/shard_map/ppermute | solution.py:33
  250.3 12.6 %collective-permute-start.33 = (bf16[320,512]{1,0:T(8,128)(2,1)S(1)}, bf16[320,512]{1,0:T(8,128)(2,1)S(1)}, u32[]{:S(2)}, u32[]{:S(2)}) collective-permute-start(bf16[320,512]{1,0:T(8,128)(2,1)S(1)} %pad_maximum_fusion.6), channel_id=1, source_target_pairs={{0,12},{1,13},{2,14},{3,15},{4,0},{5,1},{6,2},{7,3},{8,4},{9,5},{1... | collective-permute-start | bytes 983048 | tf_op jit(solution)/shard_map/ppermute | solution.py:33
  (21 other events, 269.6 us)

commit v8 on v5

--- a/solution.py
+++ b/solution.py
@@ -251,7 +251,6 @@
     item = jnp.concatenate([own, beside[:part]], axis=0)
     as_float = item.astype(f32)
     squares = jnp.sum(as_float * as_float, axis=0)
-    residual = moved_on(item, same)
     random = random_blocks[0]
     numbers = jnp.pad(random.astype(f32).reshape(-1), (0, step - random.size))
     mine = jnp.stack([squares, numbers])
@@ -261,10 +260,16 @@
     table = jnp.where(slot, jnp.pad(gain, ((0, 0), (0, step - 2 * part))), 0.0)
     table = jnp.concatenate([table, mine[:1], theirs[:1]], axis=0)
     table = table + moved(table, lambda y, x, c: (y, x ^ 1, c))
-    e = after(e, table)
+    weight = after(qkv_weight[0], theirs)
+    weight_beside = moved(weight, other_core)
     f = moved(e, by_two)
-    e_two = stacked_rows(e, moved(e, pair))
+    e_two = stacked_rows(e, moved(after(e, table), pair))
     f_two = stacked_rows(f, moved(f, pair))
+    e_ring, f_ring = [e_two], [f_two]
+    for _ in range(3):
+        e_ring.append(moved(e_ring[-1], around))
+        f_ring.append(moved(f_ring[-1], around))
+    table = after(table, e_ring[1])
     for where in (lambda y, x, c: (y, x ^ 2, c), pair, by_two):
         table = table + moved(table, where)
     factors = lax.rsqrt(table[16:] / width + 1e-05)
@@ -273,8 +278,7 @@
     gains = table[:16, : 2 * part].reshape(2, 2, 4, 2 * part)
     gains = at_index(gains, seq)
 
-    weight = after(qkv_weight[0], beside)
-    beside = moved(weight, other_core)
+    beside = weight_beside
     columns = weight.shape[1]
     weight = jnp.concatenate(
         [jnp.where(core == seq, weight, beside), jnp.where(core == seq, beside, weight)], axis=1
@@ -311,12 +315,10 @@
     allowed = block_mask(query_ids, rows, global_blocks[0], key_ids)
     bias = jnp.repeat(jnp.where(allowed.T, 0.0, NEG), BLOCK, axis=1).astype(bf16)
 
-    e, f = e_two, f_two
-    partial_e, partial_f = project(e, 0, factor_e), project(f, 0, factor_f)
-    for k in range(1, 4):
-        e, f = moved(e, around), moved(f, around)
-        partial_e = partial_e + project(e, k, factor_e)
-        partial_f = partial_f + project(f, k, factor_f)
+    partial_e = partial_f = 0.0
+    for k in range(4):
+        partial_e = partial_e + project(e_ring[k], k, factor_e)
+        partial_f = partial_f + project(f_ring[k], k, factor_f)
     order = after(jnp.stack([yl, yl ^ 2, yl ^ 1, yl ^ 3]), f_two)
     ring = (x + jnp.arange(4, dtype=jnp.int32)) % 4
     slices = column_slices(out_next, order, ring)
@@ -332,7 +334,7 @@
         joined.append((partial[:columns] + came.astype(f32)).astype(bf16))
         other.append(moved(joined[-1][head:], other_core))
 
-    flag = after((first == seq).astype(jnp.int32).reshape(1), (out_own, residual))
+    flag = after((first == seq).astype(jnp.int32).reshape(1), out_own)
     out_own = stacked_rows(*out_own)
     out_cols = out_own, moved(out_own, other_core)
     sent, kept = attention(flag, joined, other, bias)
@@ -352,12 +354,17 @@
                 cols[:, p * per : (p + 1) * per], block, preferred_element_type=f32
             )
         added.append(total)
-    total = residual.astype(f32) + jnp.concatenate([half[:part] for half in added], axis=0)
+    total = jnp.concatenate([half[:part] for half in added], axis=0)
+    shares = []
     for r in range(1, 4):
         share = jnp.concatenate(
             [half[r * part : (r + 1) * part].astype(bf16) for half in added], axis=0
         )
-        total = total + moved(share, lambda y, x, c, r=r: (y, (x - r) % 4, c)).astype(f32)
+        shares.append(moved(share, lambda y, x, c, r=r: (y, (x - r) % 4, c)))
+    residual = moved_on(after(item, shares[0]), same)
+    total = residual.astype(f32) + total
+    for share in shares:
+        total = total + share.astype(f32)
     result = total.astype(bf16)
 
     own, away = result[:part], moved(result[part:], other_core)

time: 254 us -> 266 us (1.047)
  the two profiles are of different devices: /device:TPU:1 before, /device:TPU:7 now
where the time goes in v8:
time: 266 us; the launch traced here: 265 us
  starting transfers between devices  145 us (55%)
  waiting for transfers between devices  65.4 us (25%)
  Pallas kernels  19.9 us (7%)
  matrix products  13.7 us (5%)
  other arithmetic  10.7 us (4%)
  local copies, waits for them, and re-layouts  9.07 us (3%)
    ppermute x33, starting transfers between devices, moved(): return lax.ppermute(value, PLANE, pairs_of(where))  127 us
    ppermute x33, waiting for transfers between devices, moved(): return lax.ppermute(value, PLANE, pairs_of(where))  53.5 us
    ppermute x4, starting transfers between devices, moved_on(): return lax.ppermute(value, ('section', *PLANE), pairs)  17.8 us
    ppermute x4, waiting for transfers between devices, moved_on(): return lax.ppermute(value, ('section', *PLANE), pairs)  11.9 us
    dot_general x8, matrix products, project(): return jnp.dot(weights[k], normed, preferred_element_type=f32)  10.1 us
    pallas_call x4, Pallas kernels, stacked_rows(): pl.pallas_call(rows_kernel, in_specs=[vmem] * len(parts), out_specs=vmem,...  8.11 us
    pallas_call x1, Pallas kernels, attention(): pl.pallas_call(lambda *refs: attention_kernel(1.0 / math.sqrt(size), per,...  7.57 us
  transfers between devices with their start and end apart: 37, of which 19 were waited for; matrix products, arithmetic and copies ran while one was open for 9% of the time, Pallas kernels for 5%

profile of v8, /device:TPU:7, one launch (start us, length us, event | category | flops | bytes accessed | tf_op | source)
XLA Modules:
  0.0 264.6 jit_solution(14167895586977050353)
XLA Ops:
  1.9 2.6 collective-permute-start
  7.1 4.0 %collective-permute-start.15 = (bf16[160,4096]{1,0:T(8,128)(2,1)}, bf16[160,4096]{1,0:T(8,128)(2,1)}, u32[]{:S(2)}, u32[]{:S(2)}) collective-permute-start(bf16[160,4096]{1,0:T(8,128)(2,1)} %bitcast.86), channel_id=1, source_target_pairs={{0,64},{1,65},{2,66},{3,67},{4,68},{5,69},{6,70},{7,71},{8,72},{9,... | collective-permute-start | bytes 3932168 | tf_op jit(solution)/shard_map/ppermute | solution.py:43
  12.1 12.1 %collective-permute-start.1 = (f32[2,512]{1,0:T(2,128)S(1)}, f32[2,512]{1,0:T(2,128)S(1)}, u32[]{:S(2)}, u32[]{:S(2)}) collective-permute-start(f32[2,512]{1,0:T(2,128)S(1)} %pad_maximum_fusion.19), channel_id=1, source_target_pairs={{0,1},{1,0},{2,3},{3,2},{4,5},{5,4},{6,7},{7,6},{8,9},{9,8},{10,11... | collective-permute-start | bytes 12296 | tf_op jit(solution)/shard_map/ppermute | solution.py:33
  31.3 3.7 %collective-permute-start.13 = (bf16[320,512]{1,0:T(8,128)(2,1)}, bf16[320,512]{1,0:T(8,128)(2,1)S(1)}, u32[]{:S(2)}, u32[]{:S(2)}) collective-permute-start(bf16[320,512]{1,0:T(8,128)(2,1)} %stacked_rows.4.refs_0_), channel_id=1, source_target_pairs={{0,32},{1,33},{2,34},{3,35},{4,36},{5,37},{6,38},{7,39},{8,40},{9,... | collective-permute-start | bytes 983048 | tf_op jit(solution)/shard_map/ppermute | solution.py:33
  35.0 4.6 %collective-permute-start.2 = (bf16[2560,384]{1,0:T(8,128)(2,1)S(1)}, bf16[2560,384]{1,0:T(8,128)(2,1)}, u32[]{:S(2)}, u32[]{:S(2)}) collective-permute-start(bf16[2560,384]{1,0:T(8,128)(2,1)S(1)} %bitcast.70), channel_id=1, source_target_pairs={{0,2},{1,3},{2,0},{3,1},{4,6},{5,7},{6,4},{7,5},{8,10},{9,11},{10,... | collective-permute-start | bytes 5898248 | tf_op jit(solution)/shard_map/ppermute | solution.py:33
  39.7 3.2 %collective-permute-start.6 = (bf16[320,512]{1,0:T(8,128)(2,1)}, bf16[320,512]{1,0:T(8,128)(2,1)S(1)}, u32[]{:S(2)}, u32[]{:S(2)}) collective-permute-start(bf16[320,512]{1,0:T(8,128)(2,1)} %stacked_rows.4.refs_0_), channel_id=1, source_target_pairs={{0,16},{1,17},{2,18},{3,19},{4,20},{5,21},{6,22},{7,23},{8,24},{9,... | collective-permute-start | bytes 983048 | tf_op jit(solution)/shard_map/ppermute | solution.py:33
  42.9 7.6 %collective-permute-done.13.refs_0_ = bf16[320,512]{1,0:T(8,128)(2,1)S(1)} collective-permute-done((bf16[320,512]{1,0:T(8,128)(2,1)}, bf16[320,512]{1,0:T(8,128)(2,1)S(1)}, u32[]{:S(2)}, u32[]{:S(2)}) %collective-permute-start.13) | collective-permute-done | bytes 327712 | tf_op jit(solution)/shard_map/ppermute | solution.py:33
  53.0 4.9 %collective-permute-done.6.refs_1_ = bf16[320,512]{1,0:T(8,128)(2,1)S(1)} collective-permute-done((bf16[320,512]{1,0:T(8,128)(2,1)}, bf16[320,512]{1,0:T(8,128)(2,1)S(1)}, u32[]{:S(2)}, u32[]{:S(2)}) %collective-permute-start.6) | collective-permute-done | bytes 327712 | tf_op jit(solution)/shard_map/ppermute | solution.py:33
  60.6 2.8 %collective-permute-start.7 = (bf16[640,512]{1,0:T(8,128)(2,1)}, bf16[640,512]{1,0:T(8,128)(2,1)}, u32[]{:S(2)}, u32[]{:S(2)}) collective-permute-start(bf16[640,512]{1,0:T(8,128)(2,1)} %stacked_rows.5), channel_id=1, source_target_pairs={{0,4},{1,5},{2,14},{3,15},{4,8},{5,9},{6,2},{7,3},{8,12},{9,13},{1... | collective-permute-start | bytes 1966088 | tf_op jit(solution)/shard_map/ppermute | solution.py:33
  67.6 2.8 %collective-permute-start.20 = (bf16[640,512]{1,0:T(8,128)(2,1)}, bf16[640,512]{1,0:T(8,128)(2,1)}, u32[]{:S(2)}, u32[]{:S(2)}) collective-permute-start(bf16[640,512]{1,0:T(8,128)(2,1)} %stacked_rows.6), channel_id=1, source_target_pairs={{0,4},{1,5},{2,14},{3,15},{4,8},{5,9},{6,2},{7,3},{8,12},{9,13},{1... | collective-permute-start | bytes 1966088 | tf_op jit(solution)/shard_map/ppermute | solution.py:33
  75.8 4.6 %collective-permute-done.8 = f32[18,512]{1,0:T(8,128)S(1)} collective-permute-done((f32[18,512]{1,0:T(8,128)S(1)}, f32[18,512]{1,0:T(8,128)S(1)}, u32[]{:S(2)}, u32[]{:S(2)}) %collective-permute-start.8) | collective-permute-done | bytes 36896 | tf_op jit(solution)/shard_map/ppermute | solution.py:33
  89.7 4.2 %column_slices.1 = (bf16[160,1024]{1,0:T(8,128)(2,1)}, bf16[160,1024]{1,0:T(8,128)(2,1)}, bf16[160,1024]{1,0:T(8,128)(2,1)}, bf16[160,1024]{1,0:T(8,128)(2,1)}) custom-call(s32[4]{0:T(128)} %pad_add_fusion.order_ref, s32[4]{0:T(128)} %and_select_fusion.ring_ref, bf16[160,4096]{1,0:T(8,128)(2,1)} %collective-permute-done.15.source_ref), custom_call_target="tpu_custom_call" | custom-call | bytes 2621440 | tf_op jit(solution)/shard_map/column_slices/pallas_call | solution.py:162
  94.0 3.8 %collective-permute-start.21 = (bf16[640,512]{1,0:T(8,128)(2,1)}, bf16[640,512]{1,0:T(8,128)(2,1)S(1)}, u32[]{:S(2)}, u32[]{:S(2)}) collective-permute-start(bf16[640,512]{1,0:T(8,128)(2,1)} %collective-permute-done.20), channel_id=1, source_target_pairs={{0,4},{1,5},{2,14},{3,15},{4,8},{5,9},{6,2},{7,3},{8,12},{9,13},{1... | collective-permute-start | bytes 1966088 | tf_op jit(solution)/shard_map/ppermute | solution.py:33
  102.5 5.0 %collective-permute-done.21 = bf16[640,512]{1,0:T(8,128)(2,1)S(1)} collective-permute-done((bf16[640,512]{1,0:T(8,128)(2,1)}, bf16[640,512]{1,0:T(8,128)(2,1)S(1)}, u32[]{:S(2)}, u32[]{:S(2)}) %collective-permute-start.21) | collective-permute-done | bytes 655392 | tf_op jit(solution)/shard_map/ppermute | solution.py:33
  123.4 6.5 %collective-permute-start.19 = (bf16[384,512]{1,0:T(8,128)(2,1)}, bf16[384,512]{1,0:T(8,128)(2,1)}, u32[]{:S(2)}, u32[]{:S(2)}) collective-permute-start(bf16[384,512]{1,0:T(8,128)(2,1)} %slice.223), channel_id=1, source_target_pairs={{0,1},{1,0},{2,3},{3,2},{4,5},{5,4},{6,7},{7,6},{8,9},{9,8},{10,11... | collective-permute-start | bytes 1179656 | tf_op jit(solution)/shard_map/ppermute | solution.py:33
  131.5 2.8 %collective-permute-start.23 = (bf16[384,512]{1,0:T(8,128)(2,1)}, bf16[384,512]{1,0:T(8,128)(2,1)}, u32[]{:S(2)}, u32[]{:S(2)}) collective-permute-start(bf16[384,512]{1,0:T(8,128)(2,1)} %slice.222), channel_id=1, source_target_pairs={{0,1},{1,0},{2,3},{3,2},{4,5},{5,4},{6,7},{7,6},{8,9},{9,8},{10,11... | collective-permute-start | bytes 1179656 | tf_op jit(solution)/shard_map/ppermute | solution.py:33
  134.7 4.3 %collective-permute-start.16 = (bf16[160,1024]{1,0:T(8,128)(2,1)}, bf16[160,1024]{1,0:T(8,128)(2,1)}, u32[]{:S(2)}, u32[]{:S(2)}) collective-permute-start(bf16[160,1024]{1,0:T(8,128)(2,1)} %get-tuple-element.31), channel_id=1, source_target_pairs={{0,4},{1,5},{2,6},{3,7},{4,8},{5,9},{6,10},{7,11},{8,12},{9,13},{1... | collective-permute-start | bytes 983048 | tf_op jit(solution)/shard_map/ppermute | solution.py:33
  144.6 14.6 %collective-permute-start.24 = (bf16[256,512]{1,0:T(8,128)(2,1)S(1)}, bf16[256,512]{1,0:T(8,128)(2,1)S(1)}, u32[]{:S(2)}, u32[]{:S(2)}) collective-permute-start(bf16[256,512]{1,0:T(8,128)(2,1)S(1)} %slice.160), channel_id=1, source_target_pairs={{0,2},{1,3},{2,0},{3,1},{4,6},{5,7},{6,4},{7,5},{8,10},{9,11},{10,... | collective-permute-start | bytes 786440 | tf_op jit(solution)/shard_map/ppermute | solution.py:33
  161.9 9.5 %collective-permute-start.25 = (bf16[256,512]{1,0:T(8,128)(2,1)S(1)}, bf16[256,512]{1,0:T(8,128)(2,1)S(1)}, u32[]{:S(2)}, u32[]{:S(2)}) collective-permute-start(bf16[256,512]{1,0:T(8,128)(2,1)S(1)} %slice.161), channel_id=1, source_target_pairs={{0,2},{1,3},{2,0},{3,1},{4,6},{5,7},{6,4},{7,5},{8,10},{9,11},{10,... | collective-permute-start | bytes 786440 | tf_op jit(solution)/shard_map/ppermute | solution.py:33
  174.1 7.6 %attention.1 = (bf16[128,512]{1,0:T(8,128)(2,1)}, bf16[128,512]{1,0:T(8,128)(2,1)}) custom-call(s32[1]{0:T(128)} %bitcast.31.refs_0_, bf16[384,512]{1,0:T(8,128)(2,1)} %copy-done.2, bf16[384,512]{1,0:T(8,128)(2,1)} %copy-done.3, bf16[256,512]{1,0:T(8,128)(2,1)} %copy-done.13, bf16[256,512]{1,0:T(8,128)(2,1)} %copy-done.14, ...), custom_call_target="tpu_custom_call" | custom-call | flops 1073741824 | bytes 786432 | tf_op jit(solution)/shard_map/attention/pallas_call | solution.py:127
  181.6 4.0 %collective-permute-start.26 = (bf16[128,512]{1,0:T(8,128)(2,1)}, bf16[128,512]{1,0:T(8,128)(2,1)S(1)}, u32[]{:S(2)}, u32[]{:S(2)}) collective-permute-start(bf16[128,512]{1,0:T(8,128)(2,1)} %get-tuple-element.36), channel_id=1, source_target_pairs={{0,64},{1,65},{2,66},{3,67},{4,68},{5,69},{6,70},{7,71},{8,72},{9,... | collective-permute-start | bytes 393224 | tf_op jit(solution)/shard_map/ppermute | solution.py:43
  185.6 6.6 %collective-permute-start.27 = (bf16[128,512]{1,0:T(8,128)(2,1)}, bf16[128,512]{1,0:T(8,128)(2,1)S(1)}, u32[]{:S(2)}, u32[]{:S(2)}) collective-permute-start(bf16[128,512]{1,0:T(8,128)(2,1)} %get-tuple-element.37), channel_id=1, source_target_pairs={{0,65},{1,64},{2,67},{3,66},{4,69},{5,68},{6,71},{7,70},{8,73},{9,... | collective-permute-start | bytes 393224 | tf_op jit(solution)/shard_map/ppermute | solution.py:43
  194.6 6.9 %collective-permute-done.27 = bf16[128,512]{1,0:T(8,128)(2,1)S(1)} collective-permute-done((bf16[128,512]{1,0:T(8,128)(2,1)}, bf16[128,512]{1,0:T(8,128)(2,1)S(1)}, u32[]{:S(2)}, u32[]{:S(2)}) %collective-permute-start.27) | collective-permute-done | bytes 131104 | tf_op jit(solution)/shard_map/ppermute | solution.py:43
  208.4 3.9 %collective-permute-start.29 = (bf16[256,512]{1,0:T(8,128)(2,1)S(1)}, bf16[256,512]{1,0:T(8,128)(2,1)S(1)}, u32[]{:S(2)}, u32[]{:S(2)}) collective-permute-start(bf16[256,512]{1,0:T(8,128)(2,1)S(1)} %pad_maximum_fusion.9), channel_id=1, source_target_pairs={{0,16},{1,17},{2,18},{3,19},{4,20},{5,21},{6,22},{7,23},{8,24},{9,... | collective-permute-start | bytes 786440 | tf_op jit(solution)/shard_map/ppermute | solution.py:33
  212.3 4.8 %collective-permute-done.28 = bf16[256,512]{1,0:T(8,128)(2,1)S(1)} collective-permute-done((bf16[256,512]{1,0:T(8,128)(2,1)S(1)}, bf16[256,512]{1,0:T(8,128)(2,1)S(1)}, u32[]{:S(2)}, u32[]{:S(2)}) %collective-permute-start.28) | collective-permute-done | bytes 262176 | tf_op jit(solution)/shard_map/ppermute | solution.py:33
  223.5 4.9 %collective-permute-done.30 = bf16[256,512]{1,0:T(8,128)(2,1)S(1)} collective-permute-done((bf16[256,512]{1,0:T(8,128)(2,1)S(1)}, bf16[256,512]{1,0:T(8,128)(2,1)S(1)}, u32[]{:S(2)}, u32[]{:S(2)}) %collective-permute-start.30) | collective-permute-done | bytes 262176 | tf_op jit(solution)/shard_map/ppermute | solution.py:33
  232.2 4.6 %collective-permute-start.35 = (bf16[320,512]{1,0:T(8,128)(2,1)S(1)}, bf16[320,512]{1,0:T(8,128)(2,1)S(1)}, u32[]{:S(2)}, u32[]{:S(2)}) collective-permute-start(bf16[320,512]{1,0:T(8,128)(2,1)S(1)} %pad_maximum_fusion.8), channel_id=1, source_target_pairs={{0,4},{1,5},{2,6},{3,7},{4,8},{5,9},{6,10},{7,11},{8,12},{9,13},{1... | collective-permute-start | bytes 983048 | tf_op jit(solution)/shard_map/ppermute | solution.py:33
  238.8 3.4 %collective-permute-done.32 = bf16[320,512]{1,0:T(8,128)(2,1)S(1)} collective-permute-done((bf16[320,512]{1,0:T(8,128)(2,1)S(1)}, bf16[320,512]{1,0:T(8,128)(2,1)S(1)}, u32[]{:S(2)}, u32[]{:S(2)}) %collective-permute-start.32) | collective-permute-done | bytes 327712 | tf_op jit(solution)/shard_map/ppermute | solution.py:33
  242.2 3.2 %collective-permute-start.33 = (bf16[320,512]{1,0:T(8,128)(2,1)S(1)}, bf16[320,512]{1,0:T(8,128)(2,1)S(1)}, u32[]{:S(2)}, u32[]{:S(2)}) collective-permute-start(bf16[320,512]{1,0:T(8,128)(2,1)S(1)} %pad_maximum_fusion.5), channel_id=1, source_target_pairs={{0,64},{1,65},{2,66},{3,67},{4,68},{5,69},{6,70},{7,71},{8,72},{9,... | collective-permute-start | bytes 983048 | tf_op jit(solution)/shard_map/ppermute | solution.py:43
  245.5 3.1 %collective-permute-done.34 = bf16[320,512]{1,0:T(8,128)(2,1)S(1)} collective-permute-done((bf16[320,512]{1,0:T(8,128)(2,1)S(1)}, bf16[320,512]{1,0:T(8,128)(2,1)S(1)}, u32[]{:S(2)}, u32[]{:S(2)}) %collective-permute-start.34) | collective-permute-done | bytes 327712 | tf_op jit(solution)/shard_map/ppermute | solution.py:33
  248.6 2.7 %collective-permute-done.33 = bf16[320,512]{1,0:T(8,128)(2,1)S(1)} collective-permute-done((bf16[320,512]{1,0:T(8,128)(2,1)S(1)}, bf16[320,512]{1,0:T(8,128)(2,1)S(1)}, u32[]{:S(2)}, u32[]{:S(2)}) %collective-permute-start.33) | collective-permute-done | bytes 327712 | tf_op jit(solution)/shard_map/ppermute | solution.py:43
  251.5 11.3 %collective-permute-start.36 = (bf16[160,512]{1,0:T(8,128)(2,1)S(1)}, bf16[160,512]{1,0:T(8,128)(2,1)S(1)}, u32[]{:S(2)}, u32[]{:S(2)}) collective-permute-start(bf16[160,512]{1,0:T(8,128)(2,1)S(1)} %slice.179), channel_id=1, source_target_pairs={{0,2},{1,3},{2,0},{3,1},{4,6},{5,7},{6,4},{7,5},{8,10},{9,11},{10,... | collective-permute-start | bytes 491528 | tf_op jit(solution)/shard_map/ppermute | solution.py:33
  (168 shorter events, 93.0 us)
Async XLA Ops:
  4.5 23.8 %collective-permute-start.4 = (bf16[160,512]{1,0:T(8,128)(2,1)S(1)}, bf16[160,512]{1,0:T(8,128)(2,1)S(1)}, u32[]{:S(2)}, u32[]{:S(2)}) collective-permute-start(bf16[160,512]{1,0:T(8,128)(2,1)S(1)} %get-tuple-element.73), channel_id=1, source_target_pairs={{0,2},{1,34},{2,0},{3,32},{4,6},{5,38},{6,4},{7,36},{8,10},{9,42},... | collective-permute-start | bytes 491528 | tf_op jit(solution)/shard_map/ppermute | solution.py:33
  6.4 21.9 %collective-permute-start.3 = (bf16[160,512]{1,0:T(8,128)(2,1)S(1)}, bf16[160,512]{1,0:T(8,128)(2,1)S(1)}, u32[]{:S(2)}, u32[]{:S(2)}) collective-permute-start(bf16[160,512]{1,0:T(8,128)(2,1)S(1)} %get-tuple-element.74), channel_id=1, source_target_pairs={{0,0},{1,32},{2,2},{3,34},{4,4},{5,36},{6,6},{7,38},{8,8},{9,40},{... | collective-permute-start | bytes 491528 | tf_op jit(solution)/shard_map/ppermute | solution.py:33
  7.1 82.6 %collective-permute-start.15 = (bf16[160,4096]{1,0:T(8,128)(2,1)}, bf16[160,4096]{1,0:T(8,128)(2,1)}, u32[]{:S(2)}, u32[]{:S(2)}) collective-permute-start(bf16[160,4096]{1,0:T(8,128)(2,1)} %bitcast.86), channel_id=1, source_target_pairs={{0,64},{1,65},{2,66},{3,67},{4,68},{5,69},{6,70},{7,71},{8,72},{9,... | collective-permute-start | bytes 3932168 | tf_op jit(solution)/shard_map/ppermute | solution.py:43
  12.1 13.5 %collective-permute-start.1 = (f32[2,512]{1,0:T(2,128)S(1)}, f32[2,512]{1,0:T(2,128)S(1)}, u32[]{:S(2)}, u32[]{:S(2)}) collective-permute-start(f32[2,512]{1,0:T(2,128)S(1)} %pad_maximum_fusion.19), channel_id=1, source_target_pairs={{0,1},{1,0},{2,3},{3,2},{4,5},{5,4},{6,7},{7,6},{8,9},{9,8},{10,11... | collective-permute-start | bytes 12296 | tf_op jit(solution)/shard_map/ppermute | solution.py:33
  25.7 13.9 %collective-permute-start.5 = (f32[18,512]{1,0:T(8,128)S(1)}, f32[18,512]{1,0:T(8,128)S(1)}, u32[]{:S(2)}, u32[]{:S(2)}) collective-permute-start(f32[18,512]{1,0:T(8,128)S(1)} %pad_maximum_fusion.18), channel_id=1, source_target_pairs={{0,4},{1,5},{2,6},{3,7},{4,0},{5,1},{6,2},{7,3},{8,12},{9,13},{10,... | collective-permute-start | bytes 110600 | tf_op jit(solution)/shard_map/ppermute | solution.py:33
  31.3 19.2 %collective-permute-start.13 = (bf16[320,512]{1,0:T(8,128)(2,1)}, bf16[320,512]{1,0:T(8,128)(2,1)S(1)}, u32[]{:S(2)}, u32[]{:S(2)}) collective-permute-start(bf16[320,512]{1,0:T(8,128)(2,1)} %stacked_rows.4.refs_0_), channel_id=1, source_target_pairs={{0,32},{1,33},{2,34},{3,35},{4,36},{5,37},{6,38},{7,39},{8,40},{9,... | collective-permute-start | bytes 983048 | tf_op jit(solution)/shard_map/ppermute | solution.py:33
  35.0 74.7 %collective-permute-start.2 = (bf16[2560,384]{1,0:T(8,128)(2,1)S(1)}, bf16[2560,384]{1,0:T(8,128)(2,1)}, u32[]{:S(2)}, u32[]{:S(2)}) collective-permute-start(bf16[2560,384]{1,0:T(8,128)(2,1)S(1)} %bitcast.70), channel_id=1, source_target_pairs={{0,2},{1,3},{2,0},{3,1},{4,6},{5,7},{6,4},{7,5},{8,10},{9,11},{10,... | collective-permute-start | bytes 5898248 | tf_op jit(solution)/shard_map/ppermute | solution.py:33
  39.7 18.2 %collective-permute-start.6 = (bf16[320,512]{1,0:T(8,128)(2,1)}, bf16[320,512]{1,0:T(8,128)(2,1)S(1)}, u32[]{:S(2)}, u32[]{:S(2)}) collective-permute-start(bf16[320,512]{1,0:T(8,128)(2,1)} %stacked_rows.4.refs_0_), channel_id=1, source_target_pairs={{0,16},{1,17},{2,18},{3,19},{4,20},{5,21},{6,22},{7,23},{8,24},{9,... | collective-permute-start | bytes 983048 | tf_op jit(solution)/shard_map/ppermute | solution.py:33
  50.6 14.4 %collective-permute-start.14 = (bf16[320,512]{1,0:T(8,128)(2,1)S(1)}, bf16[320,512]{1,0:T(8,128)(2,1)S(1)}, u32[]{:S(2)}, u32[]{:S(2)}) collective-permute-start(bf16[320,512]{1,0:T(8,128)(2,1)S(1)} %collective-permute-done.13.refs_0_), channel_id=1, source_target_pairs={{0,16},{1,17},{2,18},{3,19},{4,20},{5,21},{6,22},{7,23},{8,24},{9,... | collective-permute-start | bytes 983048 | tf_op jit(solution)/shard_map/ppermute | solution.py:33
  60.6 12.8 %collective-permute-start.7 = (bf16[640,512]{1,0:T(8,128)(2,1)}, bf16[640,512]{1,0:T(8,128)(2,1)}, u32[]{:S(2)}, u32[]{:S(2)}) collective-permute-start(bf16[640,512]{1,0:T(8,128)(2,1)} %stacked_rows.5), channel_id=1, source_target_pairs={{0,4},{1,5},{2,14},{3,15},{4,8},{5,9},{6,2},{7,3},{8,12},{9,13},{1... | collective-permute-start | bytes 1966088 | tf_op jit(solution)/shard_map/ppermute | solution.py:33
  67.6 26.4 %collective-permute-start.20 = (bf16[640,512]{1,0:T(8,128)(2,1)}, bf16[640,512]{1,0:T(8,128)(2,1)}, u32[]{:S(2)}, u32[]{:S(2)}) collective-permute-start(bf16[640,512]{1,0:T(8,128)(2,1)} %stacked_rows.6), channel_id=1, source_target_pairs={{0,4},{1,5},{2,14},{3,15},{4,8},{5,9},{6,2},{7,3},{8,12},{9,13},{1... | collective-permute-start | bytes 1966088 | tf_op jit(solution)/shard_map/ppermute | solution.py:33
  87.7 12.8 %collective-permute-start.11 = (bf16[640,512]{1,0:T(8,128)(2,1)}, bf16[640,512]{1,0:T(8,128)(2,1)}, u32[]{:S(2)}, u32[]{:S(2)}) collective-permute-start(bf16[640,512]{1,0:T(8,128)(2,1)} %collective-permute-done.7), channel_id=1, source_target_pairs={{0,4},{1,5},{2,14},{3,15},{4,8},{5,9},{6,2},{7,3},{8,12},{9,13},{1... | collective-permute-start | bytes 1966088 | tf_op jit(solution)/shard_map/ppermute | solution.py:33
  94.0 13.5 %collective-permute-start.21 = (bf16[640,512]{1,0:T(8,128)(2,1)}, bf16[640,512]{1,0:T(8,128)(2,1)S(1)}, u32[]{:S(2)}, u32[]{:S(2)}) collective-permute-start(bf16[640,512]{1,0:T(8,128)(2,1)} %collective-permute-done.20), channel_id=1, source_target_pairs={{0,4},{1,5},{2,14},{3,15},{4,8},{5,9},{6,2},{7,3},{8,12},{9,13},{1... | collective-permute-start | bytes 1966088 | tf_op jit(solution)/shard_map/ppermute | solution.py:33
  100.6 21.1 %collective-permute-start.12 = (bf16[640,512]{1,0:T(8,128)(2,1)}, bf16[640,512]{1,0:T(8,128)(2,1)S(1)}, u32[]{:S(2)}, u32[]{:S(2)}) collective-permute-start(bf16[640,512]{1,0:T(8,128)(2,1)} %collective-permute-done.11), channel_id=1, source_target_pairs={{0,4},{1,5},{2,14},{3,15},{4,8},{5,9},{6,2},{7,3},{8,12},{9,13},{1... | collective-permute-start | bytes 1966088 | tf_op jit(solution)/shard_map/ppermute | solution.py:33
  107.5 22.3 %collective-permute-start.22 = (bf16[640,512]{1,0:T(8,128)(2,1)S(1)}, bf16[640,512]{1,0:T(8,128)(2,1)S(1)}, u32[]{:S(2)}, u32[]{:S(2)}) collective-permute-start(bf16[640,512]{1,0:T(8,128)(2,1)S(1)} %collective-permute-done.21), channel_id=1, source_target_pairs={{0,4},{1,5},{2,14},{3,15},{4,8},{5,9},{6,2},{7,3},{8,12},{9,13},{1... | collective-permute-start | bytes 1966088 | tf_op jit(solution)/shard_map/ppermute | solution.py:33
  123.4 20.1 %collective-permute-start.19 = (bf16[384,512]{1,0:T(8,128)(2,1)}, bf16[384,512]{1,0:T(8,128)(2,1)}, u32[]{:S(2)}, u32[]{:S(2)}) collective-permute-start(bf16[384,512]{1,0:T(8,128)(2,1)} %slice.223), channel_id=1, source_target_pairs={{0,1},{1,0},{2,3},{3,2},{4,5},{5,4},{6,7},{7,6},{8,9},{9,8},{10,11... | collective-permute-start | bytes 1179656 | tf_op jit(solution)/shard_map/ppermute | solution.py:33
  131.5 29.2 %collective-permute-start.23 = (bf16[384,512]{1,0:T(8,128)(2,1)}, bf16[384,512]{1,0:T(8,128)(2,1)}, u32[]{:S(2)}, u32[]{:S(2)}) collective-permute-start(bf16[384,512]{1,0:T(8,128)(2,1)} %slice.222), channel_id=1, source_target_pairs={{0,1},{1,0},{2,3},{3,2},{4,5},{5,4},{6,7},{7,6},{8,9},{9,8},{10,11... | collective-permute-start | bytes 1179656 | tf_op jit(solution)/shard_map/ppermute | solution.py:33
  134.7 37.9 %collective-permute-start.16 = (bf16[160,1024]{1,0:T(8,128)(2,1)}, bf16[160,1024]{1,0:T(8,128)(2,1)}, u32[]{:S(2)}, u32[]{:S(2)}) collective-permute-start(bf16[160,1024]{1,0:T(8,128)(2,1)} %get-tuple-element.31), channel_id=1, source_target_pairs={{0,4},{1,5},{2,6},{3,7},{4,8},{5,9},{6,10},{7,11},{8,12},{9,13},{1... | collective-permute-start | bytes 983048 | tf_op jit(solution)/shard_map/ppermute | solution.py:33
  139.0 33.6 %collective-permute-start.17 = (bf16[160,1024]{1,0:T(8,128)(2,1)}, bf16[160,1024]{1,0:T(8,128)(2,1)}, u32[]{:S(2)}, u32[]{:S(2)}) collective-permute-start(bf16[160,1024]{1,0:T(8,128)(2,1)} %get-tuple-element.32), channel_id=1, source_target_pairs={{0,8},{1,9},{2,10},{3,11},{4,12},{5,13},{6,14},{7,15},{8,0},{9,1},... | collective-permute-start | bytes 983048 | tf_op jit(solution)/shard_map/ppermute | solution.py:33
  141.1 31.5 %collective-permute-start.18 = (bf16[160,1024]{1,0:T(8,128)(2,1)}, bf16[160,1024]{1,0:T(8,128)(2,1)}, u32[]{:S(2)}, u32[]{:S(2)}) collective-permute-start(bf16[160,1024]{1,0:T(8,128)(2,1)} %get-tuple-element.33), channel_id=1, source_target_pairs={{0,12},{1,13},{2,14},{3,15},{4,0},{5,1},{6,2},{7,3},{8,4},{9,5},{1... | collective-permute-start | bytes 983048 | tf_op jit(solution)/shard_map/ppermute | solution.py:33
  144.6 28.0 %collective-permute-start.24 = (bf16[256,512]{1,0:T(8,128)(2,1)S(1)}, bf16[256,512]{1,0:T(8,128)(2,1)S(1)}, u32[]{:S(2)}, u32[]{:S(2)}) collective-permute-start(bf16[256,512]{1,0:T(8,128)(2,1)S(1)} %slice.160), channel_id=1, source_target_pairs={{0,2},{1,3},{2,0},{3,1},{4,6},{5,7},{6,4},{7,5},{8,10},{9,11},{10,... | collective-permute-start | bytes 786440 | tf_op jit(solution)/shard_map/ppermute | solution.py:33
  161.9 10.7 %collective-permute-start.25 = (bf16[256,512]{1,0:T(8,128)(2,1)S(1)}, bf16[256,512]{1,0:T(8,128)(2,1)S(1)}, u32[]{:S(2)}, u32[]{:S(2)}) collective-permute-start(bf16[256,512]{1,0:T(8,128)(2,1)S(1)} %slice.161), channel_id=1, source_target_pairs={{0,2},{1,3},{2,0},{3,1},{4,6},{5,7},{6,4},{7,5},{8,10},{9,11},{10,... | collective-permute-start | bytes 786440 | tf_op jit(solution)/shard_map/ppermute | solution.py:33
  181.6 13.0 %collective-permute-start.26 = (bf16[128,512]{1,0:T(8,128)(2,1)}, bf16[128,512]{1,0:T(8,128)(2,1)S(1)}, u32[]{:S(2)}, u32[]{:S(2)}) collective-permute-start(bf16[128,512]{1,0:T(8,128)(2,1)} %get-tuple-element.36), channel_id=1, source_target_pairs={{0,64},{1,65},{2,66},{3,67},{4,68},{5,69},{6,70},{7,71},{8,72},{9,... | collective-permute-start | bytes 393224 | tf_op jit(solution)/shard_map/ppermute | solution.py:43
  185.6 15.9 %collective-permute-start.27 = (bf16[128,512]{1,0:T(8,128)(2,1)}, bf16[128,512]{1,0:T(8,128)(2,1)S(1)}, u32[]{:S(2)}, u32[]{:S(2)}) collective-permute-start(bf16[128,512]{1,0:T(8,128)(2,1)} %get-tuple-element.37), channel_id=1, source_target_pairs={{0,65},{1,64},{2,67},{3,66},{4,69},{5,68},{6,71},{7,70},{8,73},{9,... | collective-permute-start | bytes 393224 | tf_op jit(solution)/shard_map/ppermute | solution.py:43
  201.5 15.6 %collective-permute-start.28 = (bf16[256,512]{1,0:T(8,128)(2,1)S(1)}, bf16[256,512]{1,0:T(8,128)(2,1)S(1)}, u32[]{:S(2)}, u32[]{:S(2)}) collective-permute-start(bf16[256,512]{1,0:T(8,128)(2,1)S(1)} %pad_maximum_fusion.9), channel_id=1, source_target_pairs={{0,32},{1,33},{2,34},{3,35},{4,36},{5,37},{6,38},{7,39},{8,40},{9,... | collective-permute-start | bytes 786440 | tf_op jit(solution)/shard_map/ppermute | solution.py:33
  205.9 22.9 %collective-permute-start.31 = (bf16[640,1024]{1,0:T(8,128)(2,1)}, bf16[640,1024]{1,0:T(8,128)(2,1)S(1)}, u32[]{:S(2)}, u32[]{:S(2)}) collective-permute-start(bf16[640,1024]{1,0:T(8,128)(2,1)} %stacked_rows.7), channel_id=1, source_target_pairs={{0,2},{1,3},{2,0},{3,1},{4,6},{5,7},{6,4},{7,5},{8,10},{9,11},{10,... | collective-permute-start | bytes 3932168 | tf_op jit(solution)/shard_map/ppermute | solution.py:33
  208.4 14.4 %collective-permute-start.29 = (bf16[256,512]{1,0:T(8,128)(2,1)S(1)}, bf16[256,512]{1,0:T(8,128)(2,1)S(1)}, u32[]{:S(2)}, u32[]{:S(2)}) collective-permute-start(bf16[256,512]{1,0:T(8,128)(2,1)S(1)} %pad_maximum_fusion.9), channel_id=1, source_target_pairs={{0,16},{1,17},{2,18},{3,19},{4,20},{5,21},{6,22},{7,23},{8,24},{9,... | collective-permute-start | bytes 786440 | tf_op jit(solution)/shard_map/ppermute | solution.py:33
  217.1 11.3 %collective-permute-start.30 = (bf16[256,512]{1,0:T(8,128)(2,1)S(1)}, bf16[256,512]{1,0:T(8,128)(2,1)S(1)}, u32[]{:S(2)}, u32[]{:S(2)}) collective-permute-start(bf16[256,512]{1,0:T(8,128)(2,1)S(1)} %collective-permute-done.28), channel_id=1, source_target_pairs={{0,16},{1,17},{2,18},{3,19},{4,20},{5,21},{6,22},{7,23},{8,24},{9,... | collective-permute-start | bytes 786440 | tf_op jit(solution)/shard_map/ppermute | solution.py:33
  230.2 12.0 %collective-permute-start.32 = (bf16[320,512]{1,0:T(8,128)(2,1)S(1)}, bf16[320,512]{1,0:T(8,128)(2,1)S(1)}, u32[]{:S(2)}, u32[]{:S(2)}) collective-permute-start(bf16[320,512]{1,0:T(8,128)(2,1)S(1)} %pad_maximum_fusion.6), channel_id=1, source_target_pairs={{0,12},{1,13},{2,14},{3,15},{4,0},{5,1},{6,2},{7,3},{8,4},{9,5},{1... | collective-permute-start | bytes 983048 | tf_op jit(solution)/shard_map/ppermute | solution.py:33
  232.2 13.3 %collective-permute-start.35 = (bf16[320,512]{1,0:T(8,128)(2,1)S(1)}, bf16[320,512]{1,0:T(8,128)(2,1)S(1)}, u32[]{:S(2)}, u32[]{:S(2)}) collective-permute-start(bf16[320,512]{1,0:T(8,128)(2,1)S(1)} %pad_maximum_fusion.8), channel_id=1, source_target_pairs={{0,4},{1,5},{2,6},{3,7},{4,8},{5,9},{6,10},{7,11},{8,12},{9,13},{1... | collective-permute-start | bytes 983048 | tf_op jit(solution)/shard_map/ppermute | solution.py:33
  236.8 11.7 %collective-permute-start.34 = (bf16[320,512]{1,0:T(8,128)(2,1)S(1)}, bf16[320,512]{1,0:T(8,128)(2,1)S(1)}, u32[]{:S(2)}, u32[]{:S(2)}) collective-permute-start(bf16[320,512]{1,0:T(8,128)(2,1)S(1)} %pad_maximum_fusion.7), channel_id=1, source_target_pairs={{0,8},{1,9},{2,10},{3,11},{4,12},{5,13},{6,14},{7,15},{8,0},{9,1},... | collective-permute-start | bytes 983048 | tf_op jit(solution)/shard_map/ppermute | solution.py:33
  251.5 12.3 %collective-permute-start.36 = (bf16[160,512]{1,0:T(8,128)(2,1)S(1)}, bf16[160,512]{1,0:T(8,128)(2,1)S(1)}, u32[]{:S(2)}, u32[]{:S(2)}) collective-permute-start(bf16[160,512]{1,0:T(8,128)(2,1)S(1)} %slice.179), channel_id=1, source_target_pairs={{0,2},{1,3},{2,0},{3,1},{4,6},{5,7},{6,4},{7,5},{8,10},{9,11},{10,... | collective-permute-start | bytes 491528 | tf_op jit(solution)/shard_map/ppermute | solution.py:33
  (21 other events, 218.4 us)

commit v9 on v8

--- a/solution.py
+++ b/solution.py
@@ -263,15 +263,17 @@
     weight = after(qkv_weight[0], theirs)
     weight_beside = moved(weight, other_core)
     f = moved(e, by_two)
-    e_two = stacked_rows(e, moved(after(e, table), pair))
+    e_two = stacked_rows(e, after(moved(after(e, table), pair), f))
     f_two = stacked_rows(f, moved(f, pair))
     e_ring, f_ring = [e_two], [f_two]
-    for _ in range(3):
+    for _ in range(2):
         e_ring.append(moved(e_ring[-1], around))
         f_ring.append(moved(f_ring[-1], around))
-    table = after(table, e_ring[1])
-    for where in (lambda y, x, c: (y, x ^ 2, c), pair, by_two):
+    table = after(table, (e_ring[1], f_two))
+    for where in (lambda y, x, c: (y, x ^ 2, c), pair):
         table = table + moved(table, where)
+    table = after(table, (e_ring[2], f_ring[1]))
+    table = table + moved(table, by_two)
     factors = lax.rsqrt(table[16:] / width + 1e-05)
     factor_e = jnp.where(first == seq, factors[:1], factors[1:])
     factor_f = jnp.where(first == seq, factors[1:], factors[:1])
@@ -315,10 +317,16 @@
     allowed = block_mask(query_ids, rows, global_blocks[0], key_ids)
     bias = jnp.repeat(jnp.where(allowed.T, 0.0, NEG), BLOCK, axis=1).astype(bf16)
 
-    partial_e = partial_f = 0.0
-    for k in range(4):
-        partial_e = partial_e + project(e_ring[k], k, factor_e)
-        partial_f = partial_f + project(f_ring[k], k, factor_f)
+    partial_e = project(e_ring[0], 0, factor_e) + project(e_ring[1], 1, factor_e)
+    last, partial_e = lax.optimization_barrier((e_ring[2], partial_e))
+    partial_e = partial_e + project(last, 2, factor_e)
+    e_last = moved(last, around)
+    partial_f = project(f_ring[0], 0, factor_f) + project(f_ring[1], 1, factor_f)
+    last, partial_e, partial_f = lax.optimization_barrier((f_ring[2], partial_e, partial_f))
+    f_last = moved(last, around)
+    partial_f = partial_f + project(last, 2, factor_f)
+    partial_e = partial_e + project(e_last, 3, factor_e)
+    partial_f = partial_f + project(f_last, 3, factor_f)
     order = after(jnp.stack([yl, yl ^ 2, yl ^ 1, yl ^ 3]), f_two)
     ring = (x + jnp.arange(4, dtype=jnp.int32)) % 4
     slices = column_slices(out_next, order, ring)
@@ -329,8 +337,10 @@
         out_own.append(moved(slices[r], lambda y, x, c, r=r: (y, (x + r) % 4, c)))
     joined, other = [], []
     head = columns // 3
-    for partial, send in zip((partial_e, partial_f), sends):
+    residual = moved_on(after(item, sends[1]), same)
+    for i, (partial, send) in enumerate(zip((partial_e, partial_f), sends)):
         came = moved(send, other_seq)
+        came = after(came, residual) if i else came
         joined.append((partial[:columns] + came.astype(f32)).astype(bf16))
         other.append(moved(joined[-1][head:], other_core))
 
@@ -361,7 +371,6 @@
             [half[r * part : (r + 1) * part].astype(bf16) for half in added], axis=0
         )
         shares.append(moved(share, lambda y, x, c, r=r: (y, (x - r) % 4, c)))
-    residual = moved_on(after(item, shares[0]), same)
     total = residual.astype(f32) + total
     for share in shares:
         total = total + share.astype(f32)

time: 266 us -> 276 us (1.038)
  the two profiles are of different devices: /device:TPU:7 before, /device:TPU:1 now
where the time goes in v9:
time: 276 us; the launch traced here: 274 us
  starting transfers between devices  147 us (53%)
  waiting for transfers between devices  63 us (23%)
  Pallas kernels  20 us (7%)
  matrix products  17.5 us (6%)
  other arithmetic  15.5 us (6%)
  local copies, waits for them, and re-layouts  9.98 us (4%)
    ppermute x33, starting transfers between devices, moved(): return lax.ppermute(value, PLANE, pairs_of(where))  129 us
    ppermute x33, waiting for transfers between devices, moved(): return lax.ppermute(value, PLANE, pairs_of(where))  56.7 us
    ppermute x4, starting transfers between devices, moved_on(): return lax.ppermute(value, ('section', *PLANE), pairs)  17.8 us
    dot_general x8, matrix products, project(): return jnp.dot(weights[k], normed, preferred_element_type=f32)  13.8 us
    pallas_call x4, Pallas kernels, stacked_rows(): pl.pallas_call(rows_kernel, in_specs=[vmem] * len(parts), out_specs=vmem,...  8.17 us
    pallas_call x1, Pallas kernels, attention(): pl.pallas_call(lambda *refs: attention_kernel(1.0 / math.sqrt(size), per,...  7.56 us
    unnamed x68, local copies, waits for them, and re-layouts  6.6 us
    ppermute x4, waiting for transfers between devices, moved_on(): return lax.ppermute(value, ('section', *PLANE), pairs)  6.22 us
  transfers between devices with their start and end apart: 37, of which 15 were waited for; matrix products, arithmetic and copies ran while one was open for 11% of the time, Pallas kernels for 4%

profile of v9, /device:TPU:1, one launch (start us, length us, event | category | flops | bytes accessed | tf_op | source)
XLA Modules:
  0.0 273.8 jit_solution(10993809154092801503)
XLA Ops:
  1.9 8.8 %collective-permute-start = (bf16[176,512]{1,0:T(8,128)(2,1)S(1)}, bf16[176,512]{1,0:T(8,128)(2,1)S(1)}, u32[]{:S(2)}, u32[]{:S(2)}) collective-permute-start(bf16[176,512]{1,0:T(8,128)(2,1)S(1)} %fusion.43), channel_id=1, source_target_pairs={{0,2},{1,3},{2,0},{3,1},{4,6},{5,7},{6,4},{7,5},{8,10},{9,11},{10,... | collective-permute-start | bytes 540680 | tf_op jit(solution)/shard_map/ppermute | solution.py:33
  15.1 6.8 %collective-permute-start.7 = (f32[2,512]{1,0:T(2,128)S(1)}, f32[2,512]{1,0:T(2,128)S(1)}, u32[]{:S(2)}, u32[]{:S(2)}) collective-permute-start(f32[2,512]{1,0:T(2,128)S(1)} %pad_maximum_fusion.19), channel_id=1, source_target_pairs={{0,1},{1,0},{2,3},{3,2},{4,5},{5,4},{6,7},{7,6},{8,9},{9,8},{10,11... | collective-permute-start | bytes 12296 | tf_op jit(solution)/shard_map/ppermute | solution.py:33
  29.1 4.2 %collective-permute-start.3 = (bf16[320,512]{1,0:T(8,128)(2,1)}, bf16[320,512]{1,0:T(8,128)(2,1)S(1)}, u32[]{:S(2)}, u32[]{:S(2)}) collective-permute-start(bf16[320,512]{1,0:T(8,128)(2,1)} %stacked_rows.4.refs_0_), channel_id=1, source_target_pairs={{0,32},{1,33},{2,34},{3,35},{4,36},{5,37},{6,38},{7,39},{8,40},{9,... | collective-permute-start | bytes 983048 | tf_op jit(solution)/shard_map/ppermute | solution.py:33
  33.3 3.2 %collective-permute-start.9 = (bf16[320,512]{1,0:T(8,128)(2,1)}, bf16[320,512]{1,0:T(8,128)(2,1)S(1)}, u32[]{:S(2)}, u32[]{:S(2)}) collective-permute-start(bf16[320,512]{1,0:T(8,128)(2,1)} %stacked_rows.4.refs_0_), channel_id=1, source_target_pairs={{0,16},{1,17},{2,18},{3,19},{4,20},{5,21},{6,22},{7,23},{8,24},{9,... | collective-permute-start | bytes 983048 | tf_op jit(solution)/shard_map/ppermute | solution.py:33
  36.6 11.4 %collective-permute-done.3.refs_0_ = bf16[320,512]{1,0:T(8,128)(2,1)S(1)} collective-permute-done((bf16[320,512]{1,0:T(8,128)(2,1)}, bf16[320,512]{1,0:T(8,128)(2,1)S(1)}, u32[]{:S(2)}, u32[]{:S(2)}) %collective-permute-start.3) | collective-permute-done | bytes 327712 | tf_op jit(solution)/shard_map/ppermute | solution.py:33
  50.7 5.3 %collective-permute-start.10 = (bf16[640,512]{1,0:T(8,128)(2,1)}, bf16[640,512]{1,0:T(8,128)(2,1)}, u32[]{:S(2)}, u32[]{:S(2)}) collective-permute-start(bf16[640,512]{1,0:T(8,128)(2,1)} %stacked_rows.6), channel_id=1, source_target_pairs={{0,4},{1,5},{2,14},{3,15},{4,8},{5,9},{6,2},{7,3},{8,12},{9,13},{1... | collective-permute-start | bytes 1966088 | tf_op jit(solution)/shard_map/ppermute | solution.py:33
  56.0 3.9 %collective-permute-start.12 = (bf16[2560,384]{1,0:T(8,128)(2,1)S(1)}, bf16[2560,384]{1,0:T(8,128)(2,1)}, u32[]{:S(2)}, u32[]{:S(2)}) collective-permute-start(bf16[2560,384]{1,0:T(8,128)(2,1)S(1)} %bitcast.70), channel_id=1, source_target_pairs={{0,2},{1,3},{2,0},{3,1},{4,6},{5,7},{6,4},{7,5},{8,10},{9,11},{10,... | collective-permute-start | bytes 5898248 | tf_op jit(solution)/shard_map/ppermute | solution.py:33
  59.9 4.0 %collective-permute-start.19 = (bf16[160,4096]{1,0:T(8,128)(2,1)}, bf16[160,4096]{1,0:T(8,128)(2,1)}, u32[]{:S(2)}, u32[]{:S(2)}) collective-permute-start(bf16[160,4096]{1,0:T(8,128)(2,1)} %bitcast.86), channel_id=1, source_target_pairs={{0,64},{1,65},{2,66},{3,67},{4,68},{5,69},{6,70},{7,71},{8,72},{9,... | collective-permute-start | bytes 3932168 | tf_op jit(solution)/shard_map/ppermute | solution.py:43
  66.2 8.8 %collective-permute-done.4.refs_1_ = bf16[320,512]{1,0:T(8,128)(2,1)S(1)} collective-permute-done((bf16[320,512]{1,0:T(8,128)(2,1)S(1)}, bf16[320,512]{1,0:T(8,128)(2,1)S(1)}, u32[]{:S(2)}, u32[]{:S(2)}) %collective-permute-start.4) | collective-permute-done | bytes 327712 | tf_op jit(solution)/shard_map/ppermute | solution.py:33
  80.8 3.2 %collective-permute-start.11 = (bf16[640,512]{1,0:T(8,128)(2,1)}, bf16[640,512]{1,0:T(8,128)(2,1)}, u32[]{:S(2)}, u32[]{:S(2)}) collective-permute-start(bf16[640,512]{1,0:T(8,128)(2,1)} %collective-permute-done.10), channel_id=1, source_target_pairs={{0,4},{1,5},{2,14},{3,15},{4,8},{5,9},{6,2},{7,3},{8,12},{9,13},{1... | collective-permute-start | bytes 1966088 | tf_op jit(solution)/shard_map/ppermute | solution.py:33
  87.0 4.1 %collective-permute-done.13 = f32[18,512]{1,0:T(8,128)S(1)} collective-permute-done((f32[18,512]{1,0:T(8,128)S(1)}, f32[18,512]{1,0:T(8,128)S(1)}, u32[]{:S(2)}, u32[]{:S(2)}) %collective-permute-start.13) | collective-permute-done | bytes 36896 | tf_op jit(solution)/shard_map/ppermute | solution.py:33
  100.3 9.1 %collective-permute-start.6 = (bf16[640,512]{1,0:T(8,128)(2,1)}, bf16[640,512]{1,0:T(8,128)(2,1)}, u32[]{:S(2)}, u32[]{:S(2)}) collective-permute-start(bf16[640,512]{1,0:T(8,128)(2,1)} %collective-permute-done.5), channel_id=1, source_target_pairs={{0,4},{1,5},{2,14},{3,15},{4,8},{5,9},{6,2},{7,3},{8,12},{9,13},{1... | collective-permute-start | bytes 1966088 | tf_op jit(solution)/shard_map/ppermute | solution.py:33
  119.7 3.1 %convolution_add_fusion = f32[768,512]{1,0:T(8,128)} fusion(f32[768,512]{1,0:T(8,128)S(1)} %fusion.6, bf16[640,512]{1,0:T(8,128)(2,1)} %collective-permute-done.5, f32[512]{0:T(512)S(1)} %bitcast.83, f32[640]{0:T(1024)S(1)} %get-tuple-element.101, bf16[160,768]{1,0:T(8,128)(2,1)S(1)} %get-tuple-element.71, bf16[160,768]{1,0:T(8,128)(2,1)S(1)} %get-tuple-element.72, ...), kind=kOutput, calls=%fused_computation.4 | convolution fusion | flops 508952576 | bytes 4788736 | tf_op jit(solution)/shard_map/dot_general | solution.py:303
  122.9 3.4 %collective-permute-start.16 = (bf16[640,512]{1,0:T(8,128)(2,1)}, bf16[640,512]{1,0:T(8,128)(2,1)}, u32[]{:S(2)}, u32[]{:S(2)}) collective-permute-start(bf16[640,512]{1,0:T(8,128)(2,1)} %collective-permute-done.6), channel_id=1, source_target_pairs={{0,4},{1,5},{2,14},{3,15},{4,8},{5,9},{6,2},{7,3},{8,12},{9,13},{1... | collective-permute-start | bytes 1966088 | tf_op jit(solution)/shard_map/ppermute | solution.py:33
  128.4 4.2 %column_slices.1 = (bf16[160,1024]{1,0:T(8,128)(2,1)}, bf16[160,1024]{1,0:T(8,128)(2,1)}, bf16[160,1024]{1,0:T(8,128)(2,1)}, bf16[160,1024]{1,0:T(8,128)(2,1)}) custom-call(s32[4]{0:T(128)} %pad_add_fusion.order_ref, s32[4]{0:T(128)} %and_select_fusion.ring_ref, bf16[160,4096]{1,0:T(8,128)(2,1)} %collective-permute-done.19.source_ref), custom_call_target="tpu_custom_call" | custom-call | bytes 2621440 | tf_op jit(solution)/shard_map/column_slices/pallas_call | solution.py:162
  139.6 6.5 %collective-permute-start.24 = (bf16[384,512]{1,0:T(8,128)(2,1)S(1)}, bf16[384,512]{1,0:T(8,128)(2,1)}, u32[]{:S(2)}, u32[]{:S(2)}) collective-permute-start(bf16[384,512]{1,0:T(8,128)(2,1)S(1)} %slice.223), channel_id=1, source_target_pairs={{0,1},{1,0},{2,3},{3,2},{4,5},{5,4},{6,7},{7,6},{8,9},{9,8},{10,11... | collective-permute-start | bytes 1179656 | tf_op jit(solution)/shard_map/ppermute | solution.py:33
  146.1 3.6 %collective-permute-start.17 = (bf16[320,512]{1,0:T(8,128)(2,1)}, bf16[320,512]{1,0:T(8,128)(2,1)}, u32[]{:S(2)}, u32[]{:S(2)}) collective-permute-start(bf16[320,512]{1,0:T(8,128)(2,1)} %pad_maximum_fusion.5), channel_id=1, source_target_pairs={{0,64},{1,65},{2,66},{3,67},{4,68},{5,69},{6,70},{7,71},{8,72},{9,... | collective-permute-start | bytes 983048 | tf_op jit(solution)/shard_map/ppermute | solution.py:43
  153.0 3.2 %collective-permute-start.23 = (bf16[384,512]{1,0:T(8,128)(2,1)}, bf16[384,512]{1,0:T(8,128)(2,1)}, u32[]{:S(2)}, u32[]{:S(2)}) collective-permute-start(bf16[384,512]{1,0:T(8,128)(2,1)} %slice.222), channel_id=1, source_target_pairs={{0,1},{1,0},{2,3},{3,2},{4,5},{5,4},{6,7},{7,6},{8,9},{9,8},{10,11... | collective-permute-start | bytes 1179656 | tf_op jit(solution)/shard_map/ppermute | solution.py:33
  156.6 3.4 %collective-permute-start.20 = (bf16[160,1024]{1,0:T(8,128)(2,1)}, bf16[160,1024]{1,0:T(8,128)(2,1)}, u32[]{:S(2)}, u32[]{:S(2)}) collective-permute-start(bf16[160,1024]{1,0:T(8,128)(2,1)} %get-tuple-element.47), channel_id=1, source_target_pairs={{0,4},{1,5},{2,6},{3,7},{4,8},{5,9},{6,10},{7,11},{8,12},{9,13},{1... | collective-permute-start | bytes 983048 | tf_op jit(solution)/shard_map/ppermute | solution.py:33
  162.8 3.4 %collective-permute-start.22 = (bf16[160,1024]{1,0:T(8,128)(2,1)}, bf16[160,1024]{1,0:T(8,128)(2,1)}, u32[]{:S(2)}, u32[]{:S(2)}) collective-permute-start(bf16[160,1024]{1,0:T(8,128)(2,1)} %get-tuple-element.49), channel_id=1, source_target_pairs={{0,12},{1,13},{2,14},{3,15},{4,0},{5,1},{6,2},{7,3},{8,4},{9,5},{1... | collective-permute-start | bytes 983048 | tf_op jit(solution)/shard_map/ppermute | solution.py:33
  167.4 9.2 %collective-permute-start.26 = (bf16[256,512]{1,0:T(8,128)(2,1)S(1)}, bf16[256,512]{1,0:T(8,128)(2,1)S(1)}, u32[]{:S(2)}, u32[]{:S(2)}) collective-permute-start(bf16[256,512]{1,0:T(8,128)(2,1)S(1)} %slice.161), channel_id=1, source_target_pairs={{0,2},{1,3},{2,0},{3,1},{4,6},{5,7},{6,4},{7,5},{8,10},{9,11},{10,... | collective-permute-start | bytes 786440 | tf_op jit(solution)/shard_map/ppermute | solution.py:33
  180.3 6.9 %collective-permute-start.25 = (bf16[256,512]{1,0:T(8,128)(2,1)S(1)}, bf16[256,512]{1,0:T(8,128)(2,1)S(1)}, u32[]{:S(2)}, u32[]{:S(2)}) collective-permute-start(bf16[256,512]{1,0:T(8,128)(2,1)S(1)} %slice.160), channel_id=1, source_target_pairs={{0,2},{1,3},{2,0},{3,1},{4,6},{5,7},{6,4},{7,5},{8,10},{9,11},{10,... | collective-permute-start | bytes 786440 | tf_op jit(solution)/shard_map/ppermute | solution.py:33
  189.8 7.6 %attention.1 = (bf16[128,512]{1,0:T(8,128)(2,1)}, bf16[128,512]{1,0:T(8,128)(2,1)}) custom-call(s32[1]{0:T(128)} %bitcast.32.refs_0_, bf16[384,512]{1,0:T(8,128)(2,1)} %copy-done.6, bf16[384,512]{1,0:T(8,128)(2,1)} %copy-done.5, bf16[256,512]{1,0:T(8,128)(2,1)} %copy-done.32, bf16[256,512]{1,0:T(8,128)(2,1)} %copy-done.31, ...), custom_call_target="tpu_custom_call" | custom-call | flops 1073741824 | bytes 786432 | tf_op jit(solution)/shard_map/attention/pallas_call | solution.py:127
  199.3 8.2 %collective-permute-start.28 = (bf16[128,512]{1,0:T(8,128)(2,1)}, bf16[128,512]{1,0:T(8,128)(2,1)S(1)}, u32[]{:S(2)}, u32[]{:S(2)}) collective-permute-start(bf16[128,512]{1,0:T(8,128)(2,1)} %get-tuple-element.54), channel_id=1, source_target_pairs={{0,65},{1,64},{2,67},{3,66},{4,69},{5,68},{6,71},{7,70},{8,73},{9,... | collective-permute-start | bytes 393224 | tf_op jit(solution)/shard_map/ppermute | solution.py:43
  207.6 6.2 %collective-permute-done.28 = bf16[128,512]{1,0:T(8,128)(2,1)S(1)} collective-permute-done((bf16[128,512]{1,0:T(8,128)(2,1)}, bf16[128,512]{1,0:T(8,128)(2,1)S(1)}, u32[]{:S(2)}, u32[]{:S(2)}) %collective-permute-start.28) | collective-permute-done | bytes 131104 | tf_op jit(solution)/shard_map/ppermute | solution.py:43
  213.8 5.9 %collective-permute-start.29 = (bf16[256,512]{1,0:T(8,128)(2,1)S(1)}, bf16[256,512]{1,0:T(8,128)(2,1)S(1)}, u32[]{:S(2)}, u32[]{:S(2)}) collective-permute-start(bf16[256,512]{1,0:T(8,128)(2,1)S(1)} %pad_maximum_fusion.9), channel_id=1, source_target_pairs={{0,32},{1,33},{2,34},{3,35},{4,36},{5,37},{6,38},{7,39},{8,40},{9,... | collective-permute-start | bytes 786440 | tf_op jit(solution)/shard_map/ppermute | solution.py:33
  225.0 3.3 %collective-permute-start.30 = (bf16[256,512]{1,0:T(8,128)(2,1)S(1)}, bf16[256,512]{1,0:T(8,128)(2,1)S(1)}, u32[]{:S(2)}, u32[]{:S(2)}) collective-permute-start(bf16[256,512]{1,0:T(8,128)(2,1)S(1)} %pad_maximum_fusion.9), channel_id=1, source_target_pairs={{0,16},{1,17},{2,18},{3,19},{4,20},{5,21},{6,22},{7,23},{8,24},{9,... | collective-permute-start | bytes 786440 | tf_op jit(solution)/shard_map/ppermute | solution.py:33
  228.3 3.4 %collective-permute-done.29 = bf16[256,512]{1,0:T(8,128)(2,1)S(1)} collective-permute-done((bf16[256,512]{1,0:T(8,128)(2,1)S(1)}, bf16[256,512]{1,0:T(8,128)(2,1)S(1)}, u32[]{:S(2)}, u32[]{:S(2)}) %collective-permute-start.29) | collective-permute-done | bytes 262176 | tf_op jit(solution)/shard_map/ppermute | solution.py:33
  238.5 4.9 %collective-permute-done.31 = bf16[256,512]{1,0:T(8,128)(2,1)S(1)} collective-permute-done((bf16[256,512]{1,0:T(8,128)(2,1)S(1)}, bf16[256,512]{1,0:T(8,128)(2,1)S(1)}, u32[]{:S(2)}, u32[]{:S(2)}) %collective-permute-start.31) | collective-permute-done | bytes 262176 | tf_op jit(solution)/shard_map/ppermute | solution.py:33
  248.3 3.2 %collective-permute-start.34 = (bf16[320,512]{1,0:T(8,128)(2,1)S(1)}, bf16[320,512]{1,0:T(8,128)(2,1)S(1)}, u32[]{:S(2)}, u32[]{:S(2)}) collective-permute-start(bf16[320,512]{1,0:T(8,128)(2,1)S(1)} %pad_maximum_fusion.7), channel_id=1, source_target_pairs={{0,8},{1,9},{2,10},{3,11},{4,12},{5,13},{6,14},{7,15},{8,0},{9,1},... | collective-permute-start | bytes 983048 | tf_op jit(solution)/shard_map/ppermute | solution.py:33
  256.0 4.1 %collective-permute-done.34 = bf16[320,512]{1,0:T(8,128)(2,1)S(1)} collective-permute-done((bf16[320,512]{1,0:T(8,128)(2,1)S(1)}, bf16[320,512]{1,0:T(8,128)(2,1)S(1)}, u32[]{:S(2)}, u32[]{:S(2)}) %collective-permute-start.34) | collective-permute-done | bytes 327712 | tf_op jit(solution)/shard_map/ppermute | solution.py:33
  260.2 8.2 %collective-permute-done.35 = bf16[320,512]{1,0:T(8,128)(2,1)S(1)} collective-permute-done((bf16[320,512]{1,0:T(8,128)(2,1)S(1)}, bf16[320,512]{1,0:T(8,128)(2,1)S(1)}, u32[]{:S(2)}, u32[]{:S(2)}) %collective-permute-start.35) | collective-permute-done | bytes 327712 | tf_op jit(solution)/shard_map/ppermute | solution.py:33
  (208 shorter events, 97.8 us)
Async XLA Ops:
  1.9 12.3 %collective-permute-start = (bf16[176,512]{1,0:T(8,128)(2,1)S(1)}, bf16[176,512]{1,0:T(8,128)(2,1)S(1)}, u32[]{:S(2)}, u32[]{:S(2)}) collective-permute-start(bf16[176,512]{1,0:T(8,128)(2,1)S(1)} %fusion.43), channel_id=1, source_target_pairs={{0,2},{1,3},{2,0},{3,1},{4,6},{5,7},{6,4},{7,5},{8,10},{9,11},{10,... | collective-permute-start | bytes 540680 | tf_op jit(solution)/shard_map/ppermute | solution.py:33
  10.7 15.3 %collective-permute-start.2 = (bf16[160,512]{1,0:T(8,128)(2,1)S(1)}, bf16[160,512]{1,0:T(8,128)(2,1)S(1)}, u32[]{:S(2)}, u32[]{:S(2)}) collective-permute-start(bf16[160,512]{1,0:T(8,128)(2,1)S(1)} %get-tuple-element.89), channel_id=1, source_target_pairs={{0,2},{1,34},{2,0},{3,32},{4,6},{5,38},{6,4},{7,36},{8,10},{9,42},... | collective-permute-start | bytes 491528 | tf_op jit(solution)/shard_map/ppermute | solution.py:33
  12.6 13.4 %collective-permute-start.1 = (bf16[160,512]{1,0:T(8,128)(2,1)S(1)}, bf16[160,512]{1,0:T(8,128)(2,1)S(1)}, u32[]{:S(2)}, u32[]{:S(2)}) collective-permute-start(bf16[160,512]{1,0:T(8,128)(2,1)S(1)} %get-tuple-element.90), channel_id=1, source_target_pairs={{0,0},{1,32},{2,2},{3,34},{4,4},{5,36},{6,6},{7,38},{8,8},{9,40},{... | collective-permute-start | bytes 491528 | tf_op jit(solution)/shard_map/ppermute | solution.py:33
  23.3 9.9 %collective-permute-start.8 = (f32[18,512]{1,0:T(8,128)S(1)}, f32[18,512]{1,0:T(8,128)S(1)}, u32[]{:S(2)}, u32[]{:S(2)}) collective-permute-start(f32[18,512]{1,0:T(8,128)S(1)} %pad_maximum_fusion.18), channel_id=1, source_target_pairs={{0,4},{1,5},{2,6},{3,7},{4,0},{5,1},{6,2},{7,3},{8,12},{9,13},{10,... | collective-permute-start | bytes 110600 | tf_op jit(solution)/shard_map/ppermute | solution.py:33
  29.1 18.9 %collective-permute-start.3 = (bf16[320,512]{1,0:T(8,128)(2,1)}, bf16[320,512]{1,0:T(8,128)(2,1)S(1)}, u32[]{:S(2)}, u32[]{:S(2)}) collective-permute-start(bf16[320,512]{1,0:T(8,128)(2,1)} %stacked_rows.4.refs_0_), channel_id=1, source_target_pairs={{0,32},{1,33},{2,34},{3,35},{4,36},{5,37},{6,38},{7,39},{8,40},{9,... | collective-permute-start | bytes 983048 | tf_op jit(solution)/shard_map/ppermute | solution.py:33
  33.3 14.6 %collective-permute-start.9 = (bf16[320,512]{1,0:T(8,128)(2,1)}, bf16[320,512]{1,0:T(8,128)(2,1)S(1)}, u32[]{:S(2)}, u32[]{:S(2)}) collective-permute-start(bf16[320,512]{1,0:T(8,128)(2,1)} %stacked_rows.4.refs_0_), channel_id=1, source_target_pairs={{0,16},{1,17},{2,18},{3,19},{4,20},{5,21},{6,22},{7,23},{8,24},{9,... | collective-permute-start | bytes 983048 | tf_op jit(solution)/shard_map/ppermute | solution.py:33
  50.7 30.1 %collective-permute-start.10 = (bf16[640,512]{1,0:T(8,128)(2,1)}, bf16[640,512]{1,0:T(8,128)(2,1)}, u32[]{:S(2)}, u32[]{:S(2)}) collective-permute-start(bf16[640,512]{1,0:T(8,128)(2,1)} %stacked_rows.6), channel_id=1, source_target_pairs={{0,4},{1,5},{2,14},{3,15},{4,8},{5,9},{6,2},{7,3},{8,12},{9,13},{1... | collective-permute-start | bytes 1966088 | tf_op jit(solution)/shard_map/ppermute | solution.py:33
  56.0 53.7 %collective-permute-start.12 = (bf16[2560,384]{1,0:T(8,128)(2,1)S(1)}, bf16[2560,384]{1,0:T(8,128)(2,1)}, u32[]{:S(2)}, u32[]{:S(2)}) collective-permute-start(bf16[2560,384]{1,0:T(8,128)(2,1)S(1)} %bitcast.70), channel_id=1, source_target_pairs={{0,2},{1,3},{2,0},{3,1},{4,6},{5,7},{6,4},{7,5},{8,10},{9,11},{10,... | collective-permute-start | bytes 5898248 | tf_op jit(solution)/shard_map/ppermute | solution.py:33
  59.9 68.5 %collective-permute-start.19 = (bf16[160,4096]{1,0:T(8,128)(2,1)}, bf16[160,4096]{1,0:T(8,128)(2,1)}, u32[]{:S(2)}, u32[]{:S(2)}) collective-permute-start(bf16[160,4096]{1,0:T(8,128)(2,1)} %bitcast.86), channel_id=1, source_target_pairs={{0,64},{1,65},{2,66},{3,67},{4,68},{5,69},{6,70},{7,71},{8,72},{9,... | collective-permute-start | bytes 3932168 | tf_op jit(solution)/shard_map/ppermute | solution.py:43
  64.0 11.0 %collective-permute-start.4 = (bf16[320,512]{1,0:T(8,128)(2,1)S(1)}, bf16[320,512]{1,0:T(8,128)(2,1)S(1)}, u32[]{:S(2)}, u32[]{:S(2)}) collective-permute-start(bf16[320,512]{1,0:T(8,128)(2,1)S(1)} %collective-permute-done.3.refs_0_), channel_id=1, source_target_pairs={{0,16},{1,17},{2,18},{3,19},{4,20},{5,21},{6,22},{7,23},{8,24},{9,... | collective-permute-start | bytes 983048 | tf_op jit(solution)/shard_map/ppermute | solution.py:33
  77.7 18.7 %collective-permute-start.5 = (bf16[640,512]{1,0:T(8,128)(2,1)}, bf16[640,512]{1,0:T(8,128)(2,1)}, u32[]{:S(2)}, u32[]{:S(2)}) collective-permute-start(bf16[640,512]{1,0:T(8,128)(2,1)} %stacked_rows.5), channel_id=1, source_target_pairs={{0,4},{1,5},{2,14},{3,15},{4,8},{5,9},{6,2},{7,3},{8,12},{9,13},{1... | collective-permute-start | bytes 1966088 | tf_op jit(solution)/shard_map/ppermute | solution.py:33
  80.8 16.4 %collective-permute-start.11 = (bf16[640,512]{1,0:T(8,128)(2,1)}, bf16[640,512]{1,0:T(8,128)(2,1)}, u32[]{:S(2)}, u32[]{:S(2)}) collective-permute-start(bf16[640,512]{1,0:T(8,128)(2,1)} %collective-permute-done.10), channel_id=1, source_target_pairs={{0,4},{1,5},{2,14},{3,15},{4,8},{5,9},{6,2},{7,3},{8,12},{9,13},{1... | collective-permute-start | bytes 1966088 | tf_op jit(solution)/shard_map/ppermute | solution.py:33
  97.2 12.2 %collective-permute-start.15 = (f32[18,512]{1,0:T(8,128)S(1)}, f32[18,512]{1,0:T(8,128)S(1)}, u32[]{:S(2)}, u32[]{:S(2)}) collective-permute-start(f32[18,512]{1,0:T(8,128)S(1)} %add.453), channel_id=1, source_target_pairs={{0,32},{1,33},{2,34},{3,35},{4,36},{5,37},{6,38},{7,39},{8,40},{9,... | collective-permute-start | bytes 110600 | tf_op jit(solution)/shard_map/ppermute | solution.py:33
  100.3 22.5 %collective-permute-start.6 = (bf16[640,512]{1,0:T(8,128)(2,1)}, bf16[640,512]{1,0:T(8,128)(2,1)}, u32[]{:S(2)}, u32[]{:S(2)}) collective-permute-start(bf16[640,512]{1,0:T(8,128)(2,1)} %collective-permute-done.5), channel_id=1, source_target_pairs={{0,4},{1,5},{2,14},{3,15},{4,8},{5,9},{6,2},{7,3},{8,12},{9,13},{1... | collective-permute-start | bytes 1966088 | tf_op jit(solution)/shard_map/ppermute | solution.py:33
  122.9 14.0 %collective-permute-start.16 = (bf16[640,512]{1,0:T(8,128)(2,1)}, bf16[640,512]{1,0:T(8,128)(2,1)}, u32[]{:S(2)}, u32[]{:S(2)}) collective-permute-start(bf16[640,512]{1,0:T(8,128)(2,1)} %collective-permute-done.6), channel_id=1, source_target_pairs={{0,4},{1,5},{2,14},{3,15},{4,8},{5,9},{6,2},{7,3},{8,12},{9,13},{1... | collective-permute-start | bytes 1966088 | tf_op jit(solution)/shard_map/ppermute | solution.py:33
  132.7 17.0 %collective-permute-start.18 = (bf16[640,512]{1,0:T(8,128)(2,1)}, bf16[640,512]{1,0:T(8,128)(2,1)S(1)}, u32[]{:S(2)}, u32[]{:S(2)}) collective-permute-start(bf16[640,512]{1,0:T(8,128)(2,1)} %collective-permute-done.11), channel_id=1, source_target_pairs={{0,4},{1,5},{2,14},{3,15},{4,8},{5,9},{6,2},{7,3},{8,12},{9,13},{1... | collective-permute-start | bytes 1966088 | tf_op jit(solution)/shard_map/ppermute | solution.py:33
  139.6 26.6 %collective-permute-start.24 = (bf16[384,512]{1,0:T(8,128)(2,1)S(1)}, bf16[384,512]{1,0:T(8,128)(2,1)}, u32[]{:S(2)}, u32[]{:S(2)}) collective-permute-start(bf16[384,512]{1,0:T(8,128)(2,1)S(1)} %slice.223), channel_id=1, source_target_pairs={{0,1},{1,0},{2,3},{3,2},{4,5},{5,4},{6,7},{7,6},{8,9},{9,8},{10,11... | collective-permute-start | bytes 1179656 | tf_op jit(solution)/shard_map/ppermute | solution.py:33
  146.1 16.7 %collective-permute-start.17 = (bf16[320,512]{1,0:T(8,128)(2,1)}, bf16[320,512]{1,0:T(8,128)(2,1)}, u32[]{:S(2)}, u32[]{:S(2)}) collective-permute-start(bf16[320,512]{1,0:T(8,128)(2,1)} %pad_maximum_fusion.5), channel_id=1, source_target_pairs={{0,64},{1,65},{2,66},{3,67},{4,68},{5,69},{6,70},{7,71},{8,72},{9,... | collective-permute-start | bytes 983048 | tf_op jit(solution)/shard_map/ppermute | solution.py:43
  153.0 26.1 %collective-permute-start.23 = (bf16[384,512]{1,0:T(8,128)(2,1)}, bf16[384,512]{1,0:T(8,128)(2,1)}, u32[]{:S(2)}, u32[]{:S(2)}) collective-permute-start(bf16[384,512]{1,0:T(8,128)(2,1)} %slice.222), channel_id=1, source_target_pairs={{0,1},{1,0},{2,3},{3,2},{4,5},{5,4},{6,7},{7,6},{8,9},{9,8},{10,11... | collective-permute-start | bytes 1179656 | tf_op jit(solution)/shard_map/ppermute | solution.py:33
  156.6 31.8 %collective-permute-start.20 = (bf16[160,1024]{1,0:T(8,128)(2,1)}, bf16[160,1024]{1,0:T(8,128)(2,1)}, u32[]{:S(2)}, u32[]{:S(2)}) collective-permute-start(bf16[160,1024]{1,0:T(8,128)(2,1)} %get-tuple-element.47), channel_id=1, source_target_pairs={{0,4},{1,5},{2,6},{3,7},{4,8},{5,9},{6,10},{7,11},{8,12},{9,13},{1... | collective-permute-start | bytes 983048 | tf_op jit(solution)/shard_map/ppermute | solution.py:33
  159.9 28.5 %collective-permute-start.21 = (bf16[160,1024]{1,0:T(8,128)(2,1)}, bf16[160,1024]{1,0:T(8,128)(2,1)}, u32[]{:S(2)}, u32[]{:S(2)}) collective-permute-start(bf16[160,1024]{1,0:T(8,128)(2,1)} %get-tuple-element.48), channel_id=1, source_target_pairs={{0,8},{1,9},{2,10},{3,11},{4,12},{5,13},{6,14},{7,15},{8,0},{9,1},... | collective-permute-start | bytes 983048 | tf_op jit(solution)/shard_map/ppermute | solution.py:33
  162.8 25.6 %collective-permute-start.22 = (bf16[160,1024]{1,0:T(8,128)(2,1)}, bf16[160,1024]{1,0:T(8,128)(2,1)}, u32[]{:S(2)}, u32[]{:S(2)}) collective-permute-start(bf16[160,1024]{1,0:T(8,128)(2,1)} %get-tuple-element.49), channel_id=1, source_target_pairs={{0,12},{1,13},{2,14},{3,15},{4,0},{5,1},{6,2},{7,3},{8,4},{9,5},{1... | collective-permute-start | bytes 983048 | tf_op jit(solution)/shard_map/ppermute | solution.py:33
  167.4 21.0 %collective-permute-start.26 = (bf16[256,512]{1,0:T(8,128)(2,1)S(1)}, bf16[256,512]{1,0:T(8,128)(2,1)S(1)}, u32[]{:S(2)}, u32[]{:S(2)}) collective-permute-start(bf16[256,512]{1,0:T(8,128)(2,1)S(1)} %slice.161), channel_id=1, source_target_pairs={{0,2},{1,3},{2,0},{3,1},{4,6},{5,7},{6,4},{7,5},{8,10},{9,11},{10,... | collective-permute-start | bytes 786440 | tf_op jit(solution)/shard_map/ppermute | solution.py:33
  197.4 10.2 %collective-permute-start.27 = (bf16[128,512]{1,0:T(8,128)(2,1)}, bf16[128,512]{1,0:T(8,128)(2,1)S(1)}, u32[]{:S(2)}, u32[]{:S(2)}) collective-permute-start(bf16[128,512]{1,0:T(8,128)(2,1)} %get-tuple-element.53), channel_id=1, source_target_pairs={{0,64},{1,65},{2,66},{3,67},{4,68},{5,69},{6,70},{7,71},{8,72},{9,... | collective-permute-start | bytes 393224 | tf_op jit(solution)/shard_map/ppermute | solution.py:43
  199.3 14.5 %collective-permute-start.28 = (bf16[128,512]{1,0:T(8,128)(2,1)}, bf16[128,512]{1,0:T(8,128)(2,1)S(1)}, u32[]{:S(2)}, u32[]{:S(2)}) collective-permute-start(bf16[128,512]{1,0:T(8,128)(2,1)} %get-tuple-element.54), channel_id=1, source_target_pairs={{0,65},{1,64},{2,67},{3,66},{4,69},{5,68},{6,71},{7,70},{8,73},{9,... | collective-permute-start | bytes 393224 | tf_op jit(solution)/shard_map/ppermute | solution.py:43
  213.8 17.9 %collective-permute-start.29 = (bf16[256,512]{1,0:T(8,128)(2,1)S(1)}, bf16[256,512]{1,0:T(8,128)(2,1)S(1)}, u32[]{:S(2)}, u32[]{:S(2)}) collective-permute-start(bf16[256,512]{1,0:T(8,128)(2,1)S(1)} %pad_maximum_fusion.9), channel_id=1, source_target_pairs={{0,32},{1,33},{2,34},{3,35},{4,36},{5,37},{6,38},{7,39},{8,40},{9,... | collective-permute-start | bytes 786440 | tf_op jit(solution)/shard_map/ppermute | solution.py:33
  222.3 21.6 %collective-permute-start.32 = (bf16[640,1024]{1,0:T(8,128)(2,1)}, bf16[640,1024]{1,0:T(8,128)(2,1)S(1)}, u32[]{:S(2)}, u32[]{:S(2)}) collective-permute-start(bf16[640,1024]{1,0:T(8,128)(2,1)} %stacked_rows.7), channel_id=1, source_target_pairs={{0,2},{1,3},{2,0},{3,1},{4,6},{5,7},{6,4},{7,5},{8,10},{9,11},{10,... | collective-permute-start | bytes 3932168 | tf_op jit(solution)/shard_map/ppermute | solution.py:33
  225.0 12.8 %collective-permute-start.30 = (bf16[256,512]{1,0:T(8,128)(2,1)S(1)}, bf16[256,512]{1,0:T(8,128)(2,1)S(1)}, u32[]{:S(2)}, u32[]{:S(2)}) collective-permute-start(bf16[256,512]{1,0:T(8,128)(2,1)S(1)} %pad_maximum_fusion.9), channel_id=1, source_target_pairs={{0,16},{1,17},{2,18},{3,19},{4,20},{5,21},{6,22},{7,23},{8,24},{9,... | collective-permute-start | bytes 786440 | tf_op jit(solution)/shard_map/ppermute | solution.py:33
  231.7 11.7 %collective-permute-start.31 = (bf16[256,512]{1,0:T(8,128)(2,1)S(1)}, bf16[256,512]{1,0:T(8,128)(2,1)S(1)}, u32[]{:S(2)}, u32[]{:S(2)}) collective-permute-start(bf16[256,512]{1,0:T(8,128)(2,1)S(1)} %collective-permute-done.29), channel_id=1, source_target_pairs={{0,16},{1,17},{2,18},{3,19},{4,20},{5,21},{6,22},{7,23},{8,24},{9,... | collective-permute-start | bytes 786440 | tf_op jit(solution)/shard_map/ppermute | solution.py:33
  245.3 10.7 %collective-permute-start.33 = (bf16[320,512]{1,0:T(8,128)(2,1)S(1)}, bf16[320,512]{1,0:T(8,128)(2,1)S(1)}, u32[]{:S(2)}, u32[]{:S(2)}) collective-permute-start(bf16[320,512]{1,0:T(8,128)(2,1)S(1)} %pad_maximum_fusion.6), channel_id=1, source_target_pairs={{0,12},{1,13},{2,14},{3,15},{4,0},{5,1},{6,2},{7,3},{8,4},{9,5},{1... | collective-permute-start | bytes 983048 | tf_op jit(solution)/shard_map/ppermute | solution.py:33
  248.3 11.9 %collective-permute-start.34 = (bf16[320,512]{1,0:T(8,128)(2,1)S(1)}, bf16[320,512]{1,0:T(8,128)(2,1)S(1)}, u32[]{:S(2)}, u32[]{:S(2)}) collective-permute-start(bf16[320,512]{1,0:T(8,128)(2,1)S(1)} %pad_maximum_fusion.7), channel_id=1, source_target_pairs={{0,8},{1,9},{2,10},{3,11},{4,12},{5,13},{6,14},{7,15},{8,0},{9,1},... | collective-permute-start | bytes 983048 | tf_op jit(solution)/shard_map/ppermute | solution.py:33
  251.6 16.8 %collective-permute-start.35 = (bf16[320,512]{1,0:T(8,128)(2,1)S(1)}, bf16[320,512]{1,0:T(8,128)(2,1)S(1)}, u32[]{:S(2)}, u32[]{:S(2)}) collective-permute-start(bf16[320,512]{1,0:T(8,128)(2,1)S(1)} %pad_maximum_fusion.8), channel_id=1, source_target_pairs={{0,4},{1,5},{2,6},{3,7},{4,8},{5,9},{6,10},{7,11},{8,12},{9,13},{1... | collective-permute-start | bytes 983048 | tf_op jit(solution)/shard_map/ppermute | solution.py:33
  (39 other events, 510.4 us)

commit v10 on v5

--- a/solution.py
+++ b/solution.py
@@ -2,6 +2,7 @@
 
 import jax
 import jax.numpy as jnp
+import numpy as np
 from jax import lax
 from jax.experimental import pallas as pl
 from jax.experimental.pallas import tpu as pltpu
@@ -11,6 +12,7 @@
 PLANE = ("yl", "x", "core", "seq")
 DP = ("yl", "x", "core")
 NEG = -1e30
+TOP = 3.38e38
 
 
 def pairs_of(where):
@@ -222,6 +224,15 @@
     return y, (x + 1 - 2 * core) % 4, core
 
 
+def three_rows(values):
+    values = jnp.minimum(values, TOP)
+    high = lax.reduce_precision(values, 8, 7)
+    middle = lax.reduce_precision(values - high, 8, 7)
+    rows = [high, middle, values - high - middle]
+    rows = jnp.concatenate([row.astype(jnp.bfloat16) for row in rows], axis=0)
+    return jnp.pad(rows, ((0, 13), (0, 0)))
+
+
 def same(y, x, core):
     return y, x, core
 
@@ -239,39 +250,24 @@
         halves = array[:, :step], array[:, step:]
         return jnp.where(core == 0, *halves), jnp.where(core == 0, *halves[::-1])
 
-    own, away = of_core(tokens_t)
+    as_float = tokens_t.astype(f32)
+    gained = jnp.clip(as_float * norm_gain.astype(f32).T, -TOP, TOP).astype(bf16)
+    squares = jnp.sum(as_float * as_float, axis=0, keepdims=True)
+    own, away = of_core(jnp.concatenate([gained, three_rows(squares)], axis=0))
     crossed = moved(away, lambda *at: other_core(*swap_inner(*at)))
     e = stacked_rows(moved(own, swap_inner), crossed)
+    random = random_blocks[0]
+    random = jnp.stack([moved(random, other_seq), random])
+    f = moved(e, by_two)
+    e_two = stacked_rows(e, moved(after(e, random), pair))
+    f_two = stacked_rows(f, moved(f, pair))
+
     out_next = moved_on(out_weight[0].T, same)
 
-    gain = norm_gain
-    gain_row = jnp.pad(gain, ((0, 15), (0, step - part)))
-    beside = moved(jnp.concatenate([away, gain_row], axis=0), other_core)
-    gain = jnp.concatenate([gain, beside[part : part + 1, :part]], axis=1).astype(f32)
-    item = jnp.concatenate([own, beside[:part]], axis=0)
-    as_float = item.astype(f32)
-    squares = jnp.sum(as_float * as_float, axis=0)
+    own, away = of_core(tokens_t)
+    beside = moved(away, other_core)
+    item = jnp.concatenate([own, beside], axis=0)
     residual = moved_on(item, same)
-    random = random_blocks[0]
-    numbers = jnp.pad(random.astype(f32).reshape(-1), (0, step - random.size))
-    mine = jnp.stack([squares, numbers])
-    theirs = moved(mine, other_seq)
-    random = jnp.stack([theirs[1, : random.size].astype(jnp.int32).reshape(random.shape), random])
-    slot = (yl * 4 + x == jnp.arange(16))[:, None]
-    table = jnp.where(slot, jnp.pad(gain, ((0, 0), (0, step - 2 * part))), 0.0)
-    table = jnp.concatenate([table, mine[:1], theirs[:1]], axis=0)
-    table = table + moved(table, lambda y, x, c: (y, x ^ 1, c))
-    e = after(e, table)
-    f = moved(e, by_two)
-    e_two = stacked_rows(e, moved(e, pair))
-    f_two = stacked_rows(f, moved(f, pair))
-    for where in (lambda y, x, c: (y, x ^ 2, c), pair, by_two):
-        table = table + moved(table, where)
-    factors = lax.rsqrt(table[16:] / width + 1e-05)
-    factor_e = jnp.where(first == seq, factors[:1], factors[1:])
-    factor_f = jnp.where(first == seq, factors[1:], factors[:1])
-    gains = table[:16, : 2 * part].reshape(2, 2, 4, 2 * part)
-    gains = at_index(gains, seq)
 
     weight = after(qkv_weight[0], beside)
     beside = moved(weight, other_core)
@@ -279,22 +275,24 @@
     weight = jnp.concatenate(
         [jnp.where(core == seq, weight, beside), jnp.where(core == seq, beside, weight)], axis=1
     )
-    weight = weight.reshape(2, 4, 2, part, 2 * columns)
-    weights, scales = [], []
+    weight = weight.reshape(16, part, 2 * columns)
+    adding = np.zeros((1, part + 16, 2 * columns + 128), np.float32)
+    adding[0, part : part + 3, 2 * columns] = 1.0
+    weight = jnp.pad(weight, ((0, 0), (0, 16), (0, 128))) + jnp.asarray(adding, bf16)
+    weight = weight.reshape(2, 4, 2, part + 16, 2 * columns + 128)
+    weights = []
     for k in range(4):
         source = (x - (1 - 2 * core) * k) % 4
-        rows, scale = [], []
+        rows = []
         for ab in range(2):
-            which = ab ^ (yl % 2)
-            block = at_index(at_index(weight, which), source)
+            block = at_index(at_index(weight, ab ^ (yl % 2)), source)
             rows += [at_index(block, core), at_index(block, 1 - core)]
-            scale.append(at_index(at_index(gains, which), source))
-        weights.append(jnp.concatenate(rows, axis=0).T)
-        scales.append(jnp.concatenate(scale).reshape(4 * part, 1))
-
-    def project(block, k, factor):
-        normed = (block.astype(f32) * factor * scales[k]).astype(bf16)
-        return jnp.dot(weights[k], normed, preferred_element_type=f32)
+        weights.append(jnp.concatenate(rows, axis=0))
+
+    def project(block, k):
+        return lax.dot_general(
+            weights[k], block, (((0,), (0,)), ((), ())), preferred_element_type=f32
+        )
 
     count = step // BLOCK
     rows = lax.dynamic_slice_in_dim(random, core * count, count, axis=1).reshape(2 * count, -1)
@@ -312,15 +310,24 @@
     bias = jnp.repeat(jnp.where(allowed.T, 0.0, NEG), BLOCK, axis=1).astype(bf16)
 
     e, f = e_two, f_two
-    partial_e, partial_f = project(e, 0, factor_e), project(f, 0, factor_f)
+    partial_e, partial_f = project(e, 0), project(f, 0)
     for k in range(1, 4):
         e, f = moved(e, around), moved(f, around)
-        partial_e = partial_e + project(e, k, factor_e)
-        partial_f = partial_f + project(f, k, factor_f)
+        partial_e = partial_e + project(e, k)
+        partial_f = partial_f + project(f, k)
     order = after(jnp.stack([yl, yl ^ 2, yl ^ 1, yl ^ 3]), f_two)
     ring = (x + jnp.arange(4, dtype=jnp.int32)) % 4
     slices = column_slices(out_next, order, ring)
-    sends = [partial[columns:].astype(bf16) for partial in (partial_e, partial_f)]
+    sends = [
+        jnp.concatenate(
+            [
+                partial[columns : 2 * columns].astype(bf16),
+                three_rows(partial[2 * columns : 2 * columns + 1]),
+            ],
+            axis=0,
+        )
+        for partial in (partial_e, partial_f)
+    ]
     sends[0], slices = lax.optimization_barrier((sends[0], slices))
     out_own = [slices[0]]
     for r in range(1, 4):
@@ -329,7 +336,12 @@
     head = columns // 3
     for partial, send in zip((partial_e, partial_f), sends):
         came = moved(send, other_seq)
-        joined.append((partial[:columns] + came.astype(f32)).astype(bf16))
+        came = after(came, sends[1]).astype(f32)
+        squares = partial[2 * columns : 2 * columns + 1]
+        squares = squares + jnp.sum(came[columns : columns + 3], axis=0, keepdims=True)
+        factor = jnp.where(squares < TOP, lax.rsqrt(squares / width + 1e-05), 0.0)
+        normed = (partial[:columns] + came[:columns]) * factor
+        joined.append(jnp.where(factor > 0, normed, 0.0).astype(bf16))
         other.append(moved(joined[-1][head:], other_core))
 
     flag = after((first == seq).astype(jnp.int32).reshape(1), (out_own, residual))

time: 254 us -> 265 us (1.043)
  waiting for transfers between devices: 61.5 us -> 68.2 us
  starting transfers between devices: 135 us -> 139 us
    ppermute x33 -> x29, waiting for transfers between devices: 61.5 us -> 68.2 us  [moved(): return lax.ppermute(value, PLANE, pairs_of(where))]
    ppermute x33 -> x29, starting transfers between devices: 117 us -> 122 us  [moved(): return lax.ppermute(value, PLANE, pairs_of(where))]
  transfers between devices with their start and end apart: 37 -> 33, of which waited for: 15 -> 11; matrix products, arithmetic and copies ran while one was open for 10% -> 10% of each run, Pallas kernels for 5% -> 5%
where the time goes in v10:
time: 265 us; the launch traced here: 263 us
  starting transfers between devices  139 us (52%)
  waiting for transfers between devices  68.2 us (26%)
  Pallas kernels  20.1 us (8%)
  matrix products  14.3 us (5%)
  other arithmetic  12.6 us (5%)
  local copies, waits for them, and re-layouts  7.35 us (3%)
    ppermute x29, starting transfers between devices, moved(): return lax.ppermute(value, PLANE, pairs_of(where))  122 us
    ppermute x29, waiting for transfers between devices, moved(): return lax.ppermute(value, PLANE, pairs_of(where))  68.2 us
    ppermute x4, starting transfers between devices, moved_on(): return lax.ppermute(value, ('section', *PLANE), pairs)  17 us
    dot_general x8, matrix products, project(): lax.dot_general(weights[k], block, (((0,), (0,)), ((), ())), preferred_el...  10.7 us
    pallas_call x4, Pallas kernels, stacked_rows(): pl.pallas_call(rows_kernel, in_specs=[vmem] * len(parts), out_specs=vmem,...  8.29 us
    pallas_call x1, Pallas kernels, attention(): pl.pallas_call(lambda *refs: attention_kernel(1.0 / math.sqrt(size), per,...  7.59 us
  transfers between devices with their start and end apart: 33, of which 11 were waited for; matrix products, arithmetic and copies ran while one was open for 10% of the time, Pallas kernels for 5%

profile of v10, /device:TPU:1, one launch (start us, length us, event | category | flops | bytes accessed | tf_op | source)
XLA Modules:
  0.0 262.9 jit_solution(4380018958747977434)
XLA Ops:
  1.2 8.8 %collective-permute-start = (bf16[160,512]{1,0:T(8,128)(2,1)S(1)}, bf16[160,512]{1,0:T(8,128)(2,1)S(1)}, u32[]{:S(2)}, u32[]{:S(2)}) collective-permute-start(bf16[160,512]{1,0:T(8,128)(2,1)S(1)} %get-tuple-element.78), channel_id=1, source_target_pairs={{0,2},{1,3},{2,0},{3,1},{4,6},{5,7},{6,4},{7,5},{8,10},{9,11},{10,... | collective-permute-start | bytes 491528 | tf_op jit(solution)/shard_map/ppermute | solution.py:35
  14.5 2.5 collective-permute-start.2
  24.1 20.5 %collective-permute-start.5 = (s32[16,3]{0,1:T(4,128)S(1)}, s32[16,3]{0,1:T(4,128)S(1)}, u32[]{:S(2)}, u32[]{:S(2)}) collective-permute-start(s32[16,3]{0,1:T(4,128)S(1)} %bitcast.92), channel_id=1, source_target_pairs={{0,1},{1,0},{2,3},{3,2},{4,5},{5,4},{6,7},{7,6},{8,9},{9,8},{10,11... | collective-permute-start | bytes 584 | tf_op jit(solution)/shard_map/ppermute | solution.py:35
  48.7 4.4 %collective-permute-start.7 = (bf16[704,512]{1,0:T(8,128)(2,1)}, bf16[704,512]{1,0:T(8,128)(2,1)}, u32[]{:S(2)}, u32[]{:S(2)}) collective-permute-start(bf16[704,512]{1,0:T(8,128)(2,1)} %stacked_rows.5), channel_id=1, source_target_pairs={{0,4},{1,5},{2,14},{3,15},{4,8},{5,9},{6,2},{7,3},{8,12},{9,13},{1... | collective-permute-start | bytes 2162696 | tf_op jit(solution)/shard_map/ppermute | solution.py:35
  53.2 12.3 %collective-permute-done.10.refs_0_ = bf16[352,512]{1,0:T(8,128)(2,1)} collective-permute-done((bf16[352,512]{1,0:T(8,128)(2,1)}, bf16[352,512]{1,0:T(8,128)(2,1)}, u32[]{:S(2)}, u32[]{:S(2)}) %collective-permute-start.10) | collective-permute-done | bytes 360480 | tf_op jit(solution)/shard_map/ppermute | solution.py:35
  67.6 9.6 %collective-permute-done.11.refs_1_ = bf16[352,512]{1,0:T(8,128)(2,1)} collective-permute-done((bf16[352,512]{1,0:T(8,128)(2,1)}, bf16[352,512]{1,0:T(8,128)(2,1)}, u32[]{:S(2)}, u32[]{:S(2)}) %collective-permute-start.11) | collective-permute-done | bytes 360480 | tf_op jit(solution)/shard_map/ppermute | solution.py:35
  79.3 4.4 %collective-permute-start.17 = (bf16[704,512]{1,0:T(8,128)(2,1)}, bf16[704,512]{1,0:T(8,128)(2,1)}, u32[]{:S(2)}, u32[]{:S(2)}) collective-permute-start(bf16[704,512]{1,0:T(8,128)(2,1)} %stacked_rows.6), channel_id=1, source_target_pairs={{0,4},{1,5},{2,14},{3,15},{4,8},{5,9},{6,2},{7,3},{8,12},{9,13},{1... | collective-permute-start | bytes 2162696 | tf_op jit(solution)/shard_map/ppermute | solution.py:35
  83.7 2.5 collective-permute-start.8
  89.6 4.0 %collective-permute-start.1 = (bf16[320,512]{1,0:T(8,128)(2,1)}, bf16[320,512]{1,0:T(8,128)(2,1)}, u32[]{:S(2)}, u32[]{:S(2)}) collective-permute-start(bf16[320,512]{1,0:T(8,128)(2,1)} %pad_maximum_fusion.7), channel_id=1, source_target_pairs={{0,64},{1,65},{2,66},{3,67},{4,68},{5,69},{6,70},{7,71},{8,72},{9,... | collective-permute-start | bytes 983048 | tf_op jit(solution)/shard_map/ppermute | solution.py:45
  94.7 4.2 %column_slices.1 = (bf16[160,1024]{1,0:T(8,128)(2,1)}, bf16[160,1024]{1,0:T(8,128)(2,1)}, bf16[160,1024]{1,0:T(8,128)(2,1)}, bf16[160,1024]{1,0:T(8,128)(2,1)}) custom-call(s32[4]{0:T(128)} %pad_add_fusion.2.order_ref, s32[4]{0:T(128)} %and_select_fusion.ring_ref, bf16[160,4096]{1,0:T(8,128)(2,1)} %copy-done.2), custom_call_target="tpu_custom_call" | custom-call | bytes 2621440 | tf_op jit(solution)/shard_map/column_slices/pallas_call | solution.py:164
  98.9 2.2 collective-permute-start.18
  101.1 4.2 %collective-permute-start.9 = (bf16[704,512]{1,0:T(8,128)(2,1)}, bf16[704,512]{1,0:T(8,128)(2,1)S(1)}, u32[]{:S(2)}, u32[]{:S(2)}) collective-permute-start(bf16[704,512]{1,0:T(8,128)(2,1)} %collective-permute-done.8), channel_id=1, source_target_pairs={{0,4},{1,5},{2,14},{3,15},{4,8},{5,9},{6,2},{7,3},{8,12},{9,13},{1... | collective-permute-start | bytes 2162696 | tf_op jit(solution)/shard_map/ppermute | solution.py:35
  118.2 2.4 collective-permute-start.19
  122.6 2.9 %collective-permute-start.13 = (bf16[160,1024]{1,0:T(8,128)(2,1)}, bf16[160,1024]{1,0:T(8,128)(2,1)S(1)}, u32[]{:S(2)}, u32[]{:S(2)}) collective-permute-start(bf16[160,1024]{1,0:T(8,128)(2,1)} %get-tuple-element.30), channel_id=1, source_target_pairs={{0,4},{1,5},{2,6},{3,7},{4,8},{5,9},{6,10},{7,11},{8,12},{9,13},{1... | collective-permute-start | bytes 983048 | tf_op jit(solution)/shard_map/ppermute | solution.py:35
  125.5 2.7 %collective-permute-start.14 = (bf16[160,1024]{1,0:T(8,128)(2,1)}, bf16[160,1024]{1,0:T(8,128)(2,1)S(1)}, u32[]{:S(2)}, u32[]{:S(2)}) collective-permute-start(bf16[160,1024]{1,0:T(8,128)(2,1)} %get-tuple-element.31), channel_id=1, source_target_pairs={{0,8},{1,9},{2,10},{3,11},{4,12},{5,13},{6,14},{7,15},{8,0},{9,1},... | collective-permute-start | bytes 983048 | tf_op jit(solution)/shard_map/ppermute | solution.py:35
  128.1 3.6 %collective-permute-start.15 = (bf16[160,1024]{1,0:T(8,128)(2,1)}, bf16[160,1024]{1,0:T(8,128)(2,1)S(1)}, u32[]{:S(2)}, u32[]{:S(2)}) collective-permute-start(bf16[160,1024]{1,0:T(8,128)(2,1)} %get-tuple-element.32), channel_id=1, source_target_pairs={{0,12},{1,13},{2,14},{3,15},{4,0},{5,1},{6,2},{7,3},{8,4},{9,5},{1... | collective-permute-start | bytes 983048 | tf_op jit(solution)/shard_map/ppermute | solution.py:35
  134.7 14.5 %collective-permute-done.16 = bf16[400,512]{1,0:T(8,128)(2,1)S(1)} collective-permute-done((bf16[400,512]{1,0:T(8,128)(2,1)S(1)}, bf16[400,512]{1,0:T(8,128)(2,1)S(1)}, u32[]{:S(2)}, u32[]{:S(2)}) %collective-permute-start.16) | collective-permute-done | bytes 409632 | tf_op jit(solution)/shard_map/ppermute | solution.py:35
  151.5 11.4 %collective-permute-done.20 = bf16[400,512]{1,0:T(8,128)(2,1)S(1)} collective-permute-done((bf16[400,512]{1,0:T(8,128)(2,1)S(1)}, bf16[400,512]{1,0:T(8,128)(2,1)S(1)}, u32[]{:S(2)}, u32[]{:S(2)}) %collective-permute-start.20) | collective-permute-done | bytes 409632 | tf_op jit(solution)/shard_map/ppermute | solution.py:35
  162.9 15.6 %collective-permute-start.21 = (bf16[256,512]{1,0:T(8,128)(2,1)S(1)}, bf16[256,512]{1,0:T(8,128)(2,1)S(1)}, u32[]{:S(2)}, u32[]{:S(2)}) collective-permute-start(bf16[256,512]{1,0:T(8,128)(2,1)S(1)} %slice.161), channel_id=1, source_target_pairs={{0,2},{1,3},{2,0},{3,1},{4,6},{5,7},{6,4},{7,5},{8,10},{9,11},{10,... | collective-permute-start | bytes 786440 | tf_op jit(solution)/shard_map/ppermute | solution.py:35
  183.7 7.6 %attention.1 = (bf16[128,512]{1,0:T(8,128)(2,1)}, bf16[128,512]{1,0:T(8,128)(2,1)}) custom-call(s32[1]{0:T(128)} %bitcast.31.refs_0_, bf16[384,512]{1,0:T(8,128)(2,1)} %copy-done.3, bf16[384,512]{1,0:T(8,128)(2,1)} %copy-done.4, bf16[256,512]{1,0:T(8,128)(2,1)} %copy-done.15, bf16[256,512]{1,0:T(8,128)(2,1)} %copy-done.16, ...), custom_call_target="tpu_custom_call" | custom-call | flops 1073741824 | bytes 786432 | tf_op jit(solution)/shard_map/attention/pallas_call | solution.py:129
  191.3 3.9 %collective-permute-start.23 = (bf16[128,512]{1,0:T(8,128)(2,1)}, bf16[128,512]{1,0:T(8,128)(2,1)S(1)}, u32[]{:S(2)}, u32[]{:S(2)}) collective-permute-start(bf16[128,512]{1,0:T(8,128)(2,1)} %get-tuple-element.37), channel_id=1, source_target_pairs={{0,64},{1,65},{2,66},{3,67},{4,68},{5,69},{6,70},{7,71},{8,72},{9,... | collective-permute-start | bytes 393224 | tf_op jit(solution)/shard_map/ppermute | solution.py:45
  195.2 7.2 %collective-permute-start.24 = (bf16[128,512]{1,0:T(8,128)(2,1)}, bf16[128,512]{1,0:T(8,128)(2,1)S(1)}, u32[]{:S(2)}, u32[]{:S(2)}) collective-permute-start(bf16[128,512]{1,0:T(8,128)(2,1)} %get-tuple-element.38), channel_id=1, source_target_pairs={{0,65},{1,64},{2,67},{3,66},{4,69},{5,68},{6,71},{7,70},{8,73},{9,... | collective-permute-start | bytes 393224 | tf_op jit(solution)/shard_map/ppermute | solution.py:45
  202.4 2.5 stacked_rows.7
  204.9 3.1 %collective-permute-start.28 = (bf16[640,1024]{1,0:T(8,128)(2,1)}, bf16[640,1024]{1,0:T(8,128)(2,1)S(1)}, u32[]{:S(2)}, u32[]{:S(2)}) collective-permute-start(bf16[640,1024]{1,0:T(8,128)(2,1)} %stacked_rows.7), channel_id=1, source_target_pairs={{0,2},{1,3},{2,0},{3,1},{4,6},{5,7},{6,4},{7,5},{8,10},{9,11},{10,... | collective-permute-start | bytes 3932168 | tf_op jit(solution)/shard_map/ppermute | solution.py:35
  210.0 6.4 %collective-permute-start.26 = (bf16[256,512]{1,0:T(8,128)(2,1)S(1)}, bf16[256,512]{1,0:T(8,128)(2,1)S(1)}, u32[]{:S(2)}, u32[]{:S(2)}) collective-permute-start(bf16[256,512]{1,0:T(8,128)(2,1)S(1)} %pad_maximum_fusion.11), channel_id=1, source_target_pairs={{0,16},{1,17},{2,18},{3,19},{4,20},{5,21},{6,22},{7,23},{8,24},{9,... | collective-permute-start | bytes 786440 | tf_op jit(solution)/shard_map/ppermute | solution.py:35
  216.5 6.7 %collective-permute-done.25 = bf16[256,512]{1,0:T(8,128)(2,1)S(1)} collective-permute-done((bf16[256,512]{1,0:T(8,128)(2,1)S(1)}, bf16[256,512]{1,0:T(8,128)(2,1)S(1)}, u32[]{:S(2)}, u32[]{:S(2)}) %collective-permute-start.25) | collective-permute-done | bytes 262176 | tf_op jit(solution)/shard_map/ppermute | solution.py:35
  228.1 2.6 collective-permute-done.27
  231.5 6.1 %collective-permute-start.31 = (bf16[320,512]{1,0:T(8,128)(2,1)S(1)}, bf16[320,512]{1,0:T(8,128)(2,1)S(1)}, u32[]{:S(2)}, u32[]{:S(2)}) collective-permute-start(bf16[320,512]{1,0:T(8,128)(2,1)S(1)} %pad_maximum_fusion.10), channel_id=1, source_target_pairs={{0,4},{1,5},{2,6},{3,7},{4,8},{5,9},{6,10},{7,11},{8,12},{9,13},{1... | collective-permute-start | bytes 983048 | tf_op jit(solution)/shard_map/ppermute | solution.py:35
  237.6 5.3 %collective-permute-start.30 = (bf16[320,512]{1,0:T(8,128)(2,1)S(1)}, bf16[320,512]{1,0:T(8,128)(2,1)S(1)}, u32[]{:S(2)}, u32[]{:S(2)}) collective-permute-start(bf16[320,512]{1,0:T(8,128)(2,1)S(1)} %pad_maximum_fusion.9), channel_id=1, source_target_pairs={{0,8},{1,9},{2,10},{3,11},{4,12},{5,13},{6,14},{7,15},{8,0},{9,1},... | collective-permute-start | bytes 983048 | tf_op jit(solution)/shard_map/ppermute | solution.py:35
  243.0 2.9 %collective-permute-start.29 = (bf16[320,512]{1,0:T(8,128)(2,1)S(1)}, bf16[320,512]{1,0:T(8,128)(2,1)S(1)}, u32[]{:S(2)}, u32[]{:S(2)}) collective-permute-start(bf16[320,512]{1,0:T(8,128)(2,1)S(1)} %pad_maximum_fusion.8), channel_id=1, source_target_pairs={{0,12},{1,13},{2,14},{3,15},{4,0},{5,1},{6,2},{7,3},{8,4},{9,5},{1... | collective-permute-start | bytes 983048 | tf_op jit(solution)/shard_map/ppermute | solution.py:35
  246.2 7.9 %collective-permute-done.30 = bf16[320,512]{1,0:T(8,128)(2,1)S(1)} collective-permute-done((bf16[320,512]{1,0:T(8,128)(2,1)S(1)}, bf16[320,512]{1,0:T(8,128)(2,1)S(1)}, u32[]{:S(2)}, u32[]{:S(2)}) %collective-permute-start.30) | collective-permute-done | bytes 327712 | tf_op jit(solution)/shard_map/ppermute | solution.py:35
  257.1 4.0 %collective-permute-start.32 = (bf16[160,512]{1,0:T(8,128)(2,1)S(1)}, bf16[160,512]{1,0:T(8,128)(2,1)S(1)}, u32[]{:S(2)}, u32[]{:S(2)}) collective-permute-start(bf16[160,512]{1,0:T(8,128)(2,1)S(1)} %slice.179), channel_id=1, source_target_pairs={{0,2},{1,3},{2,0},{3,1},{4,6},{5,7},{6,4},{7,5},{8,10},{9,11},{10,... | collective-permute-start | bytes 491528 | tf_op jit(solution)/shard_map/ppermute | solution.py:35
  (157 shorter events, 63.3 us)
Async XLA Ops:
  1.2 13.3 %collective-permute-start = (bf16[160,512]{1,0:T(8,128)(2,1)S(1)}, bf16[160,512]{1,0:T(8,128)(2,1)S(1)}, u32[]{:S(2)}, u32[]{:S(2)}) collective-permute-start(bf16[160,512]{1,0:T(8,128)(2,1)S(1)} %get-tuple-element.78), channel_id=1, source_target_pairs={{0,2},{1,3},{2,0},{3,1},{4,6},{5,7},{6,4},{7,5},{8,10},{9,11},{10,... | collective-permute-start | bytes 491528 | tf_op jit(solution)/shard_map/ppermute | solution.py:35
  11.9 5.2 %collective-permute-start.3 = (bf16[176,512]{1,0:T(8,128)(2,1)S(1)}, bf16[176,512]{1,0:T(8,128)(2,1)S(1)}, u32[]{:S(2)}, u32[]{:S(2)}) collective-permute-start(bf16[176,512]{1,0:T(8,128)(2,1)S(1)} %get-tuple-element.76), channel_id=1, source_target_pairs={{0,0},{1,32},{2,2},{3,34},{4,4},{5,36},{6,6},{7,38},{8,8},{9,40},{... | collective-permute-start | bytes 540680 | tf_op jit(solution)/shard_map/ppermute | solution.py:35
  12.6 4.5 %collective-permute-start.4 = (bf16[176,512]{1,0:T(8,128)(2,1)S(1)}, bf16[176,512]{1,0:T(8,128)(2,1)S(1)}, u32[]{:S(2)}, u32[]{:S(2)}) collective-permute-start(bf16[176,512]{1,0:T(8,128)(2,1)S(1)} %get-tuple-element.75), channel_id=1, source_target_pairs={{0,2},{1,34},{2,0},{3,32},{4,6},{5,38},{6,4},{7,36},{8,10},{9,42},... | collective-permute-start | bytes 540680 | tf_op jit(solution)/shard_map/ppermute | solution.py:35
  14.5 90.7 %collective-permute-start.2 = (bf16[2560,384]{1,0:T(8,128)(2,1)S(1)}, bf16[2560,384]{1,0:T(8,128)(2,1)}, u32[]{:S(2)}, u32[]{:S(2)}) collective-permute-start(bf16[2560,384]{1,0:T(8,128)(2,1)S(1)} %bitcast.86), channel_id=1, source_target_pairs={{0,2},{1,3},{2,0},{3,1},{4,6},{5,7},{6,4},{7,5},{8,10},{9,11},{10,... | collective-permute-start | bytes 5898248 | tf_op jit(solution)/shard_map/ppermute | solution.py:35
  20.2 26.5 %collective-permute-start.6 = (bf16[352,512]{1,0:T(8,128)(2,1)}, bf16[352,512]{1,0:T(8,128)(2,1)}, u32[]{:S(2)}, u32[]{:S(2)}) collective-permute-start(bf16[352,512]{1,0:T(8,128)(2,1)} %stacked_rows.4.refs_0_), channel_id=1, source_target_pairs={{0,16},{1,17},{2,18},{3,19},{4,20},{5,21},{6,22},{7,23},{8,24},{9,... | collective-permute-start | bytes 1081352 | tf_op jit(solution)/shard_map/ppermute | solution.py:35
  22.2 71.5 %collective-permute-start.12 = (bf16[160,4096]{1,0:T(8,128)(2,1)}, bf16[160,4096]{1,0:T(8,128)(2,1)S(1)}, u32[]{:S(2)}, u32[]{:S(2)}) collective-permute-start(bf16[160,4096]{1,0:T(8,128)(2,1)} %bitcast.97), channel_id=1, source_target_pairs={{0,64},{1,65},{2,66},{3,67},{4,68},{5,69},{6,70},{7,71},{8,72},{9,... | collective-permute-start | bytes 3932168 | tf_op jit(solution)/shard_map/ppermute | solution.py:45
  24.1 63.7 %collective-permute-start.5 = (s32[16,3]{0,1:T(4,128)S(1)}, s32[16,3]{0,1:T(4,128)S(1)}, u32[]{:S(2)}, u32[]{:S(2)}) collective-permute-start(s32[16,3]{0,1:T(4,128)S(1)} %bitcast.92), channel_id=1, source_target_pairs={{0,1},{1,0},{2,3},{3,2},{4,5},{5,4},{6,7},{7,6},{8,9},{9,8},{10,11... | collective-permute-start | bytes 584 | tf_op jit(solution)/shard_map/ppermute | solution.py:35
  44.7 20.9 %collective-permute-start.10 = (bf16[352,512]{1,0:T(8,128)(2,1)}, bf16[352,512]{1,0:T(8,128)(2,1)}, u32[]{:S(2)}, u32[]{:S(2)}) collective-permute-start(bf16[352,512]{1,0:T(8,128)(2,1)} %stacked_rows.4.refs_0_), channel_id=1, source_target_pairs={{0,32},{1,33},{2,34},{3,35},{4,36},{5,37},{6,38},{7,39},{8,40},{9,... | collective-permute-start | bytes 1081352 | tf_op jit(solution)/shard_map/ppermute | solution.py:35
  48.7 35.0 %collective-permute-start.7 = (bf16[704,512]{1,0:T(8,128)(2,1)}, bf16[704,512]{1,0:T(8,128)(2,1)}, u32[]{:S(2)}, u32[]{:S(2)}) collective-permute-start(bf16[704,512]{1,0:T(8,128)(2,1)} %stacked_rows.5), channel_id=1, source_target_pairs={{0,4},{1,5},{2,14},{3,15},{4,8},{5,9},{6,2},{7,3},{8,12},{9,13},{1... | collective-permute-start | bytes 2162696 | tf_op jit(solution)/shard_map/ppermute | solution.py:35
  65.6 11.7 %collective-permute-start.11 = (bf16[352,512]{1,0:T(8,128)(2,1)}, bf16[352,512]{1,0:T(8,128)(2,1)}, u32[]{:S(2)}, u32[]{:S(2)}) collective-permute-start(bf16[352,512]{1,0:T(8,128)(2,1)} %collective-permute-done.10.refs_0_), channel_id=1, source_target_pairs={{0,16},{1,17},{2,18},{3,19},{4,20},{5,21},{6,22},{7,23},{8,24},{9,... | collective-permute-start | bytes 1081352 | tf_op jit(solution)/shard_map/ppermute | solution.py:35
  79.3 19.6 %collective-permute-start.17 = (bf16[704,512]{1,0:T(8,128)(2,1)}, bf16[704,512]{1,0:T(8,128)(2,1)}, u32[]{:S(2)}, u32[]{:S(2)}) collective-permute-start(bf16[704,512]{1,0:T(8,128)(2,1)} %stacked_rows.6), channel_id=1, source_target_pairs={{0,4},{1,5},{2,14},{3,15},{4,8},{5,9},{6,2},{7,3},{8,12},{9,13},{1... | collective-permute-start | bytes 2162696 | tf_op jit(solution)/shard_map/ppermute | solution.py:35
  83.7 17.4 %collective-permute-start.8 = (bf16[704,512]{1,0:T(8,128)(2,1)}, bf16[704,512]{1,0:T(8,128)(2,1)}, u32[]{:S(2)}, u32[]{:S(2)}) collective-permute-start(bf16[704,512]{1,0:T(8,128)(2,1)} %collective-permute-done.7), channel_id=1, source_target_pairs={{0,4},{1,5},{2,14},{3,15},{4,8},{5,9},{6,2},{7,3},{8,12},{9,13},{1... | collective-permute-start | bytes 2162696 | tf_op jit(solution)/shard_map/ppermute | solution.py:35
  89.6 89.3 %collective-permute-start.1 = (bf16[320,512]{1,0:T(8,128)(2,1)}, bf16[320,512]{1,0:T(8,128)(2,1)}, u32[]{:S(2)}, u32[]{:S(2)}) collective-permute-start(bf16[320,512]{1,0:T(8,128)(2,1)} %pad_maximum_fusion.7), channel_id=1, source_target_pairs={{0,64},{1,65},{2,66},{3,67},{4,68},{5,69},{6,70},{7,71},{8,72},{9,... | collective-permute-start | bytes 983048 | tf_op jit(solution)/shard_map/ppermute | solution.py:45
  98.9 19.3 %collective-permute-start.18 = (bf16[704,512]{1,0:T(8,128)(2,1)}, bf16[704,512]{1,0:T(8,128)(2,1)S(1)}, u32[]{:S(2)}, u32[]{:S(2)}) collective-permute-start(bf16[704,512]{1,0:T(8,128)(2,1)} %collective-permute-done.17), channel_id=1, source_target_pairs={{0,4},{1,5},{2,14},{3,15},{4,8},{5,9},{6,2},{7,3},{8,12},{9,13},{1... | collective-permute-start | bytes 2162696 | tf_op jit(solution)/shard_map/ppermute | solution.py:35
  101.1 20.4 %collective-permute-start.9 = (bf16[704,512]{1,0:T(8,128)(2,1)}, bf16[704,512]{1,0:T(8,128)(2,1)S(1)}, u32[]{:S(2)}, u32[]{:S(2)}) collective-permute-start(bf16[704,512]{1,0:T(8,128)(2,1)} %collective-permute-done.8), channel_id=1, source_target_pairs={{0,4},{1,5},{2,14},{3,15},{4,8},{5,9},{6,2},{7,3},{8,12},{9,13},{1... | collective-permute-start | bytes 2162696 | tf_op jit(solution)/shard_map/ppermute | solution.py:35
  118.2 13.5 %collective-permute-start.19 = (bf16[704,512]{1,0:T(8,128)(2,1)S(1)}, bf16[704,512]{1,0:T(8,128)(2,1)S(1)}, u32[]{:S(2)}, u32[]{:S(2)}) collective-permute-start(bf16[704,512]{1,0:T(8,128)(2,1)S(1)} %collective-permute-done.18), channel_id=1, source_target_pairs={{0,4},{1,5},{2,14},{3,15},{4,8},{5,9},{6,2},{7,3},{8,12},{9,13},{1... | collective-permute-start | bytes 2162696 | tf_op jit(solution)/shard_map/ppermute | solution.py:35
  122.6 59.6 %collective-permute-start.13 = (bf16[160,1024]{1,0:T(8,128)(2,1)}, bf16[160,1024]{1,0:T(8,128)(2,1)S(1)}, u32[]{:S(2)}, u32[]{:S(2)}) collective-permute-start(bf16[160,1024]{1,0:T(8,128)(2,1)} %get-tuple-element.30), channel_id=1, source_target_pairs={{0,4},{1,5},{2,6},{3,7},{4,8},{5,9},{6,10},{7,11},{8,12},{9,13},{1... | collective-permute-start | bytes 983048 | tf_op jit(solution)/shard_map/ppermute | solution.py:35
  125.5 56.7 %collective-permute-start.14 = (bf16[160,1024]{1,0:T(8,128)(2,1)}, bf16[160,1024]{1,0:T(8,128)(2,1)S(1)}, u32[]{:S(2)}, u32[]{:S(2)}) collective-permute-start(bf16[160,1024]{1,0:T(8,128)(2,1)} %get-tuple-element.31), channel_id=1, source_target_pairs={{0,8},{1,9},{2,10},{3,11},{4,12},{5,13},{6,14},{7,15},{8,0},{9,1},... | collective-permute-start | bytes 983048 | tf_op jit(solution)/shard_map/ppermute | solution.py:35
  128.1 54.1 %collective-permute-start.15 = (bf16[160,1024]{1,0:T(8,128)(2,1)}, bf16[160,1024]{1,0:T(8,128)(2,1)S(1)}, u32[]{:S(2)}, u32[]{:S(2)}) collective-permute-start(bf16[160,1024]{1,0:T(8,128)(2,1)} %get-tuple-element.32), channel_id=1, source_target_pairs={{0,12},{1,13},{2,14},{3,15},{4,0},{5,1},{6,2},{7,3},{8,4},{9,5},{1... | collective-permute-start | bytes 983048 | tf_op jit(solution)/shard_map/ppermute | solution.py:35
  131.7 17.5 %collective-permute-start.16 = (bf16[400,512]{1,0:T(8,128)(2,1)S(1)}, bf16[400,512]{1,0:T(8,128)(2,1)S(1)}, u32[]{:S(2)}, u32[]{:S(2)}) collective-permute-start(bf16[400,512]{1,0:T(8,128)(2,1)S(1)} %pad_maximum_fusion.5), channel_id=1, source_target_pairs={{0,1},{1,0},{2,3},{3,2},{4,5},{5,4},{6,7},{7,6},{8,9},{9,8},{10,11... | collective-permute-start | bytes 1228808 | tf_op jit(solution)/shard_map/ppermute | solution.py:35
  149.2 13.7 %collective-permute-start.20 = (bf16[400,512]{1,0:T(8,128)(2,1)S(1)}, bf16[400,512]{1,0:T(8,128)(2,1)S(1)}, u32[]{:S(2)}, u32[]{:S(2)}) collective-permute-start(bf16[400,512]{1,0:T(8,128)(2,1)S(1)} %pad_maximum_fusion.6), channel_id=1, source_target_pairs={{0,1},{1,0},{2,3},{3,2},{4,5},{5,4},{6,7},{7,6},{8,9},{9,8},{10,11... | collective-permute-start | bytes 1228808 | tf_op jit(solution)/shard_map/ppermute | solution.py:35
  162.9 19.4 %collective-permute-start.21 = (bf16[256,512]{1,0:T(8,128)(2,1)S(1)}, bf16[256,512]{1,0:T(8,128)(2,1)S(1)}, u32[]{:S(2)}, u32[]{:S(2)}) collective-permute-start(bf16[256,512]{1,0:T(8,128)(2,1)S(1)} %slice.161), channel_id=1, source_target_pairs={{0,2},{1,3},{2,0},{3,1},{4,6},{5,7},{6,4},{7,5},{8,10},{9,11},{10,... | collective-permute-start | bytes 786440 | tf_op jit(solution)/shard_map/ppermute | solution.py:35
  191.3 16.7 %collective-permute-start.23 = (bf16[128,512]{1,0:T(8,128)(2,1)}, bf16[128,512]{1,0:T(8,128)(2,1)S(1)}, u32[]{:S(2)}, u32[]{:S(2)}) collective-permute-start(bf16[128,512]{1,0:T(8,128)(2,1)} %get-tuple-element.37), channel_id=1, source_target_pairs={{0,64},{1,65},{2,66},{3,67},{4,68},{5,69},{6,70},{7,71},{8,72},{9,... | collective-permute-start | bytes 393224 | tf_op jit(solution)/shard_map/ppermute | solution.py:45
  195.2 12.8 %collective-permute-start.24 = (bf16[128,512]{1,0:T(8,128)(2,1)}, bf16[128,512]{1,0:T(8,128)(2,1)S(1)}, u32[]{:S(2)}, u32[]{:S(2)}) collective-permute-start(bf16[128,512]{1,0:T(8,128)(2,1)} %get-tuple-element.38), channel_id=1, source_target_pairs={{0,65},{1,64},{2,67},{3,66},{4,69},{5,68},{6,71},{7,70},{8,73},{9,... | collective-permute-start | bytes 393224 | tf_op jit(solution)/shard_map/ppermute | solution.py:45
  204.9 22.1 %collective-permute-start.28 = (bf16[640,1024]{1,0:T(8,128)(2,1)}, bf16[640,1024]{1,0:T(8,128)(2,1)S(1)}, u32[]{:S(2)}, u32[]{:S(2)}) collective-permute-start(bf16[640,1024]{1,0:T(8,128)(2,1)} %stacked_rows.7), channel_id=1, source_target_pairs={{0,2},{1,3},{2,0},{3,1},{4,6},{5,7},{6,4},{7,5},{8,10},{9,11},{10,... | collective-permute-start | bytes 3932168 | tf_op jit(solution)/shard_map/ppermute | solution.py:35
  208.1 15.1 %collective-permute-start.25 = (bf16[256,512]{1,0:T(8,128)(2,1)S(1)}, bf16[256,512]{1,0:T(8,128)(2,1)S(1)}, u32[]{:S(2)}, u32[]{:S(2)}) collective-permute-start(bf16[256,512]{1,0:T(8,128)(2,1)S(1)} %pad_maximum_fusion.11), channel_id=1, source_target_pairs={{0,32},{1,33},{2,34},{3,35},{4,36},{5,37},{6,38},{7,39},{8,40},{9,... | collective-permute-start | bytes 786440 | tf_op jit(solution)/shard_map/ppermute | solution.py:35
  210.0 16.3 %collective-permute-start.26 = (bf16[256,512]{1,0:T(8,128)(2,1)S(1)}, bf16[256,512]{1,0:T(8,128)(2,1)S(1)}, u32[]{:S(2)}, u32[]{:S(2)}) collective-permute-start(bf16[256,512]{1,0:T(8,128)(2,1)S(1)} %pad_maximum_fusion.11), channel_id=1, source_target_pairs={{0,16},{1,17},{2,18},{3,19},{4,20},{5,21},{6,22},{7,23},{8,24},{9,... | collective-permute-start | bytes 786440 | tf_op jit(solution)/shard_map/ppermute | solution.py:35
  223.1 7.5 %collective-permute-start.27 = (bf16[256,512]{1,0:T(8,128)(2,1)S(1)}, bf16[256,512]{1,0:T(8,128)(2,1)S(1)}, u32[]{:S(2)}, u32[]{:S(2)}) collective-permute-start(bf16[256,512]{1,0:T(8,128)(2,1)S(1)} %collective-permute-done.25), channel_id=1, source_target_pairs={{0,16},{1,17},{2,18},{3,19},{4,20},{5,21},{6,22},{7,23},{8,24},{9,... | collective-permute-start | bytes 786440 | tf_op jit(solution)/shard_map/ppermute | solution.py:35
  231.5 14.8 %collective-permute-start.31 = (bf16[320,512]{1,0:T(8,128)(2,1)S(1)}, bf16[320,512]{1,0:T(8,128)(2,1)S(1)}, u32[]{:S(2)}, u32[]{:S(2)}) collective-permute-start(bf16[320,512]{1,0:T(8,128)(2,1)S(1)} %pad_maximum_fusion.10), channel_id=1, source_target_pairs={{0,4},{1,5},{2,6},{3,7},{4,8},{5,9},{6,10},{7,11},{8,12},{9,13},{1... | collective-permute-start | bytes 983048 | tf_op jit(solution)/shard_map/ppermute | solution.py:35
  237.6 16.5 %collective-permute-start.30 = (bf16[320,512]{1,0:T(8,128)(2,1)S(1)}, bf16[320,512]{1,0:T(8,128)(2,1)S(1)}, u32[]{:S(2)}, u32[]{:S(2)}) collective-permute-start(bf16[320,512]{1,0:T(8,128)(2,1)S(1)} %pad_maximum_fusion.9), channel_id=1, source_target_pairs={{0,8},{1,9},{2,10},{3,11},{4,12},{5,13},{6,14},{7,15},{8,0},{9,1},... | collective-permute-start | bytes 983048 | tf_op jit(solution)/shard_map/ppermute | solution.py:35
  243.0 12.9 %collective-permute-start.29 = (bf16[320,512]{1,0:T(8,128)(2,1)S(1)}, bf16[320,512]{1,0:T(8,128)(2,1)S(1)}, u32[]{:S(2)}, u32[]{:S(2)}) collective-permute-start(bf16[320,512]{1,0:T(8,128)(2,1)S(1)} %pad_maximum_fusion.8), channel_id=1, source_target_pairs={{0,12},{1,13},{2,14},{3,15},{4,0},{5,1},{6,2},{7,3},{8,4},{9,5},{1... | collective-permute-start | bytes 983048 | tf_op jit(solution)/shard_map/ppermute | solution.py:35
  257.1 5.1 %collective-permute-start.32 = (bf16[160,512]{1,0:T(8,128)(2,1)S(1)}, bf16[160,512]{1,0:T(8,128)(2,1)S(1)}, u32[]{:S(2)}, u32[]{:S(2)}) collective-permute-start(bf16[160,512]{1,0:T(8,128)(2,1)S(1)} %slice.179), channel_id=1, source_target_pairs={{0,2},{1,3},{2,0},{3,1},{4,6},{5,7},{6,4},{7,5},{8,10},{9,11},{10,... | collective-permute-start | bytes 491528 | tf_op jit(solution)/shard_map/ppermute | solution.py:35
  (19 other events, 209.5 us)

commit v11 on v10

--- a/solution.py
+++ b/solution.py
@@ -256,11 +256,11 @@
     own, away = of_core(jnp.concatenate([gained, three_rows(squares)], axis=0))
     crossed = moved(away, lambda *at: other_core(*swap_inner(*at)))
     e = stacked_rows(moved(own, swap_inner), crossed)
+    f = moved(e, by_two)
+    e_two = stacked_rows(e, moved(e, pair))
+    f_two = stacked_rows(f, moved(f, pair))
     random = random_blocks[0]
-    random = jnp.stack([moved(random, other_seq), random])
-    f = moved(e, by_two)
-    e_two = stacked_rows(e, moved(after(e, random), pair))
-    f_two = stacked_rows(f, moved(f, pair))
+    random = jnp.stack([moved(after(random, f_two), other_seq), random])
 
     out_next = moved_on(out_weight[0].T, same)
 
@@ -328,7 +328,7 @@
         )
         for partial in (partial_e, partial_f)
     ]
-    sends[0], slices = lax.optimization_barrier((sends[0], slices))
+    sends[1], slices = lax.optimization_barrier((sends[1], slices))
     out_own = [slices[0]]
     for r in range(1, 4):
         out_own.append(moved(slices[r], lambda y, x, c, r=r: (y, (x + r) % 4, c)))
@@ -336,7 +336,7 @@
     head = columns // 3
     for partial, send in zip((partial_e, partial_f), sends):
         came = moved(send, other_seq)
-        came = after(came, sends[1]).astype(f32)
+        came = came.astype(f32)
         squares = partial[2 * columns : 2 * columns + 1]
         squares = squares + jnp.sum(came[columns : columns + 3], axis=0, keepdims=True)
         factor = jnp.where(squares < TOP, lax.rsqrt(squares / width + 1e-05), 0.0)

time: 265 us -> 260 us (0.981)
  starting transfers between devices: 139 us -> 129 us
  waiting for transfers between devices: 68.2 us -> 74.8 us
    ppermute x29, starting transfers between devices: 122 us -> 112 us  [moved(): return lax.ppermute(value, PLANE, pairs_of(where))]
    ppermute x4, waiting for transfers between devices: 0.01 us -> 5.68 us  [moved_on(): return lax.ppermute(value, ('section', *PLANE), pairs)]
  transfers between devices with their start and end apart: 33 -> 33, of which waited for: 11 -> 13; matrix products, arithmetic and copies ran while one was open for 10% -> 10% of each run, Pallas kernels for 5% -> 5%
where the time goes in v11:
time: 260 us; the launch traced here: 258 us
  starting transfers between devices  129 us (50%)
  waiting for transfers between devices  74.8 us (29%)
  Pallas kernels  20 us (8%)
  matrix products  14.3 us (6%)
  other arithmetic  12.6 us (5%)
  local copies, waits for them, and re-layouts  6.81 us (3%)
    ppermute x29, starting transfers between devices, moved(): return lax.ppermute(value, PLANE, pairs_of(where))  112 us
    ppermute x29, waiting for transfers between devices, moved(): return lax.ppermute(value, PLANE, pairs_of(where))  69.1 us
    ppermute x4, starting transfers between devices, moved_on(): return lax.ppermute(value, ('section', *PLANE), pairs)  16.7 us
    dot_general x8, matrix products, project(): lax.dot_general(weights[k], block, (((0,), (0,)), ((), ())), preferred_el...  10.7 us
    pallas_call x4, Pallas kernels, stacked_rows(): pl.pallas_call(rows_kernel, in_specs=[vmem] * len(parts), out_specs=vmem,...  8.28 us
    pallas_call x1, Pallas kernels, attention(): pl.pallas_call(lambda *refs: attention_kernel(1.0 / math.sqrt(size), per,...  7.55 us
    ppermute x4, waiting for transfers between devices, moved_on(): return lax.ppermute(value, ('section', *PLANE), pairs)  5.68 us
  transfers between devices with their start and end apart: 33, of which 13 were waited for; matrix products, arithmetic and copies ran while one was open for 10% of the time, Pallas kernels for 5%

profile of v11, /device:TPU:1, one launch (start us, length us, event | category | flops | bytes accessed | tf_op | source)
XLA Modules:
  0.0 257.9 jit_solution(15995924012890903235)
XLA Ops:
  1.2 8.8 %collective-permute-start = (bf16[160,512]{1,0:T(8,128)(2,1)S(1)}, bf16[160,512]{1,0:T(8,128)(2,1)S(1)}, u32[]{:S(2)}, u32[]{:S(2)}) collective-permute-start(bf16[160,512]{1,0:T(8,128)(2,1)S(1)} %get-tuple-element.74), channel_id=1, source_target_pairs={{0,2},{1,3},{2,0},{3,1},{4,6},{5,7},{6,4},{7,5},{8,10},{9,11},{10,... | collective-permute-start | bytes 491528 | tf_op jit(solution)/shard_map/ppermute | solution.py:35
  14.5 2.5 collective-permute-start.2
  24.1 16.9 %collective-permute-start.5 = (bf16[352,512]{1,0:T(8,128)(2,1)}, bf16[352,512]{1,0:T(8,128)(2,1)}, u32[]{:S(2)}, u32[]{:S(2)}) collective-permute-start(bf16[352,512]{1,0:T(8,128)(2,1)} %stacked_rows.4.refs_0_), channel_id=1, source_target_pairs={{0,32},{1,33},{2,34},{3,35},{4,36},{5,37},{6,38},{7,39},{8,40},{9,... | collective-permute-start | bytes 1081352 | tf_op jit(solution)/shard_map/ppermute | solution.py:35
  43.1 4.4 %collective-permute-start.15 = (bf16[704,512]{1,0:T(8,128)(2,1)}, bf16[704,512]{1,0:T(8,128)(2,1)}, u32[]{:S(2)}, u32[]{:S(2)}) collective-permute-start(bf16[704,512]{1,0:T(8,128)(2,1)} %stacked_rows.7), channel_id=1, source_target_pairs={{0,4},{1,5},{2,14},{3,15},{4,8},{5,9},{6,2},{7,3},{8,12},{9,13},{1... | collective-permute-start | bytes 2162696 | tf_op jit(solution)/shard_map/ppermute | solution.py:35
  47.6 9.3 %collective-permute-done.5.refs_0_ = bf16[352,512]{1,0:T(8,128)(2,1)} collective-permute-done((bf16[352,512]{1,0:T(8,128)(2,1)}, bf16[352,512]{1,0:T(8,128)(2,1)}, u32[]{:S(2)}, u32[]{:S(2)}) %collective-permute-start.5) | collective-permute-done | bytes 360480 | tf_op jit(solution)/shard_map/ppermute | solution.py:35
  57.0 3.3 %collective-permute-start.6 = (bf16[352,512]{1,0:T(8,128)(2,1)}, bf16[352,512]{1,0:T(8,128)(2,1)}, u32[]{:S(2)}, u32[]{:S(2)}) collective-permute-start(bf16[352,512]{1,0:T(8,128)(2,1)} %collective-permute-done.5.refs_0_), channel_id=1, source_target_pairs={{0,16},{1,17},{2,18},{3,19},{4,20},{5,21},{6,22},{7,23},{8,24},{9,... | collective-permute-start | bytes 1081352 | tf_op jit(solution)/shard_map/ppermute | solution.py:35
  60.4 7.4 %collective-permute-done.6.refs_1_ = bf16[352,512]{1,0:T(8,128)(2,1)} collective-permute-done((bf16[352,512]{1,0:T(8,128)(2,1)}, bf16[352,512]{1,0:T(8,128)(2,1)}, u32[]{:S(2)}, u32[]{:S(2)}) %collective-permute-start.6) | collective-permute-done | bytes 360480 | tf_op jit(solution)/shard_map/ppermute | solution.py:35
  69.9 4.4 %collective-permute-start.7 = (bf16[704,512]{1,0:T(8,128)(2,1)}, bf16[704,512]{1,0:T(8,128)(2,1)}, u32[]{:S(2)}, u32[]{:S(2)}) collective-permute-start(bf16[704,512]{1,0:T(8,128)(2,1)} %stacked_rows.5), channel_id=1, source_target_pairs={{0,4},{1,5},{2,14},{3,15},{4,8},{5,9},{6,2},{7,3},{8,12},{9,13},{1... | collective-permute-start | bytes 2162696 | tf_op jit(solution)/shard_map/ppermute | solution.py:35
  74.3 2.5 collective-permute-start.16
  78.4 9.4 %collective-permute-start.22 = (s32[16,3]{0,1:T(4,128)S(1)}, s32[16,3]{0,1:T(4,128)S(1)}, u32[]{:S(2)}, u32[]{:S(2)}) collective-permute-start(s32[16,3]{0,1:T(4,128)S(1)} %bitcast.93), channel_id=1, source_target_pairs={{0,1},{1,0},{2,3},{3,2},{4,5},{5,4},{6,7},{7,6},{8,9},{9,8},{10,11... | collective-permute-start | bytes 584 | tf_op jit(solution)/shard_map/ppermute | solution.py:35
  89.4 4.0 %collective-permute-start.1 = (bf16[320,512]{1,0:T(8,128)(2,1)}, bf16[320,512]{1,0:T(8,128)(2,1)}, u32[]{:S(2)}, u32[]{:S(2)}) collective-permute-start(bf16[320,512]{1,0:T(8,128)(2,1)} %pad_maximum_fusion.7), channel_id=1, source_target_pairs={{0,64},{1,65},{2,66},{3,67},{4,68},{5,69},{6,70},{7,71},{8,72},{9,... | collective-permute-start | bytes 983048 | tf_op jit(solution)/shard_map/ppermute | solution.py:45
  94.6 4.2 %column_slices.1 = (bf16[160,1024]{1,0:T(8,128)(2,1)}, bf16[160,1024]{1,0:T(8,128)(2,1)}, bf16[160,1024]{1,0:T(8,128)(2,1)}, bf16[160,1024]{1,0:T(8,128)(2,1)}) custom-call(s32[4]{0:T(128)} %pad_add_fusion.1.order_ref, s32[4]{0:T(128)} %and_select_fusion.ring_ref, bf16[160,4096]{1,0:T(8,128)(2,1)} %copy-done.2), custom_call_target="tpu_custom_call" | custom-call | bytes 2621440 | tf_op jit(solution)/shard_map/column_slices/pallas_call | solution.py:164
  116.1 4.4 %collective-permute-start.9 = (bf16[704,512]{1,0:T(8,128)(2,1)S(1)}, bf16[704,512]{1,0:T(8,128)(2,1)S(1)}, u32[]{:S(2)}, u32[]{:S(2)}) collective-permute-start(bf16[704,512]{1,0:T(8,128)(2,1)S(1)} %collective-permute-done.8), channel_id=1, source_target_pairs={{0,4},{1,5},{2,14},{3,15},{4,8},{5,9},{6,2},{7,3},{8,12},{9,13},{1... | collective-permute-start | bytes 2162696 | tf_op jit(solution)/shard_map/ppermute | solution.py:35
  122.5 6.7 %collective-permute-start.18 = (bf16[400,512]{1,0:T(8,128)(2,1)S(1)}, bf16[400,512]{1,0:T(8,128)(2,1)S(1)}, u32[]{:S(2)}, u32[]{:S(2)}) collective-permute-start(bf16[400,512]{1,0:T(8,128)(2,1)S(1)} %pad_maximum_fusion.6), channel_id=1, source_target_pairs={{0,1},{1,0},{2,3},{3,2},{4,5},{5,4},{6,7},{7,6},{8,9},{9,8},{10,11... | collective-permute-start | bytes 1228808 | tf_op jit(solution)/shard_map/ppermute | solution.py:35
  132.6 5.3 %collective-permute-start.12 = (bf16[160,1024]{1,0:T(8,128)(2,1)}, bf16[160,1024]{1,0:T(8,128)(2,1)S(1)}, u32[]{:S(2)}, u32[]{:S(2)}) collective-permute-start(bf16[160,1024]{1,0:T(8,128)(2,1)} %get-tuple-element.28), channel_id=1, source_target_pairs={{0,8},{1,9},{2,10},{3,11},{4,12},{5,13},{6,14},{7,15},{8,0},{9,1},... | collective-permute-start | bytes 983048 | tf_op jit(solution)/shard_map/ppermute | solution.py:35
  140.1 7.0 %collective-permute-done.18 = bf16[400,512]{1,0:T(8,128)(2,1)S(1)} collective-permute-done((bf16[400,512]{1,0:T(8,128)(2,1)S(1)}, bf16[400,512]{1,0:T(8,128)(2,1)S(1)}, u32[]{:S(2)}, u32[]{:S(2)}) %collective-permute-start.18) | collective-permute-done | bytes 409632 | tf_op jit(solution)/shard_map/ppermute | solution.py:35
  147.1 6.1 %collective-permute-start.19 = (bf16[400,512]{1,0:T(8,128)(2,1)S(1)}, bf16[400,512]{1,0:T(8,128)(2,1)S(1)}, u32[]{:S(2)}, u32[]{:S(2)}) collective-permute-start(bf16[400,512]{1,0:T(8,128)(2,1)S(1)} %pad_maximum_fusion.5), channel_id=1, source_target_pairs={{0,1},{1,0},{2,3},{3,2},{4,5},{5,4},{6,7},{7,6},{8,9},{9,8},{10,11... | collective-permute-start | bytes 1228808 | tf_op jit(solution)/shard_map/ppermute | solution.py:35
  153.6 16.8 %collective-permute-done.19 = bf16[400,512]{1,0:T(8,128)(2,1)S(1)} collective-permute-done((bf16[400,512]{1,0:T(8,128)(2,1)S(1)}, bf16[400,512]{1,0:T(8,128)(2,1)S(1)}, u32[]{:S(2)}, u32[]{:S(2)}) %collective-permute-start.19) | collective-permute-done | bytes 409632 | tf_op jit(solution)/shard_map/ppermute | solution.py:35
  177.4 7.5 %attention.1 = (bf16[128,512]{1,0:T(8,128)(2,1)}, bf16[128,512]{1,0:T(8,128)(2,1)}) custom-call(s32[1]{0:T(128)} %bitcast.30.refs_0_, bf16[384,512]{1,0:T(8,128)(2,1)} %copy-done.3, bf16[384,512]{1,0:T(8,128)(2,1)} %copy-done.4, bf16[256,512]{1,0:T(8,128)(2,1)} %collective-permute-done.20.refs_3_, bf16[256,512]{1,0:T(8,128)(2,1)} %copy-done.16, ...), custom_call_target="tpu_custom_call" | custom-call | flops 1073741824 | bytes 786432 | tf_op jit(solution)/shard_map/attention/pallas_call | solution.py:129
  185.0 4.0 %collective-permute-start.23 = (bf16[128,512]{1,0:T(8,128)(2,1)}, bf16[128,512]{1,0:T(8,128)(2,1)S(1)}, u32[]{:S(2)}, u32[]{:S(2)}) collective-permute-start(bf16[128,512]{1,0:T(8,128)(2,1)} %get-tuple-element.33), channel_id=1, source_target_pairs={{0,64},{1,65},{2,66},{3,67},{4,68},{5,69},{6,70},{7,71},{8,72},{9,... | collective-permute-start | bytes 393224 | tf_op jit(solution)/shard_map/ppermute | solution.py:45
  189.0 6.8 %collective-permute-start.24 = (bf16[128,512]{1,0:T(8,128)(2,1)}, bf16[128,512]{1,0:T(8,128)(2,1)S(1)}, u32[]{:S(2)}, u32[]{:S(2)}) collective-permute-start(bf16[128,512]{1,0:T(8,128)(2,1)} %get-tuple-element.34), channel_id=1, source_target_pairs={{0,65},{1,64},{2,67},{3,66},{4,69},{5,68},{6,71},{7,70},{8,73},{9,... | collective-permute-start | bytes 393224 | tf_op jit(solution)/shard_map/ppermute | solution.py:45
  195.9 5.7 %collective-permute-done.24 = bf16[128,512]{1,0:T(8,128)(2,1)S(1)} collective-permute-done((bf16[128,512]{1,0:T(8,128)(2,1)}, bf16[128,512]{1,0:T(8,128)(2,1)S(1)}, u32[]{:S(2)}, u32[]{:S(2)}) %collective-permute-start.24) | collective-permute-done | bytes 131104 | tf_op jit(solution)/shard_map/ppermute | solution.py:45
  203.5 2.5 stacked_rows.6
  206.0 3.5 %collective-permute-start.28 = (bf16[640,1024]{1,0:T(8,128)(2,1)}, bf16[640,1024]{1,0:T(8,128)(2,1)S(1)}, u32[]{:S(2)}, u32[]{:S(2)}) collective-permute-start(bf16[640,1024]{1,0:T(8,128)(2,1)} %stacked_rows.6), channel_id=1, source_target_pairs={{0,2},{1,3},{2,0},{3,1},{4,6},{5,7},{6,4},{7,5},{8,10},{9,11},{10,... | collective-permute-start | bytes 3932168 | tf_op jit(solution)/shard_map/ppermute | solution.py:35
  211.5 5.4 %collective-permute-done.25 = bf16[256,512]{1,0:T(8,128)(2,1)S(1)} collective-permute-done((bf16[256,512]{1,0:T(8,128)(2,1)S(1)}, bf16[256,512]{1,0:T(8,128)(2,1)S(1)}, u32[]{:S(2)}, u32[]{:S(2)}) %collective-permute-start.25) | collective-permute-done | bytes 262176 | tf_op jit(solution)/shard_map/ppermute | solution.py:35
  220.1 2.4 collective-permute-done.26
  223.2 4.9 %collective-permute-done.27 = bf16[256,512]{1,0:T(8,128)(2,1)S(1)} collective-permute-done((bf16[256,512]{1,0:T(8,128)(2,1)S(1)}, bf16[256,512]{1,0:T(8,128)(2,1)S(1)}, u32[]{:S(2)}, u32[]{:S(2)}) %collective-permute-start.27) | collective-permute-done | bytes 262176 | tf_op jit(solution)/shard_map/ppermute | solution.py:35
  230.0 2.5 collective-permute-start.29
  232.5 3.4 %collective-permute-start.30 = (bf16[320,512]{1,0:T(8,128)(2,1)S(1)}, bf16[320,512]{1,0:T(8,128)(2,1)S(1)}, u32[]{:S(2)}, u32[]{:S(2)}) collective-permute-start(bf16[320,512]{1,0:T(8,128)(2,1)S(1)} %pad_maximum_fusion.9), channel_id=1, source_target_pairs={{0,8},{1,9},{2,10},{3,11},{4,12},{5,13},{6,14},{7,15},{8,0},{9,1},... | collective-permute-start | bytes 983048 | tf_op jit(solution)/shard_map/ppermute | solution.py:35
  237.9 2.8 %collective-permute-done.29 = bf16[320,512]{1,0:T(8,128)(2,1)S(1)} collective-permute-done((bf16[320,512]{1,0:T(8,128)(2,1)S(1)}, bf16[320,512]{1,0:T(8,128)(2,1)S(1)}, u32[]{:S(2)}, u32[]{:S(2)}) %collective-permute-start.29) | collective-permute-done | bytes 327712 | tf_op jit(solution)/shard_map/ppermute | solution.py:35
  240.7 3.7 %collective-permute-done.30 = bf16[320,512]{1,0:T(8,128)(2,1)S(1)} collective-permute-done((bf16[320,512]{1,0:T(8,128)(2,1)S(1)}, bf16[320,512]{1,0:T(8,128)(2,1)S(1)}, u32[]{:S(2)}, u32[]{:S(2)}) %collective-permute-start.30) | collective-permute-done | bytes 327712 | tf_op jit(solution)/shard_map/ppermute | solution.py:35
  244.4 8.1 %collective-permute-done.31 = bf16[320,512]{1,0:T(8,128)(2,1)S(1)} collective-permute-done((bf16[320,512]{1,0:T(8,128)(2,1)S(1)}, bf16[320,512]{1,0:T(8,128)(2,1)S(1)}, u32[]{:S(2)}, u32[]{:S(2)}) %collective-permute-start.31) | collective-permute-done | bytes 327712 | tf_op jit(solution)/shard_map/ppermute | solution.py:35
  (157 shorter events, 70.5 us)
Async XLA Ops:
  1.2 13.3 %collective-permute-start = (bf16[160,512]{1,0:T(8,128)(2,1)S(1)}, bf16[160,512]{1,0:T(8,128)(2,1)S(1)}, u32[]{:S(2)}, u32[]{:S(2)}) collective-permute-start(bf16[160,512]{1,0:T(8,128)(2,1)S(1)} %get-tuple-element.74), channel_id=1, source_target_pairs={{0,2},{1,3},{2,0},{3,1},{4,6},{5,7},{6,4},{7,5},{8,10},{9,11},{10,... | collective-permute-start | bytes 491528 | tf_op jit(solution)/shard_map/ppermute | solution.py:35
  11.9 5.2 %collective-permute-start.3 = (bf16[176,512]{1,0:T(8,128)(2,1)S(1)}, bf16[176,512]{1,0:T(8,128)(2,1)S(1)}, u32[]{:S(2)}, u32[]{:S(2)}) collective-permute-start(bf16[176,512]{1,0:T(8,128)(2,1)S(1)} %get-tuple-element.72), channel_id=1, source_target_pairs={{0,0},{1,32},{2,2},{3,34},{4,4},{5,36},{6,6},{7,38},{8,8},{9,40},{... | collective-permute-start | bytes 540680 | tf_op jit(solution)/shard_map/ppermute | solution.py:35
  12.6 4.6 %collective-permute-start.4 = (bf16[176,512]{1,0:T(8,128)(2,1)S(1)}, bf16[176,512]{1,0:T(8,128)(2,1)S(1)}, u32[]{:S(2)}, u32[]{:S(2)}) collective-permute-start(bf16[176,512]{1,0:T(8,128)(2,1)S(1)} %get-tuple-element.71), channel_id=1, source_target_pairs={{0,2},{1,34},{2,0},{3,32},{4,6},{5,38},{6,4},{7,36},{8,10},{9,42},... | collective-permute-start | bytes 540680 | tf_op jit(solution)/shard_map/ppermute | solution.py:35
  14.5 88.6 %collective-permute-start.2 = (bf16[2560,384]{1,0:T(8,128)(2,1)S(1)}, bf16[2560,384]{1,0:T(8,128)(2,1)}, u32[]{:S(2)}, u32[]{:S(2)}) collective-permute-start(bf16[2560,384]{1,0:T(8,128)(2,1)S(1)} %bitcast.87), channel_id=1, source_target_pairs={{0,2},{1,3},{2,0},{3,1},{4,6},{5,7},{6,4},{7,5},{8,10},{9,11},{10,... | collective-permute-start | bytes 5898248 | tf_op jit(solution)/shard_map/ppermute | solution.py:35
  20.2 20.9 %collective-permute-start.14 = (bf16[352,512]{1,0:T(8,128)(2,1)}, bf16[352,512]{1,0:T(8,128)(2,1)}, u32[]{:S(2)}, u32[]{:S(2)}) collective-permute-start(bf16[352,512]{1,0:T(8,128)(2,1)} %stacked_rows.4.refs_0_), channel_id=1, source_target_pairs={{0,16},{1,17},{2,18},{3,19},{4,20},{5,21},{6,22},{7,23},{8,24},{9,... | collective-permute-start | bytes 1081352 | tf_op jit(solution)/shard_map/ppermute | solution.py:35
  22.2 71.4 %collective-permute-start.10 = (bf16[160,4096]{1,0:T(8,128)(2,1)}, bf16[160,4096]{1,0:T(8,128)(2,1)S(1)}, u32[]{:S(2)}, u32[]{:S(2)}) collective-permute-start(bf16[160,4096]{1,0:T(8,128)(2,1)} %bitcast.98), channel_id=1, source_target_pairs={{0,64},{1,65},{2,66},{3,67},{4,68},{5,69},{6,70},{7,71},{8,72},{9,... | collective-permute-start | bytes 3932168 | tf_op jit(solution)/shard_map/ppermute | solution.py:45
  24.1 32.9 %collective-permute-start.5 = (bf16[352,512]{1,0:T(8,128)(2,1)}, bf16[352,512]{1,0:T(8,128)(2,1)}, u32[]{:S(2)}, u32[]{:S(2)}) collective-permute-start(bf16[352,512]{1,0:T(8,128)(2,1)} %stacked_rows.4.refs_0_), channel_id=1, source_target_pairs={{0,32},{1,33},{2,34},{3,35},{4,36},{5,37},{6,38},{7,39},{8,40},{9,... | collective-permute-start | bytes 1081352 | tf_op jit(solution)/shard_map/ppermute | solution.py:35
  43.1 31.1 %collective-permute-start.15 = (bf16[704,512]{1,0:T(8,128)(2,1)}, bf16[704,512]{1,0:T(8,128)(2,1)}, u32[]{:S(2)}, u32[]{:S(2)}) collective-permute-start(bf16[704,512]{1,0:T(8,128)(2,1)} %stacked_rows.7), channel_id=1, source_target_pairs={{0,4},{1,5},{2,14},{3,15},{4,8},{5,9},{6,2},{7,3},{8,12},{9,13},{1... | collective-permute-start | bytes 2162696 | tf_op jit(solution)/shard_map/ppermute | solution.py:35
  57.0 10.9 %collective-permute-start.6 = (bf16[352,512]{1,0:T(8,128)(2,1)}, bf16[352,512]{1,0:T(8,128)(2,1)}, u32[]{:S(2)}, u32[]{:S(2)}) collective-permute-start(bf16[352,512]{1,0:T(8,128)(2,1)} %collective-permute-done.5.refs_0_), channel_id=1, source_target_pairs={{0,16},{1,17},{2,18},{3,19},{4,20},{5,21},{6,22},{7,23},{8,24},{9,... | collective-permute-start | bytes 1081352 | tf_op jit(solution)/shard_map/ppermute | solution.py:35
  69.9 29.0 %collective-permute-start.7 = (bf16[704,512]{1,0:T(8,128)(2,1)}, bf16[704,512]{1,0:T(8,128)(2,1)}, u32[]{:S(2)}, u32[]{:S(2)}) collective-permute-start(bf16[704,512]{1,0:T(8,128)(2,1)} %stacked_rows.5), channel_id=1, source_target_pairs={{0,4},{1,5},{2,14},{3,15},{4,8},{5,9},{6,2},{7,3},{8,12},{9,13},{1... | collective-permute-start | bytes 2162696 | tf_op jit(solution)/shard_map/ppermute | solution.py:35
  74.3 26.7 %collective-permute-start.16 = (bf16[704,512]{1,0:T(8,128)(2,1)}, bf16[704,512]{1,0:T(8,128)(2,1)}, u32[]{:S(2)}, u32[]{:S(2)}) collective-permute-start(bf16[704,512]{1,0:T(8,128)(2,1)} %collective-permute-done.15), channel_id=1, source_target_pairs={{0,4},{1,5},{2,14},{3,15},{4,8},{5,9},{6,2},{7,3},{8,12},{9,13},{1... | collective-permute-start | bytes 2162696 | tf_op jit(solution)/shard_map/ppermute | solution.py:35
  78.4 11.0 %collective-permute-start.22 = (s32[16,3]{0,1:T(4,128)S(1)}, s32[16,3]{0,1:T(4,128)S(1)}, u32[]{:S(2)}, u32[]{:S(2)}) collective-permute-start(s32[16,3]{0,1:T(4,128)S(1)} %bitcast.93), channel_id=1, source_target_pairs={{0,1},{1,0},{2,3},{3,2},{4,5},{5,4},{6,7},{7,6},{8,9},{9,8},{10,11... | collective-permute-start | bytes 584 | tf_op jit(solution)/shard_map/ppermute | solution.py:35
  89.4 83.8 %collective-permute-start.1 = (bf16[320,512]{1,0:T(8,128)(2,1)}, bf16[320,512]{1,0:T(8,128)(2,1)}, u32[]{:S(2)}, u32[]{:S(2)}) collective-permute-start(bf16[320,512]{1,0:T(8,128)(2,1)} %pad_maximum_fusion.7), channel_id=1, source_target_pairs={{0,64},{1,65},{2,66},{3,67},{4,68},{5,69},{6,70},{7,71},{8,72},{9,... | collective-permute-start | bytes 983048 | tf_op jit(solution)/shard_map/ppermute | solution.py:45
  98.8 17.3 %collective-permute-start.8 = (bf16[704,512]{1,0:T(8,128)(2,1)}, bf16[704,512]{1,0:T(8,128)(2,1)S(1)}, u32[]{:S(2)}, u32[]{:S(2)}) collective-permute-start(bf16[704,512]{1,0:T(8,128)(2,1)} %collective-permute-done.7), channel_id=1, source_target_pairs={{0,4},{1,5},{2,14},{3,15},{4,8},{5,9},{6,2},{7,3},{8,12},{9,13},{1... | collective-permute-start | bytes 2162696 | tf_op jit(solution)/shard_map/ppermute | solution.py:35
  101.0 20.4 %collective-permute-start.17 = (bf16[704,512]{1,0:T(8,128)(2,1)}, bf16[704,512]{1,0:T(8,128)(2,1)S(1)}, u32[]{:S(2)}, u32[]{:S(2)}) collective-permute-start(bf16[704,512]{1,0:T(8,128)(2,1)} %collective-permute-done.16), channel_id=1, source_target_pairs={{0,4},{1,5},{2,14},{3,15},{4,8},{5,9},{6,2},{7,3},{8,12},{9,13},{1... | collective-permute-start | bytes 2162696 | tf_op jit(solution)/shard_map/ppermute | solution.py:35
  116.1 13.1 %collective-permute-start.9 = (bf16[704,512]{1,0:T(8,128)(2,1)S(1)}, bf16[704,512]{1,0:T(8,128)(2,1)S(1)}, u32[]{:S(2)}, u32[]{:S(2)}) collective-permute-start(bf16[704,512]{1,0:T(8,128)(2,1)S(1)} %collective-permute-done.8), channel_id=1, source_target_pairs={{0,4},{1,5},{2,14},{3,15},{4,8},{5,9},{6,2},{7,3},{8,12},{9,13},{1... | collective-permute-start | bytes 2162696 | tf_op jit(solution)/shard_map/ppermute | solution.py:35
  122.5 24.6 %collective-permute-start.18 = (bf16[400,512]{1,0:T(8,128)(2,1)S(1)}, bf16[400,512]{1,0:T(8,128)(2,1)S(1)}, u32[]{:S(2)}, u32[]{:S(2)}) collective-permute-start(bf16[400,512]{1,0:T(8,128)(2,1)S(1)} %pad_maximum_fusion.6), channel_id=1, source_target_pairs={{0,1},{1,0},{2,3},{3,2},{4,5},{5,4},{6,7},{7,6},{8,9},{9,8},{10,11... | collective-permute-start | bytes 1228808 | tf_op jit(solution)/shard_map/ppermute | solution.py:35
  130.3 46.2 %collective-permute-start.11 = (bf16[160,1024]{1,0:T(8,128)(2,1)}, bf16[160,1024]{1,0:T(8,128)(2,1)S(1)}, u32[]{:S(2)}, u32[]{:S(2)}) collective-permute-start(bf16[160,1024]{1,0:T(8,128)(2,1)} %get-tuple-element.27), channel_id=1, source_target_pairs={{0,4},{1,5},{2,6},{3,7},{4,8},{5,9},{6,10},{7,11},{8,12},{9,13},{1... | collective-permute-start | bytes 983048 | tf_op jit(solution)/shard_map/ppermute | solution.py:35
  132.6 43.8 %collective-permute-start.12 = (bf16[160,1024]{1,0:T(8,128)(2,1)}, bf16[160,1024]{1,0:T(8,128)(2,1)S(1)}, u32[]{:S(2)}, u32[]{:S(2)}) collective-permute-start(bf16[160,1024]{1,0:T(8,128)(2,1)} %get-tuple-element.28), channel_id=1, source_target_pairs={{0,8},{1,9},{2,10},{3,11},{4,12},{5,13},{6,14},{7,15},{8,0},{9,1},... | collective-permute-start | bytes 983048 | tf_op jit(solution)/shard_map/ppermute | solution.py:35
  137.9 38.6 %collective-permute-start.13 = (bf16[160,1024]{1,0:T(8,128)(2,1)S(1)}, bf16[160,1024]{1,0:T(8,128)(2,1)S(1)}, u32[]{:S(2)}, u32[]{:S(2)}) collective-permute-start(bf16[160,1024]{1,0:T(8,128)(2,1)S(1)} %copy-done.15), channel_id=1, source_target_pairs={{0,12},{1,13},{2,14},{3,15},{4,0},{5,1},{6,2},{7,3},{8,4},{9,5},{1... | collective-permute-start | bytes 983048 | tf_op jit(solution)/shard_map/ppermute | solution.py:35
  147.1 23.3 %collective-permute-start.19 = (bf16[400,512]{1,0:T(8,128)(2,1)S(1)}, bf16[400,512]{1,0:T(8,128)(2,1)S(1)}, u32[]{:S(2)}, u32[]{:S(2)}) collective-permute-start(bf16[400,512]{1,0:T(8,128)(2,1)S(1)} %pad_maximum_fusion.5), channel_id=1, source_target_pairs={{0,1},{1,0},{2,3},{3,2},{4,5},{5,4},{6,7},{7,6},{8,9},{9,8},{10,11... | collective-permute-start | bytes 1228808 | tf_op jit(solution)/shard_map/ppermute | solution.py:35
  170.4 6.1 %collective-permute-start.20 = (bf16[256,512]{1,0:T(8,128)(2,1)S(1)}, bf16[256,512]{1,0:T(8,128)(2,1)}, u32[]{:S(2)}, u32[]{:S(2)}) collective-permute-start(bf16[256,512]{1,0:T(8,128)(2,1)S(1)} %slice.161), channel_id=1, source_target_pairs={{0,2},{1,3},{2,0},{3,1},{4,6},{5,7},{6,4},{7,5},{8,10},{9,11},{10,... | collective-permute-start | bytes 786440 | tf_op jit(solution)/shard_map/ppermute | solution.py:35
  173.2 3.4 %collective-permute-start.21 = (bf16[256,512]{1,0:T(8,128)(2,1)S(1)}, bf16[256,512]{1,0:T(8,128)(2,1)S(1)}, u32[]{:S(2)}, u32[]{:S(2)}) collective-permute-start(bf16[256,512]{1,0:T(8,128)(2,1)S(1)} %slice.162), channel_id=1, source_target_pairs={{0,2},{1,3},{2,0},{3,1},{4,6},{5,7},{6,4},{7,5},{8,10},{9,11},{10,... | collective-permute-start | bytes 786440 | tf_op jit(solution)/shard_map/ppermute | solution.py:35
  185.0 10.9 %collective-permute-start.23 = (bf16[128,512]{1,0:T(8,128)(2,1)}, bf16[128,512]{1,0:T(8,128)(2,1)S(1)}, u32[]{:S(2)}, u32[]{:S(2)}) collective-permute-start(bf16[128,512]{1,0:T(8,128)(2,1)} %get-tuple-element.33), channel_id=1, source_target_pairs={{0,64},{1,65},{2,66},{3,67},{4,68},{5,69},{6,70},{7,71},{8,72},{9,... | collective-permute-start | bytes 393224 | tf_op jit(solution)/shard_map/ppermute | solution.py:45
  189.0 12.5 %collective-permute-start.24 = (bf16[128,512]{1,0:T(8,128)(2,1)}, bf16[128,512]{1,0:T(8,128)(2,1)S(1)}, u32[]{:S(2)}, u32[]{:S(2)}) collective-permute-start(bf16[128,512]{1,0:T(8,128)(2,1)} %get-tuple-element.34), channel_id=1, source_target_pairs={{0,65},{1,64},{2,67},{3,66},{4,69},{5,68},{6,71},{7,70},{8,73},{9,... | collective-permute-start | bytes 393224 | tf_op jit(solution)/shard_map/ppermute | solution.py:45
  201.6 15.3 %collective-permute-start.25 = (bf16[256,512]{1,0:T(8,128)(2,1)S(1)}, bf16[256,512]{1,0:T(8,128)(2,1)S(1)}, u32[]{:S(2)}, u32[]{:S(2)}) collective-permute-start(bf16[256,512]{1,0:T(8,128)(2,1)S(1)} %pad_maximum_fusion.11), channel_id=1, source_target_pairs={{0,32},{1,33},{2,34},{3,35},{4,36},{5,37},{6,38},{7,39},{8,40},{9,... | collective-permute-start | bytes 786440 | tf_op jit(solution)/shard_map/ppermute | solution.py:35
  206.0 22.5 %collective-permute-start.28 = (bf16[640,1024]{1,0:T(8,128)(2,1)}, bf16[640,1024]{1,0:T(8,128)(2,1)S(1)}, u32[]{:S(2)}, u32[]{:S(2)}) collective-permute-start(bf16[640,1024]{1,0:T(8,128)(2,1)} %stacked_rows.6), channel_id=1, source_target_pairs={{0,2},{1,3},{2,0},{3,1},{4,6},{5,7},{6,4},{7,5},{8,10},{9,11},{10,... | collective-permute-start | bytes 3932168 | tf_op jit(solution)/shard_map/ppermute | solution.py:35
  209.5 13.0 %collective-permute-start.26 = (bf16[256,512]{1,0:T(8,128)(2,1)S(1)}, bf16[256,512]{1,0:T(8,128)(2,1)S(1)}, u32[]{:S(2)}, u32[]{:S(2)}) collective-permute-start(bf16[256,512]{1,0:T(8,128)(2,1)S(1)} %pad_maximum_fusion.11), channel_id=1, source_target_pairs={{0,16},{1,17},{2,18},{3,19},{4,20},{5,21},{6,22},{7,23},{8,24},{9,... | collective-permute-start | bytes 786440 | tf_op jit(solution)/shard_map/ppermute | solution.py:35
  216.9 11.2 %collective-permute-start.27 = (bf16[256,512]{1,0:T(8,128)(2,1)S(1)}, bf16[256,512]{1,0:T(8,128)(2,1)S(1)}, u32[]{:S(2)}, u32[]{:S(2)}) collective-permute-start(bf16[256,512]{1,0:T(8,128)(2,1)S(1)} %collective-permute-done.25), channel_id=1, source_target_pairs={{0,16},{1,17},{2,18},{3,19},{4,20},{5,21},{6,22},{7,23},{8,24},{9,... | collective-permute-start | bytes 786440 | tf_op jit(solution)/shard_map/ppermute | solution.py:35
  230.0 10.7 %collective-permute-start.29 = (bf16[320,512]{1,0:T(8,128)(2,1)S(1)}, bf16[320,512]{1,0:T(8,128)(2,1)S(1)}, u32[]{:S(2)}, u32[]{:S(2)}) collective-permute-start(bf16[320,512]{1,0:T(8,128)(2,1)S(1)} %pad_maximum_fusion.8), channel_id=1, source_target_pairs={{0,12},{1,13},{2,14},{3,15},{4,0},{5,1},{6,2},{7,3},{8,4},{9,5},{1... | collective-permute-start | bytes 983048 | tf_op jit(solution)/shard_map/ppermute | solution.py:35
  232.5 12.0 %collective-permute-start.30 = (bf16[320,512]{1,0:T(8,128)(2,1)S(1)}, bf16[320,512]{1,0:T(8,128)(2,1)S(1)}, u32[]{:S(2)}, u32[]{:S(2)}) collective-permute-start(bf16[320,512]{1,0:T(8,128)(2,1)S(1)} %pad_maximum_fusion.9), channel_id=1, source_target_pairs={{0,8},{1,9},{2,10},{3,11},{4,12},{5,13},{6,14},{7,15},{8,0},{9,1},... | collective-permute-start | bytes 983048 | tf_op jit(solution)/shard_map/ppermute | solution.py:35
  235.9 16.6 %collective-permute-start.31 = (bf16[320,512]{1,0:T(8,128)(2,1)S(1)}, bf16[320,512]{1,0:T(8,128)(2,1)S(1)}, u32[]{:S(2)}, u32[]{:S(2)}) collective-permute-start(bf16[320,512]{1,0:T(8,128)(2,1)S(1)} %pad_maximum_fusion.10), channel_id=1, source_target_pairs={{0,4},{1,5},{2,6},{3,7},{4,8},{5,9},{6,10},{7,11},{8,12},{9,13},{1... | collective-permute-start | bytes 983048 | tf_op jit(solution)/shard_map/ppermute | solution.py:35
  (19 other events, 239.1 us)
